TPU v7x, 256 devices: a whole 4x4x8 slice. The times are simulated.
256 devices in a mesh: group: 2 (over z_lo), dp: 16 (over y, z_hi), mp: 8 (over x, core).
Axes of the slice: x: 4, y: 4, z: 8 (z_hi: 4, z_lo: 2; z = z_hi * 2 + z_lo), core: 2. Of those that a mesh axis runs over, the one named last changes fastest.
Arguments:
- teacher_hidden: bfloat16 [2048, 8192], P('dp', ('group', 'mp')), may hold values from -6 to 6
- teacher_gain: bfloat16 [8192], P(('group', 'mp')), may hold values from 0.25 to 1.75
- teacher_head: bfloat16 [8192, 8192], P(('group', 'mp')), may hold values from -0.198873782 to 0.198873782
- student_hidden: bfloat16 [2048, 4096], P('dp'), may hold values from -6 to 6
- student_head: bfloat16 [4096, 8192], P('dp', ('group', 'mp')), may hold values from -0.28125 to 0.28125
- depth_cut: int32 [32], P('dp'), may hold values from 1 to 4
Outputs:
- kl_terms: float32 [4, 2048], P(None, 'dp')
- hidden_grad: float32 [2048, 4096], P('dp', ('group', 'mp'))
- head_grad: float32 [4096, 8192], P('dp', ('group', 'mp'))
Inputs may be any that keep to these rules, and one draw needn't show every extreme that they name: `depth_cut`: each sample's number of codebooks kept.
All inputs are finite; a program needn't handle non-finite values.
Results may differ from a plain program's by a relative error of at most 0.0053.
Values may be sent and summed in bfloat16 or wider, within the bound.
No kernel may reach another device: no remote copies, remote signals or barrier semaphores. Data moves between devices by JAX's collectives and lax.ppermute only.
A program may use at most 128 MiB of HBM per device.

v0:
```python
import jax
import jax.numpy as jnp
from jax import lax
from jax.experimental import pallas as pl
from jax.experimental.pallas import tpu as pltpu
from jax.sharding import PartitionSpec as P

DT = 8192
C = 4
FRAMES = 64
epsilon = 1e-05

ALL = ("group", "dp", "mp")
PLANE = ("group", "mp")


def place(zl, y, zh, x, core):
    return zl * 128 + (y % 4 * 4 + zh % 4) * 8 + x % 4 * 2 + core


def send(value, target):
    pairs = []
    for zl in range(2):
        for y in range(4):
            for zh in range(4):
                for x in range(4):
                    for core in range(2):
                        pairs.append((place(zl, y, zh, x, core), place(*target(zl, y, zh, x, core))))
    return lax.ppermute(value, ALL, pairs)


def to_y(value, step):
    return send(value, lambda zl, y, zh, x, core: (zl, y + step, zh, x, core))


def to_zh(value, step):
    return send(value, lambda zl, y, zh, x, core: (zl, y, zh + step, x, core))


def to_x(value, step):
    return send(value, lambda zl, y, zh, x, core: (zl, y, zh, x + step, core))


def to_zl(value):
    return send(value, lambda zl, y, zh, x, core: (1 - zl, y, zh, x, core))


def to_core(value):
    return send(value, lambda zl, y, zh, x, core: (zl, y, zh, x, 1 - core))


def pick_kernel(order_ref, hidden_ref, own_ref, *half_refs):
    def block(i):
        return hidden_ref[:, pl.ds(pl.multiple_of(order_ref[i] * 256, 256), 256)]

    for p in range(4):
        own_ref[p] = block(p)
    for k in (1, 2, 3):
        for p in range(2):
            half_refs[k - 1][p] = block(4 * k + p)


def picked_blocks(hidden, order):
    rows = hidden.shape[0]
    half = jax.ShapeDtypeStruct((2, rows, 256), hidden.dtype)
    return pl.pallas_call(
        pick_kernel,
        in_specs=[pl.BlockSpec(memory_space=pltpu.SMEM), pl.BlockSpec(memory_space=pltpu.VMEM)],
        out_shape=(jax.ShapeDtypeStruct((4, rows, 256), hidden.dtype), half, half, half),
        name="pick",
    )(order, hidden)


def teacher_kernel(order_ref, normed_ref, head_ref, out_ref):
    core = order_ref[8]
    scores = jnp.dot(normed_ref[...], head_ref[...], preferred_element_type=jnp.float32)
    for k in range(2):
        out_ref[k ^ core, 0] = scores[:, 512 * k : 512 * (k + 1)]


def teacher_parts(normed, head, order):
    rows, depth = normed.shape
    return pl.pallas_call(
        teacher_kernel,
        grid_spec=pltpu.PrefetchScalarGridSpec(
            num_scalar_prefetch=1,
            grid=(8,),
            in_specs=[
                pl.BlockSpec((rows, depth), lambda i, order_ref: (0, 0)),
                pl.BlockSpec((depth, 1024), lambda i, order_ref: (0, order_ref[i])),
            ],
            out_specs=pl.BlockSpec((2, 1, rows, 512), lambda i, order_ref: (0, i, 0, 0)),
        ),
        out_shape=jax.ShapeDtypeStruct((2, 8, rows, 512), jnp.float32),
        name="teacher",
    )(order, normed, head)


def student_kernel(core_ref, *refs):
    own_ref, near_refs, far_refs, head_refs = refs[0], refs[1:4], refs[4:7], refs[7:11]
    out_ref, hidden_ref = refs[11:]
    core = core_ref[0]
    for p in range(2):
        hidden_ref[0, 2 * core + p] = own_ref[p]
        hidden_ref[0, 2 * (1 - core) + p] = own_ref[2 + p]
        for k in (1, 2, 3):
            hidden_ref[k, 2 * core + p] = near_refs[k - 1][p]
            hidden_ref[k, 2 * (1 - core) + p] = far_refs[k - 1][p]
    for k in range(4):
        total = None
        for j in range(4):
            term = jnp.dot(hidden_ref[k, j], head_refs[j][...], preferred_element_type=jnp.float32)
            total = term if total is None else total + term
        out_ref[k] = total


def student_parts(core, own, near, far, head_slots):
    vmem = pl.BlockSpec(memory_space=pltpu.VMEM)
    return pl.pallas_call(
        student_kernel,
        in_specs=[pl.BlockSpec(memory_space=pltpu.SMEM)] + [vmem] * 11,
        out_shape=(
            jax.ShapeDtypeStruct((4, 128, 512), jnp.float32),
            jax.ShapeDtypeStruct((4, 4, 128, 256), jnp.bfloat16),
        ),
        name="student",
    )(core.reshape(1), own, *near, *far, *head_slots)


def head_grad_kernel(*refs):
    hidden_ref, grad_refs, own_ref, out_ref = refs[0], refs[1:5], refs[5], refs[6]
    for j in range(4):
        total = None
        for k in range(4):
            term = lax.dot_general(
                hidden_ref[k, j], grad_refs[k][...], (((0,), (0,)), ((), ())), preferred_element_type=jnp.float32
            )
            total = term if total is None else total + term
        if j == 0:
            own_ref[...] = total
        else:
            out_ref[j - 1] = total.astype(out_ref.dtype)


def head_grad_parts(hidden, grad_slots):
    return pl.pallas_call(
        head_grad_kernel,
        out_shape=(
            jax.ShapeDtypeStruct((256, 512), jnp.float32),
            jax.ShapeDtypeStruct((3, 256, 512), jnp.bfloat16),
        ),
        name="head_grad",
    )(hidden, *grad_slots)


def hidden_grad_kernel(*refs):
    grad_refs, head_refs, out_ref = refs[:4], refs[4:8], refs[8]
    for k in range(4):
        for j in range(4):
            out_ref[4 * k + j] = lax.dot_general(
                grad_refs[k][...], head_refs[j][...], (((1,), (1,)), ((), ())), preferred_element_type=jnp.float32
            ).astype(out_ref.dtype)


def hidden_grad_parts(grad_slots, head_slots):
    return pl.pallas_call(
        hidden_grad_kernel,
        out_shape=jax.ShapeDtypeStruct((16, 128, 256), jnp.bfloat16),
        name="hidden_grad",
    )(*grad_slots, *head_slots)


def step(teacher_hidden, teacher_gain, teacher_head, student_hidden, student_head, depth_cut):
    f32, f16, bf16 = jnp.float32, jnp.float16, jnp.bfloat16
    zl = lax.axis_index("group")
    dp, mp = lax.axis_index("dp"), lax.axis_index("mp")
    y, zh, x, core = dp // 4, dp % 4, mp // 2, mp % 2

    hidden_float = teacher_hidden.astype(f32)
    own_squares = jnp.sum(hidden_float * hidden_float, axis=1)
    squares = lax.all_to_all(
        jnp.broadcast_to(own_squares[None, None], (16, 1, 128)), PLANE, 0, 0, tiled=True
    ).sum(axis=(0, 1))

    steps = jnp.arange(4, dtype=jnp.int32)
    order = (((y - steps - 2 * core) % 4 * 4)[None, :] + ((zh + steps) % 4)[:, None]).reshape(16)
    own, *halves = picked_blocks(student_hidden, order)
    near = [to_zh(halves[k - 1], k) for k in (1, 2, 3)]
    head_slots = [student_head] + [to_y(student_head, j) for j in (1, 2, 3)]
    far = [to_core(half) for half in near]

    row_scale = lax.rsqrt(squares / DT + epsilon)
    normed = (hidden_float * row_scale[:, None] * teacher_gain.astype(f32)[None, :]).astype(bf16)
    spots = jnp.arange(8, dtype=jnp.int32)
    order = (zl ^ (spots % 2)) * 4 + (x + spots // 2) % 4
    parts = teacher_parts(normed, teacher_head, jnp.append(order, core)).reshape(2, 4, 2, 128, 512)
    by_core = parts[0] + to_core(parts[1].astype(f16)).astype(f32)
    by_x = by_core[0]
    for step in (1, 2, 3):
        by_x = by_x + to_x(by_core[step].astype(f16), step).astype(f32)
    teacher = by_x[0] + to_zl(by_x[1].astype(f16)).astype(f32)

    parts, hidden = student_parts(core, own, near, far, head_slots)
    student = parts[0]
    for k in (1, 2, 3):
        student = student + to_zh(parts[k].astype(f16), -k).astype(f32)

    teacher_max = jnp.max(teacher, axis=1)
    student_max = jnp.max(student, axis=1)
    teacher_exp = jnp.exp(teacher - teacher_max[:, None])
    student_exp = jnp.exp(student - student_max[:, None])
    stats = jnp.stack(
        [
            teacher_max,
            jnp.sum(teacher_exp, axis=1),
            jnp.sum(teacher_exp * (teacher - student), axis=1),
            student_max,
            jnp.sum(student_exp, axis=1),
        ]
    )
    every = jnp.stack(
        [
            stats,
            to_core(stats),
            send(stats, lambda zl, y, zh, x, core: (zl, y, zh, x ^ 1, core)),
            send(stats, lambda zl, y, zh, x, core: (zl, y, zh, x ^ 1, 1 - core)),
        ]
    )
    teacher_top = jnp.max(every[:, 0], axis=0)
    student_top = jnp.max(every[:, 3], axis=0)
    teacher_shift = jnp.exp(every[:, 0] - teacher_top)
    student_shift = jnp.exp(every[:, 3] - student_top)
    teacher_sum = jnp.sum(every[:, 1] * teacher_shift, axis=0)
    student_sum = jnp.sum(every[:, 4] * student_shift, axis=0)
    weighted = jnp.sum(every[:, 2] * teacher_shift, axis=0)
    divergence = (
        weighted / teacher_sum - (teacher_top + jnp.log(teacher_sum)) + (student_top + jnp.log(student_sum))
    )
    book = zl * 2 + x // 2
    depth_rows = jnp.repeat(depth_cut, FRAMES)
    depth_weight = (book < depth_rows).astype(f32) / depth_rows.astype(f32)
    teacher_factor = teacher_shift[0] / teacher_sum * depth_weight
    student_factor = student_shift[0] / student_sum * depth_weight
    score_grad = (
        student_exp * student_factor[:, None] - teacher_exp * teacher_factor[:, None]
    ).astype(bf16)

    own_kl = (divergence * depth_weight)[None]
    kl = [
        own_kl,
        send(own_kl, lambda zl, y, zh, x, core: (zl, y, zh, x ^ 2, core)),
        send(own_kl, lambda zl, y, zh, x, core: (1 - zl, y, zh, x, core)),
        send(own_kl, lambda zl, y, zh, x, core: (1 - zl, y, zh, x ^ 2, core)),
    ]
    kl = jnp.concatenate(kl)
    kl_terms = jnp.concatenate(
        [lax.dynamic_slice_in_dim(kl, book ^ i, 1, 0) for i in range(C)]
    )

    grad_slots = [score_grad] + [to_zh(score_grad, k) for k in (1, 2, 3)]
    parts = hidden_grad_parts(grad_slots, head_slots)
    parts = lax.all_to_all(parts, PLANE, 0, 0, tiled=True)
    hidden_grad = jnp.sum(parts.astype(f32), axis=0)
    head_grad, parts = head_grad_parts(hidden, grad_slots)
    for j in (1, 2, 3):
        head_grad = head_grad + to_y(parts[j - 1], -j).astype(f32)

    def home(zl, y, zh, x, core):
        k, j = zl * 2 + x // 2, x % 2 * 2 + core
        spot = (y - j) % 4 * 4 + zh
        return spot // 8, y, zh - k, spot % 8 // 2, spot % 2

    hidden_grad = send(hidden_grad, home)
    return (kl_terms, hidden_grad, head_grad)


def solution(mesh):
    return jax.shard_map(
        step,
        mesh=mesh,
        in_specs=(
            P("dp", PLANE),
            P(PLANE),
            P(PLANE, None),
            P("dp", None),
            P("dp", PLANE),
            P("dp"),
        ),
        out_specs=(P(None, "dp"), P("dp", PLANE), P("dp", PLANE)),
        check_vma=False,
    )
```

profile of v0, /device:TPU:2, one launch (start us, length us, event | category | flops | bytes accessed | tf_op | source)
XLA Modules:
  0.0 156.9 jit_solution(14829203615191814601)
XLA Ops:
  2.3 6.2 %all-to-all-start = ((f32[16,1,128]{2,1,0:T(1,128)}), f32[16,1,128]{2,1,0:T(1,128)S(1)}, u32[]{:S(2)}, u32[]{:S(2)}) async-start(f32[16,1,128]{2,1,0:T(1,128)} %broadcast_in_dim.4), calls=%async_computation | async-start | bytes 16384 | tf_op jit(solution)/shard_map/all_to_all | solution.py:181
  9.7 3.4 %all-to-all-done = f32[16,1,128]{2,1,0:T(1,128)S(1)} async-done(((f32[16,1,128]{2,1,0:T(1,128)}), f32[16,1,128]{2,1,0:T(1,128)S(1)}, u32[]{:S(2)}, u32[]{:S(2)}) %all-to-all-start) | async-done | bytes 8224 | tf_op jit(solution)/shard_map/all_to_all | solution.py:181
  14.8 9.3 %teacher.1 = f32[2,8,128,512]{3,2,1,0:T(8,128)} custom-call(s32[9]{0:T(128)} %pad_add_fusion.order_ref, bf16[128,512]{1,0:T(8,128)(2,1)} %fusion.5.normed_ref, bf16[512,8192]{1,0:T(8,128)(2,1)} %head_ref.1), custom_call_target="tpu_custom_call" | custom-call | tf_op jit(solution)/shard_map/teacher/pallas_call | solution.py:83
  24.1 2.8 %slice_convert_fusion = (f16[1,8,128,512]{3,2,1,0:T(8,128)(2,1)S(1)}, f32[1,8,128,512]{3,2,1,0:T(8,128)S(1)}) fusion(f32[2,8,128,512]{3,2,1,0:T(8,128)} %teacher.1), kind=kLoop, calls=%fused_computation | loop fusion | flops 524288 | bytes 7340032 | tf_op jit(solution)/shard_map/convert.7
  27.7 2.1 %pick.1 = (bf16[4,128,256]{2,1,0:T(8,128)(2,1)}, bf16[2,128,256]{2,1,0:T(8,128)(2,1)}, bf16[2,128,256]{2,1,0:T(8,128)(2,1)}, bf16[2,128,256]{2,1,0:T(8,128)(2,1)}) custom-call(s32[16]{0:T(128)} %add.189.order_ref, bf16[128,4096]{1,0:T(8,128)(2,1)} %hidden_ref.1), custom_call_target="tpu_custom_call" | custom-call | tf_op jit(solution)/shard_map/pick/pallas_call | solution.py:66
  29.9 3.3 %collective-permute-start.5 = (bf16[2,128,256]{2,1,0:T(8,128)(2,1)}, bf16[2,128,256]{2,1,0:T(8,128)(2,1)S(1)}, u32[]{:S(2)}, u32[]{:S(2)}) collective-permute-start(bf16[2,128,256]{2,1,0:T(8,128)(2,1)} %get-tuple-element.12), channel_id=1, source_target_pairs={{0,8},{1,9},{2,10},{3,11},{4,12},{5,13},{6,14},{7,15},{8,16},{9,17... | collective-permute-start | bytes 393224 | tf_op jit(solution)/shard_map/ppermute | solution.py:29
  34.7 2.9 %collective-permute-start.12 = (bf16[256,512]{1,0:T(8,128)(2,1)S(1)}, bf16[256,512]{1,0:T(8,128)(2,1)}, u32[]{:S(2)}, u32[]{:S(2)}) collective-permute-start(bf16[256,512]{1,0:T(8,128)(2,1)S(1)} %copy-done.1), channel_id=1, source_target_pairs={{0,64},{1,65},{2,66},{3,67},{4,68},{5,69},{6,70},{7,71},{8,72},{9,... | collective-permute-start | bytes 786440 | tf_op jit(solution)/shard_map/ppermute | solution.py:29
  37.6 4.5 %collective-permute-start.6 = (bf16[2,128,256]{2,1,0:T(8,128)(2,1)}, bf16[2,128,256]{2,1,0:T(8,128)(2,1)S(1)}, u32[]{:S(2)}, u32[]{:S(2)}) collective-permute-start(bf16[2,128,256]{2,1,0:T(8,128)(2,1)} %get-tuple-element.13), channel_id=1, source_target_pairs={{0,16},{1,17},{2,18},{3,19},{4,20},{5,21},{6,22},{7,23},{8,24},{9,... | collective-permute-start | bytes 393224 | tf_op jit(solution)/shard_map/ppermute | solution.py:29
  42.5 2.8 %collective-permute-start.7 = (bf16[2,128,256]{2,1,0:T(8,128)(2,1)}, bf16[2,128,256]{2,1,0:T(8,128)(2,1)S(1)}, u32[]{:S(2)}, u32[]{:S(2)}) collective-permute-start(bf16[2,128,256]{2,1,0:T(8,128)(2,1)} %get-tuple-element.14), channel_id=1, source_target_pairs={{0,24},{1,25},{2,26},{3,27},{4,28},{5,29},{6,30},{7,31},{8,0},{9,1... | collective-permute-start | bytes 393224 | tf_op jit(solution)/shard_map/ppermute | solution.py:29
  45.3 3.0 %fusion.26 = (f16[4,2,128,512]{3,2,1,0:T(8,128)(2,1)S(1)}, f32[4,2,128,512]{3,2,1,0:T(8,128)}) fusion(f32[4,2,128,512]{3,2,1,0:T(8,128)S(1)} %bitcast.81, f16[4,2,128,512]{3,2,1,0:T(8,128)(2,1)} %collective-permute-done), kind=kLoop, calls=%fused_computation.86 | loop fusion | flops 1572864 | bytes 6291456 | tf_op jit(solution)/shard_map/convert.6
  49.5 2.2 %collective-permute-start.13 = (bf16[256,512]{1,0:T(8,128)(2,1)S(1)}, bf16[256,512]{1,0:T(8,128)(2,1)S(1)}, u32[]{:S(2)}, u32[]{:S(2)}) collective-permute-start(bf16[256,512]{1,0:T(8,128)(2,1)S(1)} %copy-done.1), channel_id=1, source_target_pairs={{0,96},{1,97},{2,98},{3,99},{4,100},{5,101},{6,102},{7,103},{8,104... | collective-permute-start | bytes 786440 | tf_op jit(solution)/shard_map/ppermute | solution.py:29
  51.6 2.5 %collective-permute-done.7.refs_3_ = bf16[2,128,256]{2,1,0:T(8,128)(2,1)S(1)} collective-permute-done((bf16[2,128,256]{2,1,0:T(8,128)(2,1)}, bf16[2,128,256]{2,1,0:T(8,128)(2,1)S(1)}, u32[]{:S(2)}, u32[]{:S(2)}) %collective-permute-start.7) | collective-permute-done | bytes 131104 | tf_op jit(solution)/shard_map/ppermute | solution.py:29
  58.2 2.1 %collective-permute-start.1 = (f16[2,128,512]{2,1,0:T(8,128)(2,1)S(1)}, f16[2,128,512]{2,1,0:T(8,128)(2,1)S(1)}, u32[]{:S(2)}, u32[]{:S(2)}) collective-permute-start(f16[2,128,512]{2,1,0:T(8,128)(2,1)S(1)} %get-tuple-element.33), channel_id=1, source_target_pairs={{0,2},{1,3},{2,4},{3,5},{4,6},{5,7},{6,0},{7,1},{8,10},{9,11},{10,... | collective-permute-start | bytes 786440 | tf_op jit(solution)/shard_map/ppermute | solution.py:29
  61.0 3.3 %student.1 = (f32[4,128,512]{2,1,0:T(8,128)}, bf16[4,4,128,256]{3,2,1,0:T(8,128)(2,1)}) custom-call(s32[1]{0:T(128)} %bitcast.core_ref, bf16[4,128,256]{2,1,0:T(8,128)(2,1)} %get-tuple-element.11.refs_0_, bf16[2,128,256]{2,1,0:T(8,128)(2,1)} %copy-done.8, bf16[2,128,256]{2,1,0:T(8,128)(2,1)} %copy-done.9, bf16[2,128,256]{2,1,0:T(8,128)(2,1)} %copy-done.10, ...), custom_call_target="tpu_custom_call" | custom-call | tf_op jit(solution)/shard_map/student/pallas_call | solution.py:119
  65.7 1.8 %collective-permute-start.16 = (f16[128,512]{1,0:T(8,128)(2,1)S(1)}, f16[128,512]{1,0:T(8,128)(2,1)S(1)}, u32[]{:S(2)}, u32[]{:S(2)}) collective-permute-start(f16[128,512]{1,0:T(8,128)(2,1)S(1)} %get-tuple-element.40), channel_id=1, source_target_pairs={{0,8},{1,9},{2,10},{3,11},{4,12},{5,13},{6,14},{7,15},{8,16},{9,17... | collective-permute-start | bytes 393224 | tf_op jit(solution)/shard_map/ppermute | solution.py:29
  67.5 4.3 %collective-permute-start.15 = (f16[128,512]{1,0:T(8,128)(2,1)S(1)}, f16[128,512]{1,0:T(8,128)(2,1)S(1)}, u32[]{:S(2)}, u32[]{:S(2)}) collective-permute-start(f16[128,512]{1,0:T(8,128)(2,1)S(1)} %get-tuple-element.41), channel_id=1, source_target_pairs={{0,16},{1,17},{2,18},{3,19},{4,20},{5,21},{6,22},{7,23},{8,24},{9,... | collective-permute-start | bytes 393224 | tf_op jit(solution)/shard_map/ppermute | solution.py:29
  71.8 2.9 %collective-permute-start.14 = (f16[128,512]{1,0:T(8,128)(2,1)S(1)}, f16[128,512]{1,0:T(8,128)(2,1)S(1)}, u32[]{:S(2)}, u32[]{:S(2)}) collective-permute-start(f16[128,512]{1,0:T(8,128)(2,1)S(1)} %get-tuple-element.39), channel_id=1, source_target_pairs={{0,24},{1,25},{2,26},{3,27},{4,28},{5,29},{6,30},{7,31},{8,0},{9,1... | collective-permute-start | bytes 393224 | tf_op jit(solution)/shard_map/ppermute | solution.py:29
  76.8 3.6 %collective-permute-done.15 = f16[128,512]{1,0:T(8,128)(2,1)S(1)} collective-permute-done((f16[128,512]{1,0:T(8,128)(2,1)S(1)}, f16[128,512]{1,0:T(8,128)(2,1)S(1)}, u32[]{:S(2)}, u32[]{:S(2)}) %collective-permute-start.15) | collective-permute-done | bytes 131104 | tf_op jit(solution)/shard_map/ppermute | solution.py:29
  80.4 4.6 %collective-permute-done.14 = f16[128,512]{1,0:T(8,128)(2,1)S(1)} collective-permute-done((f16[128,512]{1,0:T(8,128)(2,1)S(1)}, f16[128,512]{1,0:T(8,128)(2,1)S(1)}, u32[]{:S(2)}, u32[]{:S(2)}) %collective-permute-start.14) | collective-permute-done | bytes 131104 | tf_op jit(solution)/shard_map/ppermute | solution.py:29
  86.1 2.0 %collective-permute-done.4 = f16[128,512]{1,0:T(8,128)(2,1)S(1)} collective-permute-done((f16[128,512]{1,0:T(8,128)(2,1)S(1)}, f16[128,512]{1,0:T(8,128)(2,1)S(1)}, u32[]{:S(2)}, u32[]{:S(2)}) %collective-permute-start.4) | collective-permute-done | bytes 131104 | tf_op jit(solution)/shard_map/ppermute | solution.py:29
  94.0 2.5 %collective-permute-start.24 = (bf16[128,512]{1,0:T(8,128)(2,1)S(1)}, bf16[128,512]{1,0:T(8,128)(2,1)S(1)}, u32[]{:S(2)}, u32[]{:S(2)}) collective-permute-start(bf16[128,512]{1,0:T(8,128)(2,1)S(1)} %subtract_convert_fusion.refs_0_.refs_1_), channel_id=1, source_target_pairs={{0,16},{1,17},{2,18},{3,19},{4,20},{5,21},{6,22},{7,23},{8,24},{9,... | collective-permute-start | bytes 393224 | tf_op jit(solution)/shard_map/ppermute | solution.py:29
  97.6 7.0 %collective-permute-done.23.refs_1_.refs_2_ = bf16[128,512]{1,0:T(8,128)(2,1)S(1)} collective-permute-done((bf16[128,512]{1,0:T(8,128)(2,1)S(1)}, bf16[128,512]{1,0:T(8,128)(2,1)S(1)}, u32[]{:S(2)}, u32[]{:S(2)}) %collective-permute-start.23) | collective-permute-done | bytes 131104 | tf_op jit(solution)/shard_map/ppermute | solution.py:29
  104.7 3.1 %collective-permute-done.24.refs_2_.refs_3_ = bf16[128,512]{1,0:T(8,128)(2,1)S(1)} collective-permute-done((bf16[128,512]{1,0:T(8,128)(2,1)S(1)}, bf16[128,512]{1,0:T(8,128)(2,1)S(1)}, u32[]{:S(2)}, u32[]{:S(2)}) %collective-permute-start.24) | collective-permute-done | bytes 131104 | tf_op jit(solution)/shard_map/ppermute | solution.py:29
  107.8 1.9 %collective-permute-done.25.refs_3_.refs_4_ = bf16[128,512]{1,0:T(8,128)(2,1)S(1)} collective-permute-done((bf16[128,512]{1,0:T(8,128)(2,1)S(1)}, bf16[128,512]{1,0:T(8,128)(2,1)S(1)}, u32[]{:S(2)}, u32[]{:S(2)}) %collective-permute-start.25) | collective-permute-done | bytes 131104 | tf_op jit(solution)/shard_map/ppermute | solution.py:29
  110.4 3.9 %hidden_grad.1 = bf16[16,128,256]{2,1,0:T(8,128)(2,1)} custom-call(bf16[128,512]{1,0:T(8,128)(2,1)} %copy-done, bf16[128,512]{1,0:T(8,128)(2,1)} %copy-done.5, bf16[128,512]{1,0:T(8,128)(2,1)} %copy-done.6, bf16[128,512]{1,0:T(8,128)(2,1)} %copy-done.7, bf16[256,512]{1,0:T(8,128)(2,1)} %refs_4_.1, bf16[256,512]{1,0:T(8,128)(2,1)} %copy-done.2, ...), custom_call_target="tpu_custom_call" | custom-call | tf_op jit(solution)/shard_map/hidden_grad/pallas_call | solution.py:166
  114.2 5.2 %all-to-all-start.1 = ((bf16[16,128,256]{2,1,0:T(8,128)(2,1)}), bf16[16,128,256]{2,1,0:T(8,128)(2,1)S(1)}, u32[]{:S(2)}, u32[]{:S(2)}) async-start(bf16[16,128,256]{2,1,0:T(8,128)(2,1)} %hidden_grad.1), calls=%async_computation.1 | async-start | bytes 2097152 | tf_op jit(solution)/shard_map/all_to_all | solution.py:262
  119.5 3.1 %collective-permute-start.22 = (f32[1,128]{1,0:T(1,128)S(1)}, f32[1,128]{1,0:T(1,128)S(1)}, u32[]{:S(2)}, u32[]{:S(2)}) collective-permute-start(f32[1,128]{1,0:T(1,128)S(1)} %bitcast_multiply_fusion), channel_id=1, source_target_pairs={{0,132},{1,133},{2,134},{3,135},{4,128},{5,129},{6,130},{7,131},{8... | collective-permute-start | bytes 1544 | tf_op jit(solution)/shard_map/ppermute | solution.py:29
  124.6 10.3 %collective-permute-done.22 = f32[1,128]{1,0:T(1,128)S(1)} collective-permute-done((f32[1,128]{1,0:T(1,128)S(1)}, f32[1,128]{1,0:T(1,128)S(1)}, u32[]{:S(2)}, u32[]{:S(2)}) %collective-permute-start.22) | collective-permute-done | bytes 544 | tf_op jit(solution)/shard_map/ppermute | solution.py:29
  135.0 3.6 %head_grad.1 = (f32[256,512]{1,0:T(8,128)}, bf16[3,256,512]{2,1,0:T(8,128)(2,1)}) custom-call(bf16[4,4,128,256]{3,2,1,0:T(8,128)(2,1)} %get-tuple-element.16.refs_0_, bf16[128,512]{1,0:T(8,128)(2,1)} %copy-done, bf16[128,512]{1,0:T(8,128)(2,1)} %copy-done.5, bf16[128,512]{1,0:T(8,128)(2,1)} %copy-done.6, bf16[128,512]{1,0:T(8,128)(2,1)} %copy-done.7), custom_call_target="tpu_custom_call" | custom-call | tf_op jit(solution)/shard_map/head_grad/pallas_call | solution.py:146
  139.8 3.0 %collective-permute-start.28 = (bf16[256,512]{1,0:T(8,128)(2,1)S(1)}, bf16[256,512]{1,0:T(8,128)(2,1)S(1)}, u32[]{:S(2)}, u32[]{:S(2)}) collective-permute-start(bf16[256,512]{1,0:T(8,128)(2,1)S(1)} %get-tuple-element.38), channel_id=1, source_target_pairs={{0,64},{1,65},{2,66},{3,67},{4,68},{5,69},{6,70},{7,71},{8,72},{9,... | collective-permute-start | bytes 786440 | tf_op jit(solution)/shard_map/ppermute | solution.py:29
  144.1 3.3 %collective-permute-start.26 = (f32[128,256]{1,0:T(8,128)S(1)}, f32[128,256]{1,0:T(8,128)S(1)}, u32[]{:S(2)}, u32[]{:S(2)}) collective-permute-start(f32[128,256]{1,0:T(8,128)S(1)} %convert_reduce_fusion), channel_id=1, source_target_pairs={{0,0},{1,132},{2,128},{3,4},{4,24},{5,156},{6,152},{7,28},{8,9},{9... | collective-permute-start | bytes 393224 | tf_op jit(solution)/shard_map/ppermute | solution.py:29
  147.4 6.7 %collective-permute-done.29 = bf16[256,512]{1,0:T(8,128)(2,1)S(1)} collective-permute-done((bf16[256,512]{1,0:T(8,128)(2,1)S(1)}, bf16[256,512]{1,0:T(8,128)(2,1)S(1)}, u32[]{:S(2)}, u32[]{:S(2)}) %collective-permute-start.29) | collective-permute-done | bytes 262176 | tf_op jit(solution)/shard_map/ppermute | solution.py:29
  (109 shorter events, 32.9 us)
Async XLA Ops:
  2.3 10.8 %all-to-all-start = ((f32[16,1,128]{2,1,0:T(1,128)}), f32[16,1,128]{2,1,0:T(1,128)S(1)}, u32[]{:S(2)}, u32[]{:S(2)}) async-start(f32[16,1,128]{2,1,0:T(1,128)} %broadcast_in_dim.4), calls=%async_computation | async-start | bytes 16384 | tf_op jit(solution)/shard_map/all_to_all | solution.py:181
  26.9 18.4 %collective-permute-start = (f16[4,2,128,512]{3,2,1,0:T(8,128)(2,1)S(1)}, f16[4,2,128,512]{3,2,1,0:T(8,128)(2,1)}, u32[]{:S(2)}, u32[]{:S(2)}) collective-permute-start(f16[4,2,128,512]{3,2,1,0:T(8,128)(2,1)S(1)} %bitcast.82), channel_id=1, source_target_pairs={{0,1},{1,0},{2,3},{3,2},{4,5},{5,4},{6,7},{7,6},{8,9},{9,8},{10,11... | collective-permute-start | bytes 3145736 | tf_op jit(solution)/shard_map/ppermute | solution.py:29
  29.9 12.6 %collective-permute-start.5 = (bf16[2,128,256]{2,1,0:T(8,128)(2,1)}, bf16[2,128,256]{2,1,0:T(8,128)(2,1)S(1)}, u32[]{:S(2)}, u32[]{:S(2)}) collective-permute-start(bf16[2,128,256]{2,1,0:T(8,128)(2,1)} %get-tuple-element.12), channel_id=1, source_target_pairs={{0,8},{1,9},{2,10},{3,11},{4,12},{5,13},{6,14},{7,15},{8,16},{9,17... | collective-permute-start | bytes 393224 | tf_op jit(solution)/shard_map/ppermute | solution.py:29
  33.1 24.4 %collective-permute-start.11 = (bf16[256,512]{1,0:T(8,128)(2,1)S(1)}, bf16[256,512]{1,0:T(8,128)(2,1)S(1)}, u32[]{:S(2)}, u32[]{:S(2)}) collective-permute-start(bf16[256,512]{1,0:T(8,128)(2,1)S(1)} %copy-done.1), channel_id=1, source_target_pairs={{0,32},{1,33},{2,34},{3,35},{4,36},{5,37},{6,38},{7,39},{8,40},{9,... | collective-permute-start | bytes 786440 | tf_op jit(solution)/shard_map/ppermute | solution.py:29
  34.7 25.6 %collective-permute-start.12 = (bf16[256,512]{1,0:T(8,128)(2,1)S(1)}, bf16[256,512]{1,0:T(8,128)(2,1)}, u32[]{:S(2)}, u32[]{:S(2)}) collective-permute-start(bf16[256,512]{1,0:T(8,128)(2,1)S(1)} %copy-done.1), channel_id=1, source_target_pairs={{0,64},{1,65},{2,66},{3,67},{4,68},{5,69},{6,70},{7,71},{8,72},{9,... | collective-permute-start | bytes 786440 | tf_op jit(solution)/shard_map/ppermute | solution.py:29
  37.6 11.8 %collective-permute-start.6 = (bf16[2,128,256]{2,1,0:T(8,128)(2,1)}, bf16[2,128,256]{2,1,0:T(8,128)(2,1)S(1)}, u32[]{:S(2)}, u32[]{:S(2)}) collective-permute-start(bf16[2,128,256]{2,1,0:T(8,128)(2,1)} %get-tuple-element.13), channel_id=1, source_target_pairs={{0,16},{1,17},{2,18},{3,19},{4,20},{5,21},{6,22},{7,23},{8,24},{9,... | collective-permute-start | bytes 393224 | tf_op jit(solution)/shard_map/ppermute | solution.py:29
  42.5 11.6 %collective-permute-start.7 = (bf16[2,128,256]{2,1,0:T(8,128)(2,1)}, bf16[2,128,256]{2,1,0:T(8,128)(2,1)S(1)}, u32[]{:S(2)}, u32[]{:S(2)}) collective-permute-start(bf16[2,128,256]{2,1,0:T(8,128)(2,1)} %get-tuple-element.14), channel_id=1, source_target_pairs={{0,24},{1,25},{2,26},{3,27},{4,28},{5,29},{6,30},{7,31},{8,0},{9,1... | collective-permute-start | bytes 393224 | tf_op jit(solution)/shard_map/ppermute | solution.py:29
  45.3 8.8 %collective-permute-start.8 = (bf16[2,128,256]{2,1,0:T(8,128)(2,1)S(1)}, bf16[2,128,256]{2,1,0:T(8,128)(2,1)S(1)}, u32[]{:S(2)}, u32[]{:S(2)}) collective-permute-start(bf16[2,128,256]{2,1,0:T(8,128)(2,1)S(1)} %collective-permute-done.5.refs_1_), channel_id=1, source_target_pairs={{0,1},{1,0},{2,3},{3,2},{4,5},{5,4},{6,7},{7,6},{8,9},{9,8},{10,11... | collective-permute-start | bytes 393224 | tf_op jit(solution)/shard_map/ppermute | solution.py:29
  49.5 10.8 %collective-permute-start.13 = (bf16[256,512]{1,0:T(8,128)(2,1)S(1)}, bf16[256,512]{1,0:T(8,128)(2,1)S(1)}, u32[]{:S(2)}, u32[]{:S(2)}) collective-permute-start(bf16[256,512]{1,0:T(8,128)(2,1)S(1)} %copy-done.1), channel_id=1, source_target_pairs={{0,96},{1,97},{2,98},{3,99},{4,100},{5,101},{6,102},{7,103},{8,104... | collective-permute-start | bytes 786440 | tf_op jit(solution)/shard_map/ppermute | solution.py:29
  54.1 1.3 collective-permute-start.9
  54.1 2.8 %collective-permute-start.10 = (bf16[2,128,256]{2,1,0:T(8,128)(2,1)S(1)}, bf16[2,128,256]{2,1,0:T(8,128)(2,1)S(1)}, u32[]{:S(2)}, u32[]{:S(2)}) collective-permute-start(bf16[2,128,256]{2,1,0:T(8,128)(2,1)S(1)} %collective-permute-done.7.refs_3_), channel_id=1, source_target_pairs={{0,1},{1,0},{2,3},{3,2},{4,5},{5,4},{6,7},{7,6},{8,9},{9,8},{10,11... | collective-permute-start | bytes 393224 | tf_op jit(solution)/shard_map/ppermute | solution.py:29
  55.5 16.3 %collective-permute-start.3 = (f16[2,128,512]{2,1,0:T(8,128)(2,1)S(1)}, f16[2,128,512]{2,1,0:T(8,128)(2,1)S(1)}, u32[]{:S(2)}, u32[]{:S(2)}) collective-permute-start(f16[2,128,512]{2,1,0:T(8,128)(2,1)S(1)} %get-tuple-element.34), channel_id=1, source_target_pairs={{0,6},{1,7},{2,0},{3,1},{4,2},{5,3},{6,4},{7,5},{8,14},{9,15},{10,... | collective-permute-start | bytes 786440 | tf_op jit(solution)/shard_map/ppermute | solution.py:29
  56.9 17.7 %collective-permute-start.2 = (f16[2,128,512]{2,1,0:T(8,128)(2,1)S(1)}, f16[2,128,512]{2,1,0:T(8,128)(2,1)S(1)}, u32[]{:S(2)}, u32[]{:S(2)}) collective-permute-start(f16[2,128,512]{2,1,0:T(8,128)(2,1)S(1)} %get-tuple-element.35), channel_id=1, source_target_pairs={{0,4},{1,5},{2,6},{3,7},{4,0},{5,1},{6,2},{7,3},{8,12},{9,13},{10,... | collective-permute-start | bytes 786440 | tf_op jit(solution)/shard_map/ppermute | solution.py:29
  58.2 16.4 %collective-permute-start.1 = (f16[2,128,512]{2,1,0:T(8,128)(2,1)S(1)}, f16[2,128,512]{2,1,0:T(8,128)(2,1)S(1)}, u32[]{:S(2)}, u32[]{:S(2)}) collective-permute-start(f16[2,128,512]{2,1,0:T(8,128)(2,1)S(1)} %get-tuple-element.33), channel_id=1, source_target_pairs={{0,2},{1,3},{2,4},{3,5},{4,6},{5,7},{6,0},{7,1},{8,10},{9,11},{10,... | collective-permute-start | bytes 786440 | tf_op jit(solution)/shard_map/ppermute | solution.py:29
  65.7 11.0 %collective-permute-start.16 = (f16[128,512]{1,0:T(8,128)(2,1)S(1)}, f16[128,512]{1,0:T(8,128)(2,1)S(1)}, u32[]{:S(2)}, u32[]{:S(2)}) collective-permute-start(f16[128,512]{1,0:T(8,128)(2,1)S(1)} %get-tuple-element.40), channel_id=1, source_target_pairs={{0,8},{1,9},{2,10},{3,11},{4,12},{5,13},{6,14},{7,15},{8,16},{9,17... | collective-permute-start | bytes 393224 | tf_op jit(solution)/shard_map/ppermute | solution.py:29
  67.5 12.9 %collective-permute-start.15 = (f16[128,512]{1,0:T(8,128)(2,1)S(1)}, f16[128,512]{1,0:T(8,128)(2,1)S(1)}, u32[]{:S(2)}, u32[]{:S(2)}) collective-permute-start(f16[128,512]{1,0:T(8,128)(2,1)S(1)} %get-tuple-element.41), channel_id=1, source_target_pairs={{0,16},{1,17},{2,18},{3,19},{4,20},{5,21},{6,22},{7,23},{8,24},{9,... | collective-permute-start | bytes 393224 | tf_op jit(solution)/shard_map/ppermute | solution.py:29
  71.8 13.2 %collective-permute-start.14 = (f16[128,512]{1,0:T(8,128)(2,1)S(1)}, f16[128,512]{1,0:T(8,128)(2,1)S(1)}, u32[]{:S(2)}, u32[]{:S(2)}) collective-permute-start(f16[128,512]{1,0:T(8,128)(2,1)S(1)} %get-tuple-element.39), channel_id=1, source_target_pairs={{0,24},{1,25},{2,26},{3,27},{4,28},{5,29},{6,30},{7,31},{8,0},{9,1... | collective-permute-start | bytes 393224 | tf_op jit(solution)/shard_map/ppermute | solution.py:29
  75.9 12.2 %collective-permute-start.4 = (f16[128,512]{1,0:T(8,128)(2,1)S(1)}, f16[128,512]{1,0:T(8,128)(2,1)S(1)}, u32[]{:S(2)}, u32[]{:S(2)}) collective-permute-start(f16[128,512]{1,0:T(8,128)(2,1)S(1)} %fusion.11), channel_id=1, source_target_pairs={{0,128},{1,129},{2,130},{3,131},{4,132},{5,133},{6,134},{7,135},{8... | collective-permute-start | bytes 393224 | tf_op jit(solution)/shard_map/ppermute | solution.py:29
  88.5 3.1 %collective-permute-start.19 = (f32[5,128]{1,0:T(8,128)S(1)}, f32[5,128]{1,0:T(8,128)S(1)}, u32[]{:S(2)}, u32[]{:S(2)}) collective-permute-start(f32[5,128]{1,0:T(8,128)S(1)} %stack.38), channel_id=1, source_target_pairs={{0,3},{1,2},{2,1},{3,0},{4,7},{5,6},{6,5},{7,4},{8,11},{9,10},{10,... | collective-permute-start | bytes 7688 | tf_op jit(solution)/shard_map/ppermute | solution.py:29
  88.6 3.7 %collective-permute-start.18 = (f32[5,128]{1,0:T(8,128)S(1)}, f32[5,128]{1,0:T(8,128)S(1)}, u32[]{:S(2)}, u32[]{:S(2)}) collective-permute-start(f32[5,128]{1,0:T(8,128)S(1)} %stack.38), channel_id=1, source_target_pairs={{0,2},{1,3},{2,0},{3,1},{4,6},{5,7},{6,4},{7,5},{8,10},{9,11},{10,... | collective-permute-start | bytes 7688 | tf_op jit(solution)/shard_map/ppermute | solution.py:29
  89.2 3.1 %collective-permute-start.17 = (f32[5,128]{1,0:T(8,128)S(1)}, f32[5,128]{1,0:T(8,128)S(1)}, u32[]{:S(2)}, u32[]{:S(2)}) collective-permute-start(f32[5,128]{1,0:T(8,128)S(1)} %stack.38), channel_id=1, source_target_pairs={{0,1},{1,0},{2,3},{3,2},{4,5},{5,4},{6,7},{7,6},{8,9},{9,8},{10,11... | collective-permute-start | bytes 7688 | tf_op jit(solution)/shard_map/ppermute | solution.py:29
  92.6 12.1 %collective-permute-start.23 = (bf16[128,512]{1,0:T(8,128)(2,1)S(1)}, bf16[128,512]{1,0:T(8,128)(2,1)S(1)}, u32[]{:S(2)}, u32[]{:S(2)}) collective-permute-start(bf16[128,512]{1,0:T(8,128)(2,1)S(1)} %subtract_convert_fusion.refs_0_.refs_1_), channel_id=1, source_target_pairs={{0,8},{1,9},{2,10},{3,11},{4,12},{5,13},{6,14},{7,15},{8,16},{9,17... | collective-permute-start | bytes 393224 | tf_op jit(solution)/shard_map/ppermute | solution.py:29
  94.0 13.8 %collective-permute-start.24 = (bf16[128,512]{1,0:T(8,128)(2,1)S(1)}, bf16[128,512]{1,0:T(8,128)(2,1)S(1)}, u32[]{:S(2)}, u32[]{:S(2)}) collective-permute-start(bf16[128,512]{1,0:T(8,128)(2,1)S(1)} %subtract_convert_fusion.refs_0_.refs_1_), channel_id=1, source_target_pairs={{0,16},{1,17},{2,18},{3,19},{4,20},{5,21},{6,22},{7,23},{8,24},{9,... | collective-permute-start | bytes 393224 | tf_op jit(solution)/shard_map/ppermute | solution.py:29
  96.5 13.2 %collective-permute-start.25 = (bf16[128,512]{1,0:T(8,128)(2,1)S(1)}, bf16[128,512]{1,0:T(8,128)(2,1)S(1)}, u32[]{:S(2)}, u32[]{:S(2)}) collective-permute-start(bf16[128,512]{1,0:T(8,128)(2,1)S(1)} %subtract_convert_fusion.refs_0_.refs_1_), channel_id=1, source_target_pairs={{0,24},{1,25},{2,26},{3,27},{4,28},{5,29},{6,30},{7,31},{8,0},{9,1... | collective-permute-start | bytes 393224 | tf_op jit(solution)/shard_map/ppermute | solution.py:29
  114.2 29.7 %all-to-all-start.1 = ((bf16[16,128,256]{2,1,0:T(8,128)(2,1)}), bf16[16,128,256]{2,1,0:T(8,128)(2,1)S(1)}, u32[]{:S(2)}, u32[]{:S(2)}) async-start(bf16[16,128,256]{2,1,0:T(8,128)(2,1)} %hidden_grad.1), calls=%async_computation.1 | async-start | bytes 2097152 | tf_op jit(solution)/shard_map/all_to_all | solution.py:262
  119.5 15.4 %collective-permute-start.22 = (f32[1,128]{1,0:T(1,128)S(1)}, f32[1,128]{1,0:T(1,128)S(1)}, u32[]{:S(2)}, u32[]{:S(2)}) collective-permute-start(f32[1,128]{1,0:T(1,128)S(1)} %bitcast_multiply_fusion), channel_id=1, source_target_pairs={{0,132},{1,133},{2,134},{3,135},{4,128},{5,129},{6,130},{7,131},{8... | collective-permute-start | bytes 1544 | tf_op jit(solution)/shard_map/ppermute | solution.py:29
  122.6 12.3 %collective-permute-start.21 = (f32[1,128]{1,0:T(1,128)S(1)}, f32[1,128]{1,0:T(1,128)S(1)}, u32[]{:S(2)}, u32[]{:S(2)}) collective-permute-start(f32[1,128]{1,0:T(1,128)S(1)} %bitcast_multiply_fusion), channel_id=1, source_target_pairs={{0,128},{1,129},{2,130},{3,131},{4,132},{5,133},{6,134},{7,135},{8... | collective-permute-start | bytes 1544 | tf_op jit(solution)/shard_map/ppermute | solution.py:29
  123.2 11.8 %collective-permute-start.20 = (f32[1,128]{1,0:T(1,128)S(1)}, f32[1,128]{1,0:T(1,128)S(1)}, u32[]{:S(2)}, u32[]{:S(2)}) collective-permute-start(f32[1,128]{1,0:T(1,128)S(1)} %bitcast_multiply_fusion), channel_id=1, source_target_pairs={{0,4},{1,5},{2,6},{3,7},{4,0},{5,1},{6,2},{7,3},{8,12},{9,13},{10,... | collective-permute-start | bytes 1544 | tf_op jit(solution)/shard_map/ppermute | solution.py:29
  139.8 14.4 %collective-permute-start.29 = (bf16[256,512]{1,0:T(8,128)(2,1)S(1)}, bf16[256,512]{1,0:T(8,128)(2,1)S(1)}, u32[]{:S(2)}, u32[]{:S(2)}) collective-permute-start(bf16[256,512]{1,0:T(8,128)(2,1)S(1)} %get-tuple-element.37), channel_id=1, source_target_pairs={{0,32},{1,33},{2,34},{3,35},{4,36},{5,37},{6,38},{7,39},{8,40},{9,... | collective-permute-start | bytes 786440 | tf_op jit(solution)/shard_map/ppermute | solution.py:29
  139.8 14.3 %collective-permute-start.28 = (bf16[256,512]{1,0:T(8,128)(2,1)S(1)}, bf16[256,512]{1,0:T(8,128)(2,1)S(1)}, u32[]{:S(2)}, u32[]{:S(2)}) collective-permute-start(bf16[256,512]{1,0:T(8,128)(2,1)S(1)} %get-tuple-element.38), channel_id=1, source_target_pairs={{0,64},{1,65},{2,66},{3,67},{4,68},{5,69},{6,70},{7,71},{8,72},{9,... | collective-permute-start | bytes 786440 | tf_op jit(solution)/shard_map/ppermute | solution.py:29
  142.8 11.9 %collective-permute-start.27 = (bf16[256,512]{1,0:T(8,128)(2,1)S(1)}, bf16[256,512]{1,0:T(8,128)(2,1)S(1)}, u32[]{:S(2)}, u32[]{:S(2)}) collective-permute-start(bf16[256,512]{1,0:T(8,128)(2,1)S(1)} %get-tuple-element.36), channel_id=1, source_target_pairs={{0,96},{1,97},{2,98},{3,99},{4,100},{5,101},{6,102},{7,103},{8,104... | collective-permute-start | bytes 786440 | tf_op jit(solution)/shard_map/ppermute | solution.py:29
  144.1 12.2 %collective-permute-start.26 = (f32[128,256]{1,0:T(8,128)S(1)}, f32[128,256]{1,0:T(8,128)S(1)}, u32[]{:S(2)}, u32[]{:S(2)}) collective-permute-start(f32[128,256]{1,0:T(8,128)S(1)} %convert_reduce_fusion), channel_id=1, source_target_pairs={{0,0},{1,132},{2,128},{3,4},{4,24},{5,156},{6,152},{7,28},{8,9},{9... | collective-permute-start | bytes 393224 | tf_op jit(solution)/shard_map/ppermute | solution.py:29
  (15 other events, 100.4 us)
where the time goes:
time: 160 us; the launch traced here: 157 us
  starting transfers between devices  62.1 us (39%)
  waiting for transfers between devices  50.3 us (31%)
  Pallas kernels  22.2 us (14%)
  other arithmetic  15.9 us (10%)
  local copies, waits for them, and re-layouts  5.68 us (4%)
    ppermute x30, starting transfers between devices, send(): return lax.ppermute(value, ALL, pairs)  50.7 us
    ppermute x30, waiting for transfers between devices, send(): return lax.ppermute(value, ALL, pairs)  46.9 us
    pallas_call x1, Pallas kernels, teacher_parts(): pl.pallas_call(teacher_kernel, grid_spec=pltpu.PrefetchScalarGridSpec(num...  9.28 us
    another operation x3, other arithmetic  7.18 us
    all_to_all x1, starting transfers between devices, step(): lax.all_to_all(jnp.broadcast_to(own_squares[None, None], (16, 1, 128)), P...  6.2 us
    all_to_all x1, starting transfers between devices, step(): parts = lax.all_to_all(parts, PLANE, 0, 0, tiled=True)  5.21 us
    pallas_call x1, Pallas kernels, hidden_grad_parts(): pl.pallas_call(hidden_grad_kernel, out_shape=jax.ShapeDtypeStruct((16, 12...  3.89 us
    pallas_call x1, Pallas kernels, head_grad_parts(): pl.pallas_call(head_grad_kernel, out_shape=(jax.ShapeDtypeStruct((256, 51...  3.56 us
  transfers between devices with their start and end apart: 32, of which 17 were waited for; matrix products, arithmetic and copies ran while one was open for 8% of the time, Pallas kernels for 6%

commit v1 on v0

--- a/solution.py
+++ b/solution.py
@@ -71,34 +71,49 @@
     )(order, hidden)
 
 
-def teacher_kernel(order_ref, normed_ref, head_ref, out_ref):
-    core = order_ref[8]
-    scores = jnp.dot(normed_ref[...], head_ref[...], preferred_element_type=jnp.float32)
-    for k in range(2):
-        out_ref[k ^ core, 0] = scores[:, 512 * k : 512 * (k + 1)]
-
-
-def teacher_parts(normed, head, order):
-    rows, depth = normed.shape
+def teacher_kernel(order_ref, hidden_ref, gain_ref, *refs):
+    head_refs, out_ref, both_ref = refs[:4], refs[4], refs[5]
+    rows = hidden_ref.shape[0]
+
+    @pl.when(pl.program_id(0) == 0)
+    def _():
+        product = hidden_ref[...].astype(jnp.float32) * gain_ref[...].astype(jnp.float32)
+        high = product.astype(jnp.bfloat16)
+        both_ref[:rows] = high
+        both_ref[rows:] = (product - high.astype(jnp.float32)).astype(jnp.bfloat16)
+
+    for i in range(4):
+        scores = jnp.dot(both_ref[...], head_refs[i][...], preferred_element_type=jnp.float32)
+        out_ref[i] = scores[:rows] + scores[rows:]
+
+
+def teacher_parts(hidden, gain, head, order):
+    rows, depth = hidden.shape
+
+    def block(n):
+        return pl.BlockSpec((depth, 512), lambda i, order_ref: (0, order_ref[4 * i + n]))
+
     return pl.pallas_call(
         teacher_kernel,
         grid_spec=pltpu.PrefetchScalarGridSpec(
             num_scalar_prefetch=1,
-            grid=(8,),
+            grid=(2,),
             in_specs=[
                 pl.BlockSpec((rows, depth), lambda i, order_ref: (0, 0)),
-                pl.BlockSpec((depth, 1024), lambda i, order_ref: (0, order_ref[i])),
+                pl.BlockSpec((1, depth), lambda i, order_ref: (0, 0)),
+                *(block(n) for n in range(4)),
             ],
-            out_specs=pl.BlockSpec((2, 1, rows, 512), lambda i, order_ref: (0, i, 0, 0)),
+            out_specs=pl.BlockSpec((4, rows, 512), lambda i, order_ref: (i, 0, 0)),
+            scratch_shapes=[pltpu.VMEM((2 * rows, depth), jnp.bfloat16)],
         ),
-        out_shape=jax.ShapeDtypeStruct((2, 8, rows, 512), jnp.float32),
+        out_shape=jax.ShapeDtypeStruct((8, rows, 512), jnp.float32),
         name="teacher",
-    )(order, normed, head)
+    )(order, hidden, gain[None], head, head, head, head)
 
 
 def student_kernel(core_ref, *refs):
     own_ref, near_refs, far_refs, head_refs = refs[0], refs[1:4], refs[4:7], refs[7:11]
-    out_ref, hidden_ref = refs[11:]
+    out_refs, hidden_ref = refs[11:15], refs[15]
     core = core_ref[0]
     for p in range(2):
         hidden_ref[0, 2 * core + p] = own_ref[p]
@@ -111,7 +126,7 @@
         for j in range(4):
             term = jnp.dot(hidden_ref[k, j], head_refs[j][...], preferred_element_type=jnp.float32)
             total = term if total is None else total + term
-        out_ref[k] = total
+        out_refs[k][...] = total
 
 
 def student_parts(core, own, near, far, head_slots):
@@ -120,7 +135,7 @@
         student_kernel,
         in_specs=[pl.BlockSpec(memory_space=pltpu.SMEM)] + [vmem] * 11,
         out_shape=(
-            jax.ShapeDtypeStruct((4, 128, 512), jnp.float32),
+            *[jax.ShapeDtypeStruct((128, 512), jnp.float32)] * 4,
             jax.ShapeDtypeStruct((4, 4, 128, 256), jnp.bfloat16),
         ),
         name="student",
@@ -128,7 +143,7 @@
 
 
 def head_grad_kernel(*refs):
-    hidden_ref, grad_refs, own_ref, out_ref = refs[0], refs[1:5], refs[5], refs[6]
+    hidden_ref, grad_refs, own_ref, out_refs = refs[0], refs[1:5], refs[5], refs[6:]
     for j in range(4):
         total = None
         for k in range(4):
@@ -139,7 +154,7 @@
         if j == 0:
             own_ref[...] = total
         else:
-            out_ref[j - 1] = total.astype(out_ref.dtype)
+            out_refs[j - 1][...] = total.astype(jnp.bfloat16)
 
 
 def head_grad_parts(hidden, grad_slots):
@@ -147,27 +162,45 @@
         head_grad_kernel,
         out_shape=(
             jax.ShapeDtypeStruct((256, 512), jnp.float32),
-            jax.ShapeDtypeStruct((3, 256, 512), jnp.bfloat16),
+            *[jax.ShapeDtypeStruct((256, 512), jnp.bfloat16)] * 3,
         ),
         name="head_grad",
     )(hidden, *grad_slots)
 
 
 def hidden_grad_kernel(*refs):
-    grad_refs, head_refs, out_ref = refs[:4], refs[4:8], refs[8]
-    for k in range(4):
+    grad_refs, head_refs, out_ref = refs[:3], refs[3:7], refs[7]
+    for k in range(3):
         for j in range(4):
             out_ref[4 * k + j] = lax.dot_general(
                 grad_refs[k][...], head_refs[j][...], (((1,), (1,)), ((), ())), preferred_element_type=jnp.float32
             ).astype(out_ref.dtype)
 
 
+def last_hidden_grad_kernel(parts_ref, grad_ref, *refs):
+    head_refs, out_ref = refs[:4], refs[4]
+    for j in range(4):
+        out_ref[j] = lax.dot_general(
+            grad_ref[...], head_refs[j][...], (((1,), (1,)), ((), ())), preferred_element_type=jnp.float32
+        ).astype(out_ref.dtype)
+
+
 def hidden_grad_parts(grad_slots, head_slots):
-    return pl.pallas_call(
-        hidden_grad_kernel,
-        out_shape=jax.ShapeDtypeStruct((16, 128, 256), jnp.bfloat16),
-        name="hidden_grad",
-    )(*grad_slots, *head_slots)
+    shape = jax.ShapeDtypeStruct((16, 128, 256), jnp.bfloat16)
+    parts = pl.pallas_call(hidden_grad_kernel, out_shape=shape, name="hidden_grad")(*grad_slots[:3], *head_slots)
+    return pl.pallas_call(
+        last_hidden_grad_kernel,
+        grid=(1,),
+        in_specs=[
+            pl.BlockSpec(memory_space=pl.ANY),
+            pl.BlockSpec((128, 512), lambda i: (0, 0)),
+            *[pl.BlockSpec((256, 512), lambda i: (0, 0))] * 4,
+        ],
+        out_specs=pl.BlockSpec((4, 128, 256), lambda i: (3, 0, 0)),
+        out_shape=shape,
+        input_output_aliases={0: 0},
+        name="last_hidden_grad",
+    )(parts, grad_slots[3], *head_slots)
 
 
 def step(teacher_hidden, teacher_gain, teacher_head, student_hidden, student_head, depth_cut):
@@ -175,12 +208,6 @@
     zl = lax.axis_index("group")
     dp, mp = lax.axis_index("dp"), lax.axis_index("mp")
     y, zh, x, core = dp // 4, dp % 4, mp // 2, mp % 2
-
-    hidden_float = teacher_hidden.astype(f32)
-    own_squares = jnp.sum(hidden_float * hidden_float, axis=1)
-    squares = lax.all_to_all(
-        jnp.broadcast_to(own_squares[None, None], (16, 1, 128)), PLANE, 0, 0, tiled=True
-    ).sum(axis=(0, 1))
 
     steps = jnp.arange(4, dtype=jnp.int32)
     order = (((y - steps - 2 * core) % 4 * 4)[None, :] + ((zh + steps) % 4)[:, None]).reshape(16)
@@ -189,21 +216,29 @@
     head_slots = [student_head] + [to_y(student_head, j) for j in (1, 2, 3)]
     far = [to_core(half) for half in near]
 
-    row_scale = lax.rsqrt(squares / DT + epsilon)
-    normed = (hidden_float * row_scale[:, None] * teacher_gain.astype(f32)[None, :]).astype(bf16)
     spots = jnp.arange(8, dtype=jnp.int32)
-    order = (zl ^ (spots % 2)) * 4 + (x + spots // 2) % 4
-    parts = teacher_parts(normed, teacher_head, jnp.append(order, core)).reshape(2, 4, 2, 128, 512)
-    by_core = parts[0] + to_core(parts[1].astype(f16)).astype(f32)
-    by_x = by_core[0]
+    order = ((zl ^ (spots % 2)) * 4 + (x + spots // 2) % 4) * 2
+    other = teacher_parts(teacher_hidden, teacher_gain, teacher_head, order + (1 - core))
+    other = to_core(other)
+    parts = teacher_parts(teacher_hidden, teacher_gain, teacher_head, order + core)
+    by_x = parts[:2] + other[:2]
     for step in (1, 2, 3):
-        by_x = by_x + to_x(by_core[step].astype(f16), step).astype(f32)
+        part = parts[2 * step : 2 * step + 2] + other[2 * step : 2 * step + 2]
+        by_x = by_x + to_x(part.astype(f16), step).astype(f32)
     teacher = by_x[0] + to_zl(by_x[1].astype(f16)).astype(f32)
 
-    parts, hidden = student_parts(core, own, near, far, head_slots)
+    *parts, hidden = student_parts(core, own, near, far, head_slots)
     student = parts[0]
     for k in (1, 2, 3):
         student = student + to_zh(parts[k].astype(f16), -k).astype(f32)
+
+    hidden_float = teacher_hidden.astype(f32)
+    own_squares = jnp.sum(hidden_float * hidden_float, axis=1)
+    squares = lax.all_to_all(
+        jnp.broadcast_to(own_squares[None, None], (16, 1, 128)), PLANE, 0, 0, tiled=True
+    ).sum(axis=(0, 1))
+    row_scale = lax.rsqrt(squares / DT + epsilon)
+    teacher = teacher * row_scale[:, None]
 
     teacher_max = jnp.max(teacher, axis=1)
     student_max = jnp.max(student, axis=1)
@@ -261,7 +296,7 @@
     parts = hidden_grad_parts(grad_slots, head_slots)
     parts = lax.all_to_all(parts, PLANE, 0, 0, tiled=True)
     hidden_grad = jnp.sum(parts.astype(f32), axis=0)
-    head_grad, parts = head_grad_parts(hidden, grad_slots)
+    head_grad, *parts = head_grad_parts(hidden, grad_slots)
     for j in (1, 2, 3):
         head_grad = head_grad + to_y(parts[j - 1], -j).astype(f32)
 

time: 160 us -> 152 us (0.950); the launches traced: 157 us -> 151 us
  waiting for transfers between devices: 50.3 us -> 45.4 us
  other arithmetic: 15.9 us -> 11.8 us
  Pallas kernels: 22.2 us -> 24.8 us
    ppermute x30, waiting for transfers between devices: 46.9 us -> 39 us  [send(): return lax.ppermute(value, ALL, pairs)]
    another operation x3 -> x0, other arithmetic: 7.18 us -> none
    ppermute x30, starting transfers between devices: 50.7 us -> 54.4 us  [send(): return lax.ppermute(value, ALL, pairs)]
    convert_element_type x2 -> x4, other arithmetic: 2.34 us -> 5.46 us  [the longest x3 2.95 us: step(): student = student + to_zh(parts[k].astype(f16), -k).astype(f32)]
    all_to_all x1, waiting for transfers between devices: 3.36 us -> 6.42 us  [step(): lax.all_to_all(jnp.broadcast_to(own_squares[None, None], (16, 1, 128)), P...]
    all_to_all x1, starting transfers between devices: 6.2 us -> 3.86 us  [step(): lax.all_to_all(jnp.broadcast_to(own_squares[None, None], (16, 1, 128)), P...]
    pallas_call x1 -> x2, Pallas kernels: 3.89 us -> 5.85 us  [the longest x1 3.46 us: hidden_grad_parts(): pl.pallas_call(hidden_grad_kernel, out_shape=shape, name='hidden_grad')]
    pallas_call x1 -> x2, Pallas kernels: 9.28 us -> 10 us  [teacher_parts(): pl.pallas_call(teacher_kernel, grid_spec=pltpu.PrefetchScalarGridSpec(num...]
  transfers between devices with their start and end apart: 32 -> 32, of which waited for: 17 -> 12; matrix products, arithmetic and copies ran while one was open for 8% -> 8% of each run, Pallas kernels for 6% -> 11%
where the time goes in v1:
time: 152 us; the launch traced here: 151 us
  starting transfers between devices  62.3 us (41%)
  waiting for transfers between devices  45.4 us (30%)
  Pallas kernels  24.8 us (16%)
  other arithmetic  11.8 us (8%)
  local copies, waits for them, and re-layouts  5.54 us (4%)
    ppermute x30, starting transfers between devices, send(): return lax.ppermute(value, ALL, pairs)  54.4 us
    ppermute x30, waiting for transfers between devices, send(): return lax.ppermute(value, ALL, pairs)  39 us
    pallas_call x2, Pallas kernels, teacher_parts(): pl.pallas_call(teacher_kernel, grid_spec=pltpu.PrefetchScalarGridSpec(num...  10 us
    all_to_all x1, waiting for transfers between devices, step(): lax.all_to_all(jnp.broadcast_to(own_squares[None, None], (16, 1, 128)), P...  6.42 us
    all_to_all x1, starting transfers between devices, step(): parts = lax.all_to_all(parts, PLANE, 0, 0, tiled=True)  4.03 us
    all_to_all x1, starting transfers between devices, step(): lax.all_to_all(jnp.broadcast_to(own_squares[None, None], (16, 1, 128)), P...  3.86 us
    pallas_call x1, Pallas kernels, hidden_grad_parts(): pl.pallas_call(hidden_grad_kernel, out_shape=shape, name='hidden_grad')  3.46 us
    pallas_call x1, Pallas kernels, student_parts(): pl.pallas_call(student_kernel, in_specs=[pl.BlockSpec(memory_space=pltpu....  3.4 us
  transfers between devices with their start and end apart: 32, of which 12 were waited for; matrix products, arithmetic and copies ran while one was open for 8% of the time, Pallas kernels for 11%

profile of v1, /device:TPU:2, one launch (start us, length us, event | category | flops | bytes accessed | tf_op | source)
XLA Modules:
  0.0 150.8 jit_solution(10316295187649525933)
XLA Ops:
  2.4 5.1 %teacher.3 = f32[8,128,512]{2,1,0:T(8,128)} custom-call(s32[8]{0:T(128)} %broadcast_add_fusion.1.order_ref, bf16[128,512]{1,0:T(8,128)(2,1)} %hidden_ref.4, bf16[1,512]{1,0:T(2,128)(2,1)} %broadcast_in_dim.6.gain_ref, bf16[512,8192]{1,0:T(8,128)(2,1)} %refs_3_.4, bf16[512,8192]{1,0:T(8,128)(2,1)} %refs_3_.4, bf16[512,8192]{1,0:T(8,128)(2,1)} %refs_3_.4, ...), custom_call_target="tpu_custom_call" | custom-call | tf_op jit(solution)/shard_map/teacher/pallas_call | solution.py:96
  8.3 2.1 %pick.1 = (bf16[4,128,256]{2,1,0:T(8,128)(2,1)}, bf16[2,128,256]{2,1,0:T(8,128)(2,1)}, bf16[2,128,256]{2,1,0:T(8,128)(2,1)}, bf16[2,128,256]{2,1,0:T(8,128)(2,1)}) custom-call(s32[16]{0:T(128)} %add.217.order_ref, bf16[128,4096]{1,0:T(8,128)(2,1)} %hidden_ref.5), custom_call_target="tpu_custom_call" | custom-call | tf_op jit(solution)/shard_map/pick/pallas_call | solution.py:66
  10.4 3.3 %collective-permute-start.5 = (bf16[2,128,256]{2,1,0:T(8,128)(2,1)}, bf16[2,128,256]{2,1,0:T(8,128)(2,1)S(1)}, u32[]{:S(2)}, u32[]{:S(2)}) collective-permute-start(bf16[2,128,256]{2,1,0:T(8,128)(2,1)} %get-tuple-element.17), channel_id=1, source_target_pairs={{0,8},{1,9},{2,10},{3,11},{4,12},{5,13},{6,14},{7,15},{8,16},{9,17... | collective-permute-start | bytes 393224 | tf_op jit(solution)/shard_map/ppermute | solution.py:29
  13.7 5.4 %collective-permute-start.6 = (bf16[2,128,256]{2,1,0:T(8,128)(2,1)}, bf16[2,128,256]{2,1,0:T(8,128)(2,1)S(1)}, u32[]{:S(2)}, u32[]{:S(2)}) collective-permute-start(bf16[2,128,256]{2,1,0:T(8,128)(2,1)} %get-tuple-element.18), channel_id=1, source_target_pairs={{0,16},{1,17},{2,18},{3,19},{4,20},{5,21},{6,22},{7,23},{8,24},{9,... | collective-permute-start | bytes 393224 | tf_op jit(solution)/shard_map/ppermute | solution.py:29
  19.1 2.7 %collective-permute-start.7 = (bf16[2,128,256]{2,1,0:T(8,128)(2,1)}, bf16[2,128,256]{2,1,0:T(8,128)(2,1)}, u32[]{:S(2)}, u32[]{:S(2)}) collective-permute-start(bf16[2,128,256]{2,1,0:T(8,128)(2,1)} %get-tuple-element.19), channel_id=1, source_target_pairs={{0,24},{1,25},{2,26},{3,27},{4,28},{5,29},{6,30},{7,31},{8,0},{9,1... | collective-permute-start | bytes 393224 | tf_op jit(solution)/shard_map/ppermute | solution.py:29
  23.9 4.9 %teacher.2 = f32[8,128,512]{2,1,0:T(8,128)} custom-call(s32[8]{0:T(128)} %broadcast_add_fusion.2.order_ref, bf16[128,512]{1,0:T(8,128)(2,1)} %hidden_ref.4, bf16[1,512]{1,0:T(2,128)(2,1)} %broadcast_in_dim.6.gain_ref, bf16[512,8192]{1,0:T(8,128)(2,1)} %refs_3_.4, bf16[512,8192]{1,0:T(8,128)(2,1)} %refs_3_.4, bf16[512,8192]{1,0:T(8,128)(2,1)} %refs_3_.4, ...), custom_call_target="tpu_custom_call" | custom-call | tf_op jit(solution)/shard_map/teacher/pallas_call | solution.py:96
  28.9 3.0 %collective-permute-start.12 = (bf16[256,512]{1,0:T(8,128)(2,1)S(1)}, bf16[256,512]{1,0:T(8,128)(2,1)S(1)}, u32[]{:S(2)}, u32[]{:S(2)}) collective-permute-start(bf16[256,512]{1,0:T(8,128)(2,1)S(1)} %copy-done), channel_id=1, source_target_pairs={{0,64},{1,65},{2,66},{3,67},{4,68},{5,69},{6,70},{7,71},{8,72},{9,... | collective-permute-start | bytes 786440 | tf_op jit(solution)/shard_map/ppermute | solution.py:29
  32.7 2.5 %fusion.2 = (f16[2,128,512]{2,1,0:T(8,128)(2,1)}, f16[2,128,512]{2,1,0:T(8,128)(2,1)}, f16[2,128,512]{2,1,0:T(8,128)(2,1)}) fusion(f32[8,128,512]{2,1,0:T(8,128)S(1)} %collective-permute-done, f32[8,128,512]{2,1,0:T(8,128)} %teacher.2), kind=kLoop, calls=%fused_computation.6 | loop fusion | flops 786432 | bytes 3932160 | tf_op jit(solution)/shard_map/convert_element_type | solution.py:227
  35.2 3.0 %collective-permute-start.13 = (bf16[256,512]{1,0:T(8,128)(2,1)S(1)}, bf16[256,512]{1,0:T(8,128)(2,1)S(1)}, u32[]{:S(2)}, u32[]{:S(2)}) collective-permute-start(bf16[256,512]{1,0:T(8,128)(2,1)S(1)} %copy-done), channel_id=1, source_target_pairs={{0,96},{1,97},{2,98},{3,99},{4,100},{5,101},{6,102},{7,103},{8,104... | collective-permute-start | bytes 786440 | tf_op jit(solution)/shard_map/ppermute | solution.py:29
  38.9 2.4 %collective-permute-start.2 = (f16[2,128,512]{2,1,0:T(8,128)(2,1)}, f16[2,128,512]{2,1,0:T(8,128)(2,1)}, u32[]{:S(2)}, u32[]{:S(2)}) collective-permute-start(f16[2,128,512]{2,1,0:T(8,128)(2,1)} %get-tuple-element.41), channel_id=1, source_target_pairs={{0,4},{1,5},{2,6},{3,7},{4,0},{5,1},{6,2},{7,3},{8,12},{9,13},{10,... | collective-permute-start | bytes 786440 | tf_op jit(solution)/shard_map/ppermute | solution.py:29
  43.8 3.9 %all-to-all-start = ((f32[16,1,128]{2,1,0:T(1,128)}), f32[16,1,128]{2,1,0:T(1,128)S(1)}, u32[]{:S(2)}, u32[]{:S(2)}) async-start(f32[16,1,128]{2,1,0:T(1,128)} %broadcast_in_dim.7), calls=%async_computation | async-start | bytes 16384 | tf_op jit(solution)/shard_map/all_to_all | solution.py:237
  47.7 6.4 %all-to-all-done = f32[16,1,128]{2,1,0:T(1,128)S(1)} async-done(((f32[16,1,128]{2,1,0:T(1,128)}), f32[16,1,128]{2,1,0:T(1,128)S(1)}, u32[]{:S(2)}, u32[]{:S(2)}) %all-to-all-start) | async-done | bytes 8224 | tf_op jit(solution)/shard_map/all_to_all | solution.py:237
  55.0 3.4 %student.1 = (f32[128,512]{1,0:T(8,128)}, f32[128,512]{1,0:T(8,128)}, f32[128,512]{1,0:T(8,128)}, f32[128,512]{1,0:T(8,128)}, bf16[4,4,128,256]{3,2,1,0:T(8,128)(2,1)}) custom-call(s32[1]{0:T(128)} %bitcast.5.core_ref, bf16[4,128,256]{2,1,0:T(8,128)(2,1)} %get-tuple-element.16.refs_0_, bf16[2,128,256]{2,1,0:T(8,128)(2,1)} %copy-done.10, ...), custom_call_target="tpu_custom_call" | custom-call | tf_op jit(solution)/shard_map/student/pallas_call | solution.py:134
  62.2 4.5 %collective-permute-start.15 = (f16[128,512]{1,0:T(8,128)(2,1)S(1)}, f16[128,512]{1,0:T(8,128)(2,1)S(1)}, u32[]{:S(2)}, u32[]{:S(2)}) collective-permute-start(f16[128,512]{1,0:T(8,128)(2,1)S(1)} %convert_element_type.114), channel_id=1, source_target_pairs={{0,16},{1,17},{2,18},{3,19},{4,20},{5,21},{6,22},{7,23},{8,24},{9,... | collective-permute-start | bytes 393224 | tf_op jit(solution)/shard_map/ppermute | solution.py:29
  67.6 2.6 %collective-permute-start.14 = (f16[128,512]{1,0:T(8,128)(2,1)S(1)}, f16[128,512]{1,0:T(8,128)(2,1)S(1)}, u32[]{:S(2)}, u32[]{:S(2)}) collective-permute-start(f16[128,512]{1,0:T(8,128)(2,1)S(1)} %convert_element_type.112), channel_id=1, source_target_pairs={{0,24},{1,25},{2,26},{3,27},{4,28},{5,29},{6,30},{7,31},{8,0},{9,1... | collective-permute-start | bytes 393224 | tf_op jit(solution)/shard_map/ppermute | solution.py:29
  71.7 5.0 %collective-permute-done.15 = f16[128,512]{1,0:T(8,128)(2,1)S(1)} collective-permute-done((f16[128,512]{1,0:T(8,128)(2,1)S(1)}, f16[128,512]{1,0:T(8,128)(2,1)S(1)}, u32[]{:S(2)}, u32[]{:S(2)}) %collective-permute-start.15) | collective-permute-done | bytes 131104 | tf_op jit(solution)/shard_map/ppermute | solution.py:29
  78.0 1.9 %collective-permute-done.4 = f16[128,512]{1,0:T(8,128)(2,1)S(1)} collective-permute-done((f16[128,512]{1,0:T(8,128)(2,1)S(1)}, f16[128,512]{1,0:T(8,128)(2,1)S(1)}, u32[]{:S(2)}, u32[]{:S(2)}) %collective-permute-start.4) | collective-permute-done | bytes 131104 | tf_op jit(solution)/shard_map/ppermute | solution.py:29
  83.5 2.2 %collective-permute-done.18 = f32[5,128]{1,0:T(8,128)S(1)} collective-permute-done((f32[5,128]{1,0:T(8,128)S(1)}, f32[5,128]{1,0:T(8,128)S(1)}, u32[]{:S(2)}, u32[]{:S(2)}) %collective-permute-start.18) | collective-permute-done | bytes 2592 | tf_op jit(solution)/shard_map/ppermute | solution.py:29
  87.0 3.7 %collective-permute-start.24 = (bf16[128,512]{1,0:T(8,128)(2,1)S(1)}, bf16[128,512]{1,0:T(8,128)(2,1)S(1)}, u32[]{:S(2)}, u32[]{:S(2)}) collective-permute-start(bf16[128,512]{1,0:T(8,128)(2,1)S(1)} %subtract_convert_fusion.refs_0_.refs_1_), channel_id=1, source_target_pairs={{0,16},{1,17},{2,18},{3,19},{4,20},{5,21},{6,22},{7,23},{8,24},{9,... | collective-permute-start | bytes 393224 | tf_op jit(solution)/shard_map/ppermute | solution.py:29
  90.7 2.0 %collective-permute-start.25 = (bf16[128,512]{1,0:T(8,128)(2,1)S(1)}, bf16[128,512]{1,0:T(8,128)(2,1)S(1)}, u32[]{:S(2)}, u32[]{:S(2)}) collective-permute-start(bf16[128,512]{1,0:T(8,128)(2,1)S(1)} %subtract_convert_fusion.refs_0_.refs_1_), channel_id=1, source_target_pairs={{0,24},{1,25},{2,26},{3,27},{4,28},{5,29},{6,30},{7,31},{8,0},{9,1... | collective-permute-start | bytes 393224 | tf_op jit(solution)/shard_map/ppermute | solution.py:29
  92.7 2.7 %collective-permute-done.23.refs_1_.refs_2_ = bf16[128,512]{1,0:T(8,128)(2,1)S(1)} collective-permute-done((bf16[128,512]{1,0:T(8,128)(2,1)S(1)}, bf16[128,512]{1,0:T(8,128)(2,1)S(1)}, u32[]{:S(2)}, u32[]{:S(2)}) %collective-permute-start.23) | collective-permute-done | bytes 131104 | tf_op jit(solution)/shard_map/ppermute | solution.py:29
  95.4 7.5 %collective-permute-done.24.refs_2_.refs_3_ = bf16[128,512]{1,0:T(8,128)(2,1)S(1)} collective-permute-done((bf16[128,512]{1,0:T(8,128)(2,1)S(1)}, bf16[128,512]{1,0:T(8,128)(2,1)S(1)}, u32[]{:S(2)}, u32[]{:S(2)}) %collective-permute-start.24) | collective-permute-done | bytes 131104 | tf_op jit(solution)/shard_map/ppermute | solution.py:29
  103.5 3.5 %hidden_grad.1.parts_ref = bf16[16,128,256]{2,1,0:T(8,128)(2,1)} custom-call(bf16[128,512]{1,0:T(8,128)(2,1)} %copy-done.5, bf16[128,512]{1,0:T(8,128)(2,1)} %copy-done.6, bf16[128,512]{1,0:T(8,128)(2,1)} %copy-done.7, bf16[256,512]{1,0:T(8,128)(2,1)} %refs_0_.5, bf16[256,512]{1,0:T(8,128)(2,1)} %copy-done.1, bf16[256,512]{1,0:T(8,128)(2,1)} %copy-done.2, ...), custom_call_target="tpu_custom_call" | custom-call | tf_op jit(solution)/shard_map/hidden_grad/pallas_call | solution.py:190
  107.6 2.4 %last_hidden_grad.1 = bf16[16,128,256]{2,1,0:T(8,128)(2,1)} custom-call(bf16[16,128,256]{2,1,0:T(8,128)(2,1)} %hidden_grad.1.parts_ref, bf16[128,512]{1,0:T(8,128)(2,1)} %copy-done.8, bf16[256,512]{1,0:T(8,128)(2,1)} %refs_0_.5, bf16[256,512]{1,0:T(8,128)(2,1)} %copy-done.1, bf16[256,512]{1,0:T(8,128)(2,1)} %copy-done.2, ...), custom_call_target="tpu_custom_call", output_to_operand_aliasing={{}: (0, {})} | custom-call | tf_op jit(solution)/shard_map/last_hidden_grad/pallas_call | solution.py:191
  110.0 4.0 %all-to-all-start.1 = ((bf16[16,128,256]{2,1,0:T(8,128)(2,1)}), bf16[16,128,256]{2,1,0:T(8,128)(2,1)S(1)}, u32[]{:S(2)}, u32[]{:S(2)}) async-start(bf16[16,128,256]{2,1,0:T(8,128)(2,1)} %last_hidden_grad.1), calls=%async_computation.1 | async-start | bytes 2097152 | tf_op jit(solution)/shard_map/all_to_all | solution.py:297
  114.2 3.1 %collective-permute-start.22 = (f32[1,128]{1,0:T(1,128)S(1)}, f32[1,128]{1,0:T(1,128)S(1)}, u32[]{:S(2)}, u32[]{:S(2)}) collective-permute-start(f32[1,128]{1,0:T(1,128)S(1)} %bitcast_multiply_fusion), channel_id=1, source_target_pairs={{0,132},{1,133},{2,134},{3,135},{4,128},{5,129},{6,130},{7,131},{8... | collective-permute-start | bytes 1544 | tf_op jit(solution)/shard_map/ppermute | solution.py:29
  119.2 10.4 %collective-permute-done.22 = f32[1,128]{1,0:T(1,128)S(1)} collective-permute-done((f32[1,128]{1,0:T(1,128)S(1)}, f32[1,128]{1,0:T(1,128)S(1)}, u32[]{:S(2)}, u32[]{:S(2)}) %collective-permute-start.22) | collective-permute-done | bytes 544 | tf_op jit(solution)/shard_map/ppermute | solution.py:29
  129.7 3.4 %head_grad.1 = (f32[256,512]{1,0:T(8,128)}, bf16[256,512]{1,0:T(8,128)(2,1)}, bf16[256,512]{1,0:T(8,128)(2,1)}, bf16[256,512]{1,0:T(8,128)(2,1)}) custom-call(bf16[4,4,128,256]{3,2,1,0:T(8,128)(2,1)} %get-tuple-element.24.refs_0_, bf16[128,512]{1,0:T(8,128)(2,1)} %copy-done.5, bf16[128,512]{1,0:T(8,128)(2,1)} %copy-done.6, bf16[128,512]{1,0:T(8,128)(2,1)} %copy-done.7, ...), custom_call_target="tpu_custom_call" | custom-call | tf_op jit(solution)/shard_map/head_grad/pallas_call | solution.py:161
  133.0 2.3 %collective-permute-start.28 = (bf16[256,512]{1,0:T(8,128)(2,1)}, bf16[256,512]{1,0:T(8,128)(2,1)S(1)}, u32[]{:S(2)}, u32[]{:S(2)}) collective-permute-start(bf16[256,512]{1,0:T(8,128)(2,1)} %get-tuple-element.27), channel_id=1, source_target_pairs={{0,64},{1,65},{2,66},{3,67},{4,68},{5,69},{6,70},{7,71},{8,72},{9,... | collective-permute-start | bytes 786440 | tf_op jit(solution)/shard_map/ppermute | solution.py:29
  137.0 3.3 %collective-permute-start.26 = (f32[128,256]{1,0:T(8,128)S(1)}, f32[128,256]{1,0:T(8,128)S(1)}, u32[]{:S(2)}, u32[]{:S(2)}) collective-permute-start(f32[128,256]{1,0:T(8,128)S(1)} %convert_reduce_fusion), channel_id=1, source_target_pairs={{0,0},{1,132},{2,128},{3,4},{4,24},{5,156},{6,152},{7,28},{8,9},{9... | collective-permute-start | bytes 393224 | tf_op jit(solution)/shard_map/ppermute | solution.py:29
  140.3 7.2 %collective-permute-done.29 = bf16[256,512]{1,0:T(8,128)(2,1)S(1)} collective-permute-done((bf16[256,512]{1,0:T(8,128)(2,1)}, bf16[256,512]{1,0:T(8,128)(2,1)S(1)}, u32[]{:S(2)}, u32[]{:S(2)}) %collective-permute-start.29) | collective-permute-done | bytes 262176 | tf_op jit(solution)/shard_map/ppermute | solution.py:29
  148.1 2.0 %convert_add_fusion = f32[256,512]{1,0:T(8,128)} fusion(bf16[256,512]{1,0:T(8,128)(2,1)S(1)} %collective-permute-done.29, bf16[256,512]{1,0:T(8,128)(2,1)S(1)} %collective-permute-done.28, f32[256,512]{1,0:T(8,128)} %get-tuple-element.25, bf16[256,512]{1,0:T(8,128)(2,1)S(1)} %collective-permute-done.27), kind=kLoop, calls=%fused_computation.11 | loop fusion | flops 786432 | bytes 1835008 | tf_op jit(solution)/shard_map/add | solution.py:301
  (110 shorter events, 28.2 us)
Async XLA Ops:
  7.5 24.9 %collective-permute-start = (f32[8,128,512]{2,1,0:T(8,128)}, f32[8,128,512]{2,1,0:T(8,128)S(1)}, u32[]{:S(2)}, u32[]{:S(2)}) collective-permute-start(f32[8,128,512]{2,1,0:T(8,128)} %teacher.3), channel_id=1, source_target_pairs={{0,1},{1,0},{2,3},{3,2},{4,5},{5,4},{6,7},{7,6},{8,9},{9,8},{10,11... | collective-permute-start | bytes 6291464 | tf_op jit(solution)/shard_map/ppermute | solution.py:29
  10.4 18.4 %collective-permute-start.5 = (bf16[2,128,256]{2,1,0:T(8,128)(2,1)}, bf16[2,128,256]{2,1,0:T(8,128)(2,1)S(1)}, u32[]{:S(2)}, u32[]{:S(2)}) collective-permute-start(bf16[2,128,256]{2,1,0:T(8,128)(2,1)} %get-tuple-element.17), channel_id=1, source_target_pairs={{0,8},{1,9},{2,10},{3,11},{4,12},{5,13},{6,14},{7,15},{8,16},{9,17... | collective-permute-start | bytes 393224 | tf_op jit(solution)/shard_map/ppermute | solution.py:29
  13.7 18.2 %collective-permute-start.6 = (bf16[2,128,256]{2,1,0:T(8,128)(2,1)}, bf16[2,128,256]{2,1,0:T(8,128)(2,1)S(1)}, u32[]{:S(2)}, u32[]{:S(2)}) collective-permute-start(bf16[2,128,256]{2,1,0:T(8,128)(2,1)} %get-tuple-element.18), channel_id=1, source_target_pairs={{0,16},{1,17},{2,18},{3,19},{4,20},{5,21},{6,22},{7,23},{8,24},{9,... | collective-permute-start | bytes 393224 | tf_op jit(solution)/shard_map/ppermute | solution.py:29
  19.1 13.1 %collective-permute-start.7 = (bf16[2,128,256]{2,1,0:T(8,128)(2,1)}, bf16[2,128,256]{2,1,0:T(8,128)(2,1)}, u32[]{:S(2)}, u32[]{:S(2)}) collective-permute-start(bf16[2,128,256]{2,1,0:T(8,128)(2,1)} %get-tuple-element.19), channel_id=1, source_target_pairs={{0,24},{1,25},{2,26},{3,27},{4,28},{5,29},{6,30},{7,31},{8,0},{9,1... | collective-permute-start | bytes 393224 | tf_op jit(solution)/shard_map/ppermute | solution.py:29
  21.8 19.5 %collective-permute-start.11 = (bf16[256,512]{1,0:T(8,128)(2,1)S(1)}, bf16[256,512]{1,0:T(8,128)(2,1)S(1)}, u32[]{:S(2)}, u32[]{:S(2)}) collective-permute-start(bf16[256,512]{1,0:T(8,128)(2,1)S(1)} %copy-done), channel_id=1, source_target_pairs={{0,32},{1,33},{2,34},{3,35},{4,36},{5,37},{6,38},{7,39},{8,40},{9,... | collective-permute-start | bytes 786440 | tf_op jit(solution)/shard_map/ppermute | solution.py:29
  28.9 25.3 %collective-permute-start.12 = (bf16[256,512]{1,0:T(8,128)(2,1)S(1)}, bf16[256,512]{1,0:T(8,128)(2,1)S(1)}, u32[]{:S(2)}, u32[]{:S(2)}) collective-permute-start(bf16[256,512]{1,0:T(8,128)(2,1)S(1)} %copy-done), channel_id=1, source_target_pairs={{0,64},{1,65},{2,66},{3,67},{4,68},{5,69},{6,70},{7,71},{8,72},{9,... | collective-permute-start | bytes 786440 | tf_op jit(solution)/shard_map/ppermute | solution.py:29
  31.9 3.3 %collective-permute-start.8 = (bf16[2,128,256]{2,1,0:T(8,128)(2,1)S(1)}, bf16[2,128,256]{2,1,0:T(8,128)(2,1)S(1)}, u32[]{:S(2)}, u32[]{:S(2)}) collective-permute-start(bf16[2,128,256]{2,1,0:T(8,128)(2,1)S(1)} %collective-permute-done.5.refs_1_), channel_id=1, source_target_pairs={{0,1},{1,0},{2,3},{3,2},{4,5},{5,4},{6,7},{7,6},{8,9},{9,8},{10,11... | collective-permute-start | bytes 393224 | tf_op jit(solution)/shard_map/ppermute | solution.py:29
  32.2 6.1 %collective-permute-start.9 = (bf16[2,128,256]{2,1,0:T(8,128)(2,1)S(1)}, bf16[2,128,256]{2,1,0:T(8,128)(2,1)S(1)}, u32[]{:S(2)}, u32[]{:S(2)}) collective-permute-start(bf16[2,128,256]{2,1,0:T(8,128)(2,1)S(1)} %collective-permute-done.6.refs_2_), channel_id=1, source_target_pairs={{0,1},{1,0},{2,3},{3,2},{4,5},{5,4},{6,7},{7,6},{8,9},{9,8},{10,11... | collective-permute-start | bytes 393224 | tf_op jit(solution)/shard_map/ppermute | solution.py:29
  32.4 6.5 %collective-permute-start.10 = (bf16[2,128,256]{2,1,0:T(8,128)(2,1)}, bf16[2,128,256]{2,1,0:T(8,128)(2,1)S(1)}, u32[]{:S(2)}, u32[]{:S(2)}) collective-permute-start(bf16[2,128,256]{2,1,0:T(8,128)(2,1)} %collective-permute-done.7.refs_3_), channel_id=1, source_target_pairs={{0,1},{1,0},{2,3},{3,2},{4,5},{5,4},{6,7},{7,6},{8,9},{9,8},{10,11... | collective-permute-start | bytes 393224 | tf_op jit(solution)/shard_map/ppermute | solution.py:29
  35.2 19.0 %collective-permute-start.13 = (bf16[256,512]{1,0:T(8,128)(2,1)S(1)}, bf16[256,512]{1,0:T(8,128)(2,1)S(1)}, u32[]{:S(2)}, u32[]{:S(2)}) collective-permute-start(bf16[256,512]{1,0:T(8,128)(2,1)S(1)} %copy-done), channel_id=1, source_target_pairs={{0,96},{1,97},{2,98},{3,99},{4,100},{5,101},{6,102},{7,103},{8,104... | collective-permute-start | bytes 786440 | tf_op jit(solution)/shard_map/ppermute | solution.py:29
  38.3 29.4 %collective-permute-start.3 = (f16[2,128,512]{2,1,0:T(8,128)(2,1)}, f16[2,128,512]{2,1,0:T(8,128)(2,1)S(1)}, u32[]{:S(2)}, u32[]{:S(2)}) collective-permute-start(f16[2,128,512]{2,1,0:T(8,128)(2,1)} %get-tuple-element.40), channel_id=1, source_target_pairs={{0,6},{1,7},{2,0},{3,1},{4,2},{5,3},{6,4},{7,5},{8,14},{9,15},{10,... | collective-permute-start | bytes 786440 | tf_op jit(solution)/shard_map/ppermute | solution.py:29
  38.9 31.3 %collective-permute-start.2 = (f16[2,128,512]{2,1,0:T(8,128)(2,1)}, f16[2,128,512]{2,1,0:T(8,128)(2,1)}, u32[]{:S(2)}, u32[]{:S(2)}) collective-permute-start(f16[2,128,512]{2,1,0:T(8,128)(2,1)} %get-tuple-element.41), channel_id=1, source_target_pairs={{0,4},{1,5},{2,6},{3,7},{4,0},{5,1},{6,2},{7,3},{8,12},{9,13},{10,... | collective-permute-start | bytes 786440 | tf_op jit(solution)/shard_map/ppermute | solution.py:29
  41.3 28.9 %collective-permute-start.1 = (f16[2,128,512]{2,1,0:T(8,128)(2,1)}, f16[2,128,512]{2,1,0:T(8,128)(2,1)}, u32[]{:S(2)}, u32[]{:S(2)}) collective-permute-start(f16[2,128,512]{2,1,0:T(8,128)(2,1)} %get-tuple-element.39), channel_id=1, source_target_pairs={{0,2},{1,3},{2,4},{3,5},{4,6},{5,7},{6,0},{7,1},{8,10},{9,11},{10,... | collective-permute-start | bytes 786440 | tf_op jit(solution)/shard_map/ppermute | solution.py:29
  43.8 10.3 %all-to-all-start = ((f32[16,1,128]{2,1,0:T(1,128)}), f32[16,1,128]{2,1,0:T(1,128)S(1)}, u32[]{:S(2)}, u32[]{:S(2)}) async-start(f32[16,1,128]{2,1,0:T(1,128)} %broadcast_in_dim.7), calls=%async_computation | async-start | bytes 16384 | tf_op jit(solution)/shard_map/all_to_all | solution.py:237
  59.4 12.3 %collective-permute-start.16 = (f16[128,512]{1,0:T(8,128)(2,1)S(1)}, f16[128,512]{1,0:T(8,128)(2,1)S(1)}, u32[]{:S(2)}, u32[]{:S(2)}) collective-permute-start(f16[128,512]{1,0:T(8,128)(2,1)S(1)} %convert_element_type.116), channel_id=1, source_target_pairs={{0,8},{1,9},{2,10},{3,11},{4,12},{5,13},{6,14},{7,15},{8,16},{9,17... | collective-permute-start | bytes 393224 | tf_op jit(solution)/shard_map/ppermute | solution.py:29
  62.2 14.6 %collective-permute-start.15 = (f16[128,512]{1,0:T(8,128)(2,1)S(1)}, f16[128,512]{1,0:T(8,128)(2,1)S(1)}, u32[]{:S(2)}, u32[]{:S(2)}) collective-permute-start(f16[128,512]{1,0:T(8,128)(2,1)S(1)} %convert_element_type.114), channel_id=1, source_target_pairs={{0,16},{1,17},{2,18},{3,19},{4,20},{5,21},{6,22},{7,23},{8,24},{9,... | collective-permute-start | bytes 393224 | tf_op jit(solution)/shard_map/ppermute | solution.py:29
  67.6 10.2 %collective-permute-start.14 = (f16[128,512]{1,0:T(8,128)(2,1)S(1)}, f16[128,512]{1,0:T(8,128)(2,1)S(1)}, u32[]{:S(2)}, u32[]{:S(2)}) collective-permute-start(f16[128,512]{1,0:T(8,128)(2,1)S(1)} %convert_element_type.112), channel_id=1, source_target_pairs={{0,24},{1,25},{2,26},{3,27},{4,28},{5,29},{6,30},{7,31},{8,0},{9,1... | collective-permute-start | bytes 393224 | tf_op jit(solution)/shard_map/ppermute | solution.py:29
  71.6 8.3 %collective-permute-start.4 = (f16[128,512]{1,0:T(8,128)(2,1)S(1)}, f16[128,512]{1,0:T(8,128)(2,1)S(1)}, u32[]{:S(2)}, u32[]{:S(2)}) collective-permute-start(f16[128,512]{1,0:T(8,128)(2,1)S(1)} %fusion.10), channel_id=1, source_target_pairs={{0,128},{1,129},{2,130},{3,131},{4,132},{5,133},{6,134},{7,135},{8... | collective-permute-start | bytes 393224 | tf_op jit(solution)/shard_map/ppermute | solution.py:29
  80.4 3.1 %collective-permute-start.19 = (f32[5,128]{1,0:T(8,128)S(1)}, f32[5,128]{1,0:T(8,128)S(1)}, u32[]{:S(2)}, u32[]{:S(2)}) collective-permute-start(f32[5,128]{1,0:T(8,128)S(1)} %stack.38), channel_id=1, source_target_pairs={{0,3},{1,2},{2,1},{3,0},{4,7},{5,6},{6,5},{7,4},{8,11},{9,10},{10,... | collective-permute-start | bytes 7688 | tf_op jit(solution)/shard_map/ppermute | solution.py:29
  82.1 3.6 %collective-permute-start.18 = (f32[5,128]{1,0:T(8,128)S(1)}, f32[5,128]{1,0:T(8,128)S(1)}, u32[]{:S(2)}, u32[]{:S(2)}) collective-permute-start(f32[5,128]{1,0:T(8,128)S(1)} %stack.38), channel_id=1, source_target_pairs={{0,2},{1,3},{2,0},{3,1},{4,6},{5,7},{6,4},{7,5},{8,10},{9,11},{10,... | collective-permute-start | bytes 7688 | tf_op jit(solution)/shard_map/ppermute | solution.py:29
  83.2 2.5 %collective-permute-start.17 = (f32[5,128]{1,0:T(8,128)S(1)}, f32[5,128]{1,0:T(8,128)S(1)}, u32[]{:S(2)}, u32[]{:S(2)}) collective-permute-start(f32[5,128]{1,0:T(8,128)S(1)} %stack.38), channel_id=1, source_target_pairs={{0,1},{1,0},{2,3},{3,2},{4,5},{5,4},{6,7},{7,6},{8,9},{9,8},{10,11... | collective-permute-start | bytes 7688 | tf_op jit(solution)/shard_map/ppermute | solution.py:29
  86.0 9.4 %collective-permute-start.23 = (bf16[128,512]{1,0:T(8,128)(2,1)S(1)}, bf16[128,512]{1,0:T(8,128)(2,1)S(1)}, u32[]{:S(2)}, u32[]{:S(2)}) collective-permute-start(bf16[128,512]{1,0:T(8,128)(2,1)S(1)} %subtract_convert_fusion.refs_0_.refs_1_), channel_id=1, source_target_pairs={{0,8},{1,9},{2,10},{3,11},{4,12},{5,13},{6,14},{7,15},{8,16},{9,17... | collective-permute-start | bytes 393224 | tf_op jit(solution)/shard_map/ppermute | solution.py:29
  87.0 15.9 %collective-permute-start.24 = (bf16[128,512]{1,0:T(8,128)(2,1)S(1)}, bf16[128,512]{1,0:T(8,128)(2,1)S(1)}, u32[]{:S(2)}, u32[]{:S(2)}) collective-permute-start(bf16[128,512]{1,0:T(8,128)(2,1)S(1)} %subtract_convert_fusion.refs_0_.refs_1_), channel_id=1, source_target_pairs={{0,16},{1,17},{2,18},{3,19},{4,20},{5,21},{6,22},{7,23},{8,24},{9,... | collective-permute-start | bytes 393224 | tf_op jit(solution)/shard_map/ppermute | solution.py:29
  90.7 16.3 %collective-permute-start.25 = (bf16[128,512]{1,0:T(8,128)(2,1)S(1)}, bf16[128,512]{1,0:T(8,128)(2,1)S(1)}, u32[]{:S(2)}, u32[]{:S(2)}) collective-permute-start(bf16[128,512]{1,0:T(8,128)(2,1)S(1)} %subtract_convert_fusion.refs_0_.refs_1_), channel_id=1, source_target_pairs={{0,24},{1,25},{2,26},{3,27},{4,28},{5,29},{6,30},{7,31},{8,0},{9,1... | collective-permute-start | bytes 393224 | tf_op jit(solution)/shard_map/ppermute | solution.py:29
  110.0 26.8 %all-to-all-start.1 = ((bf16[16,128,256]{2,1,0:T(8,128)(2,1)}), bf16[16,128,256]{2,1,0:T(8,128)(2,1)S(1)}, u32[]{:S(2)}, u32[]{:S(2)}) async-start(bf16[16,128,256]{2,1,0:T(8,128)(2,1)} %last_hidden_grad.1), calls=%async_computation.1 | async-start | bytes 2097152 | tf_op jit(solution)/shard_map/all_to_all | solution.py:297
  114.2 15.5 %collective-permute-start.22 = (f32[1,128]{1,0:T(1,128)S(1)}, f32[1,128]{1,0:T(1,128)S(1)}, u32[]{:S(2)}, u32[]{:S(2)}) collective-permute-start(f32[1,128]{1,0:T(1,128)S(1)} %bitcast_multiply_fusion), channel_id=1, source_target_pairs={{0,132},{1,133},{2,134},{3,135},{4,128},{5,129},{6,130},{7,131},{8... | collective-permute-start | bytes 1544 | tf_op jit(solution)/shard_map/ppermute | solution.py:29
  117.3 12.3 %collective-permute-start.21 = (f32[1,128]{1,0:T(1,128)S(1)}, f32[1,128]{1,0:T(1,128)S(1)}, u32[]{:S(2)}, u32[]{:S(2)}) collective-permute-start(f32[1,128]{1,0:T(1,128)S(1)} %bitcast_multiply_fusion), channel_id=1, source_target_pairs={{0,128},{1,129},{2,130},{3,131},{4,132},{5,133},{6,134},{7,135},{8... | collective-permute-start | bytes 1544 | tf_op jit(solution)/shard_map/ppermute | solution.py:29
  117.8 11.8 %collective-permute-start.20 = (f32[1,128]{1,0:T(1,128)S(1)}, f32[1,128]{1,0:T(1,128)S(1)}, u32[]{:S(2)}, u32[]{:S(2)}) collective-permute-start(f32[1,128]{1,0:T(1,128)S(1)} %bitcast_multiply_fusion), channel_id=1, source_target_pairs={{0,4},{1,5},{2,6},{3,7},{4,0},{5,1},{6,2},{7,3},{8,12},{9,13},{10,... | collective-permute-start | bytes 1544 | tf_op jit(solution)/shard_map/ppermute | solution.py:29
  133.0 14.5 %collective-permute-start.29 = (bf16[256,512]{1,0:T(8,128)(2,1)}, bf16[256,512]{1,0:T(8,128)(2,1)S(1)}, u32[]{:S(2)}, u32[]{:S(2)}) collective-permute-start(bf16[256,512]{1,0:T(8,128)(2,1)} %get-tuple-element.28), channel_id=1, source_target_pairs={{0,32},{1,33},{2,34},{3,35},{4,36},{5,37},{6,38},{7,39},{8,40},{9,... | collective-permute-start | bytes 786440 | tf_op jit(solution)/shard_map/ppermute | solution.py:29
  133.0 14.5 %collective-permute-start.28 = (bf16[256,512]{1,0:T(8,128)(2,1)}, bf16[256,512]{1,0:T(8,128)(2,1)S(1)}, u32[]{:S(2)}, u32[]{:S(2)}) collective-permute-start(bf16[256,512]{1,0:T(8,128)(2,1)} %get-tuple-element.27), channel_id=1, source_target_pairs={{0,64},{1,65},{2,66},{3,67},{4,68},{5,69},{6,70},{7,71},{8,72},{9,... | collective-permute-start | bytes 786440 | tf_op jit(solution)/shard_map/ppermute | solution.py:29
  135.3 12.8 %collective-permute-start.27 = (bf16[256,512]{1,0:T(8,128)(2,1)}, bf16[256,512]{1,0:T(8,128)(2,1)S(1)}, u32[]{:S(2)}, u32[]{:S(2)}) collective-permute-start(bf16[256,512]{1,0:T(8,128)(2,1)} %get-tuple-element.26), channel_id=1, source_target_pairs={{0,96},{1,97},{2,98},{3,99},{4,100},{5,101},{6,102},{7,103},{8,104... | collective-permute-start | bytes 786440 | tf_op jit(solution)/shard_map/ppermute | solution.py:29
  137.0 13.1 %collective-permute-start.26 = (f32[128,256]{1,0:T(8,128)S(1)}, f32[128,256]{1,0:T(8,128)S(1)}, u32[]{:S(2)}, u32[]{:S(2)}) collective-permute-start(f32[128,256]{1,0:T(8,128)S(1)} %convert_reduce_fusion), channel_id=1, source_target_pairs={{0,0},{1,132},{2,128},{3,4},{4,24},{5,156},{6,152},{7,28},{8,9},{9... | collective-permute-start | bytes 393224 | tf_op jit(solution)/shard_map/ppermute | solution.py:29
  (16 other events, 152.8 us)

commit v2 on v0

--- a/solution.py
+++ b/solution.py
@@ -49,18 +49,25 @@
     return send(value, lambda zl, y, zh, x, core: (zl, y, zh, x, 1 - core))
 
 
-def pick_kernel(order_ref, hidden_ref, own_ref, *half_refs):
-    def block(i):
-        return hidden_ref[:, pl.ds(pl.multiple_of(order_ref[i] * 256, 256), 256)]
+def coordinates(index):
+    return index // 128, index // 32 % 4, index // 8 % 4, index // 2 % 4, index % 2
+
+
+def pick_kernel(index_ref, hidden_ref, own_ref, *half_refs):
+    _, y, zh, _, core = coordinates(index_ref[0])
+
+    def block(k, p):
+        spot = (y + 8 - p - 2 * core) % 4 * 4 + (zh + k) % 4
+        return hidden_ref[:, pl.ds(pl.multiple_of(spot * 256, 256), 256)]
 
     for p in range(4):
-        own_ref[p] = block(p)
+        own_ref[p] = block(0, p)
     for k in (1, 2, 3):
         for p in range(2):
-            half_refs[k - 1][p] = block(4 * k + p)
-
-
-def picked_blocks(hidden, order):
+            half_refs[k - 1][p] = block(k, p)
+
+
+def picked_blocks(index, hidden):
     rows = hidden.shape[0]
     half = jax.ShapeDtypeStruct((2, rows, 256), hidden.dtype)
     return pl.pallas_call(
@@ -68,38 +75,71 @@
         in_specs=[pl.BlockSpec(memory_space=pltpu.SMEM), pl.BlockSpec(memory_space=pltpu.VMEM)],
         out_shape=(jax.ShapeDtypeStruct((4, rows, 256), hidden.dtype), half, half, half),
         name="pick",
-    )(order, hidden)
-
-
-def teacher_kernel(order_ref, normed_ref, head_ref, out_ref):
-    core = order_ref[8]
-    scores = jnp.dot(normed_ref[...], head_ref[...], preferred_element_type=jnp.float32)
-    for k in range(2):
-        out_ref[k ^ core, 0] = scores[:, 512 * k : 512 * (k + 1)]
-
-
-def teacher_parts(normed, head, order):
-    rows, depth = normed.shape
+    )(index, hidden)
+
+
+def split(value):
+    high = value.astype(jnp.bfloat16)
+    return high, (value - high.astype(jnp.float32)).astype(jnp.bfloat16)
+
+
+def teacher_kernel(index_ref, hidden_ref, gain_ref, *refs):
+    head_refs, out_ref, both_ref, squares_ref = refs[:4], refs[4], refs[5], refs[6]
+    rows, depth = hidden_ref.shape
+
+    @pl.when(pl.program_id(0) == 0)
+    def _():
+        hidden = hidden_ref[...].astype(jnp.float32)
+        high, low = split(hidden * gain_ref[...].astype(jnp.float32).reshape(1, depth))
+        both_ref[:rows] = high
+        both_ref[rows:] = low
+        eighth = jnp.full((8, depth), 0.125, jnp.bfloat16)
+        squares = sum(
+            lax.dot_general(eighth, part, (((1,), (1,)), ((), ())), preferred_element_type=jnp.float32)
+            for part in split(hidden * hidden)
+        )
+        squares_ref[...] = jnp.zeros_like(squares_ref)
+        squares_ref[:, :rows] = squares
+
+    for i in range(4):
+        scores = jnp.dot(both_ref[...], head_refs[i][...], preferred_element_type=jnp.float32)
+        out_ref[i, :rows] = scores[:rows] + scores[rows:]
+        out_ref[i, rows:] = squares_ref[...]
+
+
+def teacher_parts(index, hidden, gain, head, other):
+    rows, depth = hidden.shape
+
+    def block(n):
+        def spot(i, index_ref):
+            zl, _, _, x, core = coordinates(index_ref[0])
+            zl = (zl + n) % 2
+            return 0, (zl * 4 + (x + 2 * i + n // 2) % 4) * 2 + (core + other) % 2
+
+        return pl.BlockSpec((depth, 512), spot)
+
     return pl.pallas_call(
         teacher_kernel,
         grid_spec=pltpu.PrefetchScalarGridSpec(
             num_scalar_prefetch=1,
-            grid=(8,),
+            grid=(2,),
             in_specs=[
-                pl.BlockSpec((rows, depth), lambda i, order_ref: (0, 0)),
-                pl.BlockSpec((depth, 1024), lambda i, order_ref: (0, order_ref[i])),
+                pl.BlockSpec((rows, depth), lambda i, index_ref: (0, 0)),
+                pl.BlockSpec((depth,), lambda i, index_ref: (0,)),
+                *(block(n) for n in range(4)),
             ],
-            out_specs=pl.BlockSpec((2, 1, rows, 512), lambda i, order_ref: (0, i, 0, 0)),
+            out_specs=pl.BlockSpec((4, rows + 8, 512), lambda i, index_ref: (i, 0, 0)),
+            scratch_shapes=[pltpu.VMEM((2 * rows, depth), jnp.bfloat16), pltpu.VMEM((8, 512), jnp.float32)],
         ),
-        out_shape=jax.ShapeDtypeStruct((2, 8, rows, 512), jnp.float32),
+        out_shape=jax.ShapeDtypeStruct((8, rows + 8, 512), jnp.float32),
         name="teacher",
-    )(order, normed, head)
-
-
-def student_kernel(core_ref, *refs):
+    )(index, hidden, gain, head, head, head, head)
+
+
+def student_kernel(index_ref, *refs):
     own_ref, near_refs, far_refs, head_refs = refs[0], refs[1:4], refs[4:7], refs[7:11]
-    out_ref, hidden_ref = refs[11:]
-    core = core_ref[0]
+    first_ref, out_ref, hidden_ref = refs[11:]
+    core = index_ref[0] % 2
     for p in range(2):
         hidden_ref[0, 2 * core + p] = own_ref[p]
         hidden_ref[0, 2 * (1 - core) + p] = own_ref[2 + p]
@@ -111,24 +151,28 @@
         for j in range(4):
             term = jnp.dot(hidden_ref[k, j], head_refs[j][...], preferred_element_type=jnp.float32)
             total = term if total is None else total + term
-        out_ref[k] = total
-
-
-def student_parts(core, own, near, far, head_slots):
+        if k == 0:
+            first_ref[...] = total
+        else:
+            out_ref[k - 1] = total
+
+
+def student_parts(index, own, near, far, head_slots):
     vmem = pl.BlockSpec(memory_space=pltpu.VMEM)
     return pl.pallas_call(
         student_kernel,
         in_specs=[pl.BlockSpec(memory_space=pltpu.SMEM)] + [vmem] * 11,
         out_shape=(
-            jax.ShapeDtypeStruct((4, 128, 512), jnp.float32),
+            jax.ShapeDtypeStruct((128, 512), jnp.float32),
+            jax.ShapeDtypeStruct((3, 128, 512), jnp.float32),
             jax.ShapeDtypeStruct((4, 4, 128, 256), jnp.bfloat16),
         ),
         name="student",
-    )(core.reshape(1), own, *near, *far, *head_slots)
+    )(index, own, *near, *far, *head_slots)
 
 
 def head_grad_kernel(*refs):
-    hidden_ref, grad_refs, own_ref, out_ref = refs[0], refs[1:5], refs[5], refs[6]
+    hidden_ref, grad_refs, own_ref, out_refs = refs[0], refs[1:5], refs[5], refs[6:]
     for j in range(4):
         total = None
         for k in range(4):
@@ -139,7 +183,7 @@
         if j == 0:
             own_ref[...] = total
         else:
-            out_ref[j - 1] = total.astype(out_ref.dtype)
+            out_refs[j - 1][...] = total.astype(jnp.bfloat16)
 
 
 def head_grad_parts(hidden, grad_slots):
@@ -147,63 +191,68 @@
         head_grad_kernel,
         out_shape=(
             jax.ShapeDtypeStruct((256, 512), jnp.float32),
-            jax.ShapeDtypeStruct((3, 256, 512), jnp.bfloat16),
+            *[jax.ShapeDtypeStruct((256, 512), jnp.bfloat16)] * 3,
         ),
         name="head_grad",
     )(hidden, *grad_slots)
 
 
-def hidden_grad_kernel(*refs):
-    grad_refs, head_refs, out_ref = refs[:4], refs[4:8], refs[8]
+def hidden_grad_kernel(index_ref, *refs):
+    grad_refs, head_refs, own_ref, other_ref = refs[:4], refs[4:8], refs[8], refs[9]
+    zl, _, _, x, core = coordinates(index_ref[0])
     for k in range(4):
         for j in range(4):
-            out_ref[4 * k + j] = lax.dot_general(
+            spot = (k % 2 * 2 + j // 2 + 4 - x) % 4 * 2 + (k // 2 + zl) % 2
+            term = lax.dot_general(
                 grad_refs[k][...], head_refs[j][...], (((1,), (1,)), ((), ())), preferred_element_type=jnp.float32
-            ).astype(out_ref.dtype)
-
-
-def hidden_grad_parts(grad_slots, head_slots):
+            )
+
+            @pl.when(core == j % 2)
+            def _():
+                own_ref[spot] = term
+
+            @pl.when(core != j % 2)
+            def _():
+                other_ref[spot] = term
+
+
+def hidden_grad_parts(index, grad_slots, head_slots):
+    vmem = pl.BlockSpec(memory_space=pltpu.VMEM)
     return pl.pallas_call(
         hidden_grad_kernel,
-        out_shape=jax.ShapeDtypeStruct((16, 128, 256), jnp.bfloat16),
+        in_specs=[pl.BlockSpec(memory_space=pltpu.SMEM)] + [vmem] * 8,
+        out_shape=(jax.ShapeDtypeStruct((8, 128, 256), jnp.float32),) * 2,
         name="hidden_grad",
-    )(*grad_slots, *head_slots)
+    )(index, *grad_slots, *head_slots)
 
 
 def step(teacher_hidden, teacher_gain, teacher_head, student_hidden, student_head, depth_cut):
     f32, f16, bf16 = jnp.float32, jnp.float16, jnp.bfloat16
     zl = lax.axis_index("group")
-    dp, mp = lax.axis_index("dp"), lax.axis_index("mp")
-    y, zh, x, core = dp // 4, dp % 4, mp // 2, mp % 2
-
-    hidden_float = teacher_hidden.astype(f32)
-    own_squares = jnp.sum(hidden_float * hidden_float, axis=1)
-    squares = lax.all_to_all(
-        jnp.broadcast_to(own_squares[None, None], (16, 1, 128)), PLANE, 0, 0, tiled=True
-    ).sum(axis=(0, 1))
-
-    steps = jnp.arange(4, dtype=jnp.int32)
-    order = (((y - steps - 2 * core) % 4 * 4)[None, :] + ((zh + steps) % 4)[:, None]).reshape(16)
-    own, *halves = picked_blocks(student_hidden, order)
+    x = lax.axis_index("mp") // 2
+    index = lax.axis_index(ALL).reshape(1)
+
+    own, *halves = picked_blocks(index, student_hidden)
     near = [to_zh(halves[k - 1], k) for k in (1, 2, 3)]
     head_slots = [student_head] + [to_y(student_head, j) for j in (1, 2, 3)]
     far = [to_core(half) for half in near]
 
-    row_scale = lax.rsqrt(squares / DT + epsilon)
-    normed = (hidden_float * row_scale[:, None] * teacher_gain.astype(f32)[None, :]).astype(bf16)
-    spots = jnp.arange(8, dtype=jnp.int32)
-    order = (zl ^ (spots % 2)) * 4 + (x + spots // 2) % 4
-    parts = teacher_parts(normed, teacher_head, jnp.append(order, core)).reshape(2, 4, 2, 128, 512)
-    by_core = parts[0] + to_core(parts[1].astype(f16)).astype(f32)
-    by_x = by_core[0]
+    other = teacher_parts(index, teacher_hidden, teacher_gain, teacher_head, 1)
+    other = to_core(other)
+    parts = teacher_parts(index, teacher_hidden, teacher_gain, teacher_head, 0)
+    by_x = parts[:2] + other[:2]
     for step in (1, 2, 3):
-        by_x = by_x + to_x(by_core[step].astype(f16), step).astype(f32)
+        part = parts[2 * step : 2 * step + 2] + other[2 * step : 2 * step + 2]
+        by_x = by_x + to_x(part.astype(f16), step).astype(f32)
     teacher = by_x[0] + to_zl(by_x[1].astype(f16)).astype(f32)
 
-    parts, hidden = student_parts(core, own, near, far, head_slots)
-    student = parts[0]
+    student, parts, hidden = student_parts(index, own, near, far, head_slots)
+    parts = parts.astype(f16)
     for k in (1, 2, 3):
-        student = student + to_zh(parts[k].astype(f16), -k).astype(f32)
+        student = student + to_zh(parts[k - 1], -k).astype(f32)
+
+    row_scale = lax.rsqrt(teacher[128, :128] * (8 / DT) + epsilon)
+    teacher = teacher[:128] * row_scale[:, None]
 
     teacher_max = jnp.max(teacher, axis=1)
     student_max = jnp.max(student, axis=1)
@@ -258,19 +307,24 @@
     )
 
     grad_slots = [score_grad] + [to_zh(score_grad, k) for k in (1, 2, 3)]
-    parts = hidden_grad_parts(grad_slots, head_slots)
-    parts = lax.all_to_all(parts, PLANE, 0, 0, tiled=True)
-    hidden_grad = jnp.sum(parts.astype(f32), axis=0)
-    head_grad, parts = head_grad_parts(hidden, grad_slots)
+    own, other = hidden_grad_parts(index, grad_slots, head_slots)
+    other = to_core(other)
+    head_grad, *parts = head_grad_parts(hidden, grad_slots)
     for j in (1, 2, 3):
         head_grad = head_grad + to_y(parts[j - 1], -j).astype(f32)
+    by_x = own[:2] + other[:2]
+    for step in (1, 2, 3):
+        part = own[2 * step : 2 * step + 2] + other[2 * step : 2 * step + 2]
+        by_x = by_x + to_x(part.astype(bf16), step).astype(f32)
 
     def home(zl, y, zh, x, core):
         k, j = zl * 2 + x // 2, x % 2 * 2 + core
         spot = (y - j) % 4 * 4 + zh
         return spot // 8, y, zh - k, spot % 8 // 2, spot % 2
 
-    hidden_grad = send(hidden_grad, home)
+    hidden_grad = send(by_x[0], home) + send(
+        by_x[1], lambda zl, y, zh, x, core: home(1 - zl, y, zh, x, core)
+    )
     return (kl_terms, hidden_grad, head_grad)
 
 

time: 160 us -> 141 us (0.88)
  the two profiles are of different devices: /device:TPU:2 before, /device:TPU:14 now
where the time goes in v2:
time: 141 us
  starting transfers between devices  61.6 us (44%)
  waiting for transfers between devices  38.6 us (27%)
  Pallas kernels  25.3 us (18%)
  other arithmetic  11.7 us (8%)
  local copies, waits for them, and re-layouts  2.83 us (2%)
    ppermute x35, starting transfers between devices, send(): return lax.ppermute(value, ALL, pairs)  61.6 us
    ppermute x35, waiting for transfers between devices, send(): return lax.ppermute(value, ALL, pairs)  38.6 us
    pallas_call x2, Pallas kernels, teacher_parts(): pl.pallas_call(teacher_kernel, grid_spec=pltpu.PrefetchScalarGridSpec(num...  8.79 us
    pallas_call x1, Pallas kernels, hidden_grad_parts(): pl.pallas_call(hidden_grad_kernel, in_specs=[pl.BlockSpec(memory_space=pl...  7.37 us
    pallas_call x1, Pallas kernels, student_parts(): pl.pallas_call(student_kernel, in_specs=[pl.BlockSpec(memory_space=pltpu....  3.64 us
    pallas_call x1, Pallas kernels, head_grad_parts(): pl.pallas_call(head_grad_kernel, out_shape=(jax.ShapeDtypeStruct((256, 51...  3.39 us
  transfers between devices with their start and end apart: 35, of which 16 were waited for; matrix products, arithmetic and copies ran while one was open for 7% of the time, Pallas kernels for 10%

profile of v2, /device:TPU:14, one launch (start us, length us, event | category | flops | bytes accessed | tf_op | source)
XLA Modules:
  0.0 141.0 jit_solution(10625331893762412545)
XLA Ops:
  0.7 4.5 %teacher.3 = f32[8,136,512]{2,1,0:T(8,128)} custom-call(s32[1]{0:T(128)} %bitcast.index_ref, bf16[128,512]{1,0:T(8,128)(2,1)} %hidden_ref.4, bf16[512]{0:T(512)(128)(2,1)} %gain_ref.3, bf16[512,8192]{1,0:T(8,128)(2,1)} %refs_3_.3, bf16[512,8192]{1,0:T(8,128)(2,1)} %refs_3_.3, bf16[512,8192]{1,0:T(8,128)(2,1)} %refs_3_.3, bf16[512,8192]{1,0:T(8,128)(2,1)} %refs_3_.3), custom_call_target="tpu_custom_call" | custom-call | tf_op jit(solution)/shard_map/teacher/pallas_call | solution.py:121
  5.1 2.1 %pick.1 = (bf16[4,128,256]{2,1,0:T(8,128)(2,1)}, bf16[2,128,256]{2,1,0:T(8,128)(2,1)}, bf16[2,128,256]{2,1,0:T(8,128)(2,1)}, bf16[2,128,256]{2,1,0:T(8,128)(2,1)}) custom-call(s32[1]{0:T(128)} %bitcast.index_ref, bf16[128,4096]{1,0:T(8,128)(2,1)} %hidden_ref.5), custom_call_target="tpu_custom_call" | custom-call | tf_op jit(solution)/shard_map/pick/pallas_call | solution.py:73
  7.3 3.3 %collective-permute-start.5 = (bf16[2,128,256]{2,1,0:T(8,128)(2,1)}, bf16[2,128,256]{2,1,0:T(8,128)(2,1)S(1)}, u32[]{:S(2)}, u32[]{:S(2)}) collective-permute-start(bf16[2,128,256]{2,1,0:T(8,128)(2,1)} %get-tuple-element.17), channel_id=1, source_target_pairs={{0,8},{1,9},{2,10},{3,11},{4,12},{5,13},{6,14},{7,15},{8,16},{9,17... | collective-permute-start | bytes 393224 | tf_op jit(solution)/shard_map/ppermute | solution.py:29
  10.5 5.4 %collective-permute-start.6 = (bf16[2,128,256]{2,1,0:T(8,128)(2,1)}, bf16[2,128,256]{2,1,0:T(8,128)(2,1)}, u32[]{:S(2)}, u32[]{:S(2)}) collective-permute-start(bf16[2,128,256]{2,1,0:T(8,128)(2,1)} %get-tuple-element.18), channel_id=1, source_target_pairs={{0,16},{1,17},{2,18},{3,19},{4,20},{5,21},{6,22},{7,23},{8,24},{9,... | collective-permute-start | bytes 393224 | tf_op jit(solution)/shard_map/ppermute | solution.py:29
  15.9 2.7 %collective-permute-start.7 = (bf16[2,128,256]{2,1,0:T(8,128)(2,1)}, bf16[2,128,256]{2,1,0:T(8,128)(2,1)}, u32[]{:S(2)}, u32[]{:S(2)}) collective-permute-start(bf16[2,128,256]{2,1,0:T(8,128)(2,1)} %get-tuple-element.19), channel_id=1, source_target_pairs={{0,24},{1,25},{2,26},{3,27},{4,28},{5,29},{6,30},{7,31},{8,0},{9,1... | collective-permute-start | bytes 393224 | tf_op jit(solution)/shard_map/ppermute | solution.py:29
  18.6 1.7 %collective-permute-start.11 = (bf16[256,512]{1,0:T(8,128)(2,1)S(1)}, bf16[256,512]{1,0:T(8,128)(2,1)S(1)}, u32[]{:S(2)}, u32[]{:S(2)}) collective-permute-start(bf16[256,512]{1,0:T(8,128)(2,1)S(1)} %copy-done.1), channel_id=1, source_target_pairs={{0,32},{1,33},{2,34},{3,35},{4,36},{5,37},{6,38},{7,39},{8,40},{9,... | collective-permute-start | bytes 786440 | tf_op jit(solution)/shard_map/ppermute | solution.py:29
  20.3 4.3 %teacher.2 = f32[8,136,512]{2,1,0:T(8,128)} custom-call(s32[1]{0:T(128)} %bitcast.index_ref, bf16[128,512]{1,0:T(8,128)(2,1)} %hidden_ref.4, bf16[512]{0:T(512)(128)(2,1)} %gain_ref.3, bf16[512,8192]{1,0:T(8,128)(2,1)} %refs_3_.3, bf16[512,8192]{1,0:T(8,128)(2,1)} %refs_3_.3, bf16[512,8192]{1,0:T(8,128)(2,1)} %refs_3_.3, bf16[512,8192]{1,0:T(8,128)(2,1)} %refs_3_.3), custom_call_target="tpu_custom_call" | custom-call | tf_op jit(solution)/shard_map/teacher/pallas_call | solution.py:121
  26.0 2.3 %collective-permute-start.12 = (bf16[256,512]{1,0:T(8,128)(2,1)S(1)}, bf16[256,512]{1,0:T(8,128)(2,1)S(1)}, u32[]{:S(2)}, u32[]{:S(2)}) collective-permute-start(bf16[256,512]{1,0:T(8,128)(2,1)S(1)} %copy-done.1), channel_id=1, source_target_pairs={{0,64},{1,65},{2,66},{3,67},{4,68},{5,69},{6,70},{7,71},{8,72},{9,... | collective-permute-start | bytes 786440 | tf_op jit(solution)/shard_map/ppermute | solution.py:29
  30.3 2.6 %fusion.2 = (f16[2,136,512]{2,1,0:T(8,128)(2,1)S(1)}, f16[2,136,512]{2,1,0:T(8,128)(2,1)}, f16[2,136,512]{2,1,0:T(8,128)(2,1)}) fusion(f32[8,136,512]{2,1,0:T(8,128)S(1)} %collective-permute-done, f32[8,136,512]{2,1,0:T(8,128)} %teacher.2), kind=kLoop, calls=%fused_computation.5 | loop fusion | flops 835584 | bytes 4177920 | tf_op jit(solution)/shard_map/convert_element_type | solution.py:246
  34.9 2.2 %collective-permute-start.1 = (f16[2,136,512]{2,1,0:T(8,128)(2,1)S(1)}, f16[2,136,512]{2,1,0:T(8,128)(2,1)}, u32[]{:S(2)}, u32[]{:S(2)}) collective-permute-start(f16[2,136,512]{2,1,0:T(8,128)(2,1)S(1)} %get-tuple-element.39), channel_id=1, source_target_pairs={{0,2},{1,3},{2,4},{3,5},{4,6},{5,7},{6,0},{7,1},{8,10},{9,11},{10,... | collective-permute-start | bytes 835592 | tf_op jit(solution)/shard_map/ppermute | solution.py:29
  37.1 3.7 %collective-permute-done.13.refs_10_.refs_7_ = bf16[256,512]{1,0:T(8,128)(2,1)S(1)} collective-permute-done((bf16[256,512]{1,0:T(8,128)(2,1)S(1)}, bf16[256,512]{1,0:T(8,128)(2,1)S(1)}, u32[]{:S(2)}, u32[]{:S(2)}) %collective-permute-start.13) | collective-permute-done | bytes 262176 | tf_op jit(solution)/shard_map/ppermute | solution.py:29
  41.5 3.6 %student.1 = (f32[128,512]{1,0:T(8,128)}, f32[3,128,512]{2,1,0:T(8,128)}, bf16[4,4,128,256]{3,2,1,0:T(8,128)(2,1)}) custom-call(s32[1]{0:T(128)} %bitcast.index_ref, bf16[4,128,256]{2,1,0:T(8,128)(2,1)} %get-tuple-element.16.refs_0_, bf16[2,128,256]{2,1,0:T(8,128)(2,1)} %copy-done.9, bf16[2,128,256]{2,1,0:T(8,128)(2,1)} %collective-permute-done.6.refs_2_, ...), custom_call_target="tpu_custom_call" | custom-call | tf_op jit(solution)/shard_map/student/pallas_call | solution.py:162
  46.4 4.3 %collective-permute-start.16 = (f16[128,512]{1,0:T(8,128)(2,1)S(1)}, f16[128,512]{1,0:T(8,128)(2,1)S(1)}, u32[]{:S(2)}, u32[]{:S(2)}) collective-permute-start(f16[128,512]{1,0:T(8,128)(2,1)S(1)} %get-tuple-element.46), channel_id=1, source_target_pairs={{0,8},{1,9},{2,10},{3,11},{4,12},{5,13},{6,14},{7,15},{8,16},{9,17... | collective-permute-start | bytes 393224 | tf_op jit(solution)/shard_map/ppermute | solution.py:29
  50.7 4.1 %collective-permute-start.15 = (f16[128,512]{1,0:T(8,128)(2,1)S(1)}, f16[128,512]{1,0:T(8,128)(2,1)S(1)}, u32[]{:S(2)}, u32[]{:S(2)}) collective-permute-start(f16[128,512]{1,0:T(8,128)(2,1)S(1)} %get-tuple-element.47), channel_id=1, source_target_pairs={{0,16},{1,17},{2,18},{3,19},{4,20},{5,21},{6,22},{7,23},{8,24},{9,... | collective-permute-start | bytes 393224 | tf_op jit(solution)/shard_map/ppermute | solution.py:29
  54.9 3.9 %collective-permute-start.14 = (f16[128,512]{1,0:T(8,128)(2,1)S(1)}, f16[128,512]{1,0:T(8,128)(2,1)S(1)}, u32[]{:S(2)}, u32[]{:S(2)}) collective-permute-start(f16[128,512]{1,0:T(8,128)(2,1)S(1)} %get-tuple-element.45), channel_id=1, source_target_pairs={{0,24},{1,25},{2,26},{3,27},{4,28},{5,29},{6,30},{7,31},{8,0},{9,1... | collective-permute-start | bytes 393224 | tf_op jit(solution)/shard_map/ppermute | solution.py:29
  60.4 4.5 %collective-permute-done.15 = f16[128,512]{1,0:T(8,128)(2,1)S(1)} collective-permute-done((f16[128,512]{1,0:T(8,128)(2,1)S(1)}, f16[128,512]{1,0:T(8,128)(2,1)S(1)}, u32[]{:S(2)}, u32[]{:S(2)}) %collective-permute-start.15) | collective-permute-done | bytes 131104 | tf_op jit(solution)/shard_map/ppermute | solution.py:29
  72.4 2.0 %collective-permute-start.23 = (bf16[128,512]{1,0:T(8,128)(2,1)S(1)}, bf16[128,512]{1,0:T(8,128)(2,1)S(1)}, u32[]{:S(2)}, u32[]{:S(2)}) collective-permute-start(bf16[128,512]{1,0:T(8,128)(2,1)S(1)} %subtract_convert_fusion.refs_0_.refs_1_), channel_id=1, source_target_pairs={{0,8},{1,9},{2,10},{3,11},{4,12},{5,13},{6,14},{7,15},{8,16},{9,17... | collective-permute-start | bytes 393224 | tf_op jit(solution)/shard_map/ppermute | solution.py:29
  74.4 3.2 %collective-permute-start.24 = (bf16[128,512]{1,0:T(8,128)(2,1)S(1)}, bf16[128,512]{1,0:T(8,128)(2,1)S(1)}, u32[]{:S(2)}, u32[]{:S(2)}) collective-permute-start(bf16[128,512]{1,0:T(8,128)(2,1)S(1)} %subtract_convert_fusion.refs_0_.refs_1_), channel_id=1, source_target_pairs={{0,16},{1,17},{2,18},{3,19},{4,20},{5,21},{6,22},{7,23},{8,24},{9,... | collective-permute-start | bytes 393224 | tf_op jit(solution)/shard_map/ppermute | solution.py:29
  79.0 2.6 %collective-permute-done.23.refs_1_.refs_2_ = bf16[128,512]{1,0:T(8,128)(2,1)S(1)} collective-permute-done((bf16[128,512]{1,0:T(8,128)(2,1)S(1)}, bf16[128,512]{1,0:T(8,128)(2,1)S(1)}, u32[]{:S(2)}, u32[]{:S(2)}) %collective-permute-start.23) | collective-permute-done | bytes 131104 | tf_op jit(solution)/shard_map/ppermute | solution.py:29
  81.6 7.4 %collective-permute-done.24.refs_2_.refs_3_ = bf16[128,512]{1,0:T(8,128)(2,1)S(1)} collective-permute-done((bf16[128,512]{1,0:T(8,128)(2,1)S(1)}, bf16[128,512]{1,0:T(8,128)(2,1)S(1)}, u32[]{:S(2)}, u32[]{:S(2)}) %collective-permute-start.24) | collective-permute-done | bytes 131104 | tf_op jit(solution)/shard_map/ppermute | solution.py:29
  90.4 7.4 %hidden_grad.1 = (f32[8,128,256]{2,1,0:T(8,128)}, f32[8,128,256]{2,1,0:T(8,128)}) custom-call(s32[1]{0:T(128)} %bitcast.index_ref, bf16[128,512]{1,0:T(8,128)(2,1)} %copy-done, bf16[128,512]{1,0:T(8,128)(2,1)} %copy-done.5, bf16[128,512]{1,0:T(8,128)(2,1)} %copy-done.6, bf16[128,512]{1,0:T(8,128)(2,1)} %copy-done.7, bf16[256,512]{1,0:T(8,128)(2,1)} %refs_4_.1, ...), custom_call_target="tpu_custom_call" | custom-call | tf_op jit(solution)/shard_map/hidden_grad/pallas_call | solution.py:221
  97.9 2.6 %collective-permute-start.21 = (f32[1,128]{1,0:T(1,128)S(1)}, f32[1,128]{1,0:T(1,128)S(1)}, u32[]{:S(2)}, u32[]{:S(2)}) collective-permute-start(f32[1,128]{1,0:T(1,128)S(1)} %bitcast_multiply_fusion), channel_id=1, source_target_pairs={{0,128},{1,129},{2,130},{3,131},{4,132},{5,133},{6,134},{7,135},{8... | collective-permute-start | bytes 1544 | tf_op jit(solution)/shard_map/ppermute | solution.py:29
  100.5 2.4 %collective-permute-start.20 = (f32[1,128]{1,0:T(1,128)S(1)}, f32[1,128]{1,0:T(1,128)S(1)}, u32[]{:S(2)}, u32[]{:S(2)}) collective-permute-start(f32[1,128]{1,0:T(1,128)S(1)} %bitcast_multiply_fusion), channel_id=1, source_target_pairs={{0,4},{1,5},{2,6},{3,7},{4,0},{5,1},{6,2},{7,3},{8,12},{9,13},{10,... | collective-permute-start | bytes 1544 | tf_op jit(solution)/shard_map/ppermute | solution.py:29
  103.9 1.7 %collective-permute-done.20 = f32[1,128]{1,0:T(1,128)S(1)} collective-permute-done((f32[1,128]{1,0:T(1,128)S(1)}, f32[1,128]{1,0:T(1,128)S(1)}, u32[]{:S(2)}, u32[]{:S(2)}) %collective-permute-start.20) | collective-permute-done | bytes 544 | tf_op jit(solution)/shard_map/ppermute | solution.py:29
  107.8 3.3 %collective-permute-start.28 = (bf16[2,128,256]{2,1,0:T(8,128)(2,1)S(1)}, bf16[2,128,256]{2,1,0:T(8,128)(2,1)S(1)}, u32[]{:S(2)}, u32[]{:S(2)}) collective-permute-start(bf16[2,128,256]{2,1,0:T(8,128)(2,1)S(1)} %get-tuple-element.44), channel_id=1, source_target_pairs={{0,4},{1,5},{2,6},{3,7},{4,0},{5,1},{6,2},{7,3},{8,12},{9,13},{10,... | collective-permute-start | bytes 393224 | tf_op jit(solution)/shard_map/ppermute | solution.py:29
  112.5 3.4 %head_grad.1 = (f32[256,512]{1,0:T(8,128)}, bf16[256,512]{1,0:T(8,128)(2,1)}, bf16[256,512]{1,0:T(8,128)(2,1)}, bf16[256,512]{1,0:T(8,128)(2,1)}) custom-call(bf16[4,4,128,256]{3,2,1,0:T(8,128)(2,1)} %get-tuple-element.24.refs_0_, bf16[128,512]{1,0:T(8,128)(2,1)} %copy-done, bf16[128,512]{1,0:T(8,128)(2,1)} %copy-done.5, bf16[128,512]{1,0:T(8,128)(2,1)} %copy-done.6, ...), custom_call_target="tpu_custom_call" | custom-call | tf_op jit(solution)/shard_map/head_grad/pallas_call | solution.py:190
  118.4 2.4 %collective-permute-start.32 = (bf16[256,512]{1,0:T(8,128)(2,1)}, bf16[256,512]{1,0:T(8,128)(2,1)S(1)}, u32[]{:S(2)}, u32[]{:S(2)}) collective-permute-start(bf16[256,512]{1,0:T(8,128)(2,1)} %get-tuple-element.26), channel_id=1, source_target_pairs={{0,96},{1,97},{2,98},{3,99},{4,100},{5,101},{6,102},{7,103},{8,104... | collective-permute-start | bytes 786440 | tf_op jit(solution)/shard_map/ppermute | solution.py:29
  121.9 3.5 %collective-permute-start.30 = (f32[128,256]{1,0:T(8,128)S(1)}, f32[128,256]{1,0:T(8,128)S(1)}, u32[]{:S(2)}, u32[]{:S(2)}) collective-permute-start(f32[128,256]{1,0:T(8,128)S(1)} %get-tuple-element.49), channel_id=1, source_target_pairs={{0,0},{1,132},{2,128},{3,4},{4,24},{5,156},{6,152},{7,28},{8,9},{9... | collective-permute-start | bytes 393224 | tf_op jit(solution)/shard_map/ppermute | solution.py:29
  125.4 2.1 %collective-permute-start.31 = (f32[128,256]{1,0:T(8,128)S(1)}, f32[128,256]{1,0:T(8,128)S(1)}, u32[]{:S(2)}, u32[]{:S(2)}) collective-permute-start(f32[128,256]{1,0:T(8,128)S(1)} %get-tuple-element.48), channel_id=1, source_target_pairs={{0,16},{1,148},{2,144},{3,20},{4,8},{5,140},{6,136},{7,12},{8,25},... | collective-permute-start | bytes 393224 | tf_op jit(solution)/shard_map/ppermute | solution.py:29
  127.5 2.4 %collective-permute-done.32 = bf16[256,512]{1,0:T(8,128)(2,1)S(1)} collective-permute-done((bf16[256,512]{1,0:T(8,128)(2,1)}, bf16[256,512]{1,0:T(8,128)(2,1)S(1)}, u32[]{:S(2)}, u32[]{:S(2)}) %collective-permute-start.32) | collective-permute-done | bytes 262176 | tf_op jit(solution)/shard_map/ppermute | solution.py:29
  129.9 2.0 %convert_add_fusion = f32[256,512]{1,0:T(8,128)} fusion(bf16[256,512]{1,0:T(8,128)(2,1)S(1)} %collective-permute-done.34, bf16[256,512]{1,0:T(8,128)(2,1)S(1)} %collective-permute-done.33, f32[256,512]{1,0:T(8,128)} %get-tuple-element.25, bf16[256,512]{1,0:T(8,128)(2,1)S(1)} %collective-permute-done.32), kind=kLoop, calls=%fused_computation.10 | loop fusion | flops 786432 | bytes 1835008 | tf_op jit(solution)/shard_map/add | solution.py:314
  131.9 8.4 %collective-permute-done.30 = f32[128,256]{1,0:T(8,128)S(1)} collective-permute-done((f32[128,256]{1,0:T(8,128)S(1)}, f32[128,256]{1,0:T(8,128)S(1)}, u32[]{:S(2)}, u32[]{:S(2)}) %collective-permute-start.30) | collective-permute-done | bytes 131104 | tf_op jit(solution)/shard_map/ppermute | solution.py:29
  (103 shorter events, 28.1 us)
Async XLA Ops:
  5.1 24.5 %collective-permute-start = (f32[8,136,512]{2,1,0:T(8,128)}, f32[8,136,512]{2,1,0:T(8,128)S(1)}, u32[]{:S(2)}, u32[]{:S(2)}) collective-permute-start(f32[8,136,512]{2,1,0:T(8,128)} %teacher.3), channel_id=1, source_target_pairs={{0,1},{1,0},{2,3},{3,2},{4,5},{5,4},{6,7},{7,6},{8,9},{9,8},{10,11... | collective-permute-start | bytes 6684680 | tf_op jit(solution)/shard_map/ppermute | solution.py:29
  7.3 11.3 %collective-permute-start.5 = (bf16[2,128,256]{2,1,0:T(8,128)(2,1)}, bf16[2,128,256]{2,1,0:T(8,128)(2,1)S(1)}, u32[]{:S(2)}, u32[]{:S(2)}) collective-permute-start(bf16[2,128,256]{2,1,0:T(8,128)(2,1)} %get-tuple-element.17), channel_id=1, source_target_pairs={{0,8},{1,9},{2,10},{3,11},{4,12},{5,13},{6,14},{7,15},{8,16},{9,17... | collective-permute-start | bytes 393224 | tf_op jit(solution)/shard_map/ppermute | solution.py:29
  10.5 15.4 %collective-permute-start.6 = (bf16[2,128,256]{2,1,0:T(8,128)(2,1)}, bf16[2,128,256]{2,1,0:T(8,128)(2,1)}, u32[]{:S(2)}, u32[]{:S(2)}) collective-permute-start(bf16[2,128,256]{2,1,0:T(8,128)(2,1)} %get-tuple-element.18), channel_id=1, source_target_pairs={{0,16},{1,17},{2,18},{3,19},{4,20},{5,21},{6,22},{7,23},{8,24},{9,... | collective-permute-start | bytes 393224 | tf_op jit(solution)/shard_map/ppermute | solution.py:29
  15.9 13.1 %collective-permute-start.7 = (bf16[2,128,256]{2,1,0:T(8,128)(2,1)}, bf16[2,128,256]{2,1,0:T(8,128)(2,1)}, u32[]{:S(2)}, u32[]{:S(2)}) collective-permute-start(bf16[2,128,256]{2,1,0:T(8,128)(2,1)} %get-tuple-element.19), channel_id=1, source_target_pairs={{0,24},{1,25},{2,26},{3,27},{4,28},{5,29},{6,30},{7,31},{8,0},{9,1... | collective-permute-start | bytes 393224 | tf_op jit(solution)/shard_map/ppermute | solution.py:29
  18.6 11.0 %collective-permute-start.8 = (bf16[2,128,256]{2,1,0:T(8,128)(2,1)S(1)}, bf16[2,128,256]{2,1,0:T(8,128)(2,1)S(1)}, u32[]{:S(2)}, u32[]{:S(2)}) collective-permute-start(bf16[2,128,256]{2,1,0:T(8,128)(2,1)S(1)} %collective-permute-done.5.refs_1_), channel_id=1, source_target_pairs={{0,1},{1,0},{2,3},{3,2},{4,5},{5,4},{6,7},{7,6},{8,9},{9,8},{10,11... | collective-permute-start | bytes 393224 | tf_op jit(solution)/shard_map/ppermute | solution.py:29
  18.6 16.3 %collective-permute-start.11 = (bf16[256,512]{1,0:T(8,128)(2,1)S(1)}, bf16[256,512]{1,0:T(8,128)(2,1)S(1)}, u32[]{:S(2)}, u32[]{:S(2)}) collective-permute-start(bf16[256,512]{1,0:T(8,128)(2,1)S(1)} %copy-done.1), channel_id=1, source_target_pairs={{0,32},{1,33},{2,34},{3,35},{4,36},{5,37},{6,38},{7,39},{8,40},{9,... | collective-permute-start | bytes 786440 | tf_op jit(solution)/shard_map/ppermute | solution.py:29
  26.0 11.1 %collective-permute-start.12 = (bf16[256,512]{1,0:T(8,128)(2,1)S(1)}, bf16[256,512]{1,0:T(8,128)(2,1)S(1)}, u32[]{:S(2)}, u32[]{:S(2)}) collective-permute-start(bf16[256,512]{1,0:T(8,128)(2,1)S(1)} %copy-done.1), channel_id=1, source_target_pairs={{0,64},{1,65},{2,66},{3,67},{4,68},{5,69},{6,70},{7,71},{8,72},{9,... | collective-permute-start | bytes 786440 | tf_op jit(solution)/shard_map/ppermute | solution.py:29
  29.0 11.8 %collective-permute-start.13 = (bf16[256,512]{1,0:T(8,128)(2,1)S(1)}, bf16[256,512]{1,0:T(8,128)(2,1)S(1)}, u32[]{:S(2)}, u32[]{:S(2)}) collective-permute-start(bf16[256,512]{1,0:T(8,128)(2,1)S(1)} %copy-done.1), channel_id=1, source_target_pairs={{0,96},{1,97},{2,98},{3,99},{4,100},{5,101},{6,102},{7,103},{8,104... | collective-permute-start | bytes 786440 | tf_op jit(solution)/shard_map/ppermute | solution.py:29
  30.3 3.5 %collective-permute-start.10 = (bf16[2,128,256]{2,1,0:T(8,128)(2,1)}, bf16[2,128,256]{2,1,0:T(8,128)(2,1)S(1)}, u32[]{:S(2)}, u32[]{:S(2)}) collective-permute-start(bf16[2,128,256]{2,1,0:T(8,128)(2,1)} %collective-permute-done.7.refs_3_), channel_id=1, source_target_pairs={{0,1},{1,0},{2,3},{3,2},{4,5},{5,4},{6,7},{7,6},{8,9},{9,8},{10,11... | collective-permute-start | bytes 393224 | tf_op jit(solution)/shard_map/ppermute | solution.py:29
  32.9 21.9 %collective-permute-start.3 = (f16[2,136,512]{2,1,0:T(8,128)(2,1)}, f16[2,136,512]{2,1,0:T(8,128)(2,1)}, u32[]{:S(2)}, u32[]{:S(2)}) collective-permute-start(f16[2,136,512]{2,1,0:T(8,128)(2,1)} %get-tuple-element.40), channel_id=1, source_target_pairs={{0,6},{1,7},{2,0},{3,1},{4,2},{5,3},{6,4},{7,5},{8,14},{9,15},{10,... | collective-permute-start | bytes 835592 | tf_op jit(solution)/shard_map/ppermute | solution.py:29
  33.8 25.0 %collective-permute-start.2 = (f16[2,136,512]{2,1,0:T(8,128)(2,1)}, f16[2,136,512]{2,1,0:T(8,128)(2,1)}, u32[]{:S(2)}, u32[]{:S(2)}) collective-permute-start(f16[2,136,512]{2,1,0:T(8,128)(2,1)} %get-tuple-element.41), channel_id=1, source_target_pairs={{0,4},{1,5},{2,6},{3,7},{4,0},{5,1},{6,2},{7,3},{8,12},{9,13},{10,... | collective-permute-start | bytes 835592 | tf_op jit(solution)/shard_map/ppermute | solution.py:29
  34.9 23.8 %collective-permute-start.1 = (f16[2,136,512]{2,1,0:T(8,128)(2,1)S(1)}, f16[2,136,512]{2,1,0:T(8,128)(2,1)}, u32[]{:S(2)}, u32[]{:S(2)}) collective-permute-start(f16[2,136,512]{2,1,0:T(8,128)(2,1)S(1)} %get-tuple-element.39), channel_id=1, source_target_pairs={{0,2},{1,3},{2,4},{3,5},{4,6},{5,7},{6,0},{7,1},{8,10},{9,11},{10,... | collective-permute-start | bytes 835592 | tf_op jit(solution)/shard_map/ppermute | solution.py:29
  46.4 13.9 %collective-permute-start.16 = (f16[128,512]{1,0:T(8,128)(2,1)S(1)}, f16[128,512]{1,0:T(8,128)(2,1)S(1)}, u32[]{:S(2)}, u32[]{:S(2)}) collective-permute-start(f16[128,512]{1,0:T(8,128)(2,1)S(1)} %get-tuple-element.46), channel_id=1, source_target_pairs={{0,8},{1,9},{2,10},{3,11},{4,12},{5,13},{6,14},{7,15},{8,16},{9,17... | collective-permute-start | bytes 393224 | tf_op jit(solution)/shard_map/ppermute | solution.py:29
  50.7 14.1 %collective-permute-start.15 = (f16[128,512]{1,0:T(8,128)(2,1)S(1)}, f16[128,512]{1,0:T(8,128)(2,1)S(1)}, u32[]{:S(2)}, u32[]{:S(2)}) collective-permute-start(f16[128,512]{1,0:T(8,128)(2,1)S(1)} %get-tuple-element.47), channel_id=1, source_target_pairs={{0,16},{1,17},{2,18},{3,19},{4,20},{5,21},{6,22},{7,23},{8,24},{9,... | collective-permute-start | bytes 393224 | tf_op jit(solution)/shard_map/ppermute | solution.py:29
  54.9 11.2 %collective-permute-start.14 = (f16[128,512]{1,0:T(8,128)(2,1)S(1)}, f16[128,512]{1,0:T(8,128)(2,1)S(1)}, u32[]{:S(2)}, u32[]{:S(2)}) collective-permute-start(f16[128,512]{1,0:T(8,128)(2,1)S(1)} %get-tuple-element.45), channel_id=1, source_target_pairs={{0,24},{1,25},{2,26},{3,27},{4,28},{5,29},{6,30},{7,31},{8,0},{9,1... | collective-permute-start | bytes 393224 | tf_op jit(solution)/shard_map/ppermute | solution.py:29
  60.3 7.5 %collective-permute-start.4 = (f16[136,512]{1,0:T(8,128)(2,1)S(1)}, f16[136,512]{1,0:T(8,128)(2,1)S(1)}, u32[]{:S(2)}, u32[]{:S(2)}) collective-permute-start(f16[136,512]{1,0:T(8,128)(2,1)S(1)} %fusion.16), channel_id=1, source_target_pairs={{0,128},{1,129},{2,130},{3,131},{4,132},{5,133},{6,134},{7,135},{8... | collective-permute-start | bytes 417800 | tf_op jit(solution)/shard_map/ppermute | solution.py:29
  68.4 3.7 %collective-permute-start.18 = (f32[5,128]{1,0:T(8,128)S(1)}, f32[5,128]{1,0:T(8,128)S(1)}, u32[]{:S(2)}, u32[]{:S(2)}) collective-permute-start(f32[5,128]{1,0:T(8,128)S(1)} %stack.38), channel_id=1, source_target_pairs={{0,2},{1,3},{2,0},{3,1},{4,6},{5,7},{6,4},{7,5},{8,10},{9,11},{10,... | collective-permute-start | bytes 7688 | tf_op jit(solution)/shard_map/ppermute | solution.py:29
  72.4 9.3 %collective-permute-start.23 = (bf16[128,512]{1,0:T(8,128)(2,1)S(1)}, bf16[128,512]{1,0:T(8,128)(2,1)S(1)}, u32[]{:S(2)}, u32[]{:S(2)}) collective-permute-start(bf16[128,512]{1,0:T(8,128)(2,1)S(1)} %subtract_convert_fusion.refs_0_.refs_1_), channel_id=1, source_target_pairs={{0,8},{1,9},{2,10},{3,11},{4,12},{5,13},{6,14},{7,15},{8,16},{9,17... | collective-permute-start | bytes 393224 | tf_op jit(solution)/shard_map/ppermute | solution.py:29
  74.4 14.7 %collective-permute-start.24 = (bf16[128,512]{1,0:T(8,128)(2,1)S(1)}, bf16[128,512]{1,0:T(8,128)(2,1)S(1)}, u32[]{:S(2)}, u32[]{:S(2)}) collective-permute-start(bf16[128,512]{1,0:T(8,128)(2,1)S(1)} %subtract_convert_fusion.refs_0_.refs_1_), channel_id=1, source_target_pairs={{0,16},{1,17},{2,18},{3,19},{4,20},{5,21},{6,22},{7,23},{8,24},{9,... | collective-permute-start | bytes 393224 | tf_op jit(solution)/shard_map/ppermute | solution.py:29
  77.6 11.7 %collective-permute-start.25 = (bf16[128,512]{1,0:T(8,128)(2,1)S(1)}, bf16[128,512]{1,0:T(8,128)(2,1)S(1)}, u32[]{:S(2)}, u32[]{:S(2)}) collective-permute-start(bf16[128,512]{1,0:T(8,128)(2,1)S(1)} %subtract_convert_fusion.refs_0_.refs_1_), channel_id=1, source_target_pairs={{0,24},{1,25},{2,26},{3,27},{4,28},{5,29},{6,30},{7,31},{8,0},{9,1... | collective-permute-start | bytes 393224 | tf_op jit(solution)/shard_map/ppermute | solution.py:29
  97.7 7.9 %collective-permute-start.26 = (f32[8,128,256]{2,1,0:T(8,128)}, f32[8,128,256]{2,1,0:T(8,128)S(1)}, u32[]{:S(2)}, u32[]{:S(2)}) collective-permute-start(f32[8,128,256]{2,1,0:T(8,128)} %get-tuple-element.23), channel_id=1, source_target_pairs={{0,1},{1,0},{2,3},{3,2},{4,5},{5,4},{6,7},{7,6},{8,9},{9,8},{10,11... | collective-permute-start | bytes 3145736 | tf_op jit(solution)/shard_map/ppermute | solution.py:29
  97.8 6.1 %collective-permute-start.22 = (f32[1,128]{1,0:T(1,128)S(1)}, f32[1,128]{1,0:T(1,128)S(1)}, u32[]{:S(2)}, u32[]{:S(2)}) collective-permute-start(f32[1,128]{1,0:T(1,128)S(1)} %bitcast_multiply_fusion), channel_id=1, source_target_pairs={{0,132},{1,133},{2,134},{3,135},{4,128},{5,129},{6,130},{7,131},{8... | collective-permute-start | bytes 1544 | tf_op jit(solution)/shard_map/ppermute | solution.py:29
  97.9 6.0 %collective-permute-start.21 = (f32[1,128]{1,0:T(1,128)S(1)}, f32[1,128]{1,0:T(1,128)S(1)}, u32[]{:S(2)}, u32[]{:S(2)}) collective-permute-start(f32[1,128]{1,0:T(1,128)S(1)} %bitcast_multiply_fusion), channel_id=1, source_target_pairs={{0,128},{1,129},{2,130},{3,131},{4,132},{5,133},{6,134},{7,135},{8... | collective-permute-start | bytes 1544 | tf_op jit(solution)/shard_map/ppermute | solution.py:29
  100.5 5.1 %collective-permute-start.20 = (f32[1,128]{1,0:T(1,128)S(1)}, f32[1,128]{1,0:T(1,128)S(1)}, u32[]{:S(2)}, u32[]{:S(2)}) collective-permute-start(f32[1,128]{1,0:T(1,128)S(1)} %bitcast_multiply_fusion), channel_id=1, source_target_pairs={{0,4},{1,5},{2,6},{3,7},{4,0},{5,1},{6,2},{7,3},{8,12},{9,13},{10,... | collective-permute-start | bytes 1544 | tf_op jit(solution)/shard_map/ppermute | solution.py:29
  106.8 11.6 %collective-permute-start.29 = (bf16[2,128,256]{2,1,0:T(8,128)(2,1)S(1)}, bf16[2,128,256]{2,1,0:T(8,128)(2,1)S(1)}, u32[]{:S(2)}, u32[]{:S(2)}) collective-permute-start(bf16[2,128,256]{2,1,0:T(8,128)(2,1)S(1)} %get-tuple-element.43), channel_id=1, source_target_pairs={{0,6},{1,7},{2,0},{3,1},{4,2},{5,3},{6,4},{7,5},{8,14},{9,15},{10,... | collective-permute-start | bytes 393224 | tf_op jit(solution)/shard_map/ppermute | solution.py:29
  107.8 13.1 %collective-permute-start.28 = (bf16[2,128,256]{2,1,0:T(8,128)(2,1)S(1)}, bf16[2,128,256]{2,1,0:T(8,128)(2,1)S(1)}, u32[]{:S(2)}, u32[]{:S(2)}) collective-permute-start(bf16[2,128,256]{2,1,0:T(8,128)(2,1)S(1)} %get-tuple-element.44), channel_id=1, source_target_pairs={{0,4},{1,5},{2,6},{3,7},{4,0},{5,1},{6,2},{7,3},{8,12},{9,13},{10,... | collective-permute-start | bytes 393224 | tf_op jit(solution)/shard_map/ppermute | solution.py:29
  111.1 9.7 %collective-permute-start.27 = (bf16[2,128,256]{2,1,0:T(8,128)(2,1)S(1)}, bf16[2,128,256]{2,1,0:T(8,128)(2,1)S(1)}, u32[]{:S(2)}, u32[]{:S(2)}) collective-permute-start(bf16[2,128,256]{2,1,0:T(8,128)(2,1)S(1)} %get-tuple-element.42), channel_id=1, source_target_pairs={{0,2},{1,3},{2,4},{3,5},{4,6},{5,7},{6,0},{7,1},{8,10},{9,11},{10,... | collective-permute-start | bytes 393224 | tf_op jit(solution)/shard_map/ppermute | solution.py:29
  115.9 11.5 %collective-permute-start.34 = (bf16[256,512]{1,0:T(8,128)(2,1)}, bf16[256,512]{1,0:T(8,128)(2,1)S(1)}, u32[]{:S(2)}, u32[]{:S(2)}) collective-permute-start(bf16[256,512]{1,0:T(8,128)(2,1)} %get-tuple-element.28), channel_id=1, source_target_pairs={{0,32},{1,33},{2,34},{3,35},{4,36},{5,37},{6,38},{7,39},{8,40},{9,... | collective-permute-start | bytes 786440 | tf_op jit(solution)/shard_map/ppermute | solution.py:29
  117.1 10.4 %collective-permute-start.33 = (bf16[256,512]{1,0:T(8,128)(2,1)}, bf16[256,512]{1,0:T(8,128)(2,1)S(1)}, u32[]{:S(2)}, u32[]{:S(2)}) collective-permute-start(bf16[256,512]{1,0:T(8,128)(2,1)} %get-tuple-element.27), channel_id=1, source_target_pairs={{0,64},{1,65},{2,66},{3,67},{4,68},{5,69},{6,70},{7,71},{8,72},{9,... | collective-permute-start | bytes 786440 | tf_op jit(solution)/shard_map/ppermute | solution.py:29
  118.4 11.5 %collective-permute-start.32 = (bf16[256,512]{1,0:T(8,128)(2,1)}, bf16[256,512]{1,0:T(8,128)(2,1)S(1)}, u32[]{:S(2)}, u32[]{:S(2)}) collective-permute-start(bf16[256,512]{1,0:T(8,128)(2,1)} %get-tuple-element.26), channel_id=1, source_target_pairs={{0,96},{1,97},{2,98},{3,99},{4,100},{5,101},{6,102},{7,103},{8,104... | collective-permute-start | bytes 786440 | tf_op jit(solution)/shard_map/ppermute | solution.py:29
  121.9 18.4 %collective-permute-start.30 = (f32[128,256]{1,0:T(8,128)S(1)}, f32[128,256]{1,0:T(8,128)S(1)}, u32[]{:S(2)}, u32[]{:S(2)}) collective-permute-start(f32[128,256]{1,0:T(8,128)S(1)} %get-tuple-element.49), channel_id=1, source_target_pairs={{0,0},{1,132},{2,128},{3,4},{4,24},{5,156},{6,152},{7,28},{8,9},{9... | collective-permute-start | bytes 393224 | tf_op jit(solution)/shard_map/ppermute | solution.py:29
  125.4 15.0 %collective-permute-start.31 = (f32[128,256]{1,0:T(8,128)S(1)}, f32[128,256]{1,0:T(8,128)S(1)}, u32[]{:S(2)}, u32[]{:S(2)}) collective-permute-start(f32[128,256]{1,0:T(8,128)S(1)} %get-tuple-element.48), channel_id=1, source_target_pairs={{0,16},{1,148},{2,144},{3,20},{4,8},{5,140},{6,136},{7,12},{8,25},... | collective-permute-start | bytes 393224 | tf_op jit(solution)/shard_map/ppermute | solution.py:29
  (17 other events, 109.3 us)

commit v3 on v2

--- a/solution.py
+++ b/solution.py
@@ -53,29 +53,33 @@
     return index // 128, index // 32 % 4, index // 8 % 4, index // 2 % 4, index % 2
 
 
-def pick_kernel(index_ref, hidden_ref, own_ref, *half_refs):
-    _, y, zh, _, core = coordinates(index_ref[0])
-
-    def block(k, p):
-        spot = (y + 8 - p - 2 * core) % 4 * 4 + (zh + k) % 4
-        return hidden_ref[:, pl.ds(pl.multiple_of(spot * 256, 256), 256)]
-
-    for p in range(4):
-        own_ref[p] = block(0, p)
-    for k in (1, 2, 3):
+def hidden_block(k, p):
+    def spot(i, index_ref):
+        _, y, zh, _, core = coordinates(index_ref[0])
+        return 0, (y + 8 - p - 2 * core) % 4 * 4 + (zh + k) % 4
+
+    return pl.BlockSpec((128, 256), spot)
+
+
+def pick_kernel(index_ref, *refs):
+    block_refs, out_refs = refs[:6], refs[6:]
+    for k in range(3):
         for p in range(2):
-            half_refs[k - 1][p] = block(k, p)
+            out_refs[k][p] = block_refs[2 * k + p][...]
 
 
 def picked_blocks(index, hidden):
-    rows = hidden.shape[0]
-    half = jax.ShapeDtypeStruct((2, rows, 256), hidden.dtype)
     return pl.pallas_call(
         pick_kernel,
-        in_specs=[pl.BlockSpec(memory_space=pltpu.SMEM), pl.BlockSpec(memory_space=pltpu.VMEM)],
-        out_shape=(jax.ShapeDtypeStruct((4, rows, 256), hidden.dtype), half, half, half),
+        grid_spec=pltpu.PrefetchScalarGridSpec(
+            num_scalar_prefetch=1,
+            grid=(1,),
+            in_specs=[hidden_block(k, p) for k in (1, 2, 3) for p in range(2)],
+            out_specs=[pl.BlockSpec((2, 128, 256), lambda i, index_ref: (0, 0, 0))] * 3,
+        ),
+        out_shape=[jax.ShapeDtypeStruct((2, 128, 256), hidden.dtype)] * 3,
         name="pick",
-    )(index, hidden)
+    )(index, *[hidden] * 6)
 
 
 def split(value):
@@ -137,12 +141,12 @@
 
 
 def student_kernel(index_ref, *refs):
-    own_ref, near_refs, far_refs, head_refs = refs[0], refs[1:4], refs[4:7], refs[7:11]
-    first_ref, out_ref, hidden_ref = refs[11:]
+    own_refs, near_refs, far_refs, head_refs = refs[:4], refs[4:7], refs[7:10], refs[10:14]
+    first_ref, out_ref, hidden_ref = refs[14:]
     core = index_ref[0] % 2
     for p in range(2):
-        hidden_ref[0, 2 * core + p] = own_ref[p]
-        hidden_ref[0, 2 * (1 - core) + p] = own_ref[2 + p]
+        hidden_ref[0, 2 * core + p] = own_refs[p][...]
+        hidden_ref[0, 2 * (1 - core) + p] = own_refs[2 + p][...]
         for k in (1, 2, 3):
             hidden_ref[k, 2 * core + p] = near_refs[k - 1][p]
             hidden_ref[k, 2 * (1 - core) + p] = far_refs[k - 1][p]
@@ -158,17 +162,26 @@
 
 
 def student_parts(index, own, near, far, head_slots):
-    vmem = pl.BlockSpec(memory_space=pltpu.VMEM)
+    def whole(*shape):
+        return pl.BlockSpec(shape, lambda i, index_ref: (0,) * len(shape))
+
     return pl.pallas_call(
         student_kernel,
-        in_specs=[pl.BlockSpec(memory_space=pltpu.SMEM)] + [vmem] * 11,
+        grid_spec=pltpu.PrefetchScalarGridSpec(
+            num_scalar_prefetch=1,
+            grid=(1,),
+            in_specs=[hidden_block(0, p) for p in range(4)]
+            + [whole(2, 128, 256)] * 6
+            + [whole(256, 512)] * 4,
+            out_specs=(whole(128, 512), whole(3, 128, 512), whole(4, 4, 128, 256)),
+        ),
         out_shape=(
             jax.ShapeDtypeStruct((128, 512), jnp.float32),
             jax.ShapeDtypeStruct((3, 128, 512), jnp.float32),
             jax.ShapeDtypeStruct((4, 4, 128, 256), jnp.bfloat16),
         ),
         name="student",
-    )(index, own, *near, *far, *head_slots)
+    )(index, *[own] * 4, *near, *far, *head_slots)
 
 
 def head_grad_kernel(*refs):
@@ -198,22 +211,22 @@
 
 
 def hidden_grad_kernel(index_ref, *refs):
-    grad_refs, head_refs, own_ref, other_ref = refs[:4], refs[4:8], refs[8], refs[9]
-    zl, _, _, x, core = coordinates(index_ref[0])
+    grad_refs, head_refs, own_ref, other_ref, slots_ref = refs[:4], refs[4:8], refs[8], refs[9], refs[10]
+    zl, y, zh, x, core = coordinates(index_ref[0])
     for k in range(4):
+        slots_ref[k] = grad_refs[k][...]
+    for m in range(2):
         for j in range(4):
-            spot = (k % 2 * 2 + j // 2 + 4 - x) % 4 * 2 + (k // 2 + zl) % 2
-            term = lax.dot_general(
-                grad_refs[k][...], head_refs[j][...], (((1,), (1,)), ((), ())), preferred_element_type=jnp.float32
-            )
-
-            @pl.when(core == j % 2)
-            def _():
-                own_ref[spot] = term
-
-            @pl.when(core != j % 2)
-            def _():
-                other_ref[spot] = term
+            a = (y + 4 - j) % 4
+            for out_ref, side in ((own_ref, core), (other_ref, 1 - core)):
+                goal = 2 * m + side
+                spot = (a % 2 * 2 + m + 4 - x) % 4 * 2 + (a // 2 + zl) % 2
+                out_ref[spot] = lax.dot_general(
+                    slots_ref[(zh + 4 - goal) % 4],
+                    head_refs[j][...],
+                    (((1,), (1,)), ((), ())),
+                    preferred_element_type=jnp.float32,
+                )
 
 
 def hidden_grad_parts(index, grad_slots, head_slots):
@@ -222,6 +235,7 @@
         hidden_grad_kernel,
         in_specs=[pl.BlockSpec(memory_space=pltpu.SMEM)] + [vmem] * 8,
         out_shape=(jax.ShapeDtypeStruct((8, 128, 256), jnp.float32),) * 2,
+        scratch_shapes=[pltpu.VMEM((4, 128, 512), jnp.bfloat16)],
         name="hidden_grad",
     )(index, *grad_slots, *head_slots)
 
@@ -232,7 +246,7 @@
     x = lax.axis_index("mp") // 2
     index = lax.axis_index(ALL).reshape(1)
 
-    own, *halves = picked_blocks(index, student_hidden)
+    halves = picked_blocks(index, student_hidden)
     near = [to_zh(halves[k - 1], k) for k in (1, 2, 3)]
     head_slots = [student_head] + [to_y(student_head, j) for j in (1, 2, 3)]
     far = [to_core(half) for half in near]
@@ -246,7 +260,7 @@
         by_x = by_x + to_x(part.astype(f16), step).astype(f32)
     teacher = by_x[0] + to_zl(by_x[1].astype(f16)).astype(f32)
 
-    student, parts, hidden = student_parts(index, own, near, far, head_slots)
+    student, parts, hidden = student_parts(index, student_hidden, near, far, head_slots)
     parts = parts.astype(f16)
     for k in (1, 2, 3):
         student = student + to_zh(parts[k - 1], -k).astype(f32)
@@ -318,13 +332,12 @@
         by_x = by_x + to_x(part.astype(bf16), step).astype(f32)
 
     def home(zl, y, zh, x, core):
-        k, j = zl * 2 + x // 2, x % 2 * 2 + core
-        spot = (y - j) % 4 * 4 + zh
-        return spot // 8, y, zh - k, spot % 8 // 2, spot % 2
-
-    hidden_grad = send(by_x[0], home) + send(
+        return zl, y, x % 2 * 2 + core, x // 2 * 2 + zh // 2, zh % 2
+
+    by_x = by_x.astype(bf16)
+    hidden_grad = send(by_x[0], home).astype(f32) + send(
         by_x[1], lambda zl, y, zh, x, core: home(1 - zl, y, zh, x, core)
-    )
+    ).astype(f32)
     return (kl_terms, hidden_grad, head_grad)
 
 

time: 141 us -> 133 us (0.943)
  the two profiles are of different devices: /device:TPU:14 before, /device:TPU:2 now
where the time goes in v3:
time: 133 us; the launch traced here: 131 us
  starting transfers between devices  66.4 us (50%)
  waiting for transfers between devices  27.6 us (21%)
  Pallas kernels  21.8 us (16%)
  other arithmetic  11.7 us (9%)
  local copies, waits for them, and re-layouts  2.98 us (2%)
    ppermute x35, starting transfers between devices, send(): return lax.ppermute(value, ALL, pairs)  66.4 us
    ppermute x35, waiting for transfers between devices, send(): return lax.ppermute(value, ALL, pairs)  27.6 us
    pallas_call x2, Pallas kernels, teacher_parts(): pl.pallas_call(teacher_kernel, grid_spec=pltpu.PrefetchScalarGridSpec(num...  8.79 us
    pallas_call x1, Pallas kernels, hidden_grad_parts(): pl.pallas_call(hidden_grad_kernel, in_specs=[pl.BlockSpec(memory_space=pl...  4.12 us
    pallas_call x1, Pallas kernels, student_parts(): pl.pallas_call(student_kernel, grid_spec=pltpu.PrefetchScalarGridSpec(num...  3.66 us
    pallas_call x1, Pallas kernels, head_grad_parts(): pl.pallas_call(head_grad_kernel, out_shape=(jax.ShapeDtypeStruct((256, 51...  3.4 us
  transfers between devices with their start and end apart: 35, of which 13 were waited for; matrix products, arithmetic and copies ran while one was open for 7% of the time, Pallas kernels for 10%

profile of v3, /device:TPU:2, one launch (start us, length us, event | category | flops | bytes accessed | tf_op | source)
XLA Modules:
  0.0 131.4 jit_solution(2285482338449427826)
XLA Ops:
  0.6 4.5 %teacher.3 = f32[8,136,512]{2,1,0:T(8,128)} custom-call(s32[1]{0:T(128)} %bitcast.index_ref, bf16[128,512]{1,0:T(8,128)(2,1)} %hidden_ref.3, bf16[512]{0:T(512)(128)(2,1)} %gain_ref.3, bf16[512,8192]{1,0:T(8,128)(2,1)} %refs_3_.5, bf16[512,8192]{1,0:T(8,128)(2,1)} %refs_3_.5, bf16[512,8192]{1,0:T(8,128)(2,1)} %refs_3_.5, bf16[512,8192]{1,0:T(8,128)(2,1)} %refs_3_.5), custom_call_target="tpu_custom_call" | custom-call | tf_op jit(solution)/shard_map/teacher/pallas_call | solution.py:125
  5.1 1.8 %pick.1 = (bf16[2,128,256]{2,1,0:T(8,128)(2,1)}, bf16[2,128,256]{2,1,0:T(8,128)(2,1)}, bf16[2,128,256]{2,1,0:T(8,128)(2,1)}) custom-call(s32[1]{0:T(128)} %bitcast.index_ref, bf16[128,4096]{1,0:T(8,128)(2,1)} %refs_3_.7, bf16[128,4096]{1,0:T(8,128)(2,1)} %refs_3_.7, bf16[128,4096]{1,0:T(8,128)(2,1)} %refs_3_.7, bf16[128,4096]{1,0:T(8,128)(2,1)} %refs_3_.7, ...), custom_call_target="tpu_custom_call" | custom-call | tf_op jit(solution)/shard_map/pick/pallas_call | solution.py:72
  6.9 3.3 %collective-permute-start.5 = (bf16[2,128,256]{2,1,0:T(8,128)(2,1)}, bf16[2,128,256]{2,1,0:T(8,128)(2,1)S(1)}, u32[]{:S(2)}, u32[]{:S(2)}) collective-permute-start(bf16[2,128,256]{2,1,0:T(8,128)(2,1)} %get-tuple-element.15), channel_id=1, source_target_pairs={{0,8},{1,9},{2,10},{3,11},{4,12},{5,13},{6,14},{7,15},{8,16},{9,17... | collective-permute-start | bytes 393224 | tf_op jit(solution)/shard_map/ppermute | solution.py:29
  10.2 5.4 %collective-permute-start.6 = (bf16[2,128,256]{2,1,0:T(8,128)(2,1)}, bf16[2,128,256]{2,1,0:T(8,128)(2,1)}, u32[]{:S(2)}, u32[]{:S(2)}) collective-permute-start(bf16[2,128,256]{2,1,0:T(8,128)(2,1)} %get-tuple-element.16), channel_id=1, source_target_pairs={{0,16},{1,17},{2,18},{3,19},{4,20},{5,21},{6,22},{7,23},{8,24},{9,... | collective-permute-start | bytes 393224 | tf_op jit(solution)/shard_map/ppermute | solution.py:29
  15.6 2.7 %collective-permute-start.7 = (bf16[2,128,256]{2,1,0:T(8,128)(2,1)}, bf16[2,128,256]{2,1,0:T(8,128)(2,1)}, u32[]{:S(2)}, u32[]{:S(2)}) collective-permute-start(bf16[2,128,256]{2,1,0:T(8,128)(2,1)} %get-tuple-element.17), channel_id=1, source_target_pairs={{0,24},{1,25},{2,26},{3,27},{4,28},{5,29},{6,30},{7,31},{8,0},{9,1... | collective-permute-start | bytes 393224 | tf_op jit(solution)/shard_map/ppermute | solution.py:29
  18.3 1.7 %collective-permute-start.11 = (bf16[256,512]{1,0:T(8,128)(2,1)S(1)}, bf16[256,512]{1,0:T(8,128)(2,1)S(1)}, u32[]{:S(2)}, u32[]{:S(2)}) collective-permute-start(bf16[256,512]{1,0:T(8,128)(2,1)S(1)} %copy-done.1), channel_id=1, source_target_pairs={{0,32},{1,33},{2,34},{3,35},{4,36},{5,37},{6,38},{7,39},{8,40},{9,... | collective-permute-start | bytes 786440 | tf_op jit(solution)/shard_map/ppermute | solution.py:29
  19.9 4.3 %teacher.2 = f32[8,136,512]{2,1,0:T(8,128)} custom-call(s32[1]{0:T(128)} %bitcast.index_ref, bf16[128,512]{1,0:T(8,128)(2,1)} %hidden_ref.3, bf16[512]{0:T(512)(128)(2,1)} %gain_ref.3, bf16[512,8192]{1,0:T(8,128)(2,1)} %refs_3_.5, bf16[512,8192]{1,0:T(8,128)(2,1)} %refs_3_.5, bf16[512,8192]{1,0:T(8,128)(2,1)} %refs_3_.5, bf16[512,8192]{1,0:T(8,128)(2,1)} %refs_3_.5), custom_call_target="tpu_custom_call" | custom-call | tf_op jit(solution)/shard_map/teacher/pallas_call | solution.py:125
  25.6 3.2 %collective-permute-start.12 = (bf16[256,512]{1,0:T(8,128)(2,1)S(1)}, bf16[256,512]{1,0:T(8,128)(2,1)S(1)}, u32[]{:S(2)}, u32[]{:S(2)}) collective-permute-start(bf16[256,512]{1,0:T(8,128)(2,1)S(1)} %copy-done.1), channel_id=1, source_target_pairs={{0,64},{1,65},{2,66},{3,67},{4,68},{5,69},{6,70},{7,71},{8,72},{9,... | collective-permute-start | bytes 786440 | tf_op jit(solution)/shard_map/ppermute | solution.py:29
  28.8 2.8 %collective-permute-start.13 = (bf16[256,512]{1,0:T(8,128)(2,1)S(1)}, bf16[256,512]{1,0:T(8,128)(2,1)S(1)}, u32[]{:S(2)}, u32[]{:S(2)}) collective-permute-start(bf16[256,512]{1,0:T(8,128)(2,1)S(1)} %copy-done.1), channel_id=1, source_target_pairs={{0,96},{1,97},{2,98},{3,99},{4,100},{5,101},{6,102},{7,103},{8,104... | collective-permute-start | bytes 786440 | tf_op jit(solution)/shard_map/ppermute | solution.py:29
  32.3 2.6 %fusion.2 = (f16[2,136,512]{2,1,0:T(8,128)(2,1)S(1)}, f16[2,136,512]{2,1,0:T(8,128)(2,1)}, f16[2,136,512]{2,1,0:T(8,128)(2,1)}) fusion(f32[8,136,512]{2,1,0:T(8,128)S(1)} %collective-permute-done, f32[8,136,512]{2,1,0:T(8,128)} %teacher.2), kind=kLoop, calls=%fused_computation.5 | loop fusion | flops 835584 | bytes 4177920 | tf_op jit(solution)/shard_map/convert_element_type | solution.py:260
  35.5 2.4 %collective-permute-start.2 = (f16[2,136,512]{2,1,0:T(8,128)(2,1)}, f16[2,136,512]{2,1,0:T(8,128)(2,1)}, u32[]{:S(2)}, u32[]{:S(2)}) collective-permute-start(f16[2,136,512]{2,1,0:T(8,128)(2,1)} %get-tuple-element.39), channel_id=1, source_target_pairs={{0,4},{1,5},{2,6},{3,7},{4,0},{5,1},{6,2},{7,3},{8,12},{9,13},{10,... | collective-permute-start | bytes 835592 | tf_op jit(solution)/shard_map/ppermute | solution.py:29
  37.9 1.9 %collective-permute-start.1 = (f16[2,136,512]{2,1,0:T(8,128)(2,1)S(1)}, f16[2,136,512]{2,1,0:T(8,128)(2,1)}, u32[]{:S(2)}, u32[]{:S(2)}) collective-permute-start(f16[2,136,512]{2,1,0:T(8,128)(2,1)S(1)} %get-tuple-element.37), channel_id=1, source_target_pairs={{0,2},{1,3},{2,4},{3,5},{4,6},{5,7},{6,0},{7,1},{8,10},{9,11},{10,... | collective-permute-start | bytes 835592 | tf_op jit(solution)/shard_map/ppermute | solution.py:29
  41.4 3.7 %student.1 = (f32[128,512]{1,0:T(8,128)}, f32[3,128,512]{2,1,0:T(8,128)}, bf16[4,4,128,256]{3,2,1,0:T(8,128)(2,1)}) custom-call(s32[1]{0:T(128)} %bitcast.index_ref, bf16[128,4096]{1,0:T(8,128)(2,1)} %refs_3_.7, bf16[128,4096]{1,0:T(8,128)(2,1)} %refs_3_.7, bf16[128,4096]{1,0:T(8,128)(2,1)} %refs_3_.7, bf16[128,4096]{1,0:T(8,128)(2,1)} %refs_3_.7, ...), custom_call_target="tpu_custom_call" | custom-call | tf_op jit(solution)/shard_map/student/pallas_call | solution.py:168
  46.3 3.8 %collective-permute-start.16 = (f16[128,512]{1,0:T(8,128)(2,1)S(1)}, f16[128,512]{1,0:T(8,128)(2,1)S(1)}, u32[]{:S(2)}, u32[]{:S(2)}) collective-permute-start(f16[128,512]{1,0:T(8,128)(2,1)S(1)} %get-tuple-element.44), channel_id=1, source_target_pairs={{0,8},{1,9},{2,10},{3,11},{4,12},{5,13},{6,14},{7,15},{8,16},{9,17... | collective-permute-start | bytes 393224 | tf_op jit(solution)/shard_map/ppermute | solution.py:29
  50.2 4.3 %collective-permute-start.15 = (f16[128,512]{1,0:T(8,128)(2,1)S(1)}, f16[128,512]{1,0:T(8,128)(2,1)S(1)}, u32[]{:S(2)}, u32[]{:S(2)}) collective-permute-start(f16[128,512]{1,0:T(8,128)(2,1)S(1)} %get-tuple-element.45), channel_id=1, source_target_pairs={{0,16},{1,17},{2,18},{3,19},{4,20},{5,21},{6,22},{7,23},{8,24},{9,... | collective-permute-start | bytes 393224 | tf_op jit(solution)/shard_map/ppermute | solution.py:29
  54.4 3.9 %collective-permute-start.14 = (f16[128,512]{1,0:T(8,128)(2,1)S(1)}, f16[128,512]{1,0:T(8,128)(2,1)S(1)}, u32[]{:S(2)}, u32[]{:S(2)}) collective-permute-start(f16[128,512]{1,0:T(8,128)(2,1)S(1)} %get-tuple-element.43), channel_id=1, source_target_pairs={{0,24},{1,25},{2,26},{3,27},{4,28},{5,29},{6,30},{7,31},{8,0},{9,1... | collective-permute-start | bytes 393224 | tf_op jit(solution)/shard_map/ppermute | solution.py:29
  59.9 3.7 %collective-permute-done.15 = f16[128,512]{1,0:T(8,128)(2,1)S(1)} collective-permute-done((f16[128,512]{1,0:T(8,128)(2,1)S(1)}, f16[128,512]{1,0:T(8,128)(2,1)S(1)}, u32[]{:S(2)}, u32[]{:S(2)}) %collective-permute-start.15) | collective-permute-done | bytes 131104 | tf_op jit(solution)/shard_map/ppermute | solution.py:29
  63.6 2.1 %collective-permute-done.14 = f16[128,512]{1,0:T(8,128)(2,1)S(1)} collective-permute-done((f16[128,512]{1,0:T(8,128)(2,1)S(1)}, f16[128,512]{1,0:T(8,128)(2,1)S(1)}, u32[]{:S(2)}, u32[]{:S(2)}) %collective-permute-start.14) | collective-permute-done | bytes 131104 | tf_op jit(solution)/shard_map/ppermute | solution.py:29
  71.8 2.2 %collective-permute-start.23 = (bf16[128,512]{1,0:T(8,128)(2,1)S(1)}, bf16[128,512]{1,0:T(8,128)(2,1)S(1)}, u32[]{:S(2)}, u32[]{:S(2)}) collective-permute-start(bf16[128,512]{1,0:T(8,128)(2,1)S(1)} %subtract_convert_fusion.refs_0_.refs_1_), channel_id=1, source_target_pairs={{0,8},{1,9},{2,10},{3,11},{4,12},{5,13},{6,14},{7,15},{8,16},{9,17... | collective-permute-start | bytes 393224 | tf_op jit(solution)/shard_map/ppermute | solution.py:29
  74.0 3.2 %collective-permute-start.24 = (bf16[128,512]{1,0:T(8,128)(2,1)S(1)}, bf16[128,512]{1,0:T(8,128)(2,1)S(1)}, u32[]{:S(2)}, u32[]{:S(2)}) collective-permute-start(bf16[128,512]{1,0:T(8,128)(2,1)S(1)} %subtract_convert_fusion.refs_0_.refs_1_), channel_id=1, source_target_pairs={{0,16},{1,17},{2,18},{3,19},{4,20},{5,21},{6,22},{7,23},{8,24},{9,... | collective-permute-start | bytes 393224 | tf_op jit(solution)/shard_map/ppermute | solution.py:29
  78.7 2.3 %collective-permute-done.23.refs_1_.refs_2_ = bf16[128,512]{1,0:T(8,128)(2,1)S(1)} collective-permute-done((bf16[128,512]{1,0:T(8,128)(2,1)S(1)}, bf16[128,512]{1,0:T(8,128)(2,1)S(1)}, u32[]{:S(2)}, u32[]{:S(2)}) %collective-permute-start.23) | collective-permute-done | bytes 131104 | tf_op jit(solution)/shard_map/ppermute | solution.py:29
  81.1 7.4 %collective-permute-done.24.refs_2_.refs_3_ = bf16[128,512]{1,0:T(8,128)(2,1)S(1)} collective-permute-done((bf16[128,512]{1,0:T(8,128)(2,1)S(1)}, bf16[128,512]{1,0:T(8,128)(2,1)S(1)}, u32[]{:S(2)}, u32[]{:S(2)}) %collective-permute-start.24) | collective-permute-done | bytes 131104 | tf_op jit(solution)/shard_map/ppermute | solution.py:29
  89.7 4.1 %hidden_grad.1 = (f32[8,128,256]{2,1,0:T(8,128)}, f32[8,128,256]{2,1,0:T(8,128)}) custom-call(s32[1]{0:T(128)} %bitcast.index_ref, bf16[128,512]{1,0:T(8,128)(2,1)} %copy-done, bf16[128,512]{1,0:T(8,128)(2,1)} %copy-done.5, bf16[128,512]{1,0:T(8,128)(2,1)} %copy-done.6, bf16[128,512]{1,0:T(8,128)(2,1)} %copy-done.7, bf16[256,512]{1,0:T(8,128)(2,1)} %refs_4_.3, ...), custom_call_target="tpu_custom_call" | custom-call | tf_op jit(solution)/shard_map/hidden_grad/pallas_call | solution.py:234
  94.0 3.8 %collective-permute-start.21 = (f32[1,128]{1,0:T(1,128)S(1)}, f32[1,128]{1,0:T(1,128)S(1)}, u32[]{:S(2)}, u32[]{:S(2)}) collective-permute-start(f32[1,128]{1,0:T(1,128)S(1)} %bitcast_multiply_fusion), channel_id=1, source_target_pairs={{0,128},{1,129},{2,130},{3,131},{4,132},{5,133},{6,134},{7,135},{8... | collective-permute-start | bytes 1544 | tf_op jit(solution)/shard_map/ppermute | solution.py:29
  100.0 3.0 %collective-permute-done.20 = f32[1,128]{1,0:T(1,128)S(1)} collective-permute-done((f32[1,128]{1,0:T(1,128)S(1)}, f32[1,128]{1,0:T(1,128)S(1)}, u32[]{:S(2)}, u32[]{:S(2)}) %collective-permute-start.20) | collective-permute-done | bytes 544 | tf_op jit(solution)/shard_map/ppermute | solution.py:29
  104.2 1.9 %collective-permute-start.29 = (bf16[2,128,256]{2,1,0:T(8,128)(2,1)S(1)}, bf16[2,128,256]{2,1,0:T(8,128)(2,1)S(1)}, u32[]{:S(2)}, u32[]{:S(2)}) collective-permute-start(bf16[2,128,256]{2,1,0:T(8,128)(2,1)S(1)} %get-tuple-element.41), channel_id=1, source_target_pairs={{0,6},{1,7},{2,0},{3,1},{4,2},{5,3},{6,4},{7,5},{8,14},{9,15},{10,... | collective-permute-start | bytes 393224 | tf_op jit(solution)/shard_map/ppermute | solution.py:29
  106.2 1.8 %collective-permute-start.27 = (bf16[2,128,256]{2,1,0:T(8,128)(2,1)S(1)}, bf16[2,128,256]{2,1,0:T(8,128)(2,1)S(1)}, u32[]{:S(2)}, u32[]{:S(2)}) collective-permute-start(bf16[2,128,256]{2,1,0:T(8,128)(2,1)S(1)} %get-tuple-element.40), channel_id=1, source_target_pairs={{0,2},{1,3},{2,4},{3,5},{4,6},{5,7},{6,0},{7,1},{8,10},{9,11},{10,... | collective-permute-start | bytes 393224 | tf_op jit(solution)/shard_map/ppermute | solution.py:29
  108.6 3.4 %head_grad.1 = (f32[256,512]{1,0:T(8,128)}, bf16[256,512]{1,0:T(8,128)(2,1)}, bf16[256,512]{1,0:T(8,128)(2,1)}, bf16[256,512]{1,0:T(8,128)(2,1)}) custom-call(bf16[4,4,128,256]{3,2,1,0:T(8,128)(2,1)} %get-tuple-element.22.refs_0_, bf16[128,512]{1,0:T(8,128)(2,1)} %copy-done, bf16[128,512]{1,0:T(8,128)(2,1)} %copy-done.5, bf16[128,512]{1,0:T(8,128)(2,1)} %copy-done.6, ...), custom_call_target="tpu_custom_call" | custom-call | tf_op jit(solution)/shard_map/head_grad/pallas_call | solution.py:203
  113.6 3.0 %collective-permute-start.33 = (bf16[256,512]{1,0:T(8,128)(2,1)}, bf16[256,512]{1,0:T(8,128)(2,1)S(1)}, u32[]{:S(2)}, u32[]{:S(2)}) collective-permute-start(bf16[256,512]{1,0:T(8,128)(2,1)} %get-tuple-element.25), channel_id=1, source_target_pairs={{0,64},{1,65},{2,66},{3,67},{4,68},{5,69},{6,70},{7,71},{8,72},{9,... | collective-permute-start | bytes 786440 | tf_op jit(solution)/shard_map/ppermute | solution.py:29
  119.8 6.1 %collective-permute-start.30 = (bf16[128,256]{1,0:T(8,128)(2,1)S(1)}, bf16[128,256]{1,0:T(8,128)(2,1)S(1)}, u32[]{:S(2)}, u32[]{:S(2)}) collective-permute-start(bf16[128,256]{1,0:T(8,128)(2,1)S(1)} %get-tuple-element.46), channel_id=1, source_target_pairs={{0,0},{1,8},{2,16},{3,24},{4,4},{5,12},{6,20},{7,28},{8,1},{9,9},{... | collective-permute-start | bytes 196616 | tf_op jit(solution)/shard_map/ppermute | solution.py:29
  126.6 2.0 %convert_add_fusion = f32[256,512]{1,0:T(8,128)} fusion(bf16[256,512]{1,0:T(8,128)(2,1)S(1)} %collective-permute-done.34, bf16[256,512]{1,0:T(8,128)(2,1)S(1)} %collective-permute-done.33, f32[256,512]{1,0:T(8,128)} %get-tuple-element.23, bf16[256,512]{1,0:T(8,128)(2,1)S(1)} %collective-permute-done.32), kind=kLoop, calls=%fused_computation.10 | loop fusion | flops 786432 | bytes 1835008 | tf_op jit(solution)/shard_map/add | solution.py:328
  128.5 2.2 %collective-permute-done.30 = bf16[128,256]{1,0:T(8,128)(2,1)S(1)} collective-permute-done((bf16[128,256]{1,0:T(8,128)(2,1)S(1)}, bf16[128,256]{1,0:T(8,128)(2,1)S(1)}, u32[]{:S(2)}, u32[]{:S(2)}) %collective-permute-start.30) | collective-permute-done | bytes 65568 | tf_op jit(solution)/shard_map/ppermute | solution.py:29
  (103 shorter events, 26.3 us)
Async XLA Ops:
  5.1 26.5 %collective-permute-start = (f32[8,136,512]{2,1,0:T(8,128)}, f32[8,136,512]{2,1,0:T(8,128)S(1)}, u32[]{:S(2)}, u32[]{:S(2)}) collective-permute-start(f32[8,136,512]{2,1,0:T(8,128)} %teacher.3), channel_id=1, source_target_pairs={{0,1},{1,0},{2,3},{3,2},{4,5},{5,4},{6,7},{7,6},{8,9},{9,8},{10,11... | collective-permute-start | bytes 6684680 | tf_op jit(solution)/shard_map/ppermute | solution.py:29
  6.9 11.3 %collective-permute-start.5 = (bf16[2,128,256]{2,1,0:T(8,128)(2,1)}, bf16[2,128,256]{2,1,0:T(8,128)(2,1)S(1)}, u32[]{:S(2)}, u32[]{:S(2)}) collective-permute-start(bf16[2,128,256]{2,1,0:T(8,128)(2,1)} %get-tuple-element.15), channel_id=1, source_target_pairs={{0,8},{1,9},{2,10},{3,11},{4,12},{5,13},{6,14},{7,15},{8,16},{9,17... | collective-permute-start | bytes 393224 | tf_op jit(solution)/shard_map/ppermute | solution.py:29
  10.2 15.4 %collective-permute-start.6 = (bf16[2,128,256]{2,1,0:T(8,128)(2,1)}, bf16[2,128,256]{2,1,0:T(8,128)(2,1)}, u32[]{:S(2)}, u32[]{:S(2)}) collective-permute-start(bf16[2,128,256]{2,1,0:T(8,128)(2,1)} %get-tuple-element.16), channel_id=1, source_target_pairs={{0,16},{1,17},{2,18},{3,19},{4,20},{5,21},{6,22},{7,23},{8,24},{9,... | collective-permute-start | bytes 393224 | tf_op jit(solution)/shard_map/ppermute | solution.py:29
  15.6 13.2 %collective-permute-start.7 = (bf16[2,128,256]{2,1,0:T(8,128)(2,1)}, bf16[2,128,256]{2,1,0:T(8,128)(2,1)}, u32[]{:S(2)}, u32[]{:S(2)}) collective-permute-start(bf16[2,128,256]{2,1,0:T(8,128)(2,1)} %get-tuple-element.17), channel_id=1, source_target_pairs={{0,24},{1,25},{2,26},{3,27},{4,28},{5,29},{6,30},{7,31},{8,0},{9,1... | collective-permute-start | bytes 393224 | tf_op jit(solution)/shard_map/ppermute | solution.py:29
  18.3 13.4 %collective-permute-start.8 = (bf16[2,128,256]{2,1,0:T(8,128)(2,1)S(1)}, bf16[2,128,256]{2,1,0:T(8,128)(2,1)S(1)}, u32[]{:S(2)}, u32[]{:S(2)}) collective-permute-start(bf16[2,128,256]{2,1,0:T(8,128)(2,1)S(1)} %collective-permute-done.5.refs_4_), channel_id=1, source_target_pairs={{0,1},{1,0},{2,3},{3,2},{4,5},{5,4},{6,7},{7,6},{8,9},{9,8},{10,11... | collective-permute-start | bytes 393224 | tf_op jit(solution)/shard_map/ppermute | solution.py:29
  18.3 19.6 %collective-permute-start.11 = (bf16[256,512]{1,0:T(8,128)(2,1)S(1)}, bf16[256,512]{1,0:T(8,128)(2,1)S(1)}, u32[]{:S(2)}, u32[]{:S(2)}) collective-permute-start(bf16[256,512]{1,0:T(8,128)(2,1)S(1)} %copy-done.1), channel_id=1, source_target_pairs={{0,32},{1,33},{2,34},{3,35},{4,36},{5,37},{6,38},{7,39},{8,40},{9,... | collective-permute-start | bytes 786440 | tf_op jit(solution)/shard_map/ppermute | solution.py:29
  25.6 14.2 %collective-permute-start.12 = (bf16[256,512]{1,0:T(8,128)(2,1)S(1)}, bf16[256,512]{1,0:T(8,128)(2,1)S(1)}, u32[]{:S(2)}, u32[]{:S(2)}) collective-permute-start(bf16[256,512]{1,0:T(8,128)(2,1)S(1)} %copy-done.1), channel_id=1, source_target_pairs={{0,64},{1,65},{2,66},{3,67},{4,68},{5,69},{6,70},{7,71},{8,72},{9,... | collective-permute-start | bytes 786440 | tf_op jit(solution)/shard_map/ppermute | solution.py:29
  28.8 11.9 %collective-permute-start.13 = (bf16[256,512]{1,0:T(8,128)(2,1)S(1)}, bf16[256,512]{1,0:T(8,128)(2,1)S(1)}, u32[]{:S(2)}, u32[]{:S(2)}) collective-permute-start(bf16[256,512]{1,0:T(8,128)(2,1)S(1)} %copy-done.1), channel_id=1, source_target_pairs={{0,96},{1,97},{2,98},{3,99},{4,100},{5,101},{6,102},{7,103},{8,104... | collective-permute-start | bytes 786440 | tf_op jit(solution)/shard_map/ppermute | solution.py:29
  31.6 3.3 %collective-permute-start.9 = (bf16[2,128,256]{2,1,0:T(8,128)(2,1)}, bf16[2,128,256]{2,1,0:T(8,128)(2,1)S(1)}, u32[]{:S(2)}, u32[]{:S(2)}) collective-permute-start(bf16[2,128,256]{2,1,0:T(8,128)(2,1)} %collective-permute-done.6.refs_5_), channel_id=1, source_target_pairs={{0,1},{1,0},{2,3},{3,2},{4,5},{5,4},{6,7},{7,6},{8,9},{9,8},{10,11... | collective-permute-start | bytes 393224 | tf_op jit(solution)/shard_map/ppermute | solution.py:29
  34.9 19.5 %collective-permute-start.3 = (f16[2,136,512]{2,1,0:T(8,128)(2,1)}, f16[2,136,512]{2,1,0:T(8,128)(2,1)}, u32[]{:S(2)}, u32[]{:S(2)}) collective-permute-start(f16[2,136,512]{2,1,0:T(8,128)(2,1)} %get-tuple-element.38), channel_id=1, source_target_pairs={{0,6},{1,7},{2,0},{3,1},{4,2},{5,3},{6,4},{7,5},{8,14},{9,15},{10,... | collective-permute-start | bytes 835592 | tf_op jit(solution)/shard_map/ppermute | solution.py:29
  35.5 22.8 %collective-permute-start.2 = (f16[2,136,512]{2,1,0:T(8,128)(2,1)}, f16[2,136,512]{2,1,0:T(8,128)(2,1)}, u32[]{:S(2)}, u32[]{:S(2)}) collective-permute-start(f16[2,136,512]{2,1,0:T(8,128)(2,1)} %get-tuple-element.39), channel_id=1, source_target_pairs={{0,4},{1,5},{2,6},{3,7},{4,0},{5,1},{6,2},{7,3},{8,12},{9,13},{10,... | collective-permute-start | bytes 835592 | tf_op jit(solution)/shard_map/ppermute | solution.py:29
  37.9 20.4 %collective-permute-start.1 = (f16[2,136,512]{2,1,0:T(8,128)(2,1)S(1)}, f16[2,136,512]{2,1,0:T(8,128)(2,1)}, u32[]{:S(2)}, u32[]{:S(2)}) collective-permute-start(f16[2,136,512]{2,1,0:T(8,128)(2,1)S(1)} %get-tuple-element.37), channel_id=1, source_target_pairs={{0,2},{1,3},{2,4},{3,5},{4,6},{5,7},{6,0},{7,1},{8,10},{9,11},{10,... | collective-permute-start | bytes 835592 | tf_op jit(solution)/shard_map/ppermute | solution.py:29
  46.3 13.6 %collective-permute-start.16 = (f16[128,512]{1,0:T(8,128)(2,1)S(1)}, f16[128,512]{1,0:T(8,128)(2,1)S(1)}, u32[]{:S(2)}, u32[]{:S(2)}) collective-permute-start(f16[128,512]{1,0:T(8,128)(2,1)S(1)} %get-tuple-element.44), channel_id=1, source_target_pairs={{0,8},{1,9},{2,10},{3,11},{4,12},{5,13},{6,14},{7,15},{8,16},{9,17... | collective-permute-start | bytes 393224 | tf_op jit(solution)/shard_map/ppermute | solution.py:29
  50.2 13.4 %collective-permute-start.15 = (f16[128,512]{1,0:T(8,128)(2,1)S(1)}, f16[128,512]{1,0:T(8,128)(2,1)S(1)}, u32[]{:S(2)}, u32[]{:S(2)}) collective-permute-start(f16[128,512]{1,0:T(8,128)(2,1)S(1)} %get-tuple-element.45), channel_id=1, source_target_pairs={{0,16},{1,17},{2,18},{3,19},{4,20},{5,21},{6,22},{7,23},{8,24},{9,... | collective-permute-start | bytes 393224 | tf_op jit(solution)/shard_map/ppermute | solution.py:29
  54.4 11.3 %collective-permute-start.14 = (f16[128,512]{1,0:T(8,128)(2,1)S(1)}, f16[128,512]{1,0:T(8,128)(2,1)S(1)}, u32[]{:S(2)}, u32[]{:S(2)}) collective-permute-start(f16[128,512]{1,0:T(8,128)(2,1)S(1)} %get-tuple-element.43), channel_id=1, source_target_pairs={{0,24},{1,25},{2,26},{3,27},{4,28},{5,29},{6,30},{7,31},{8,0},{9,1... | collective-permute-start | bytes 393224 | tf_op jit(solution)/shard_map/ppermute | solution.py:29
  59.8 7.4 %collective-permute-start.4 = (f16[136,512]{1,0:T(8,128)(2,1)S(1)}, f16[136,512]{1,0:T(8,128)(2,1)S(1)}, u32[]{:S(2)}, u32[]{:S(2)}) collective-permute-start(f16[136,512]{1,0:T(8,128)(2,1)S(1)} %fusion.17), channel_id=1, source_target_pairs={{0,128},{1,129},{2,130},{3,131},{4,132},{5,133},{6,134},{7,135},{8... | collective-permute-start | bytes 417800 | tf_op jit(solution)/shard_map/ppermute | solution.py:29
  67.8 3.7 %collective-permute-start.18 = (f32[5,128]{1,0:T(8,128)S(1)}, f32[5,128]{1,0:T(8,128)S(1)}, u32[]{:S(2)}, u32[]{:S(2)}) collective-permute-start(f32[5,128]{1,0:T(8,128)S(1)} %stack.38), channel_id=1, source_target_pairs={{0,2},{1,3},{2,0},{3,1},{4,6},{5,7},{6,4},{7,5},{8,10},{9,11},{10,... | collective-permute-start | bytes 7688 | tf_op jit(solution)/shard_map/ppermute | solution.py:29
  71.8 9.2 %collective-permute-start.23 = (bf16[128,512]{1,0:T(8,128)(2,1)S(1)}, bf16[128,512]{1,0:T(8,128)(2,1)S(1)}, u32[]{:S(2)}, u32[]{:S(2)}) collective-permute-start(bf16[128,512]{1,0:T(8,128)(2,1)S(1)} %subtract_convert_fusion.refs_0_.refs_1_), channel_id=1, source_target_pairs={{0,8},{1,9},{2,10},{3,11},{4,12},{5,13},{6,14},{7,15},{8,16},{9,17... | collective-permute-start | bytes 393224 | tf_op jit(solution)/shard_map/ppermute | solution.py:29
  74.0 14.4 %collective-permute-start.24 = (bf16[128,512]{1,0:T(8,128)(2,1)S(1)}, bf16[128,512]{1,0:T(8,128)(2,1)S(1)}, u32[]{:S(2)}, u32[]{:S(2)}) collective-permute-start(bf16[128,512]{1,0:T(8,128)(2,1)S(1)} %subtract_convert_fusion.refs_0_.refs_1_), channel_id=1, source_target_pairs={{0,16},{1,17},{2,18},{3,19},{4,20},{5,21},{6,22},{7,23},{8,24},{9,... | collective-permute-start | bytes 393224 | tf_op jit(solution)/shard_map/ppermute | solution.py:29
  77.2 11.2 %collective-permute-start.25 = (bf16[128,512]{1,0:T(8,128)(2,1)S(1)}, bf16[128,512]{1,0:T(8,128)(2,1)S(1)}, u32[]{:S(2)}, u32[]{:S(2)}) collective-permute-start(bf16[128,512]{1,0:T(8,128)(2,1)S(1)} %subtract_convert_fusion.refs_0_.refs_1_), channel_id=1, source_target_pairs={{0,24},{1,25},{2,26},{3,27},{4,28},{5,29},{6,30},{7,31},{8,0},{9,1... | collective-permute-start | bytes 393224 | tf_op jit(solution)/shard_map/ppermute | solution.py:29
  93.8 9.1 %collective-permute-start.26 = (f32[8,128,256]{2,1,0:T(8,128)}, f32[8,128,256]{2,1,0:T(8,128)S(1)}, u32[]{:S(2)}, u32[]{:S(2)}) collective-permute-start(f32[8,128,256]{2,1,0:T(8,128)} %get-tuple-element.21), channel_id=1, source_target_pairs={{0,1},{1,0},{2,3},{3,2},{4,5},{5,4},{6,7},{7,6},{8,9},{9,8},{10,11... | collective-permute-start | bytes 3145736 | tf_op jit(solution)/shard_map/ppermute | solution.py:29
  93.9 6.1 %collective-permute-start.22 = (f32[1,128]{1,0:T(1,128)S(1)}, f32[1,128]{1,0:T(1,128)S(1)}, u32[]{:S(2)}, u32[]{:S(2)}) collective-permute-start(f32[1,128]{1,0:T(1,128)S(1)} %bitcast_multiply_fusion), channel_id=1, source_target_pairs={{0,132},{1,133},{2,134},{3,135},{4,128},{5,129},{6,130},{7,131},{8... | collective-permute-start | bytes 1544 | tf_op jit(solution)/shard_map/ppermute | solution.py:29
  94.0 6.0 %collective-permute-start.21 = (f32[1,128]{1,0:T(1,128)S(1)}, f32[1,128]{1,0:T(1,128)S(1)}, u32[]{:S(2)}, u32[]{:S(2)}) collective-permute-start(f32[1,128]{1,0:T(1,128)S(1)} %bitcast_multiply_fusion), channel_id=1, source_target_pairs={{0,128},{1,129},{2,130},{3,131},{4,132},{5,133},{6,134},{7,135},{8... | collective-permute-start | bytes 1544 | tf_op jit(solution)/shard_map/ppermute | solution.py:29
  97.9 5.1 %collective-permute-start.20 = (f32[1,128]{1,0:T(1,128)S(1)}, f32[1,128]{1,0:T(1,128)S(1)}, u32[]{:S(2)}, u32[]{:S(2)}) collective-permute-start(f32[1,128]{1,0:T(1,128)S(1)} %bitcast_multiply_fusion), channel_id=1, source_target_pairs={{0,4},{1,5},{2,6},{3,7},{4,0},{5,1},{6,2},{7,3},{8,12},{9,13},{10,... | collective-permute-start | bytes 1544 | tf_op jit(solution)/shard_map/ppermute | solution.py:29
  104.2 12.4 %collective-permute-start.29 = (bf16[2,128,256]{2,1,0:T(8,128)(2,1)S(1)}, bf16[2,128,256]{2,1,0:T(8,128)(2,1)S(1)}, u32[]{:S(2)}, u32[]{:S(2)}) collective-permute-start(bf16[2,128,256]{2,1,0:T(8,128)(2,1)S(1)} %get-tuple-element.41), channel_id=1, source_target_pairs={{0,6},{1,7},{2,0},{3,1},{4,2},{5,3},{6,4},{7,5},{8,14},{9,15},{10,... | collective-permute-start | bytes 393224 | tf_op jit(solution)/shard_map/ppermute | solution.py:29
  106.0 11.4 %collective-permute-start.28 = (bf16[2,128,256]{2,1,0:T(8,128)(2,1)S(1)}, bf16[2,128,256]{2,1,0:T(8,128)(2,1)S(1)}, u32[]{:S(2)}, u32[]{:S(2)}) collective-permute-start(bf16[2,128,256]{2,1,0:T(8,128)(2,1)S(1)} %get-tuple-element.42), channel_id=1, source_target_pairs={{0,4},{1,5},{2,6},{3,7},{4,0},{5,1},{6,2},{7,3},{8,12},{9,13},{10,... | collective-permute-start | bytes 393224 | tf_op jit(solution)/shard_map/ppermute | solution.py:29
  106.2 11.2 %collective-permute-start.27 = (bf16[2,128,256]{2,1,0:T(8,128)(2,1)S(1)}, bf16[2,128,256]{2,1,0:T(8,128)(2,1)S(1)}, u32[]{:S(2)}, u32[]{:S(2)}) collective-permute-start(bf16[2,128,256]{2,1,0:T(8,128)(2,1)S(1)} %get-tuple-element.40), channel_id=1, source_target_pairs={{0,2},{1,3},{2,4},{3,5},{4,6},{5,7},{6,0},{7,1},{8,10},{9,11},{10,... | collective-permute-start | bytes 393224 | tf_op jit(solution)/shard_map/ppermute | solution.py:29
  112.0 13.8 %collective-permute-start.34 = (bf16[256,512]{1,0:T(8,128)(2,1)}, bf16[256,512]{1,0:T(8,128)(2,1)S(1)}, u32[]{:S(2)}, u32[]{:S(2)}) collective-permute-start(bf16[256,512]{1,0:T(8,128)(2,1)} %get-tuple-element.26), channel_id=1, source_target_pairs={{0,32},{1,33},{2,34},{3,35},{4,36},{5,37},{6,38},{7,39},{8,40},{9,... | collective-permute-start | bytes 786440 | tf_op jit(solution)/shard_map/ppermute | solution.py:29
  113.6 12.9 %collective-permute-start.33 = (bf16[256,512]{1,0:T(8,128)(2,1)}, bf16[256,512]{1,0:T(8,128)(2,1)S(1)}, u32[]{:S(2)}, u32[]{:S(2)}) collective-permute-start(bf16[256,512]{1,0:T(8,128)(2,1)} %get-tuple-element.25), channel_id=1, source_target_pairs={{0,64},{1,65},{2,66},{3,67},{4,68},{5,69},{6,70},{7,71},{8,72},{9,... | collective-permute-start | bytes 786440 | tf_op jit(solution)/shard_map/ppermute | solution.py:29
  116.6 10.0 %collective-permute-start.32 = (bf16[256,512]{1,0:T(8,128)(2,1)}, bf16[256,512]{1,0:T(8,128)(2,1)S(1)}, u32[]{:S(2)}, u32[]{:S(2)}) collective-permute-start(bf16[256,512]{1,0:T(8,128)(2,1)} %get-tuple-element.24), channel_id=1, source_target_pairs={{0,96},{1,97},{2,98},{3,99},{4,100},{5,101},{6,102},{7,103},{8,104... | collective-permute-start | bytes 786440 | tf_op jit(solution)/shard_map/ppermute | solution.py:29
  118.5 10.0 %collective-permute-start.31 = (bf16[128,256]{1,0:T(8,128)(2,1)S(1)}, bf16[128,256]{1,0:T(8,128)(2,1)S(1)}, u32[]{:S(2)}, u32[]{:S(2)}) collective-permute-start(bf16[128,256]{1,0:T(8,128)(2,1)S(1)} %get-tuple-element.47), channel_id=1, source_target_pairs={{0,128},{1,136},{2,144},{3,152},{4,132},{5,140},{6,148},{7,156},{8... | collective-permute-start | bytes 196616 | tf_op jit(solution)/shard_map/ppermute | solution.py:29
  119.8 11.0 %collective-permute-start.30 = (bf16[128,256]{1,0:T(8,128)(2,1)S(1)}, bf16[128,256]{1,0:T(8,128)(2,1)S(1)}, u32[]{:S(2)}, u32[]{:S(2)}) collective-permute-start(bf16[128,256]{1,0:T(8,128)(2,1)S(1)} %get-tuple-element.46), channel_id=1, source_target_pairs={{0,0},{1,8},{2,16},{3,24},{4,4},{5,12},{6,20},{7,28},{8,1},{9,9},{... | collective-permute-start | bytes 196616 | tf_op jit(solution)/shard_map/ppermute | solution.py:29
  (17 other events, 100.1 us)

commit v4 on v3

--- a/solution.py
+++ b/solution.py
@@ -140,20 +140,38 @@
     )(index, hidden, gain, head, head, head, head)
 
 
+ANYWHERE = pl.BlockSpec(memory_space=pl.ANY)
+
+
+def loads(sources, targets, sems):
+    copies = [
+        pltpu.make_async_copy(source, target, sems.at[i]) for i, (source, target) in enumerate(zip(sources, targets))
+    ]
+    for copy in copies:
+        copy.start()
+    return copies
+
+
 def student_kernel(index_ref, *refs):
     own_refs, near_refs, far_refs, head_refs = refs[:4], refs[4:7], refs[7:10], refs[10:14]
-    first_ref, out_ref, hidden_ref = refs[14:]
+    first_ref, out_ref, hidden_ref, head_ref, sems = refs[14:]
     core = index_ref[0] % 2
+    copies = loads(
+        [*head_refs, *near_refs, *far_refs],
+        [head_ref.at[j] for j in range(4)]
+        + [hidden_ref.at[k, pl.ds(2 * core, 2)] for k in (1, 2, 3)]
+        + [hidden_ref.at[k, pl.ds(2 * (1 - core), 2)] for k in (1, 2, 3)],
+        sems,
+    )
     for p in range(2):
         hidden_ref[0, 2 * core + p] = own_refs[p][...]
         hidden_ref[0, 2 * (1 - core) + p] = own_refs[2 + p][...]
-        for k in (1, 2, 3):
-            hidden_ref[k, 2 * core + p] = near_refs[k - 1][p]
-            hidden_ref[k, 2 * (1 - core) + p] = far_refs[k - 1][p]
+    for copy in copies:
+        copy.wait()
     for k in range(4):
         total = None
         for j in range(4):
-            term = jnp.dot(hidden_ref[k, j], head_refs[j][...], preferred_element_type=jnp.float32)
+            term = jnp.dot(hidden_ref[k, j], head_ref[j], preferred_element_type=jnp.float32)
             total = term if total is None else total + term
         if k == 0:
             first_ref[...] = total
@@ -171,26 +189,26 @@
             num_scalar_prefetch=1,
             grid=(1,),
             in_specs=[hidden_block(0, p) for p in range(4)]
-            + [whole(2, 128, 256)] * 6
-            + [whole(256, 512)] * 4,
-            out_specs=(whole(128, 512), whole(3, 128, 512), whole(4, 4, 128, 256)),
+            + [ANYWHERE] * 10,
+            out_specs=(whole(128, 512), whole(3, 128, 512), whole(4, 4, 128, 256), whole(4, 256, 512)),
+            scratch_shapes=[pltpu.SemaphoreType.DMA((10,))],
         ),
         out_shape=(
             jax.ShapeDtypeStruct((128, 512), jnp.float32),
             jax.ShapeDtypeStruct((3, 128, 512), jnp.float32),
             jax.ShapeDtypeStruct((4, 4, 128, 256), jnp.bfloat16),
+            jax.ShapeDtypeStruct((4, 256, 512), jnp.bfloat16),
         ),
         name="student",
     )(index, *[own] * 4, *near, *far, *head_slots)
 
 
-def head_grad_kernel(*refs):
-    hidden_ref, grad_refs, own_ref, out_refs = refs[0], refs[1:5], refs[5], refs[6:]
+def head_grad_kernel(states_ref, slots_ref, own_ref, *out_refs):
     for j in range(4):
         total = None
         for k in range(4):
             term = lax.dot_general(
-                hidden_ref[k, j], grad_refs[k][...], (((0,), (0,)), ((), ())), preferred_element_type=jnp.float32
+                states_ref[k, j], slots_ref[k], (((0,), (0,)), ((), ())), preferred_element_type=jnp.float32
             )
             total = term if total is None else total + term
         if j == 0:
@@ -199,7 +217,7 @@
             out_refs[j - 1][...] = total.astype(jnp.bfloat16)
 
 
-def head_grad_parts(hidden, grad_slots):
+def head_grad_parts(hidden, slots):
     return pl.pallas_call(
         head_grad_kernel,
         out_shape=(
@@ -207,37 +225,41 @@
             *[jax.ShapeDtypeStruct((256, 512), jnp.bfloat16)] * 3,
         ),
         name="head_grad",
-    )(hidden, *grad_slots)
+    )(hidden, slots)
 
 
 def hidden_grad_kernel(index_ref, *refs):
-    grad_refs, head_refs, own_ref, other_ref, slots_ref = refs[:4], refs[4:8], refs[8], refs[9], refs[10]
+    grad_refs, head_ref, own_ref, other_ref, slots_ref, sems = refs[:4], *refs[4:]
     zl, y, zh, x, core = coordinates(index_ref[0])
-    for k in range(4):
-        slots_ref[k] = grad_refs[k][...]
-    for m in range(2):
-        for j in range(4):
+    for copy in loads(grad_refs, [slots_ref.at[k] for k in range(4)], sems):
+        copy.wait()
+    for j in range(4):
+        for m in range(2):
             a = (y + 4 - j) % 4
             for out_ref, side in ((own_ref, core), (other_ref, 1 - core)):
                 goal = 2 * m + side
                 spot = (a % 2 * 2 + m + 4 - x) % 4 * 2 + (a // 2 + zl) % 2
                 out_ref[spot] = lax.dot_general(
                     slots_ref[(zh + 4 - goal) % 4],
-                    head_refs[j][...],
+                    head_ref[j],
                     (((1,), (1,)), ((), ())),
                     preferred_element_type=jnp.float32,
                 )
 
 
-def hidden_grad_parts(index, grad_slots, head_slots):
-    vmem = pl.BlockSpec(memory_space=pltpu.VMEM)
+def hidden_grad_parts(index, grad_slots, head):
     return pl.pallas_call(
         hidden_grad_kernel,
-        in_specs=[pl.BlockSpec(memory_space=pltpu.SMEM)] + [vmem] * 8,
-        out_shape=(jax.ShapeDtypeStruct((8, 128, 256), jnp.float32),) * 2,
-        scratch_shapes=[pltpu.VMEM((4, 128, 512), jnp.bfloat16)],
+        in_specs=[pl.BlockSpec(memory_space=pltpu.SMEM)]
+        + [ANYWHERE] * 4
+        + [pl.BlockSpec(memory_space=pltpu.VMEM)],
+        out_shape=(
+            *[jax.ShapeDtypeStruct((8, 128, 256), jnp.float32)] * 2,
+            jax.ShapeDtypeStruct((4, 128, 512), jnp.bfloat16),
+        ),
+        scratch_shapes=[pltpu.SemaphoreType.DMA((4,))],
         name="hidden_grad",
-    )(index, *grad_slots, *head_slots)
+    )(index, *grad_slots, head)
 
 
 def step(teacher_hidden, teacher_gain, teacher_head, student_hidden, student_head, depth_cut):
@@ -260,7 +282,7 @@
         by_x = by_x + to_x(part.astype(f16), step).astype(f32)
     teacher = by_x[0] + to_zl(by_x[1].astype(f16)).astype(f32)
 
-    student, parts, hidden = student_parts(index, student_hidden, near, far, head_slots)
+    student, parts, hidden, head = student_parts(index, student_hidden, near, far, head_slots)
     parts = parts.astype(f16)
     for k in (1, 2, 3):
         student = student + to_zh(parts[k - 1], -k).astype(f32)
@@ -321,9 +343,9 @@
     )
 
     grad_slots = [score_grad] + [to_zh(score_grad, k) for k in (1, 2, 3)]
-    own, other = hidden_grad_parts(index, grad_slots, head_slots)
+    own, other, slots = hidden_grad_parts(index, grad_slots, head)
     other = to_core(other)
-    head_grad, *parts = head_grad_parts(hidden, grad_slots)
+    head_grad, *parts = head_grad_parts(hidden, slots)
     for j in (1, 2, 3):
         head_grad = head_grad + to_y(parts[j - 1], -j).astype(f32)
     by_x = own[:2] + other[:2]

time: 133 us -> 135 us (1.015)
  local copies, waits for them, and re-layouts: 2.98 us -> 1.09 us
  Pallas kernels: 21.8 us -> 23.6 us
    unnamed x28 -> x24, local copies, waits for them, and re-layouts: 2.63 us -> 0.74 us
where the time goes in v4:
time: 135 us; the launch traced here: 133 us
  starting transfers between devices  67.3 us (50%)
  waiting for transfers between devices  28.6 us (21%)
  Pallas kernels  23.6 us (17%)
  other arithmetic  11.5 us (9%)
    ppermute x35, starting transfers between devices, send(): return lax.ppermute(value, ALL, pairs)  67.3 us
    ppermute x35, waiting for transfers between devices, send(): return lax.ppermute(value, ALL, pairs)  28.6 us
    pallas_call x2, Pallas kernels, teacher_parts(): pl.pallas_call(teacher_kernel, grid_spec=pltpu.PrefetchScalarGridSpec(num...  8.82 us
    pallas_call x1, Pallas kernels, hidden_grad_parts(): pl.pallas_call(hidden_grad_kernel, in_specs=[pl.BlockSpec(memory_space=pl...  5.27 us
    pallas_call x1, Pallas kernels, student_parts(): pl.pallas_call(student_kernel, grid_spec=pltpu.PrefetchScalarGridSpec(num...  4.42 us
    pallas_call x1, Pallas kernels, head_grad_parts(): pl.pallas_call(head_grad_kernel, out_shape=(jax.ShapeDtypeStruct((256, 51...  3.32 us
  transfers between devices with their start and end apart: 35, of which 13 were waited for; matrix products, arithmetic and copies ran while one was open for 7% of the time, Pallas kernels for 10%

profile of v4, /device:TPU:2, one launch (start us, length us, event | category | flops | bytes accessed | tf_op | source)
XLA Modules:
  0.0 133.0 jit_solution(18232103976414556009)
XLA Ops:
  0.6 4.5 %teacher.3 = f32[8,136,512]{2,1,0:T(8,128)} custom-call(s32[1]{0:T(128)} %bitcast.index_ref, bf16[128,512]{1,0:T(8,128)(2,1)} %hidden_ref.3, bf16[512]{0:T(512)(128)(2,1)} %gain_ref.3, bf16[512,8192]{1,0:T(8,128)(2,1)} %refs_3_.5, bf16[512,8192]{1,0:T(8,128)(2,1)} %refs_3_.5, bf16[512,8192]{1,0:T(8,128)(2,1)} %refs_3_.5, bf16[512,8192]{1,0:T(8,128)(2,1)} %refs_3_.5), custom_call_target="tpu_custom_call" | custom-call | tf_op jit(solution)/shard_map/teacher/pallas_call | solution.py:125
  5.1 1.8 %pick.1 = (bf16[2,128,256]{2,1,0:T(8,128)(2,1)}, bf16[2,128,256]{2,1,0:T(8,128)(2,1)}, bf16[2,128,256]{2,1,0:T(8,128)(2,1)}) custom-call(s32[1]{0:T(128)} %bitcast.index_ref, bf16[128,4096]{1,0:T(8,128)(2,1)} %refs_3_.7, bf16[128,4096]{1,0:T(8,128)(2,1)} %refs_3_.7, bf16[128,4096]{1,0:T(8,128)(2,1)} %refs_3_.7, bf16[128,4096]{1,0:T(8,128)(2,1)} %refs_3_.7, ...), custom_call_target="tpu_custom_call" | custom-call | tf_op jit(solution)/shard_map/pick/pallas_call | solution.py:72
  6.9 3.3 %collective-permute-start.5 = (bf16[2,128,256]{2,1,0:T(8,128)(2,1)}, bf16[2,128,256]{2,1,0:T(8,128)(2,1)S(1)}, u32[]{:S(2)}, u32[]{:S(2)}) collective-permute-start(bf16[2,128,256]{2,1,0:T(8,128)(2,1)} %get-tuple-element.17), channel_id=1, source_target_pairs={{0,8},{1,9},{2,10},{3,11},{4,12},{5,13},{6,14},{7,15},{8,16},{9,17... | collective-permute-start | bytes 393224 | tf_op jit(solution)/shard_map/ppermute | solution.py:29
  10.2 5.4 %collective-permute-start.6 = (bf16[2,128,256]{2,1,0:T(8,128)(2,1)}, bf16[2,128,256]{2,1,0:T(8,128)(2,1)S(1)}, u32[]{:S(2)}, u32[]{:S(2)}) collective-permute-start(bf16[2,128,256]{2,1,0:T(8,128)(2,1)} %get-tuple-element.18), channel_id=1, source_target_pairs={{0,16},{1,17},{2,18},{3,19},{4,20},{5,21},{6,22},{7,23},{8,24},{9,... | collective-permute-start | bytes 393224 | tf_op jit(solution)/shard_map/ppermute | solution.py:29
  15.6 2.7 %collective-permute-start.7 = (bf16[2,128,256]{2,1,0:T(8,128)(2,1)}, bf16[2,128,256]{2,1,0:T(8,128)(2,1)S(1)}, u32[]{:S(2)}, u32[]{:S(2)}) collective-permute-start(bf16[2,128,256]{2,1,0:T(8,128)(2,1)} %get-tuple-element.19), channel_id=1, source_target_pairs={{0,24},{1,25},{2,26},{3,27},{4,28},{5,29},{6,30},{7,31},{8,0},{9,1... | collective-permute-start | bytes 393224 | tf_op jit(solution)/shard_map/ppermute | solution.py:29
  19.9 4.3 %teacher.2 = f32[8,136,512]{2,1,0:T(8,128)} custom-call(s32[1]{0:T(128)} %bitcast.index_ref, bf16[128,512]{1,0:T(8,128)(2,1)} %hidden_ref.3, bf16[512]{0:T(512)(128)(2,1)} %gain_ref.3, bf16[512,8192]{1,0:T(8,128)(2,1)} %refs_3_.5, bf16[512,8192]{1,0:T(8,128)(2,1)} %refs_3_.5, bf16[512,8192]{1,0:T(8,128)(2,1)} %refs_3_.5, bf16[512,8192]{1,0:T(8,128)(2,1)} %refs_3_.5), custom_call_target="tpu_custom_call" | custom-call | tf_op jit(solution)/shard_map/teacher/pallas_call | solution.py:125
  25.5 3.2 %collective-permute-start.12 = (bf16[256,512]{1,0:T(8,128)(2,1)}, bf16[256,512]{1,0:T(8,128)(2,1)}, u32[]{:S(2)}, u32[]{:S(2)}) collective-permute-start(bf16[256,512]{1,0:T(8,128)(2,1)} %refs_10_.1), channel_id=1, source_target_pairs={{0,64},{1,65},{2,66},{3,67},{4,68},{5,69},{6,70},{7,71},{8,72},{9,... | collective-permute-start | bytes 786440 | tf_op jit(solution)/shard_map/ppermute | solution.py:29
  28.7 2.8 %collective-permute-start.13 = (bf16[256,512]{1,0:T(8,128)(2,1)}, bf16[256,512]{1,0:T(8,128)(2,1)}, u32[]{:S(2)}, u32[]{:S(2)}) collective-permute-start(bf16[256,512]{1,0:T(8,128)(2,1)} %refs_10_.1), channel_id=1, source_target_pairs={{0,96},{1,97},{2,98},{3,99},{4,100},{5,101},{6,102},{7,103},{8,104... | collective-permute-start | bytes 786440 | tf_op jit(solution)/shard_map/ppermute | solution.py:29
  32.1 2.5 %fusion.2 = (f16[2,136,512]{2,1,0:T(8,128)(2,1)S(1)}, f16[2,136,512]{2,1,0:T(8,128)(2,1)}, f16[2,136,512]{2,1,0:T(8,128)(2,1)S(1)}) fusion(f32[8,136,512]{2,1,0:T(8,128)S(1)} %collective-permute-done, f32[8,136,512]{2,1,0:T(8,128)} %teacher.2), kind=kLoop, calls=%fused_computation.5 | loop fusion | flops 835584 | bytes 4177920 | tf_op jit(solution)/shard_map/convert_element_type | solution.py:282
  35.2 2.5 %collective-permute-start.2 = (f16[2,136,512]{2,1,0:T(8,128)(2,1)S(1)}, f16[2,136,512]{2,1,0:T(8,128)(2,1)S(1)}, u32[]{:S(2)}, u32[]{:S(2)}) collective-permute-start(f16[2,136,512]{2,1,0:T(8,128)(2,1)S(1)} %get-tuple-element.43), channel_id=1, source_target_pairs={{0,4},{1,5},{2,6},{3,7},{4,0},{5,1},{6,2},{7,3},{8,12},{9,13},{10,... | collective-permute-start | bytes 835592 | tf_op jit(solution)/shard_map/ppermute | solution.py:29
  37.7 1.8 %collective-permute-start.1 = (f16[2,136,512]{2,1,0:T(8,128)(2,1)S(1)}, f16[2,136,512]{2,1,0:T(8,128)(2,1)}, u32[]{:S(2)}, u32[]{:S(2)}) collective-permute-start(f16[2,136,512]{2,1,0:T(8,128)(2,1)S(1)} %get-tuple-element.41), channel_id=1, source_target_pairs={{0,2},{1,3},{2,4},{3,5},{4,6},{5,7},{6,0},{7,1},{8,10},{9,11},{10,... | collective-permute-start | bytes 835592 | tf_op jit(solution)/shard_map/ppermute | solution.py:29
  40.9 4.4 %student.1 = (f32[128,512]{1,0:T(8,128)}, f32[3,128,512]{2,1,0:T(8,128)}, bf16[4,4,128,256]{3,2,1,0:T(8,128)(2,1)}, bf16[4,256,512]{2,1,0:T(8,128)(2,1)}) custom-call(s32[1]{0:T(128)} %bitcast.index_ref, bf16[128,4096]{1,0:T(8,128)(2,1)} %refs_3_.7, bf16[128,4096]{1,0:T(8,128)(2,1)} %refs_3_.7, bf16[128,4096]{1,0:T(8,128)(2,1)} %refs_3_.7, ...), custom_call_target="tpu_custom_call" | custom-call | tf_op jit(solution)/shard_map/student/pallas_call | solution.py:186
  46.7 3.8 %collective-permute-start.16 = (f16[128,512]{1,0:T(8,128)(2,1)S(1)}, f16[128,512]{1,0:T(8,128)(2,1)S(1)}, u32[]{:S(2)}, u32[]{:S(2)}) collective-permute-start(f16[128,512]{1,0:T(8,128)(2,1)S(1)} %get-tuple-element.48), channel_id=1, source_target_pairs={{0,8},{1,9},{2,10},{3,11},{4,12},{5,13},{6,14},{7,15},{8,16},{9,17... | collective-permute-start | bytes 393224 | tf_op jit(solution)/shard_map/ppermute | solution.py:29
  50.5 4.3 %collective-permute-start.15 = (f16[128,512]{1,0:T(8,128)(2,1)S(1)}, f16[128,512]{1,0:T(8,128)(2,1)S(1)}, u32[]{:S(2)}, u32[]{:S(2)}) collective-permute-start(f16[128,512]{1,0:T(8,128)(2,1)S(1)} %get-tuple-element.49), channel_id=1, source_target_pairs={{0,16},{1,17},{2,18},{3,19},{4,20},{5,21},{6,22},{7,23},{8,24},{9,... | collective-permute-start | bytes 393224 | tf_op jit(solution)/shard_map/ppermute | solution.py:29
  54.9 3.9 %collective-permute-start.14 = (f16[128,512]{1,0:T(8,128)(2,1)S(1)}, f16[128,512]{1,0:T(8,128)(2,1)S(1)}, u32[]{:S(2)}, u32[]{:S(2)}) collective-permute-start(f16[128,512]{1,0:T(8,128)(2,1)S(1)} %get-tuple-element.47), channel_id=1, source_target_pairs={{0,24},{1,25},{2,26},{3,27},{4,28},{5,29},{6,30},{7,31},{8,0},{9,1... | collective-permute-start | bytes 393224 | tf_op jit(solution)/shard_map/ppermute | solution.py:29
  60.2 3.8 %collective-permute-done.15 = f16[128,512]{1,0:T(8,128)(2,1)S(1)} collective-permute-done((f16[128,512]{1,0:T(8,128)(2,1)S(1)}, f16[128,512]{1,0:T(8,128)(2,1)S(1)}, u32[]{:S(2)}, u32[]{:S(2)}) %collective-permute-start.15) | collective-permute-done | bytes 131104 | tf_op jit(solution)/shard_map/ppermute | solution.py:29
  64.0 2.1 %collective-permute-done.14 = f16[128,512]{1,0:T(8,128)(2,1)S(1)} collective-permute-done((f16[128,512]{1,0:T(8,128)(2,1)S(1)}, f16[128,512]{1,0:T(8,128)(2,1)S(1)}, u32[]{:S(2)}, u32[]{:S(2)}) %collective-permute-start.14) | collective-permute-done | bytes 131104 | tf_op jit(solution)/shard_map/ppermute | solution.py:29
  72.1 2.3 %collective-permute-start.23 = (bf16[128,512]{1,0:T(8,128)(2,1)S(1)}, bf16[128,512]{1,0:T(8,128)(2,1)S(1)}, u32[]{:S(2)}, u32[]{:S(2)}) collective-permute-start(bf16[128,512]{1,0:T(8,128)(2,1)S(1)} %subtract_convert_fusion.refs_0_), channel_id=1, source_target_pairs={{0,8},{1,9},{2,10},{3,11},{4,12},{5,13},{6,14},{7,15},{8,16},{9,17... | collective-permute-start | bytes 393224 | tf_op jit(solution)/shard_map/ppermute | solution.py:29
  74.4 3.2 %collective-permute-start.24 = (bf16[128,512]{1,0:T(8,128)(2,1)S(1)}, bf16[128,512]{1,0:T(8,128)(2,1)S(1)}, u32[]{:S(2)}, u32[]{:S(2)}) collective-permute-start(bf16[128,512]{1,0:T(8,128)(2,1)S(1)} %subtract_convert_fusion.refs_0_), channel_id=1, source_target_pairs={{0,16},{1,17},{2,18},{3,19},{4,20},{5,21},{6,22},{7,23},{8,24},{9,... | collective-permute-start | bytes 393224 | tf_op jit(solution)/shard_map/ppermute | solution.py:29
  79.1 2.3 %collective-permute-done.23.refs_1_ = bf16[128,512]{1,0:T(8,128)(2,1)S(1)} collective-permute-done((bf16[128,512]{1,0:T(8,128)(2,1)S(1)}, bf16[128,512]{1,0:T(8,128)(2,1)S(1)}, u32[]{:S(2)}, u32[]{:S(2)}) %collective-permute-start.23) | collective-permute-done | bytes 131104 | tf_op jit(solution)/shard_map/ppermute | solution.py:29
  81.5 7.4 %collective-permute-done.24.refs_2_ = bf16[128,512]{1,0:T(8,128)(2,1)S(1)} collective-permute-done((bf16[128,512]{1,0:T(8,128)(2,1)S(1)}, bf16[128,512]{1,0:T(8,128)(2,1)S(1)}, u32[]{:S(2)}, u32[]{:S(2)}) %collective-permute-start.24) | collective-permute-done | bytes 131104 | tf_op jit(solution)/shard_map/ppermute | solution.py:29
  89.6 5.3 %hidden_grad.1 = (f32[8,128,256]{2,1,0:T(8,128)}, f32[8,128,256]{2,1,0:T(8,128)}, bf16[4,128,512]{2,1,0:T(8,128)(2,1)}) custom-call(s32[1]{0:T(128)} %bitcast.index_ref, bf16[128,512]{1,0:T(8,128)(2,1)} %copy-done, bf16[128,512]{1,0:T(8,128)(2,1)} %copy-done.8, bf16[128,512]{1,0:T(8,128)(2,1)} %copy-done.9, bf16[128,512]{1,0:T(8,128)(2,1)} %copy-done.10, ...), custom_call_target="tpu_custom_call" | custom-call | tf_op jit(solution)/shard_map/hidden_grad/pallas_call | solution.py:251
  95.1 3.8 %collective-permute-start.21 = (f32[1,128]{1,0:T(1,128)S(1)}, f32[1,128]{1,0:T(1,128)S(1)}, u32[]{:S(2)}, u32[]{:S(2)}) collective-permute-start(f32[1,128]{1,0:T(1,128)S(1)} %bitcast_multiply_fusion), channel_id=1, source_target_pairs={{0,128},{1,129},{2,130},{3,131},{4,132},{5,133},{6,134},{7,135},{8... | collective-permute-start | bytes 1544 | tf_op jit(solution)/shard_map/ppermute | solution.py:29
  101.1 2.9 %collective-permute-done.20 = f32[1,128]{1,0:T(1,128)S(1)} collective-permute-done((f32[1,128]{1,0:T(1,128)S(1)}, f32[1,128]{1,0:T(1,128)S(1)}, u32[]{:S(2)}, u32[]{:S(2)}) %collective-permute-start.20) | collective-permute-done | bytes 544 | tf_op jit(solution)/shard_map/ppermute | solution.py:29
  105.2 1.9 %collective-permute-start.29 = (bf16[2,128,256]{2,1,0:T(8,128)(2,1)S(1)}, bf16[2,128,256]{2,1,0:T(8,128)(2,1)S(1)}, u32[]{:S(2)}, u32[]{:S(2)}) collective-permute-start(bf16[2,128,256]{2,1,0:T(8,128)(2,1)S(1)} %get-tuple-element.45), channel_id=1, source_target_pairs={{0,6},{1,7},{2,0},{3,1},{4,2},{5,3},{6,4},{7,5},{8,14},{9,15},{10,... | collective-permute-start | bytes 393224 | tf_op jit(solution)/shard_map/ppermute | solution.py:29
  107.3 1.8 %collective-permute-start.27 = (bf16[2,128,256]{2,1,0:T(8,128)(2,1)S(1)}, bf16[2,128,256]{2,1,0:T(8,128)(2,1)S(1)}, u32[]{:S(2)}, u32[]{:S(2)}) collective-permute-start(bf16[2,128,256]{2,1,0:T(8,128)(2,1)S(1)} %get-tuple-element.44), channel_id=1, source_target_pairs={{0,2},{1,3},{2,4},{3,5},{4,6},{5,7},{6,0},{7,1},{8,10},{9,11},{10,... | collective-permute-start | bytes 393224 | tf_op jit(solution)/shard_map/ppermute | solution.py:29
  109.7 3.3 %head_grad.1 = (f32[256,512]{1,0:T(8,128)}, bf16[256,512]{1,0:T(8,128)(2,1)}, bf16[256,512]{1,0:T(8,128)(2,1)}, bf16[256,512]{1,0:T(8,128)(2,1)}) custom-call(bf16[4,4,128,256]{3,2,1,0:T(8,128)(2,1)} %get-tuple-element.25.states_ref, bf16[4,128,512]{2,1,0:T(8,128)(2,1)} %get-tuple-element.26.slots_ref), custom_call_target="tpu_custom_call" | custom-call | tf_op jit(solution)/shard_map/head_grad/pallas_call | solution.py:221
  114.6 3.0 %collective-permute-start.33 = (bf16[256,512]{1,0:T(8,128)(2,1)}, bf16[256,512]{1,0:T(8,128)(2,1)S(1)}, u32[]{:S(2)}, u32[]{:S(2)}) collective-permute-start(bf16[256,512]{1,0:T(8,128)(2,1)} %get-tuple-element.29), channel_id=1, source_target_pairs={{0,64},{1,65},{2,66},{3,67},{4,68},{5,69},{6,70},{7,71},{8,72},{9,... | collective-permute-start | bytes 786440 | tf_op jit(solution)/shard_map/ppermute | solution.py:29
  119.5 1.8 %collective-permute-start.31 = (bf16[128,256]{1,0:T(8,128)(2,1)S(1)}, bf16[128,256]{1,0:T(8,128)(2,1)S(1)}, u32[]{:S(2)}, u32[]{:S(2)}) collective-permute-start(bf16[128,256]{1,0:T(8,128)(2,1)S(1)} %get-tuple-element.51), channel_id=1, source_target_pairs={{0,128},{1,136},{2,144},{3,152},{4,132},{5,140},{6,148},{7,156},{8... | collective-permute-start | bytes 196616 | tf_op jit(solution)/shard_map/ppermute | solution.py:29
  121.4 5.5 %collective-permute-start.30 = (bf16[128,256]{1,0:T(8,128)(2,1)S(1)}, bf16[128,256]{1,0:T(8,128)(2,1)S(1)}, u32[]{:S(2)}, u32[]{:S(2)}) collective-permute-start(bf16[128,256]{1,0:T(8,128)(2,1)S(1)} %get-tuple-element.50), channel_id=1, source_target_pairs={{0,0},{1,8},{2,16},{3,24},{4,4},{5,12},{6,20},{7,28},{8,1},{9,9},{... | collective-permute-start | bytes 196616 | tf_op jit(solution)/shard_map/ppermute | solution.py:29
  127.5 2.0 %convert_add_fusion = f32[256,512]{1,0:T(8,128)} fusion(bf16[256,512]{1,0:T(8,128)(2,1)S(1)} %collective-permute-done.34, bf16[256,512]{1,0:T(8,128)(2,1)S(1)} %collective-permute-done.33, f32[256,512]{1,0:T(8,128)} %get-tuple-element.27, bf16[256,512]{1,0:T(8,128)(2,1)S(1)} %collective-permute-done.32), kind=kLoop, calls=%fused_computation.10 | loop fusion | flops 786432 | bytes 1835008 | tf_op jit(solution)/shard_map/add | solution.py:350
  129.5 2.8 %collective-permute-done.30 = bf16[128,256]{1,0:T(8,128)(2,1)S(1)} collective-permute-done((bf16[128,256]{1,0:T(8,128)(2,1)S(1)}, bf16[128,256]{1,0:T(8,128)(2,1)S(1)}, u32[]{:S(2)}, u32[]{:S(2)}) %collective-permute-start.30) | collective-permute-done | bytes 65568 | tf_op jit(solution)/shard_map/ppermute | solution.py:29
  (99 shorter events, 25.6 us)
Async XLA Ops:
  5.1 26.4 %collective-permute-start = (f32[8,136,512]{2,1,0:T(8,128)}, f32[8,136,512]{2,1,0:T(8,128)S(1)}, u32[]{:S(2)}, u32[]{:S(2)}) collective-permute-start(f32[8,136,512]{2,1,0:T(8,128)} %teacher.3), channel_id=1, source_target_pairs={{0,1},{1,0},{2,3},{3,2},{4,5},{5,4},{6,7},{7,6},{8,9},{9,8},{10,11... | collective-permute-start | bytes 6684680 | tf_op jit(solution)/shard_map/ppermute | solution.py:29
  6.9 11.3 %collective-permute-start.5 = (bf16[2,128,256]{2,1,0:T(8,128)(2,1)}, bf16[2,128,256]{2,1,0:T(8,128)(2,1)S(1)}, u32[]{:S(2)}, u32[]{:S(2)}) collective-permute-start(bf16[2,128,256]{2,1,0:T(8,128)(2,1)} %get-tuple-element.17), channel_id=1, source_target_pairs={{0,8},{1,9},{2,10},{3,11},{4,12},{5,13},{6,14},{7,15},{8,16},{9,17... | collective-permute-start | bytes 393224 | tf_op jit(solution)/shard_map/ppermute | solution.py:29
  10.2 15.3 %collective-permute-start.6 = (bf16[2,128,256]{2,1,0:T(8,128)(2,1)}, bf16[2,128,256]{2,1,0:T(8,128)(2,1)S(1)}, u32[]{:S(2)}, u32[]{:S(2)}) collective-permute-start(bf16[2,128,256]{2,1,0:T(8,128)(2,1)} %get-tuple-element.18), channel_id=1, source_target_pairs={{0,16},{1,17},{2,18},{3,19},{4,20},{5,21},{6,22},{7,23},{8,24},{9,... | collective-permute-start | bytes 393224 | tf_op jit(solution)/shard_map/ppermute | solution.py:29
  15.6 13.1 %collective-permute-start.7 = (bf16[2,128,256]{2,1,0:T(8,128)(2,1)}, bf16[2,128,256]{2,1,0:T(8,128)(2,1)S(1)}, u32[]{:S(2)}, u32[]{:S(2)}) collective-permute-start(bf16[2,128,256]{2,1,0:T(8,128)(2,1)} %get-tuple-element.19), channel_id=1, source_target_pairs={{0,24},{1,25},{2,26},{3,27},{4,28},{5,29},{6,30},{7,31},{8,0},{9,1... | collective-permute-start | bytes 393224 | tf_op jit(solution)/shard_map/ppermute | solution.py:29
  18.3 13.3 %collective-permute-start.8 = (bf16[2,128,256]{2,1,0:T(8,128)(2,1)S(1)}, bf16[2,128,256]{2,1,0:T(8,128)(2,1)S(1)}, u32[]{:S(2)}, u32[]{:S(2)}) collective-permute-start(bf16[2,128,256]{2,1,0:T(8,128)(2,1)S(1)} %collective-permute-done.5.refs_4_), channel_id=1, source_target_pairs={{0,1},{1,0},{2,3},{3,2},{4,5},{5,4},{6,7},{7,6},{8,9},{9,8},{10,11... | collective-permute-start | bytes 393224 | tf_op jit(solution)/shard_map/ppermute | solution.py:29
  18.3 19.5 %collective-permute-start.11 = (bf16[256,512]{1,0:T(8,128)(2,1)}, bf16[256,512]{1,0:T(8,128)(2,1)}, u32[]{:S(2)}, u32[]{:S(2)}) collective-permute-start(bf16[256,512]{1,0:T(8,128)(2,1)} %refs_10_.1), channel_id=1, source_target_pairs={{0,32},{1,33},{2,34},{3,35},{4,36},{5,37},{6,38},{7,39},{8,40},{9,... | collective-permute-start | bytes 786440 | tf_op jit(solution)/shard_map/ppermute | solution.py:29
  25.5 14.0 %collective-permute-start.12 = (bf16[256,512]{1,0:T(8,128)(2,1)}, bf16[256,512]{1,0:T(8,128)(2,1)}, u32[]{:S(2)}, u32[]{:S(2)}) collective-permute-start(bf16[256,512]{1,0:T(8,128)(2,1)} %refs_10_.1), channel_id=1, source_target_pairs={{0,64},{1,65},{2,66},{3,67},{4,68},{5,69},{6,70},{7,71},{8,72},{9,... | collective-permute-start | bytes 786440 | tf_op jit(solution)/shard_map/ppermute | solution.py:29
  28.7 12.2 %collective-permute-start.13 = (bf16[256,512]{1,0:T(8,128)(2,1)}, bf16[256,512]{1,0:T(8,128)(2,1)}, u32[]{:S(2)}, u32[]{:S(2)}) collective-permute-start(bf16[256,512]{1,0:T(8,128)(2,1)} %refs_10_.1), channel_id=1, source_target_pairs={{0,96},{1,97},{2,98},{3,99},{4,100},{5,101},{6,102},{7,103},{8,104... | collective-permute-start | bytes 786440 | tf_op jit(solution)/shard_map/ppermute | solution.py:29
  31.6 3.6 %collective-permute-start.10 = (bf16[2,128,256]{2,1,0:T(8,128)(2,1)S(1)}, bf16[2,128,256]{2,1,0:T(8,128)(2,1)S(1)}, u32[]{:S(2)}, u32[]{:S(2)}) collective-permute-start(bf16[2,128,256]{2,1,0:T(8,128)(2,1)S(1)} %collective-permute-done.7.refs_6_), channel_id=1, source_target_pairs={{0,1},{1,0},{2,3},{3,2},{4,5},{5,4},{6,7},{7,6},{8,9},{9,8},{10,11... | collective-permute-start | bytes 393224 | tf_op jit(solution)/shard_map/ppermute | solution.py:29
  34.6 20.2 %collective-permute-start.3 = (f16[2,136,512]{2,1,0:T(8,128)(2,1)}, f16[2,136,512]{2,1,0:T(8,128)(2,1)S(1)}, u32[]{:S(2)}, u32[]{:S(2)}) collective-permute-start(f16[2,136,512]{2,1,0:T(8,128)(2,1)} %get-tuple-element.42), channel_id=1, source_target_pairs={{0,6},{1,7},{2,0},{3,1},{4,2},{5,3},{6,4},{7,5},{8,14},{9,15},{10,... | collective-permute-start | bytes 835592 | tf_op jit(solution)/shard_map/ppermute | solution.py:29
  35.2 23.5 %collective-permute-start.2 = (f16[2,136,512]{2,1,0:T(8,128)(2,1)S(1)}, f16[2,136,512]{2,1,0:T(8,128)(2,1)S(1)}, u32[]{:S(2)}, u32[]{:S(2)}) collective-permute-start(f16[2,136,512]{2,1,0:T(8,128)(2,1)S(1)} %get-tuple-element.43), channel_id=1, source_target_pairs={{0,4},{1,5},{2,6},{3,7},{4,0},{5,1},{6,2},{7,3},{8,12},{9,13},{10,... | collective-permute-start | bytes 835592 | tf_op jit(solution)/shard_map/ppermute | solution.py:29
  37.7 21.0 %collective-permute-start.1 = (f16[2,136,512]{2,1,0:T(8,128)(2,1)S(1)}, f16[2,136,512]{2,1,0:T(8,128)(2,1)}, u32[]{:S(2)}, u32[]{:S(2)}) collective-permute-start(f16[2,136,512]{2,1,0:T(8,128)(2,1)S(1)} %get-tuple-element.41), channel_id=1, source_target_pairs={{0,2},{1,3},{2,4},{3,5},{4,6},{5,7},{6,0},{7,1},{8,10},{9,11},{10,... | collective-permute-start | bytes 835592 | tf_op jit(solution)/shard_map/ppermute | solution.py:29
  46.7 13.5 %collective-permute-start.16 = (f16[128,512]{1,0:T(8,128)(2,1)S(1)}, f16[128,512]{1,0:T(8,128)(2,1)S(1)}, u32[]{:S(2)}, u32[]{:S(2)}) collective-permute-start(f16[128,512]{1,0:T(8,128)(2,1)S(1)} %get-tuple-element.48), channel_id=1, source_target_pairs={{0,8},{1,9},{2,10},{3,11},{4,12},{5,13},{6,14},{7,15},{8,16},{9,17... | collective-permute-start | bytes 393224 | tf_op jit(solution)/shard_map/ppermute | solution.py:29
  50.5 13.5 %collective-permute-start.15 = (f16[128,512]{1,0:T(8,128)(2,1)S(1)}, f16[128,512]{1,0:T(8,128)(2,1)S(1)}, u32[]{:S(2)}, u32[]{:S(2)}) collective-permute-start(f16[128,512]{1,0:T(8,128)(2,1)S(1)} %get-tuple-element.49), channel_id=1, source_target_pairs={{0,16},{1,17},{2,18},{3,19},{4,20},{5,21},{6,22},{7,23},{8,24},{9,... | collective-permute-start | bytes 393224 | tf_op jit(solution)/shard_map/ppermute | solution.py:29
  54.9 11.3 %collective-permute-start.14 = (f16[128,512]{1,0:T(8,128)(2,1)S(1)}, f16[128,512]{1,0:T(8,128)(2,1)S(1)}, u32[]{:S(2)}, u32[]{:S(2)}) collective-permute-start(f16[128,512]{1,0:T(8,128)(2,1)S(1)} %get-tuple-element.47), channel_id=1, source_target_pairs={{0,24},{1,25},{2,26},{3,27},{4,28},{5,29},{6,30},{7,31},{8,0},{9,1... | collective-permute-start | bytes 393224 | tf_op jit(solution)/shard_map/ppermute | solution.py:29
  60.1 7.4 %collective-permute-start.4 = (f16[136,512]{1,0:T(8,128)(2,1)S(1)}, f16[136,512]{1,0:T(8,128)(2,1)S(1)}, u32[]{:S(2)}, u32[]{:S(2)}) collective-permute-start(f16[136,512]{1,0:T(8,128)(2,1)S(1)} %fusion.17), channel_id=1, source_target_pairs={{0,128},{1,129},{2,130},{3,131},{4,132},{5,133},{6,134},{7,135},{8... | collective-permute-start | bytes 417800 | tf_op jit(solution)/shard_map/ppermute | solution.py:29
  68.1 3.7 %collective-permute-start.18 = (f32[5,128]{1,0:T(8,128)S(1)}, f32[5,128]{1,0:T(8,128)S(1)}, u32[]{:S(2)}, u32[]{:S(2)}) collective-permute-start(f32[5,128]{1,0:T(8,128)S(1)} %stack.38), channel_id=1, source_target_pairs={{0,2},{1,3},{2,0},{3,1},{4,6},{5,7},{6,4},{7,5},{8,10},{9,11},{10,... | collective-permute-start | bytes 7688 | tf_op jit(solution)/shard_map/ppermute | solution.py:29
  72.1 9.3 %collective-permute-start.23 = (bf16[128,512]{1,0:T(8,128)(2,1)S(1)}, bf16[128,512]{1,0:T(8,128)(2,1)S(1)}, u32[]{:S(2)}, u32[]{:S(2)}) collective-permute-start(bf16[128,512]{1,0:T(8,128)(2,1)S(1)} %subtract_convert_fusion.refs_0_), channel_id=1, source_target_pairs={{0,8},{1,9},{2,10},{3,11},{4,12},{5,13},{6,14},{7,15},{8,16},{9,17... | collective-permute-start | bytes 393224 | tf_op jit(solution)/shard_map/ppermute | solution.py:29
  74.4 14.5 %collective-permute-start.24 = (bf16[128,512]{1,0:T(8,128)(2,1)S(1)}, bf16[128,512]{1,0:T(8,128)(2,1)S(1)}, u32[]{:S(2)}, u32[]{:S(2)}) collective-permute-start(bf16[128,512]{1,0:T(8,128)(2,1)S(1)} %subtract_convert_fusion.refs_0_), channel_id=1, source_target_pairs={{0,16},{1,17},{2,18},{3,19},{4,20},{5,21},{6,22},{7,23},{8,24},{9,... | collective-permute-start | bytes 393224 | tf_op jit(solution)/shard_map/ppermute | solution.py:29
  77.6 11.2 %collective-permute-start.25 = (bf16[128,512]{1,0:T(8,128)(2,1)S(1)}, bf16[128,512]{1,0:T(8,128)(2,1)S(1)}, u32[]{:S(2)}, u32[]{:S(2)}) collective-permute-start(bf16[128,512]{1,0:T(8,128)(2,1)S(1)} %subtract_convert_fusion.refs_0_), channel_id=1, source_target_pairs={{0,24},{1,25},{2,26},{3,27},{4,28},{5,29},{6,30},{7,31},{8,0},{9,1... | collective-permute-start | bytes 393224 | tf_op jit(solution)/shard_map/ppermute | solution.py:29
  94.8 9.2 %collective-permute-start.26 = (f32[8,128,256]{2,1,0:T(8,128)}, f32[8,128,256]{2,1,0:T(8,128)S(1)}, u32[]{:S(2)}, u32[]{:S(2)}) collective-permute-start(f32[8,128,256]{2,1,0:T(8,128)} %get-tuple-element.24), channel_id=1, source_target_pairs={{0,1},{1,0},{2,3},{3,2},{4,5},{5,4},{6,7},{7,6},{8,9},{9,8},{10,11... | collective-permute-start | bytes 3145736 | tf_op jit(solution)/shard_map/ppermute | solution.py:29
  95.0 6.1 %collective-permute-start.22 = (f32[1,128]{1,0:T(1,128)S(1)}, f32[1,128]{1,0:T(1,128)S(1)}, u32[]{:S(2)}, u32[]{:S(2)}) collective-permute-start(f32[1,128]{1,0:T(1,128)S(1)} %bitcast_multiply_fusion), channel_id=1, source_target_pairs={{0,132},{1,133},{2,134},{3,135},{4,128},{5,129},{6,130},{7,131},{8... | collective-permute-start | bytes 1544 | tf_op jit(solution)/shard_map/ppermute | solution.py:29
  95.1 6.0 %collective-permute-start.21 = (f32[1,128]{1,0:T(1,128)S(1)}, f32[1,128]{1,0:T(1,128)S(1)}, u32[]{:S(2)}, u32[]{:S(2)}) collective-permute-start(f32[1,128]{1,0:T(1,128)S(1)} %bitcast_multiply_fusion), channel_id=1, source_target_pairs={{0,128},{1,129},{2,130},{3,131},{4,132},{5,133},{6,134},{7,135},{8... | collective-permute-start | bytes 1544 | tf_op jit(solution)/shard_map/ppermute | solution.py:29
  99.0 5.1 %collective-permute-start.20 = (f32[1,128]{1,0:T(1,128)S(1)}, f32[1,128]{1,0:T(1,128)S(1)}, u32[]{:S(2)}, u32[]{:S(2)}) collective-permute-start(f32[1,128]{1,0:T(1,128)S(1)} %bitcast_multiply_fusion), channel_id=1, source_target_pairs={{0,4},{1,5},{2,6},{3,7},{4,0},{5,1},{6,2},{7,3},{8,12},{9,13},{10,... | collective-permute-start | bytes 1544 | tf_op jit(solution)/shard_map/ppermute | solution.py:29
  105.2 12.3 %collective-permute-start.29 = (bf16[2,128,256]{2,1,0:T(8,128)(2,1)S(1)}, bf16[2,128,256]{2,1,0:T(8,128)(2,1)S(1)}, u32[]{:S(2)}, u32[]{:S(2)}) collective-permute-start(bf16[2,128,256]{2,1,0:T(8,128)(2,1)S(1)} %get-tuple-element.45), channel_id=1, source_target_pairs={{0,6},{1,7},{2,0},{3,1},{4,2},{5,3},{6,4},{7,5},{8,14},{9,15},{10,... | collective-permute-start | bytes 393224 | tf_op jit(solution)/shard_map/ppermute | solution.py:29
  107.1 11.3 %collective-permute-start.28 = (bf16[2,128,256]{2,1,0:T(8,128)(2,1)S(1)}, bf16[2,128,256]{2,1,0:T(8,128)(2,1)S(1)}, u32[]{:S(2)}, u32[]{:S(2)}) collective-permute-start(bf16[2,128,256]{2,1,0:T(8,128)(2,1)S(1)} %get-tuple-element.46), channel_id=1, source_target_pairs={{0,4},{1,5},{2,6},{3,7},{4,0},{5,1},{6,2},{7,3},{8,12},{9,13},{10,... | collective-permute-start | bytes 393224 | tf_op jit(solution)/shard_map/ppermute | solution.py:29
  107.3 11.1 %collective-permute-start.27 = (bf16[2,128,256]{2,1,0:T(8,128)(2,1)S(1)}, bf16[2,128,256]{2,1,0:T(8,128)(2,1)S(1)}, u32[]{:S(2)}, u32[]{:S(2)}) collective-permute-start(bf16[2,128,256]{2,1,0:T(8,128)(2,1)S(1)} %get-tuple-element.44), channel_id=1, source_target_pairs={{0,2},{1,3},{2,4},{3,5},{4,6},{5,7},{6,0},{7,1},{8,10},{9,11},{10,... | collective-permute-start | bytes 393224 | tf_op jit(solution)/shard_map/ppermute | solution.py:29
  113.0 13.8 %collective-permute-start.34 = (bf16[256,512]{1,0:T(8,128)(2,1)}, bf16[256,512]{1,0:T(8,128)(2,1)S(1)}, u32[]{:S(2)}, u32[]{:S(2)}) collective-permute-start(bf16[256,512]{1,0:T(8,128)(2,1)} %get-tuple-element.30), channel_id=1, source_target_pairs={{0,32},{1,33},{2,34},{3,35},{4,36},{5,37},{6,38},{7,39},{8,40},{9,... | collective-permute-start | bytes 786440 | tf_op jit(solution)/shard_map/ppermute | solution.py:29
  114.6 13.0 %collective-permute-start.33 = (bf16[256,512]{1,0:T(8,128)(2,1)}, bf16[256,512]{1,0:T(8,128)(2,1)S(1)}, u32[]{:S(2)}, u32[]{:S(2)}) collective-permute-start(bf16[256,512]{1,0:T(8,128)(2,1)} %get-tuple-element.29), channel_id=1, source_target_pairs={{0,64},{1,65},{2,66},{3,67},{4,68},{5,69},{6,70},{7,71},{8,72},{9,... | collective-permute-start | bytes 786440 | tf_op jit(solution)/shard_map/ppermute | solution.py:29
  117.6 10.0 %collective-permute-start.32 = (bf16[256,512]{1,0:T(8,128)(2,1)}, bf16[256,512]{1,0:T(8,128)(2,1)S(1)}, u32[]{:S(2)}, u32[]{:S(2)}) collective-permute-start(bf16[256,512]{1,0:T(8,128)(2,1)} %get-tuple-element.28), channel_id=1, source_target_pairs={{0,96},{1,97},{2,98},{3,99},{4,100},{5,101},{6,102},{7,103},{8,104... | collective-permute-start | bytes 786440 | tf_op jit(solution)/shard_map/ppermute | solution.py:29
  119.5 10.0 %collective-permute-start.31 = (bf16[128,256]{1,0:T(8,128)(2,1)S(1)}, bf16[128,256]{1,0:T(8,128)(2,1)S(1)}, u32[]{:S(2)}, u32[]{:S(2)}) collective-permute-start(bf16[128,256]{1,0:T(8,128)(2,1)S(1)} %get-tuple-element.51), channel_id=1, source_target_pairs={{0,128},{1,136},{2,144},{3,152},{4,132},{5,140},{6,148},{7,156},{8... | collective-permute-start | bytes 196616 | tf_op jit(solution)/shard_map/ppermute | solution.py:29
  121.4 11.0 %collective-permute-start.30 = (bf16[128,256]{1,0:T(8,128)(2,1)S(1)}, bf16[128,256]{1,0:T(8,128)(2,1)S(1)}, u32[]{:S(2)}, u32[]{:S(2)}) collective-permute-start(bf16[128,256]{1,0:T(8,128)(2,1)S(1)} %get-tuple-element.50), channel_id=1, source_target_pairs={{0,0},{1,8},{2,16},{3,24},{4,4},{5,12},{6,20},{7,28},{8,1},{9,9},{... | collective-permute-start | bytes 196616 | tf_op jit(solution)/shard_map/ppermute | solution.py:29
  (15 other events, 104.7 us)

commit v5 on v4

--- a/solution.py
+++ b/solution.py
@@ -156,27 +156,28 @@
     own_refs, near_refs, far_refs, head_refs = refs[:4], refs[4:7], refs[7:10], refs[10:14]
     first_ref, out_ref, hidden_ref, head_ref, sems = refs[14:]
     core = index_ref[0] % 2
+
+    def spot(k, side, p):
+        return pl.ds(128 * k, 128), pl.ds(pl.multiple_of((2 * side + p) * 256, 256), 256)
+
     copies = loads(
-        [*head_refs, *near_refs, *far_refs],
-        [head_ref.at[j] for j in range(4)]
-        + [hidden_ref.at[k, pl.ds(2 * core, 2)] for k in (1, 2, 3)]
-        + [hidden_ref.at[k, pl.ds(2 * (1 - core), 2)] for k in (1, 2, 3)],
+        [*head_refs]
+        + [near_refs[k - 1].at[p] for k in (1, 2, 3) for p in range(2)]
+        + [far_refs[k - 1].at[p] for k in (1, 2, 3) for p in range(2)],
+        [head_ref.at[pl.ds(256 * j, 256)] for j in range(4)]
+        + [hidden_ref.at[spot(k, core, p)] for k in (1, 2, 3) for p in range(2)]
+        + [hidden_ref.at[spot(k, 1 - core, p)] for k in (1, 2, 3) for p in range(2)],
         sems,
     )
     for p in range(2):
-        hidden_ref[0, 2 * core + p] = own_refs[p][...]
-        hidden_ref[0, 2 * (1 - core) + p] = own_refs[2 + p][...]
+        hidden_ref[spot(0, core, p)] = own_refs[p][...]
+        hidden_ref[spot(0, 1 - core, p)] = own_refs[2 + p][...]
     for copy in copies:
         copy.wait()
-    for k in range(4):
-        total = None
-        for j in range(4):
-            term = jnp.dot(hidden_ref[k, j], head_ref[j], preferred_element_type=jnp.float32)
-            total = term if total is None else total + term
-        if k == 0:
-            first_ref[...] = total
-        else:
-            out_ref[k - 1] = total
+    scores = jnp.dot(hidden_ref[...], head_ref[...], preferred_element_type=jnp.float32)
+    first_ref[...] = scores[:128]
+    for k in (1, 2, 3):
+        out_ref[k - 1] = scores[128 * k : 128 * (k + 1)]
 
 
 def student_parts(index, own, near, far, head_slots):
@@ -190,74 +191,76 @@
             grid=(1,),
             in_specs=[hidden_block(0, p) for p in range(4)]
             + [ANYWHERE] * 10,
-            out_specs=(whole(128, 512), whole(3, 128, 512), whole(4, 4, 128, 256), whole(4, 256, 512)),
-            scratch_shapes=[pltpu.SemaphoreType.DMA((10,))],
+            out_specs=(whole(128, 512), whole(3, 128, 512), whole(512, 1024), whole(1024, 512)),
+            scratch_shapes=[pltpu.SemaphoreType.DMA((16,))],
         ),
         out_shape=(
             jax.ShapeDtypeStruct((128, 512), jnp.float32),
             jax.ShapeDtypeStruct((3, 128, 512), jnp.float32),
-            jax.ShapeDtypeStruct((4, 4, 128, 256), jnp.bfloat16),
-            jax.ShapeDtypeStruct((4, 256, 512), jnp.bfloat16),
+            jax.ShapeDtypeStruct((512, 1024), jnp.bfloat16),
+            jax.ShapeDtypeStruct((1024, 512), jnp.bfloat16),
         ),
         name="student",
     )(index, *[own] * 4, *near, *far, *head_slots)
 
 
-def head_grad_kernel(states_ref, slots_ref, own_ref, *out_refs):
-    for j in range(4):
-        total = None
-        for k in range(4):
-            term = lax.dot_general(
-                states_ref[k, j], slots_ref[k], (((0,), (0,)), ((), ())), preferred_element_type=jnp.float32
-            )
-            total = term if total is None else total + term
+def head_grad_kernel(hidden_ref, *refs):
+    grad_refs, own_ref, out_refs, slots_ref = refs[:4], refs[4], refs[5:8], refs[8]
+    for k in range(4):
+        slots_ref[128 * k : 128 * (k + 1)] = grad_refs[k][...]
+    for j in (1, 2, 3, 0):
+        total = lax.dot_general(
+            hidden_ref[:, 256 * j : 256 * (j + 1)],
+            slots_ref[...],
+            (((0,), (0,)), ((), ())),
+            preferred_element_type=jnp.float32,
+        )
         if j == 0:
             own_ref[...] = total
         else:
             out_refs[j - 1][...] = total.astype(jnp.bfloat16)
 
 
-def head_grad_parts(hidden, slots):
+def head_grad_parts(hidden, grad_slots):
     return pl.pallas_call(
         head_grad_kernel,
         out_shape=(
             jax.ShapeDtypeStruct((256, 512), jnp.float32),
             *[jax.ShapeDtypeStruct((256, 512), jnp.bfloat16)] * 3,
         ),
+        scratch_shapes=[pltpu.VMEM((512, 512), jnp.bfloat16)],
         name="head_grad",
-    )(hidden, slots)
+    )(hidden, *grad_slots)
 
 
 def hidden_grad_kernel(index_ref, *refs):
-    grad_refs, head_ref, own_ref, other_ref, slots_ref, sems = refs[:4], *refs[4:]
+    grad_refs, head_ref, own_ref, other_ref, slots_ref, sorted_ref = refs[:4], *refs[4:]
     zl, y, zh, x, core = coordinates(index_ref[0])
-    for copy in loads(grad_refs, [slots_ref.at[k] for k in range(4)], sems):
-        copy.wait()
+    for k in range(4):
+        slots_ref[k] = grad_refs[k][...]
+    goals = [2 * m + side for side in (core, 1 - core) for m in range(2)]
+    for i, goal in enumerate(goals):
+        sorted_ref[128 * i : 128 * (i + 1)] = slots_ref[(zh + 4 - goal) % 4]
     for j in range(4):
+        a = (y + 4 - j) % 4
+        terms = lax.dot_general(
+            sorted_ref[...],
+            head_ref[256 * j : 256 * (j + 1)],
+            (((1,), (1,)), ((), ())),
+            preferred_element_type=jnp.float32,
+        )
         for m in range(2):
-            a = (y + 4 - j) % 4
-            for out_ref, side in ((own_ref, core), (other_ref, 1 - core)):
-                goal = 2 * m + side
-                spot = (a % 2 * 2 + m + 4 - x) % 4 * 2 + (a // 2 + zl) % 2
-                out_ref[spot] = lax.dot_general(
-                    slots_ref[(zh + 4 - goal) % 4],
-                    head_ref[j],
-                    (((1,), (1,)), ((), ())),
-                    preferred_element_type=jnp.float32,
-                )
+            spot = (a % 2 * 2 + m + 4 - x) % 4 * 2 + (a // 2 + zl) % 2
+            own_ref[spot] = terms[128 * m : 128 * (m + 1)]
+            other_ref[spot] = terms[128 * (2 + m) : 128 * (3 + m)]
 
 
 def hidden_grad_parts(index, grad_slots, head):
     return pl.pallas_call(
         hidden_grad_kernel,
-        in_specs=[pl.BlockSpec(memory_space=pltpu.SMEM)]
-        + [ANYWHERE] * 4
-        + [pl.BlockSpec(memory_space=pltpu.VMEM)],
-        out_shape=(
-            *[jax.ShapeDtypeStruct((8, 128, 256), jnp.float32)] * 2,
-            jax.ShapeDtypeStruct((4, 128, 512), jnp.bfloat16),
-        ),
-        scratch_shapes=[pltpu.SemaphoreType.DMA((4,))],
+        in_specs=[pl.BlockSpec(memory_space=pltpu.SMEM)] + [pl.BlockSpec(memory_space=pltpu.VMEM)] * 5,
+        out_shape=(jax.ShapeDtypeStruct((8, 128, 256), jnp.float32),) * 2,
+        scratch_shapes=[pltpu.VMEM((4, 128, 512), jnp.bfloat16), pltpu.VMEM((512, 512), jnp.bfloat16)],
         name="hidden_grad",
     )(index, *grad_slots, head)
 
@@ -343,9 +346,9 @@
     )
 
     grad_slots = [score_grad] + [to_zh(score_grad, k) for k in (1, 2, 3)]
-    own, other, slots = hidden_grad_parts(index, grad_slots, head)
+    own, other = hidden_grad_parts(index, grad_slots, head)
     other = to_core(other)
-    head_grad, *parts = head_grad_parts(hidden, slots)
+    head_grad, *parts = head_grad_parts(hidden, grad_slots)
     for j in (1, 2, 3):
         head_grad = head_grad + to_y(parts[j - 1], -j).astype(f32)
     by_x = own[:2] + other[:2]

time: 135 us -> 133 us (0.985)
  Pallas kernels: 23.6 us -> 21.5 us
    pallas_call x1, Pallas kernels: 5.27 us -> 3.53 us  [hidden_grad_parts(): pl.pallas_call(hidden_grad_kernel, in_specs=[pl.BlockSpec(memory_space=pl...]
where the time goes in v5:
time: 133 us; the launch traced here: 131 us
  starting transfers between devices  67.2 us (51%)
  waiting for transfers between devices  28.7 us (22%)
  Pallas kernels  21.5 us (16%)
  other arithmetic  11.5 us (9%)
    ppermute x35, starting transfers between devices, send(): return lax.ppermute(value, ALL, pairs)  67.2 us
    ppermute x35, waiting for transfers between devices, send(): return lax.ppermute(value, ALL, pairs)  28.7 us
    pallas_call x2, Pallas kernels, teacher_parts(): pl.pallas_call(teacher_kernel, grid_spec=pltpu.PrefetchScalarGridSpec(num...  8.82 us
    pallas_call x1, Pallas kernels, student_parts(): pl.pallas_call(student_kernel, grid_spec=pltpu.PrefetchScalarGridSpec(num...  4.42 us
    pallas_call x1, Pallas kernels, hidden_grad_parts(): pl.pallas_call(hidden_grad_kernel, in_specs=[pl.BlockSpec(memory_space=pl...  3.53 us
    pallas_call x1, Pallas kernels, head_grad_parts(): pl.pallas_call(head_grad_kernel, out_shape=(jax.ShapeDtypeStruct((256, 51...  2.94 us
  transfers between devices with their start and end apart: 35, of which 13 were waited for; matrix products, arithmetic and copies ran while one was open for 7% of the time, Pallas kernels for 10%

profile of v5, /device:TPU:2, one launch (start us, length us, event | category | flops | bytes accessed | tf_op | source)
XLA Modules:
  0.0 130.8 jit_solution(11412685358003321417)
XLA Ops:
  0.6 4.5 %teacher.3 = f32[8,136,512]{2,1,0:T(8,128)} custom-call(s32[1]{0:T(128)} %bitcast.index_ref, bf16[128,512]{1,0:T(8,128)(2,1)} %hidden_ref.3, bf16[512]{0:T(512)(128)(2,1)} %gain_ref.3, bf16[512,8192]{1,0:T(8,128)(2,1)} %refs_3_.5, bf16[512,8192]{1,0:T(8,128)(2,1)} %refs_3_.5, bf16[512,8192]{1,0:T(8,128)(2,1)} %refs_3_.5, bf16[512,8192]{1,0:T(8,128)(2,1)} %refs_3_.5), custom_call_target="tpu_custom_call" | custom-call | tf_op jit(solution)/shard_map/teacher/pallas_call | solution.py:125
  5.1 1.8 %pick.1 = (bf16[2,128,256]{2,1,0:T(8,128)(2,1)}, bf16[2,128,256]{2,1,0:T(8,128)(2,1)}, bf16[2,128,256]{2,1,0:T(8,128)(2,1)}) custom-call(s32[1]{0:T(128)} %bitcast.index_ref, bf16[128,4096]{1,0:T(8,128)(2,1)} %refs_3_.7, bf16[128,4096]{1,0:T(8,128)(2,1)} %refs_3_.7, bf16[128,4096]{1,0:T(8,128)(2,1)} %refs_3_.7, bf16[128,4096]{1,0:T(8,128)(2,1)} %refs_3_.7, ...), custom_call_target="tpu_custom_call" | custom-call | tf_op jit(solution)/shard_map/pick/pallas_call | solution.py:72
  6.9 3.3 %collective-permute-start.5 = (bf16[2,128,256]{2,1,0:T(8,128)(2,1)}, bf16[2,128,256]{2,1,0:T(8,128)(2,1)S(1)}, u32[]{:S(2)}, u32[]{:S(2)}) collective-permute-start(bf16[2,128,256]{2,1,0:T(8,128)(2,1)} %get-tuple-element.16), channel_id=1, source_target_pairs={{0,8},{1,9},{2,10},{3,11},{4,12},{5,13},{6,14},{7,15},{8,16},{9,17... | collective-permute-start | bytes 393224 | tf_op jit(solution)/shard_map/ppermute | solution.py:29
  10.2 5.4 %collective-permute-start.6 = (bf16[2,128,256]{2,1,0:T(8,128)(2,1)}, bf16[2,128,256]{2,1,0:T(8,128)(2,1)S(1)}, u32[]{:S(2)}, u32[]{:S(2)}) collective-permute-start(bf16[2,128,256]{2,1,0:T(8,128)(2,1)} %get-tuple-element.17), channel_id=1, source_target_pairs={{0,16},{1,17},{2,18},{3,19},{4,20},{5,21},{6,22},{7,23},{8,24},{9,... | collective-permute-start | bytes 393224 | tf_op jit(solution)/shard_map/ppermute | solution.py:29
  15.6 2.7 %collective-permute-start.7 = (bf16[2,128,256]{2,1,0:T(8,128)(2,1)}, bf16[2,128,256]{2,1,0:T(8,128)(2,1)S(1)}, u32[]{:S(2)}, u32[]{:S(2)}) collective-permute-start(bf16[2,128,256]{2,1,0:T(8,128)(2,1)} %get-tuple-element.18), channel_id=1, source_target_pairs={{0,24},{1,25},{2,26},{3,27},{4,28},{5,29},{6,30},{7,31},{8,0},{9,1... | collective-permute-start | bytes 393224 | tf_op jit(solution)/shard_map/ppermute | solution.py:29
  19.9 4.3 %teacher.2 = f32[8,136,512]{2,1,0:T(8,128)} custom-call(s32[1]{0:T(128)} %bitcast.index_ref, bf16[128,512]{1,0:T(8,128)(2,1)} %hidden_ref.3, bf16[512]{0:T(512)(128)(2,1)} %gain_ref.3, bf16[512,8192]{1,0:T(8,128)(2,1)} %refs_3_.5, bf16[512,8192]{1,0:T(8,128)(2,1)} %refs_3_.5, bf16[512,8192]{1,0:T(8,128)(2,1)} %refs_3_.5, bf16[512,8192]{1,0:T(8,128)(2,1)} %refs_3_.5), custom_call_target="tpu_custom_call" | custom-call | tf_op jit(solution)/shard_map/teacher/pallas_call | solution.py:125
  25.5 3.2 %collective-permute-start.12 = (bf16[256,512]{1,0:T(8,128)(2,1)}, bf16[256,512]{1,0:T(8,128)(2,1)}, u32[]{:S(2)}, u32[]{:S(2)}) collective-permute-start(bf16[256,512]{1,0:T(8,128)(2,1)} %refs_10_.1), channel_id=1, source_target_pairs={{0,64},{1,65},{2,66},{3,67},{4,68},{5,69},{6,70},{7,71},{8,72},{9,... | collective-permute-start | bytes 786440 | tf_op jit(solution)/shard_map/ppermute | solution.py:29
  28.7 2.8 %collective-permute-start.13 = (bf16[256,512]{1,0:T(8,128)(2,1)}, bf16[256,512]{1,0:T(8,128)(2,1)}, u32[]{:S(2)}, u32[]{:S(2)}) collective-permute-start(bf16[256,512]{1,0:T(8,128)(2,1)} %refs_10_.1), channel_id=1, source_target_pairs={{0,96},{1,97},{2,98},{3,99},{4,100},{5,101},{6,102},{7,103},{8,104... | collective-permute-start | bytes 786440 | tf_op jit(solution)/shard_map/ppermute | solution.py:29
  32.1 2.5 %fusion.2 = (f16[2,136,512]{2,1,0:T(8,128)(2,1)S(1)}, f16[2,136,512]{2,1,0:T(8,128)(2,1)}, f16[2,136,512]{2,1,0:T(8,128)(2,1)S(1)}) fusion(f32[8,136,512]{2,1,0:T(8,128)S(1)} %collective-permute-done, f32[8,136,512]{2,1,0:T(8,128)} %teacher.2), kind=kLoop, calls=%fused_computation.5 | loop fusion | flops 835584 | bytes 4177920 | tf_op jit(solution)/shard_map/convert_element_type | solution.py:285
  35.2 2.5 %collective-permute-start.2 = (f16[2,136,512]{2,1,0:T(8,128)(2,1)S(1)}, f16[2,136,512]{2,1,0:T(8,128)(2,1)S(1)}, u32[]{:S(2)}, u32[]{:S(2)}) collective-permute-start(f16[2,136,512]{2,1,0:T(8,128)(2,1)S(1)} %get-tuple-element.41), channel_id=1, source_target_pairs={{0,4},{1,5},{2,6},{3,7},{4,0},{5,1},{6,2},{7,3},{8,12},{9,13},{10,... | collective-permute-start | bytes 835592 | tf_op jit(solution)/shard_map/ppermute | solution.py:29
  37.7 1.8 %collective-permute-start.1 = (f16[2,136,512]{2,1,0:T(8,128)(2,1)S(1)}, f16[2,136,512]{2,1,0:T(8,128)(2,1)}, u32[]{:S(2)}, u32[]{:S(2)}) collective-permute-start(f16[2,136,512]{2,1,0:T(8,128)(2,1)S(1)} %get-tuple-element.39), channel_id=1, source_target_pairs={{0,2},{1,3},{2,4},{3,5},{4,6},{5,7},{6,0},{7,1},{8,10},{9,11},{10,... | collective-permute-start | bytes 835592 | tf_op jit(solution)/shard_map/ppermute | solution.py:29
  40.9 4.4 %student.1 = (f32[128,512]{1,0:T(8,128)}, f32[3,128,512]{2,1,0:T(8,128)}, bf16[512,1024]{1,0:T(8,128)(2,1)}, bf16[1024,512]{1,0:T(8,128)(2,1)}) custom-call(s32[1]{0:T(128)} %bitcast.index_ref, bf16[128,4096]{1,0:T(8,128)(2,1)} %refs_3_.7, bf16[128,4096]{1,0:T(8,128)(2,1)} %refs_3_.7, bf16[128,4096]{1,0:T(8,128)(2,1)} %refs_3_.7, bf16[128,4096]{1,0:T(8,128)(2,1)} %refs_3_.7, ...), custom_call_target="tpu_custom_call" | custom-call | tf_op jit(solution)/shard_map/student/pallas_call | solution.py:187
  46.7 3.8 %collective-permute-start.16 = (f16[128,512]{1,0:T(8,128)(2,1)S(1)}, f16[128,512]{1,0:T(8,128)(2,1)S(1)}, u32[]{:S(2)}, u32[]{:S(2)}) collective-permute-start(f16[128,512]{1,0:T(8,128)(2,1)S(1)} %get-tuple-element.46), channel_id=1, source_target_pairs={{0,8},{1,9},{2,10},{3,11},{4,12},{5,13},{6,14},{7,15},{8,16},{9,17... | collective-permute-start | bytes 393224 | tf_op jit(solution)/shard_map/ppermute | solution.py:29
  50.5 4.3 %collective-permute-start.15 = (f16[128,512]{1,0:T(8,128)(2,1)S(1)}, f16[128,512]{1,0:T(8,128)(2,1)S(1)}, u32[]{:S(2)}, u32[]{:S(2)}) collective-permute-start(f16[128,512]{1,0:T(8,128)(2,1)S(1)} %get-tuple-element.47), channel_id=1, source_target_pairs={{0,16},{1,17},{2,18},{3,19},{4,20},{5,21},{6,22},{7,23},{8,24},{9,... | collective-permute-start | bytes 393224 | tf_op jit(solution)/shard_map/ppermute | solution.py:29
  54.8 3.9 %collective-permute-start.14 = (f16[128,512]{1,0:T(8,128)(2,1)S(1)}, f16[128,512]{1,0:T(8,128)(2,1)S(1)}, u32[]{:S(2)}, u32[]{:S(2)}) collective-permute-start(f16[128,512]{1,0:T(8,128)(2,1)S(1)} %get-tuple-element.45), channel_id=1, source_target_pairs={{0,24},{1,25},{2,26},{3,27},{4,28},{5,29},{6,30},{7,31},{8,0},{9,1... | collective-permute-start | bytes 393224 | tf_op jit(solution)/shard_map/ppermute | solution.py:29
  60.2 3.8 %collective-permute-done.15 = f16[128,512]{1,0:T(8,128)(2,1)S(1)} collective-permute-done((f16[128,512]{1,0:T(8,128)(2,1)S(1)}, f16[128,512]{1,0:T(8,128)(2,1)S(1)}, u32[]{:S(2)}, u32[]{:S(2)}) %collective-permute-start.15) | collective-permute-done | bytes 131104 | tf_op jit(solution)/shard_map/ppermute | solution.py:29
  64.0 2.1 %collective-permute-done.14 = f16[128,512]{1,0:T(8,128)(2,1)S(1)} collective-permute-done((f16[128,512]{1,0:T(8,128)(2,1)S(1)}, f16[128,512]{1,0:T(8,128)(2,1)S(1)}, u32[]{:S(2)}, u32[]{:S(2)}) %collective-permute-start.14) | collective-permute-done | bytes 131104 | tf_op jit(solution)/shard_map/ppermute | solution.py:29
  72.1 2.3 %collective-permute-start.23 = (bf16[128,512]{1,0:T(8,128)(2,1)S(1)}, bf16[128,512]{1,0:T(8,128)(2,1)S(1)}, u32[]{:S(2)}, u32[]{:S(2)}) collective-permute-start(bf16[128,512]{1,0:T(8,128)(2,1)S(1)} %subtract_convert_fusion.refs_0_), channel_id=1, source_target_pairs={{0,8},{1,9},{2,10},{3,11},{4,12},{5,13},{6,14},{7,15},{8,16},{9,17... | collective-permute-start | bytes 393224 | tf_op jit(solution)/shard_map/ppermute | solution.py:29
  74.4 3.2 %collective-permute-start.24 = (bf16[128,512]{1,0:T(8,128)(2,1)S(1)}, bf16[128,512]{1,0:T(8,128)(2,1)S(1)}, u32[]{:S(2)}, u32[]{:S(2)}) collective-permute-start(bf16[128,512]{1,0:T(8,128)(2,1)S(1)} %subtract_convert_fusion.refs_0_), channel_id=1, source_target_pairs={{0,16},{1,17},{2,18},{3,19},{4,20},{5,21},{6,22},{7,23},{8,24},{9,... | collective-permute-start | bytes 393224 | tf_op jit(solution)/shard_map/ppermute | solution.py:29
  79.1 2.3 %collective-permute-done.23.refs_1_ = bf16[128,512]{1,0:T(8,128)(2,1)S(1)} collective-permute-done((bf16[128,512]{1,0:T(8,128)(2,1)S(1)}, bf16[128,512]{1,0:T(8,128)(2,1)S(1)}, u32[]{:S(2)}, u32[]{:S(2)}) %collective-permute-start.23) | collective-permute-done | bytes 131104 | tf_op jit(solution)/shard_map/ppermute | solution.py:29
  81.4 7.4 %collective-permute-done.24.refs_2_ = bf16[128,512]{1,0:T(8,128)(2,1)S(1)} collective-permute-done((bf16[128,512]{1,0:T(8,128)(2,1)S(1)}, bf16[128,512]{1,0:T(8,128)(2,1)S(1)}, u32[]{:S(2)}, u32[]{:S(2)}) %collective-permute-start.24) | collective-permute-done | bytes 131104 | tf_op jit(solution)/shard_map/ppermute | solution.py:29
  89.6 3.5 %hidden_grad.1 = (f32[8,128,256]{2,1,0:T(8,128)}, f32[8,128,256]{2,1,0:T(8,128)}) custom-call(s32[1]{0:T(128)} %bitcast.index_ref, bf16[128,512]{1,0:T(8,128)(2,1)} %copy-done, bf16[128,512]{1,0:T(8,128)(2,1)} %copy-done.1, bf16[128,512]{1,0:T(8,128)(2,1)} %copy-done.2, bf16[128,512]{1,0:T(8,128)(2,1)} %copy-done.3, bf16[1024,512]{1,0:T(8,128)(2,1)} %get-tuple-element.21.refs_4_), custom_call_target="tpu_custom_call" | custom-call | tf_op jit(solution)/shard_map/hidden_grad/pallas_call | solution.py:259
  93.3 3.8 %collective-permute-start.21 = (f32[1,128]{1,0:T(1,128)S(1)}, f32[1,128]{1,0:T(1,128)S(1)}, u32[]{:S(2)}, u32[]{:S(2)}) collective-permute-start(f32[1,128]{1,0:T(1,128)S(1)} %bitcast_multiply_fusion), channel_id=1, source_target_pairs={{0,128},{1,129},{2,130},{3,131},{4,132},{5,133},{6,134},{7,135},{8... | collective-permute-start | bytes 1544 | tf_op jit(solution)/shard_map/ppermute | solution.py:29
  99.2 3.0 %collective-permute-done.20 = f32[1,128]{1,0:T(1,128)S(1)} collective-permute-done((f32[1,128]{1,0:T(1,128)S(1)}, f32[1,128]{1,0:T(1,128)S(1)}, u32[]{:S(2)}, u32[]{:S(2)}) %collective-permute-start.20) | collective-permute-done | bytes 544 | tf_op jit(solution)/shard_map/ppermute | solution.py:29
  103.4 1.9 %collective-permute-start.29 = (bf16[2,128,256]{2,1,0:T(8,128)(2,1)S(1)}, bf16[2,128,256]{2,1,0:T(8,128)(2,1)S(1)}, u32[]{:S(2)}, u32[]{:S(2)}) collective-permute-start(bf16[2,128,256]{2,1,0:T(8,128)(2,1)S(1)} %get-tuple-element.43), channel_id=1, source_target_pairs={{0,6},{1,7},{2,0},{3,1},{4,2},{5,3},{6,4},{7,5},{8,14},{9,15},{10,... | collective-permute-start | bytes 393224 | tf_op jit(solution)/shard_map/ppermute | solution.py:29
  105.5 1.8 %collective-permute-start.27 = (bf16[2,128,256]{2,1,0:T(8,128)(2,1)S(1)}, bf16[2,128,256]{2,1,0:T(8,128)(2,1)S(1)}, u32[]{:S(2)}, u32[]{:S(2)}) collective-permute-start(bf16[2,128,256]{2,1,0:T(8,128)(2,1)S(1)} %get-tuple-element.42), channel_id=1, source_target_pairs={{0,2},{1,3},{2,4},{3,5},{4,6},{5,7},{6,0},{7,1},{8,10},{9,11},{10,... | collective-permute-start | bytes 393224 | tf_op jit(solution)/shard_map/ppermute | solution.py:29
  107.9 2.9 %head_grad.1 = (f32[256,512]{1,0:T(8,128)}, bf16[256,512]{1,0:T(8,128)(2,1)}, bf16[256,512]{1,0:T(8,128)(2,1)}, bf16[256,512]{1,0:T(8,128)(2,1)}) custom-call(bf16[512,1024]{1,0:T(8,128)(2,1)} %get-tuple-element.24.hidden_ref, bf16[128,512]{1,0:T(8,128)(2,1)} %copy-done, bf16[128,512]{1,0:T(8,128)(2,1)} %copy-done.1, bf16[128,512]{1,0:T(8,128)(2,1)} %copy-done.2, ...), custom_call_target="tpu_custom_call" | custom-call | tf_op jit(solution)/shard_map/head_grad/pallas_call | solution.py:225
  112.4 3.0 %collective-permute-start.33 = (bf16[256,512]{1,0:T(8,128)(2,1)}, bf16[256,512]{1,0:T(8,128)(2,1)S(1)}, u32[]{:S(2)}, u32[]{:S(2)}) collective-permute-start(bf16[256,512]{1,0:T(8,128)(2,1)} %get-tuple-element.27), channel_id=1, source_target_pairs={{0,64},{1,65},{2,66},{3,67},{4,68},{5,69},{6,70},{7,71},{8,72},{9,... | collective-permute-start | bytes 786440 | tf_op jit(solution)/shard_map/ppermute | solution.py:29
  117.3 1.9 %collective-permute-start.31 = (bf16[128,256]{1,0:T(8,128)(2,1)S(1)}, bf16[128,256]{1,0:T(8,128)(2,1)S(1)}, u32[]{:S(2)}, u32[]{:S(2)}) collective-permute-start(bf16[128,256]{1,0:T(8,128)(2,1)S(1)} %get-tuple-element.49), channel_id=1, source_target_pairs={{0,128},{1,136},{2,144},{3,152},{4,132},{5,140},{6,148},{7,156},{8... | collective-permute-start | bytes 196616 | tf_op jit(solution)/shard_map/ppermute | solution.py:29
  119.1 5.5 %collective-permute-start.30 = (bf16[128,256]{1,0:T(8,128)(2,1)S(1)}, bf16[128,256]{1,0:T(8,128)(2,1)S(1)}, u32[]{:S(2)}, u32[]{:S(2)}) collective-permute-start(bf16[128,256]{1,0:T(8,128)(2,1)S(1)} %get-tuple-element.48), channel_id=1, source_target_pairs={{0,0},{1,8},{2,16},{3,24},{4,4},{5,12},{6,20},{7,28},{8,1},{9,9},{... | collective-permute-start | bytes 196616 | tf_op jit(solution)/shard_map/ppermute | solution.py:29
  125.3 2.0 %convert_add_fusion = f32[256,512]{1,0:T(8,128)} fusion(bf16[256,512]{1,0:T(8,128)(2,1)S(1)} %collective-permute-done.34, bf16[256,512]{1,0:T(8,128)(2,1)S(1)} %collective-permute-done.33, f32[256,512]{1,0:T(8,128)} %get-tuple-element.25, bf16[256,512]{1,0:T(8,128)(2,1)S(1)} %collective-permute-done.32), kind=kLoop, calls=%fused_computation.10 | loop fusion | flops 786432 | bytes 1835008 | tf_op jit(solution)/shard_map/add | solution.py:353
  127.3 2.8 %collective-permute-done.30 = bf16[128,256]{1,0:T(8,128)(2,1)S(1)} collective-permute-done((bf16[128,256]{1,0:T(8,128)(2,1)S(1)}, bf16[128,256]{1,0:T(8,128)(2,1)S(1)}, u32[]{:S(2)}, u32[]{:S(2)}) %collective-permute-start.30) | collective-permute-done | bytes 65568 | tf_op jit(solution)/shard_map/ppermute | solution.py:29
  (99 shorter events, 25.5 us)
Async XLA Ops:
  5.1 26.4 %collective-permute-start = (f32[8,136,512]{2,1,0:T(8,128)}, f32[8,136,512]{2,1,0:T(8,128)S(1)}, u32[]{:S(2)}, u32[]{:S(2)}) collective-permute-start(f32[8,136,512]{2,1,0:T(8,128)} %teacher.3), channel_id=1, source_target_pairs={{0,1},{1,0},{2,3},{3,2},{4,5},{5,4},{6,7},{7,6},{8,9},{9,8},{10,11... | collective-permute-start | bytes 6684680 | tf_op jit(solution)/shard_map/ppermute | solution.py:29
  6.9 11.3 %collective-permute-start.5 = (bf16[2,128,256]{2,1,0:T(8,128)(2,1)}, bf16[2,128,256]{2,1,0:T(8,128)(2,1)S(1)}, u32[]{:S(2)}, u32[]{:S(2)}) collective-permute-start(bf16[2,128,256]{2,1,0:T(8,128)(2,1)} %get-tuple-element.16), channel_id=1, source_target_pairs={{0,8},{1,9},{2,10},{3,11},{4,12},{5,13},{6,14},{7,15},{8,16},{9,17... | collective-permute-start | bytes 393224 | tf_op jit(solution)/shard_map/ppermute | solution.py:29
  10.2 15.3 %collective-permute-start.6 = (bf16[2,128,256]{2,1,0:T(8,128)(2,1)}, bf16[2,128,256]{2,1,0:T(8,128)(2,1)S(1)}, u32[]{:S(2)}, u32[]{:S(2)}) collective-permute-start(bf16[2,128,256]{2,1,0:T(8,128)(2,1)} %get-tuple-element.17), channel_id=1, source_target_pairs={{0,16},{1,17},{2,18},{3,19},{4,20},{5,21},{6,22},{7,23},{8,24},{9,... | collective-permute-start | bytes 393224 | tf_op jit(solution)/shard_map/ppermute | solution.py:29
  15.6 13.1 %collective-permute-start.7 = (bf16[2,128,256]{2,1,0:T(8,128)(2,1)}, bf16[2,128,256]{2,1,0:T(8,128)(2,1)S(1)}, u32[]{:S(2)}, u32[]{:S(2)}) collective-permute-start(bf16[2,128,256]{2,1,0:T(8,128)(2,1)} %get-tuple-element.18), channel_id=1, source_target_pairs={{0,24},{1,25},{2,26},{3,27},{4,28},{5,29},{6,30},{7,31},{8,0},{9,1... | collective-permute-start | bytes 393224 | tf_op jit(solution)/shard_map/ppermute | solution.py:29
  18.3 13.3 %collective-permute-start.8 = (bf16[2,128,256]{2,1,0:T(8,128)(2,1)S(1)}, bf16[2,128,256]{2,1,0:T(8,128)(2,1)S(1)}, u32[]{:S(2)}, u32[]{:S(2)}) collective-permute-start(bf16[2,128,256]{2,1,0:T(8,128)(2,1)S(1)} %collective-permute-done.5.refs_4_), channel_id=1, source_target_pairs={{0,1},{1,0},{2,3},{3,2},{4,5},{5,4},{6,7},{7,6},{8,9},{9,8},{10,11... | collective-permute-start | bytes 393224 | tf_op jit(solution)/shard_map/ppermute | solution.py:29
  18.3 19.5 %collective-permute-start.11 = (bf16[256,512]{1,0:T(8,128)(2,1)}, bf16[256,512]{1,0:T(8,128)(2,1)}, u32[]{:S(2)}, u32[]{:S(2)}) collective-permute-start(bf16[256,512]{1,0:T(8,128)(2,1)} %refs_10_.1), channel_id=1, source_target_pairs={{0,32},{1,33},{2,34},{3,35},{4,36},{5,37},{6,38},{7,39},{8,40},{9,... | collective-permute-start | bytes 786440 | tf_op jit(solution)/shard_map/ppermute | solution.py:29
  25.5 14.0 %collective-permute-start.12 = (bf16[256,512]{1,0:T(8,128)(2,1)}, bf16[256,512]{1,0:T(8,128)(2,1)}, u32[]{:S(2)}, u32[]{:S(2)}) collective-permute-start(bf16[256,512]{1,0:T(8,128)(2,1)} %refs_10_.1), channel_id=1, source_target_pairs={{0,64},{1,65},{2,66},{3,67},{4,68},{5,69},{6,70},{7,71},{8,72},{9,... | collective-permute-start | bytes 786440 | tf_op jit(solution)/shard_map/ppermute | solution.py:29
  28.7 12.2 %collective-permute-start.13 = (bf16[256,512]{1,0:T(8,128)(2,1)}, bf16[256,512]{1,0:T(8,128)(2,1)}, u32[]{:S(2)}, u32[]{:S(2)}) collective-permute-start(bf16[256,512]{1,0:T(8,128)(2,1)} %refs_10_.1), channel_id=1, source_target_pairs={{0,96},{1,97},{2,98},{3,99},{4,100},{5,101},{6,102},{7,103},{8,104... | collective-permute-start | bytes 786440 | tf_op jit(solution)/shard_map/ppermute | solution.py:29
  31.6 3.6 %collective-permute-start.10 = (bf16[2,128,256]{2,1,0:T(8,128)(2,1)S(1)}, bf16[2,128,256]{2,1,0:T(8,128)(2,1)S(1)}, u32[]{:S(2)}, u32[]{:S(2)}) collective-permute-start(bf16[2,128,256]{2,1,0:T(8,128)(2,1)S(1)} %collective-permute-done.7.refs_6_), channel_id=1, source_target_pairs={{0,1},{1,0},{2,3},{3,2},{4,5},{5,4},{6,7},{7,6},{8,9},{9,8},{10,11... | collective-permute-start | bytes 393224 | tf_op jit(solution)/shard_map/ppermute | solution.py:29
  34.6 20.2 %collective-permute-start.3 = (f16[2,136,512]{2,1,0:T(8,128)(2,1)}, f16[2,136,512]{2,1,0:T(8,128)(2,1)S(1)}, u32[]{:S(2)}, u32[]{:S(2)}) collective-permute-start(f16[2,136,512]{2,1,0:T(8,128)(2,1)} %get-tuple-element.40), channel_id=1, source_target_pairs={{0,6},{1,7},{2,0},{3,1},{4,2},{5,3},{6,4},{7,5},{8,14},{9,15},{10,... | collective-permute-start | bytes 835592 | tf_op jit(solution)/shard_map/ppermute | solution.py:29
  35.2 23.5 %collective-permute-start.2 = (f16[2,136,512]{2,1,0:T(8,128)(2,1)S(1)}, f16[2,136,512]{2,1,0:T(8,128)(2,1)S(1)}, u32[]{:S(2)}, u32[]{:S(2)}) collective-permute-start(f16[2,136,512]{2,1,0:T(8,128)(2,1)S(1)} %get-tuple-element.41), channel_id=1, source_target_pairs={{0,4},{1,5},{2,6},{3,7},{4,0},{5,1},{6,2},{7,3},{8,12},{9,13},{10,... | collective-permute-start | bytes 835592 | tf_op jit(solution)/shard_map/ppermute | solution.py:29
  37.7 21.0 %collective-permute-start.1 = (f16[2,136,512]{2,1,0:T(8,128)(2,1)S(1)}, f16[2,136,512]{2,1,0:T(8,128)(2,1)}, u32[]{:S(2)}, u32[]{:S(2)}) collective-permute-start(f16[2,136,512]{2,1,0:T(8,128)(2,1)S(1)} %get-tuple-element.39), channel_id=1, source_target_pairs={{0,2},{1,3},{2,4},{3,5},{4,6},{5,7},{6,0},{7,1},{8,10},{9,11},{10,... | collective-permute-start | bytes 835592 | tf_op jit(solution)/shard_map/ppermute | solution.py:29
  46.7 13.5 %collective-permute-start.16 = (f16[128,512]{1,0:T(8,128)(2,1)S(1)}, f16[128,512]{1,0:T(8,128)(2,1)S(1)}, u32[]{:S(2)}, u32[]{:S(2)}) collective-permute-start(f16[128,512]{1,0:T(8,128)(2,1)S(1)} %get-tuple-element.46), channel_id=1, source_target_pairs={{0,8},{1,9},{2,10},{3,11},{4,12},{5,13},{6,14},{7,15},{8,16},{9,17... | collective-permute-start | bytes 393224 | tf_op jit(solution)/shard_map/ppermute | solution.py:29
  50.5 13.5 %collective-permute-start.15 = (f16[128,512]{1,0:T(8,128)(2,1)S(1)}, f16[128,512]{1,0:T(8,128)(2,1)S(1)}, u32[]{:S(2)}, u32[]{:S(2)}) collective-permute-start(f16[128,512]{1,0:T(8,128)(2,1)S(1)} %get-tuple-element.47), channel_id=1, source_target_pairs={{0,16},{1,17},{2,18},{3,19},{4,20},{5,21},{6,22},{7,23},{8,24},{9,... | collective-permute-start | bytes 393224 | tf_op jit(solution)/shard_map/ppermute | solution.py:29
  54.8 11.3 %collective-permute-start.14 = (f16[128,512]{1,0:T(8,128)(2,1)S(1)}, f16[128,512]{1,0:T(8,128)(2,1)S(1)}, u32[]{:S(2)}, u32[]{:S(2)}) collective-permute-start(f16[128,512]{1,0:T(8,128)(2,1)S(1)} %get-tuple-element.45), channel_id=1, source_target_pairs={{0,24},{1,25},{2,26},{3,27},{4,28},{5,29},{6,30},{7,31},{8,0},{9,1... | collective-permute-start | bytes 393224 | tf_op jit(solution)/shard_map/ppermute | solution.py:29
  60.0 7.4 %collective-permute-start.4 = (f16[136,512]{1,0:T(8,128)(2,1)S(1)}, f16[136,512]{1,0:T(8,128)(2,1)S(1)}, u32[]{:S(2)}, u32[]{:S(2)}) collective-permute-start(f16[136,512]{1,0:T(8,128)(2,1)S(1)} %fusion.17), channel_id=1, source_target_pairs={{0,128},{1,129},{2,130},{3,131},{4,132},{5,133},{6,134},{7,135},{8... | collective-permute-start | bytes 417800 | tf_op jit(solution)/shard_map/ppermute | solution.py:29
  68.1 3.7 %collective-permute-start.18 = (f32[5,128]{1,0:T(8,128)S(1)}, f32[5,128]{1,0:T(8,128)S(1)}, u32[]{:S(2)}, u32[]{:S(2)}) collective-permute-start(f32[5,128]{1,0:T(8,128)S(1)} %stack.38), channel_id=1, source_target_pairs={{0,2},{1,3},{2,0},{3,1},{4,6},{5,7},{6,4},{7,5},{8,10},{9,11},{10,... | collective-permute-start | bytes 7688 | tf_op jit(solution)/shard_map/ppermute | solution.py:29
  72.1 9.3 %collective-permute-start.23 = (bf16[128,512]{1,0:T(8,128)(2,1)S(1)}, bf16[128,512]{1,0:T(8,128)(2,1)S(1)}, u32[]{:S(2)}, u32[]{:S(2)}) collective-permute-start(bf16[128,512]{1,0:T(8,128)(2,1)S(1)} %subtract_convert_fusion.refs_0_), channel_id=1, source_target_pairs={{0,8},{1,9},{2,10},{3,11},{4,12},{5,13},{6,14},{7,15},{8,16},{9,17... | collective-permute-start | bytes 393224 | tf_op jit(solution)/shard_map/ppermute | solution.py:29
  74.4 14.4 %collective-permute-start.24 = (bf16[128,512]{1,0:T(8,128)(2,1)S(1)}, bf16[128,512]{1,0:T(8,128)(2,1)S(1)}, u32[]{:S(2)}, u32[]{:S(2)}) collective-permute-start(bf16[128,512]{1,0:T(8,128)(2,1)S(1)} %subtract_convert_fusion.refs_0_), channel_id=1, source_target_pairs={{0,16},{1,17},{2,18},{3,19},{4,20},{5,21},{6,22},{7,23},{8,24},{9,... | collective-permute-start | bytes 393224 | tf_op jit(solution)/shard_map/ppermute | solution.py:29
  77.6 11.2 %collective-permute-start.25 = (bf16[128,512]{1,0:T(8,128)(2,1)S(1)}, bf16[128,512]{1,0:T(8,128)(2,1)S(1)}, u32[]{:S(2)}, u32[]{:S(2)}) collective-permute-start(bf16[128,512]{1,0:T(8,128)(2,1)S(1)} %subtract_convert_fusion.refs_0_), channel_id=1, source_target_pairs={{0,24},{1,25},{2,26},{3,27},{4,28},{5,29},{6,30},{7,31},{8,0},{9,1... | collective-permute-start | bytes 393224 | tf_op jit(solution)/shard_map/ppermute | solution.py:29
  93.1 9.1 %collective-permute-start.26 = (f32[8,128,256]{2,1,0:T(8,128)}, f32[8,128,256]{2,1,0:T(8,128)S(1)}, u32[]{:S(2)}, u32[]{:S(2)}) collective-permute-start(f32[8,128,256]{2,1,0:T(8,128)} %get-tuple-element.23), channel_id=1, source_target_pairs={{0,1},{1,0},{2,3},{3,2},{4,5},{5,4},{6,7},{7,6},{8,9},{9,8},{10,11... | collective-permute-start | bytes 3145736 | tf_op jit(solution)/shard_map/ppermute | solution.py:29
  93.2 6.1 %collective-permute-start.22 = (f32[1,128]{1,0:T(1,128)S(1)}, f32[1,128]{1,0:T(1,128)S(1)}, u32[]{:S(2)}, u32[]{:S(2)}) collective-permute-start(f32[1,128]{1,0:T(1,128)S(1)} %bitcast_multiply_fusion), channel_id=1, source_target_pairs={{0,132},{1,133},{2,134},{3,135},{4,128},{5,129},{6,130},{7,131},{8... | collective-permute-start | bytes 1544 | tf_op jit(solution)/shard_map/ppermute | solution.py:29
  93.3 6.0 %collective-permute-start.21 = (f32[1,128]{1,0:T(1,128)S(1)}, f32[1,128]{1,0:T(1,128)S(1)}, u32[]{:S(2)}, u32[]{:S(2)}) collective-permute-start(f32[1,128]{1,0:T(1,128)S(1)} %bitcast_multiply_fusion), channel_id=1, source_target_pairs={{0,128},{1,129},{2,130},{3,131},{4,132},{5,133},{6,134},{7,135},{8... | collective-permute-start | bytes 1544 | tf_op jit(solution)/shard_map/ppermute | solution.py:29
  97.1 5.1 %collective-permute-start.20 = (f32[1,128]{1,0:T(1,128)S(1)}, f32[1,128]{1,0:T(1,128)S(1)}, u32[]{:S(2)}, u32[]{:S(2)}) collective-permute-start(f32[1,128]{1,0:T(1,128)S(1)} %bitcast_multiply_fusion), channel_id=1, source_target_pairs={{0,4},{1,5},{2,6},{3,7},{4,0},{5,1},{6,2},{7,3},{8,12},{9,13},{10,... | collective-permute-start | bytes 1544 | tf_op jit(solution)/shard_map/ppermute | solution.py:29
  103.4 11.9 %collective-permute-start.29 = (bf16[2,128,256]{2,1,0:T(8,128)(2,1)S(1)}, bf16[2,128,256]{2,1,0:T(8,128)(2,1)S(1)}, u32[]{:S(2)}, u32[]{:S(2)}) collective-permute-start(bf16[2,128,256]{2,1,0:T(8,128)(2,1)S(1)} %get-tuple-element.43), channel_id=1, source_target_pairs={{0,6},{1,7},{2,0},{3,1},{4,2},{5,3},{6,4},{7,5},{8,14},{9,15},{10,... | collective-permute-start | bytes 393224 | tf_op jit(solution)/shard_map/ppermute | solution.py:29
  105.3 10.9 %collective-permute-start.28 = (bf16[2,128,256]{2,1,0:T(8,128)(2,1)S(1)}, bf16[2,128,256]{2,1,0:T(8,128)(2,1)S(1)}, u32[]{:S(2)}, u32[]{:S(2)}) collective-permute-start(bf16[2,128,256]{2,1,0:T(8,128)(2,1)S(1)} %get-tuple-element.44), channel_id=1, source_target_pairs={{0,4},{1,5},{2,6},{3,7},{4,0},{5,1},{6,2},{7,3},{8,12},{9,13},{10,... | collective-permute-start | bytes 393224 | tf_op jit(solution)/shard_map/ppermute | solution.py:29
  105.5 10.8 %collective-permute-start.27 = (bf16[2,128,256]{2,1,0:T(8,128)(2,1)S(1)}, bf16[2,128,256]{2,1,0:T(8,128)(2,1)S(1)}, u32[]{:S(2)}, u32[]{:S(2)}) collective-permute-start(bf16[2,128,256]{2,1,0:T(8,128)(2,1)S(1)} %get-tuple-element.42), channel_id=1, source_target_pairs={{0,2},{1,3},{2,4},{3,5},{4,6},{5,7},{6,0},{7,1},{8,10},{9,11},{10,... | collective-permute-start | bytes 393224 | tf_op jit(solution)/shard_map/ppermute | solution.py:29
  110.8 13.8 %collective-permute-start.34 = (bf16[256,512]{1,0:T(8,128)(2,1)}, bf16[256,512]{1,0:T(8,128)(2,1)S(1)}, u32[]{:S(2)}, u32[]{:S(2)}) collective-permute-start(bf16[256,512]{1,0:T(8,128)(2,1)} %get-tuple-element.28), channel_id=1, source_target_pairs={{0,32},{1,33},{2,34},{3,35},{4,36},{5,37},{6,38},{7,39},{8,40},{9,... | collective-permute-start | bytes 786440 | tf_op jit(solution)/shard_map/ppermute | solution.py:29
  112.4 13.0 %collective-permute-start.33 = (bf16[256,512]{1,0:T(8,128)(2,1)}, bf16[256,512]{1,0:T(8,128)(2,1)S(1)}, u32[]{:S(2)}, u32[]{:S(2)}) collective-permute-start(bf16[256,512]{1,0:T(8,128)(2,1)} %get-tuple-element.27), channel_id=1, source_target_pairs={{0,64},{1,65},{2,66},{3,67},{4,68},{5,69},{6,70},{7,71},{8,72},{9,... | collective-permute-start | bytes 786440 | tf_op jit(solution)/shard_map/ppermute | solution.py:29
  115.4 10.0 %collective-permute-start.32 = (bf16[256,512]{1,0:T(8,128)(2,1)}, bf16[256,512]{1,0:T(8,128)(2,1)S(1)}, u32[]{:S(2)}, u32[]{:S(2)}) collective-permute-start(bf16[256,512]{1,0:T(8,128)(2,1)} %get-tuple-element.26), channel_id=1, source_target_pairs={{0,96},{1,97},{2,98},{3,99},{4,100},{5,101},{6,102},{7,103},{8,104... | collective-permute-start | bytes 786440 | tf_op jit(solution)/shard_map/ppermute | solution.py:29
  117.3 10.0 %collective-permute-start.31 = (bf16[128,256]{1,0:T(8,128)(2,1)S(1)}, bf16[128,256]{1,0:T(8,128)(2,1)S(1)}, u32[]{:S(2)}, u32[]{:S(2)}) collective-permute-start(bf16[128,256]{1,0:T(8,128)(2,1)S(1)} %get-tuple-element.49), channel_id=1, source_target_pairs={{0,128},{1,136},{2,144},{3,152},{4,132},{5,140},{6,148},{7,156},{8... | collective-permute-start | bytes 196616 | tf_op jit(solution)/shard_map/ppermute | solution.py:29
  119.1 11.0 %collective-permute-start.30 = (bf16[128,256]{1,0:T(8,128)(2,1)S(1)}, bf16[128,256]{1,0:T(8,128)(2,1)S(1)}, u32[]{:S(2)}, u32[]{:S(2)}) collective-permute-start(bf16[128,256]{1,0:T(8,128)(2,1)S(1)} %get-tuple-element.48), channel_id=1, source_target_pairs={{0,0},{1,8},{2,16},{3,24},{4,4},{5,12},{6,20},{7,28},{8,1},{9,9},{... | collective-permute-start | bytes 196616 | tf_op jit(solution)/shard_map/ppermute | solution.py:29
  (15 other events, 104.7 us)

commit v6 on v5

--- a/solution.py
+++ b/solution.py
@@ -154,7 +154,7 @@
 
 def student_kernel(index_ref, *refs):
     own_refs, near_refs, far_refs, head_refs = refs[:4], refs[4:7], refs[7:10], refs[10:14]
-    first_ref, out_ref, hidden_ref, head_ref, sems = refs[14:]
+    first_ref, out_ref, hidden_out, head_out, hidden_ref, head_ref, sems = refs[14:]
     core = index_ref[0] % 2
 
     def spot(k, side, p):
@@ -174,10 +174,13 @@
         hidden_ref[spot(0, 1 - core, p)] = own_refs[2 + p][...]
     for copy in copies:
         copy.wait()
+    copies = loads([hidden_ref, head_ref], [hidden_out, head_out], sems)
     scores = jnp.dot(hidden_ref[...], head_ref[...], preferred_element_type=jnp.float32)
     first_ref[...] = scores[:128]
     for k in (1, 2, 3):
         out_ref[k - 1] = scores[128 * k : 128 * (k + 1)]
+    for copy in copies:
+        copy.wait()
 
 
 def student_parts(index, own, near, far, head_slots):
@@ -191,8 +194,12 @@
             grid=(1,),
             in_specs=[hidden_block(0, p) for p in range(4)]
             + [ANYWHERE] * 10,
-            out_specs=(whole(128, 512), whole(3, 128, 512), whole(512, 1024), whole(1024, 512)),
-            scratch_shapes=[pltpu.SemaphoreType.DMA((16,))],
+            out_specs=(whole(128, 512), whole(3, 128, 512), ANYWHERE, ANYWHERE),
+            scratch_shapes=[
+                pltpu.VMEM((512, 1024), jnp.bfloat16),
+                pltpu.VMEM((1024, 512), jnp.bfloat16),
+                pltpu.SemaphoreType.DMA((16,)),
+            ],
         ),
         out_shape=(
             jax.ShapeDtypeStruct((128, 512), jnp.float32),
@@ -204,63 +211,102 @@
     )(index, *[own] * 4, *near, *far, *head_slots)
 
 
-def head_grad_kernel(hidden_ref, *refs):
-    grad_refs, own_ref, out_refs, slots_ref = refs[:4], refs[4], refs[5:8], refs[8]
+def head_grad_kernel(hidden_hbm, *refs):
+    grad_refs, out_refs = refs[:4], refs[4:8]
+    slots_ref, hidden_ref, own_ref, other_ref, in_sems, out_sems = refs[8:]
+    order = (1, 2, 3, 0)
+    copies = loads(
+        [hidden_hbm.at[:, pl.ds(256 * j, 256)] for j in order], [hidden_ref.at[i] for i in range(4)], in_sems
+    )
     for k in range(4):
         slots_ref[128 * k : 128 * (k + 1)] = grad_refs[k][...]
-    for j in (1, 2, 3, 0):
+    results = []
+    for i, j in enumerate(order):
+        copies[i].wait()
         total = lax.dot_general(
-            hidden_ref[:, 256 * j : 256 * (j + 1)],
-            slots_ref[...],
-            (((0,), (0,)), ((), ())),
-            preferred_element_type=jnp.float32,
+            hidden_ref[i], slots_ref[...], (((0,), (0,)), ((), ())), preferred_element_type=jnp.float32
         )
         if j == 0:
             own_ref[...] = total
+            result = pltpu.make_async_copy(own_ref, out_refs[0], out_sems.at[0])
         else:
-            out_refs[j - 1][...] = total.astype(jnp.bfloat16)
+            other_ref[j - 1] = total.astype(jnp.bfloat16)
+            result = pltpu.make_async_copy(other_ref.at[j - 1], out_refs[j], out_sems.at[j])
+        result.start()
+        results.append(result)
+    for result in results:
+        result.wait()
 
 
 def head_grad_parts(hidden, grad_slots):
     return pl.pallas_call(
         head_grad_kernel,
+        in_specs=[ANYWHERE] + [pl.BlockSpec(memory_space=pltpu.VMEM)] * 4,
+        out_specs=[ANYWHERE] * 4,
         out_shape=(
             jax.ShapeDtypeStruct((256, 512), jnp.float32),
             *[jax.ShapeDtypeStruct((256, 512), jnp.bfloat16)] * 3,
         ),
-        scratch_shapes=[pltpu.VMEM((512, 512), jnp.bfloat16)],
+        scratch_shapes=[
+            pltpu.VMEM((512, 512), jnp.bfloat16),
+            pltpu.VMEM((4, 512, 256), jnp.bfloat16),
+            pltpu.VMEM((256, 512), jnp.float32),
+            pltpu.VMEM((3, 256, 512), jnp.bfloat16),
+            pltpu.SemaphoreType.DMA((4,)),
+            pltpu.SemaphoreType.DMA((4,)),
+        ],
         name="head_grad",
     )(hidden, *grad_slots)
 
 
 def hidden_grad_kernel(index_ref, *refs):
-    grad_refs, head_ref, own_ref, other_ref, slots_ref, sorted_ref = refs[:4], *refs[4:]
+    grad_refs, head_hbm, own_out, other_out = refs[:4], *refs[4:7]
+    slots_ref, sorted_ref, head_ref, own_ref, other_ref, in_sems, out_sems = refs[7:]
     zl, y, zh, x, core = coordinates(index_ref[0])
+    copies = loads(
+        [head_hbm.at[pl.ds(256 * j, 256)] for j in range(4)], [head_ref.at[j] for j in range(4)], in_sems
+    )
     for k in range(4):
         slots_ref[k] = grad_refs[k][...]
     goals = [2 * m + side for side in (core, 1 - core) for m in range(2)]
     for i, goal in enumerate(goals):
         sorted_ref[128 * i : 128 * (i + 1)] = slots_ref[(zh + 4 - goal) % 4]
+    results = []
     for j in range(4):
         a = (y + 4 - j) % 4
+        copies[j].wait()
         terms = lax.dot_general(
-            sorted_ref[...],
-            head_ref[256 * j : 256 * (j + 1)],
-            (((1,), (1,)), ((), ())),
-            preferred_element_type=jnp.float32,
+            sorted_ref[...], head_ref[j], (((1,), (1,)), ((), ())), preferred_element_type=jnp.float32
         )
         for m in range(2):
+            own_ref[j, m] = terms[128 * m : 128 * (m + 1)]
+            other_ref[j, m] = terms[128 * (2 + m) : 128 * (3 + m)]
             spot = (a % 2 * 2 + m + 4 - x) % 4 * 2 + (a // 2 + zl) % 2
-            own_ref[spot] = terms[128 * m : 128 * (m + 1)]
-            other_ref[spot] = terms[128 * (2 + m) : 128 * (3 + m)]
+            for n, (part, out) in enumerate(((own_ref, own_out), (other_ref, other_out))):
+                result = pltpu.make_async_copy(part.at[j, m], out.at[spot], out_sems.at[4 * j + 2 * m + n])
+                result.start()
+                results.append(result)
+    for result in results:
+        result.wait()
 
 
 def hidden_grad_parts(index, grad_slots, head):
     return pl.pallas_call(
         hidden_grad_kernel,
-        in_specs=[pl.BlockSpec(memory_space=pltpu.SMEM)] + [pl.BlockSpec(memory_space=pltpu.VMEM)] * 5,
+        in_specs=[pl.BlockSpec(memory_space=pltpu.SMEM)]
+        + [pl.BlockSpec(memory_space=pltpu.VMEM)] * 4
+        + [ANYWHERE],
+        out_specs=[ANYWHERE] * 2,
         out_shape=(jax.ShapeDtypeStruct((8, 128, 256), jnp.float32),) * 2,
-        scratch_shapes=[pltpu.VMEM((4, 128, 512), jnp.bfloat16), pltpu.VMEM((512, 512), jnp.bfloat16)],
+        scratch_shapes=[
+            pltpu.VMEM((4, 128, 512), jnp.bfloat16),
+            pltpu.VMEM((512, 512), jnp.bfloat16),
+            pltpu.VMEM((4, 256, 512), jnp.bfloat16),
+            pltpu.VMEM((4, 2, 128, 256), jnp.float32),
+            pltpu.VMEM((4, 2, 128, 256), jnp.float32),
+            pltpu.SemaphoreType.DMA((4,)),
+            pltpu.SemaphoreType.DMA((16,)),
+        ],
         name="hidden_grad",
     )(index, *grad_slots, head)
 
@@ -349,8 +395,9 @@
     own, other = hidden_grad_parts(index, grad_slots, head)
     other = to_core(other)
     head_grad, *parts = head_grad_parts(hidden, grad_slots)
-    for j in (1, 2, 3):
-        head_grad = head_grad + to_y(parts[j - 1], -j).astype(f32)
+    parts = [to_y(parts[j - 1], -j) for j in (1, 2, 3)]
+    for part in parts:
+        head_grad = head_grad + part.astype(f32)
     by_x = own[:2] + other[:2]
     for step in (1, 2, 3):
         part = own[2 * step : 2 * step + 2] + other[2 * step : 2 * step + 2]
@@ -359,10 +406,8 @@
     def home(zl, y, zh, x, core):
         return zl, y, x % 2 * 2 + core, x // 2 * 2 + zh // 2, zh % 2
 
-    by_x = by_x.astype(bf16)
-    hidden_grad = send(by_x[0], home).astype(f32) + send(
-        by_x[1], lambda zl, y, zh, x, core: home(1 - zl, y, zh, x, core)
-    ).astype(f32)
+    by_zl = by_x[0] + to_zl(by_x[1])
+    hidden_grad = send(by_zl.astype(bf16), home).astype(f32)
     return (kl_terms, hidden_grad, head_grad)
 
 

time: 133 us -> 139 us (1.045); the launches traced: 131 us -> 139 us
  waiting for transfers between devices: 28.7 us -> 34.5 us
  Pallas kernels: 21.5 us -> 24.4 us
    ppermute x35, waiting for transfers between devices: 28.7 us -> 34.5 us  [send(): return lax.ppermute(value, ALL, pairs)]
  transfers between devices with their start and end apart: 35 -> 35, of which waited for: 13 -> 14; matrix products, arithmetic and copies ran while one was open for 7% -> 6% of each run, Pallas kernels for 10% -> 11%
where the time goes in v6:
time: 139 us
  starting transfers between devices  66.1 us (48%)
  waiting for transfers between devices  34.5 us (25%)
  Pallas kernels  24.4 us (18%)
  other arithmetic  11.5 us (8%)
    ppermute x35, starting transfers between devices, send(): return lax.ppermute(value, ALL, pairs)  66.1 us
    ppermute x35, waiting for transfers between devices, send(): return lax.ppermute(value, ALL, pairs)  34.5 us
    pallas_call x2, Pallas kernels, teacher_parts(): pl.pallas_call(teacher_kernel, grid_spec=pltpu.PrefetchScalarGridSpec(num...  8.82 us
    pallas_call x1, Pallas kernels, student_parts(): pl.pallas_call(student_kernel, grid_spec=pltpu.PrefetchScalarGridSpec(num...  4.8 us
    pallas_call x1, Pallas kernels, hidden_grad_parts(): pl.pallas_call(hidden_grad_kernel, in_specs=[pl.BlockSpec(memory_space=pl...  4.79 us
    pallas_call x1, Pallas kernels, head_grad_parts(): pl.pallas_call(head_grad_kernel, in_specs=[ANYWHERE] + [pl.BlockSpec(memo...  4.21 us
  transfers between devices with their start and end apart: 35, of which 14 were waited for; matrix products, arithmetic and copies ran while one was open for 6% of the time, Pallas kernels for 11%

profile of v6, /device:TPU:2, one launch (start us, length us, event | category | flops | bytes accessed | tf_op | source)
XLA Modules:
  0.0 138.5 jit_solution(9648553944303917923)
XLA Ops:
  0.6 4.5 %teacher.3 = f32[8,136,512]{2,1,0:T(8,128)} custom-call(s32[1]{0:T(128)} %bitcast.index_ref, bf16[128,512]{1,0:T(8,128)(2,1)} %hidden_ref.3, bf16[512]{0:T(512)(128)(2,1)} %gain_ref.3, bf16[512,8192]{1,0:T(8,128)(2,1)} %refs_3_.5, bf16[512,8192]{1,0:T(8,128)(2,1)} %refs_3_.5, bf16[512,8192]{1,0:T(8,128)(2,1)} %refs_3_.5, bf16[512,8192]{1,0:T(8,128)(2,1)} %refs_3_.5), custom_call_target="tpu_custom_call" | custom-call | tf_op jit(solution)/shard_map/teacher/pallas_call | solution.py:125
  5.1 1.8 %pick.1 = (bf16[2,128,256]{2,1,0:T(8,128)(2,1)}, bf16[2,128,256]{2,1,0:T(8,128)(2,1)}, bf16[2,128,256]{2,1,0:T(8,128)(2,1)}) custom-call(s32[1]{0:T(128)} %bitcast.index_ref, bf16[128,4096]{1,0:T(8,128)(2,1)} %refs_3_.7, bf16[128,4096]{1,0:T(8,128)(2,1)} %refs_3_.7, bf16[128,4096]{1,0:T(8,128)(2,1)} %refs_3_.7, bf16[128,4096]{1,0:T(8,128)(2,1)} %refs_3_.7, ...), custom_call_target="tpu_custom_call" | custom-call | tf_op jit(solution)/shard_map/pick/pallas_call | solution.py:72
  6.9 3.3 %collective-permute-start.5 = (bf16[2,128,256]{2,1,0:T(8,128)(2,1)}, bf16[2,128,256]{2,1,0:T(8,128)(2,1)S(1)}, u32[]{:S(2)}, u32[]{:S(2)}) collective-permute-start(bf16[2,128,256]{2,1,0:T(8,128)(2,1)} %get-tuple-element.16), channel_id=1, source_target_pairs={{0,8},{1,9},{2,10},{3,11},{4,12},{5,13},{6,14},{7,15},{8,16},{9,17... | collective-permute-start | bytes 393224 | tf_op jit(solution)/shard_map/ppermute | solution.py:29
  10.2 5.4 %collective-permute-start.6 = (bf16[2,128,256]{2,1,0:T(8,128)(2,1)}, bf16[2,128,256]{2,1,0:T(8,128)(2,1)S(1)}, u32[]{:S(2)}, u32[]{:S(2)}) collective-permute-start(bf16[2,128,256]{2,1,0:T(8,128)(2,1)} %get-tuple-element.17), channel_id=1, source_target_pairs={{0,16},{1,17},{2,18},{3,19},{4,20},{5,21},{6,22},{7,23},{8,24},{9,... | collective-permute-start | bytes 393224 | tf_op jit(solution)/shard_map/ppermute | solution.py:29
  15.6 2.7 %collective-permute-start.7 = (bf16[2,128,256]{2,1,0:T(8,128)(2,1)}, bf16[2,128,256]{2,1,0:T(8,128)(2,1)S(1)}, u32[]{:S(2)}, u32[]{:S(2)}) collective-permute-start(bf16[2,128,256]{2,1,0:T(8,128)(2,1)} %get-tuple-element.18), channel_id=1, source_target_pairs={{0,24},{1,25},{2,26},{3,27},{4,28},{5,29},{6,30},{7,31},{8,0},{9,1... | collective-permute-start | bytes 393224 | tf_op jit(solution)/shard_map/ppermute | solution.py:29
  19.9 4.3 %teacher.2 = f32[8,136,512]{2,1,0:T(8,128)} custom-call(s32[1]{0:T(128)} %bitcast.index_ref, bf16[128,512]{1,0:T(8,128)(2,1)} %hidden_ref.3, bf16[512]{0:T(512)(128)(2,1)} %gain_ref.3, bf16[512,8192]{1,0:T(8,128)(2,1)} %refs_3_.5, bf16[512,8192]{1,0:T(8,128)(2,1)} %refs_3_.5, bf16[512,8192]{1,0:T(8,128)(2,1)} %refs_3_.5, bf16[512,8192]{1,0:T(8,128)(2,1)} %refs_3_.5), custom_call_target="tpu_custom_call" | custom-call | tf_op jit(solution)/shard_map/teacher/pallas_call | solution.py:125
  25.5 3.2 %collective-permute-start.12 = (bf16[256,512]{1,0:T(8,128)(2,1)}, bf16[256,512]{1,0:T(8,128)(2,1)}, u32[]{:S(2)}, u32[]{:S(2)}) collective-permute-start(bf16[256,512]{1,0:T(8,128)(2,1)} %refs_10_.1), channel_id=1, source_target_pairs={{0,64},{1,65},{2,66},{3,67},{4,68},{5,69},{6,70},{7,71},{8,72},{9,... | collective-permute-start | bytes 786440 | tf_op jit(solution)/shard_map/ppermute | solution.py:29
  28.7 2.8 %collective-permute-start.13 = (bf16[256,512]{1,0:T(8,128)(2,1)}, bf16[256,512]{1,0:T(8,128)(2,1)}, u32[]{:S(2)}, u32[]{:S(2)}) collective-permute-start(bf16[256,512]{1,0:T(8,128)(2,1)} %refs_10_.1), channel_id=1, source_target_pairs={{0,96},{1,97},{2,98},{3,99},{4,100},{5,101},{6,102},{7,103},{8,104... | collective-permute-start | bytes 786440 | tf_op jit(solution)/shard_map/ppermute | solution.py:29
  32.1 2.5 %fusion.2 = (f16[2,136,512]{2,1,0:T(8,128)(2,1)S(1)}, f16[2,136,512]{2,1,0:T(8,128)(2,1)}, f16[2,136,512]{2,1,0:T(8,128)(2,1)S(1)}) fusion(f32[8,136,512]{2,1,0:T(8,128)S(1)} %collective-permute-done, f32[8,136,512]{2,1,0:T(8,128)} %teacher.2), kind=kLoop, calls=%fused_computation.5 | loop fusion | flops 835584 | bytes 4177920 | tf_op jit(solution)/shard_map/convert_element_type | solution.py:331
  35.2 2.5 %collective-permute-start.2 = (f16[2,136,512]{2,1,0:T(8,128)(2,1)S(1)}, f16[2,136,512]{2,1,0:T(8,128)(2,1)S(1)}, u32[]{:S(2)}, u32[]{:S(2)}) collective-permute-start(f16[2,136,512]{2,1,0:T(8,128)(2,1)S(1)} %get-tuple-element.41), channel_id=1, source_target_pairs={{0,4},{1,5},{2,6},{3,7},{4,0},{5,1},{6,2},{7,3},{8,12},{9,13},{10,... | collective-permute-start | bytes 835592 | tf_op jit(solution)/shard_map/ppermute | solution.py:29
  37.7 1.8 %collective-permute-start.1 = (f16[2,136,512]{2,1,0:T(8,128)(2,1)S(1)}, f16[2,136,512]{2,1,0:T(8,128)(2,1)}, u32[]{:S(2)}, u32[]{:S(2)}) collective-permute-start(f16[2,136,512]{2,1,0:T(8,128)(2,1)S(1)} %get-tuple-element.39), channel_id=1, source_target_pairs={{0,2},{1,3},{2,4},{3,5},{4,6},{5,7},{6,0},{7,1},{8,10},{9,11},{10,... | collective-permute-start | bytes 835592 | tf_op jit(solution)/shard_map/ppermute | solution.py:29
  40.9 4.8 %student.1 = (f32[128,512]{1,0:T(8,128)}, f32[3,128,512]{2,1,0:T(8,128)}, bf16[512,1024]{1,0:T(8,128)(2,1)}, bf16[1024,512]{1,0:T(8,128)(2,1)}) custom-call(s32[1]{0:T(128)} %bitcast.index_ref, bf16[128,4096]{1,0:T(8,128)(2,1)} %refs_3_.7, bf16[128,4096]{1,0:T(8,128)(2,1)} %refs_3_.7, bf16[128,4096]{1,0:T(8,128)(2,1)} %refs_3_.7, bf16[128,4096]{1,0:T(8,128)(2,1)} %refs_3_.7, ...), custom_call_target="tpu_custom_call" | custom-call | tf_op jit(solution)/shard_map/student/pallas_call | solution.py:190
  47.1 3.8 %collective-permute-start.16 = (f16[128,512]{1,0:T(8,128)(2,1)S(1)}, f16[128,512]{1,0:T(8,128)(2,1)S(1)}, u32[]{:S(2)}, u32[]{:S(2)}) collective-permute-start(f16[128,512]{1,0:T(8,128)(2,1)S(1)} %get-tuple-element.46), channel_id=1, source_target_pairs={{0,8},{1,9},{2,10},{3,11},{4,12},{5,13},{6,14},{7,15},{8,16},{9,17... | collective-permute-start | bytes 393224 | tf_op jit(solution)/shard_map/ppermute | solution.py:29
  50.9 4.3 %collective-permute-start.15 = (f16[128,512]{1,0:T(8,128)(2,1)S(1)}, f16[128,512]{1,0:T(8,128)(2,1)S(1)}, u32[]{:S(2)}, u32[]{:S(2)}) collective-permute-start(f16[128,512]{1,0:T(8,128)(2,1)S(1)} %get-tuple-element.47), channel_id=1, source_target_pairs={{0,16},{1,17},{2,18},{3,19},{4,20},{5,21},{6,22},{7,23},{8,24},{9,... | collective-permute-start | bytes 393224 | tf_op jit(solution)/shard_map/ppermute | solution.py:29
  55.2 3.9 %collective-permute-start.14 = (f16[128,512]{1,0:T(8,128)(2,1)S(1)}, f16[128,512]{1,0:T(8,128)(2,1)S(1)}, u32[]{:S(2)}, u32[]{:S(2)}) collective-permute-start(f16[128,512]{1,0:T(8,128)(2,1)S(1)} %get-tuple-element.45), channel_id=1, source_target_pairs={{0,24},{1,25},{2,26},{3,27},{4,28},{5,29},{6,30},{7,31},{8,0},{9,1... | collective-permute-start | bytes 393224 | tf_op jit(solution)/shard_map/ppermute | solution.py:29
  60.5 3.8 %collective-permute-done.15 = f16[128,512]{1,0:T(8,128)(2,1)S(1)} collective-permute-done((f16[128,512]{1,0:T(8,128)(2,1)S(1)}, f16[128,512]{1,0:T(8,128)(2,1)S(1)}, u32[]{:S(2)}, u32[]{:S(2)}) %collective-permute-start.15) | collective-permute-done | bytes 131104 | tf_op jit(solution)/shard_map/ppermute | solution.py:29
  64.4 2.1 %collective-permute-done.14 = f16[128,512]{1,0:T(8,128)(2,1)S(1)} collective-permute-done((f16[128,512]{1,0:T(8,128)(2,1)S(1)}, f16[128,512]{1,0:T(8,128)(2,1)S(1)}, u32[]{:S(2)}, u32[]{:S(2)}) %collective-permute-start.14) | collective-permute-done | bytes 131104 | tf_op jit(solution)/shard_map/ppermute | solution.py:29
  72.5 2.3 %collective-permute-start.23 = (bf16[128,512]{1,0:T(8,128)(2,1)S(1)}, bf16[128,512]{1,0:T(8,128)(2,1)S(1)}, u32[]{:S(2)}, u32[]{:S(2)}) collective-permute-start(bf16[128,512]{1,0:T(8,128)(2,1)S(1)} %subtract_convert_fusion.refs_0_), channel_id=1, source_target_pairs={{0,8},{1,9},{2,10},{3,11},{4,12},{5,13},{6,14},{7,15},{8,16},{9,17... | collective-permute-start | bytes 393224 | tf_op jit(solution)/shard_map/ppermute | solution.py:29
  74.8 3.2 %collective-permute-start.24 = (bf16[128,512]{1,0:T(8,128)(2,1)S(1)}, bf16[128,512]{1,0:T(8,128)(2,1)S(1)}, u32[]{:S(2)}, u32[]{:S(2)}) collective-permute-start(bf16[128,512]{1,0:T(8,128)(2,1)S(1)} %subtract_convert_fusion.refs_0_), channel_id=1, source_target_pairs={{0,16},{1,17},{2,18},{3,19},{4,20},{5,21},{6,22},{7,23},{8,24},{9,... | collective-permute-start | bytes 393224 | tf_op jit(solution)/shard_map/ppermute | solution.py:29
  79.5 2.3 %collective-permute-done.23.refs_1_ = bf16[128,512]{1,0:T(8,128)(2,1)S(1)} collective-permute-done((bf16[128,512]{1,0:T(8,128)(2,1)S(1)}, bf16[128,512]{1,0:T(8,128)(2,1)S(1)}, u32[]{:S(2)}, u32[]{:S(2)}) %collective-permute-start.23) | collective-permute-done | bytes 131104 | tf_op jit(solution)/shard_map/ppermute | solution.py:29
  81.8 7.4 %collective-permute-done.24.refs_2_ = bf16[128,512]{1,0:T(8,128)(2,1)S(1)} collective-permute-done((bf16[128,512]{1,0:T(8,128)(2,1)S(1)}, bf16[128,512]{1,0:T(8,128)(2,1)S(1)}, u32[]{:S(2)}, u32[]{:S(2)}) %collective-permute-start.24) | collective-permute-done | bytes 131104 | tf_op jit(solution)/shard_map/ppermute | solution.py:29
  89.9 4.8 %hidden_grad.1 = (f32[8,128,256]{2,1,0:T(8,128)}, f32[8,128,256]{2,1,0:T(8,128)}) custom-call(s32[1]{0:T(128)} %bitcast.index_ref, bf16[128,512]{1,0:T(8,128)(2,1)} %copy-done, bf16[128,512]{1,0:T(8,128)(2,1)} %copy-done.1, bf16[128,512]{1,0:T(8,128)(2,1)} %copy-done.2, bf16[128,512]{1,0:T(8,128)(2,1)} %copy-done.3, bf16[1024,512]{1,0:T(8,128)(2,1)} %get-tuple-element.21.refs_4_), custom_call_target="tpu_custom_call" | custom-call | tf_op jit(solution)/shard_map/hidden_grad/pallas_call | solution.py:294
  94.9 2.8 %collective-permute-done.26 = f32[8,128,256]{2,1,0:T(8,128)S(1)} collective-permute-done((f32[8,128,256]{2,1,0:T(8,128)}, f32[8,128,256]{2,1,0:T(8,128)S(1)}, u32[]{:S(2)}, u32[]{:S(2)}) %collective-permute-start.26) | collective-permute-done | bytes 1048608 | tf_op jit(solution)/shard_map/ppermute | solution.py:29
  100.4 2.1 %collective-permute-start.28 = (bf16[2,128,256]{2,1,0:T(8,128)(2,1)S(1)}, bf16[2,128,256]{2,1,0:T(8,128)(2,1)S(1)}, u32[]{:S(2)}, u32[]{:S(2)}) collective-permute-start(bf16[2,128,256]{2,1,0:T(8,128)(2,1)S(1)} %get-tuple-element.44), channel_id=1, source_target_pairs={{0,4},{1,5},{2,6},{3,7},{4,0},{5,1},{6,2},{7,3},{8,12},{9,13},{10,... | collective-permute-start | bytes 393224 | tf_op jit(solution)/shard_map/ppermute | solution.py:29
  104.1 2.8 %collective-permute-start.21 = (f32[1,128]{1,0:T(1,128)S(1)}, f32[1,128]{1,0:T(1,128)S(1)}, u32[]{:S(2)}, u32[]{:S(2)}) collective-permute-start(f32[1,128]{1,0:T(1,128)S(1)} %bitcast_multiply_fusion), channel_id=1, source_target_pairs={{0,128},{1,129},{2,130},{3,131},{4,132},{5,133},{6,134},{7,135},{8... | collective-permute-start | bytes 1544 | tf_op jit(solution)/shard_map/ppermute | solution.py:29
  106.9 3.2 %collective-permute-done.22 = f32[1,128]{1,0:T(1,128)S(1)} collective-permute-done((f32[1,128]{1,0:T(1,128)S(1)}, f32[1,128]{1,0:T(1,128)S(1)}, u32[]{:S(2)}, u32[]{:S(2)}) %collective-permute-start.22) | collective-permute-done | bytes 544 | tf_op jit(solution)/shard_map/ppermute | solution.py:29
  111.4 3.7 %collective-permute-done.20 = f32[1,128]{1,0:T(1,128)S(1)} collective-permute-done((f32[1,128]{1,0:T(1,128)S(1)}, f32[1,128]{1,0:T(1,128)S(1)}, u32[]{:S(2)}, u32[]{:S(2)}) %collective-permute-start.20) | collective-permute-done | bytes 544 | tf_op jit(solution)/shard_map/ppermute | solution.py:29
  116.5 4.2 %head_grad.1 = (f32[256,512]{1,0:T(8,128)}, bf16[256,512]{1,0:T(8,128)(2,1)}, bf16[256,512]{1,0:T(8,128)(2,1)}, bf16[256,512]{1,0:T(8,128)(2,1)}) custom-call(bf16[512,1024]{1,0:T(8,128)(2,1)} %get-tuple-element.24.hidden_hbm, bf16[128,512]{1,0:T(8,128)(2,1)} %copy-done, bf16[128,512]{1,0:T(8,128)(2,1)} %copy-done.1, bf16[128,512]{1,0:T(8,128)(2,1)} %copy-done.2, ...), custom_call_target="tpu_custom_call" | custom-call | tf_op jit(solution)/shard_map/head_grad/pallas_call | solution.py:242
  122.4 3.0 %collective-permute-start.33 = (bf16[256,512]{1,0:T(8,128)(2,1)}, bf16[256,512]{1,0:T(8,128)(2,1)S(1)}, u32[]{:S(2)}, u32[]{:S(2)}) collective-permute-start(bf16[256,512]{1,0:T(8,128)(2,1)} %get-tuple-element.27), channel_id=1, source_target_pairs={{0,64},{1,65},{2,66},{3,67},{4,68},{5,69},{6,70},{7,71},{8,72},{9,... | collective-permute-start | bytes 786440 | tf_op jit(solution)/shard_map/ppermute | solution.py:29
  126.9 5.4 %collective-permute-start.31 = (bf16[128,256]{1,0:T(8,128)(2,1)S(1)}, bf16[128,256]{1,0:T(8,128)(2,1)S(1)}, u32[]{:S(2)}, u32[]{:S(2)}) collective-permute-start(bf16[128,256]{1,0:T(8,128)(2,1)S(1)} %fusion.18), channel_id=1, source_target_pairs={{0,0},{1,8},{2,16},{3,24},{4,4},{5,12},{6,20},{7,28},{8,1},{9,9},{... | collective-permute-start | bytes 196616 | tf_op jit(solution)/shard_map/ppermute | solution.py:29
  132.3 2.1 %collective-permute-done.33 = bf16[256,512]{1,0:T(8,128)(2,1)S(1)} collective-permute-done((bf16[256,512]{1,0:T(8,128)(2,1)}, bf16[256,512]{1,0:T(8,128)(2,1)S(1)}, u32[]{:S(2)}, u32[]{:S(2)}) %collective-permute-start.33) | collective-permute-done | bytes 262176 | tf_op jit(solution)/shard_map/ppermute | solution.py:29
  134.4 2.0 %convert_add_fusion = f32[256,512]{1,0:T(8,128)} fusion(bf16[256,512]{1,0:T(8,128)(2,1)S(1)} %collective-permute-done.34, bf16[256,512]{1,0:T(8,128)(2,1)S(1)} %collective-permute-done.33, f32[256,512]{1,0:T(8,128)} %get-tuple-element.25, bf16[256,512]{1,0:T(8,128)(2,1)S(1)} %collective-permute-done.32), kind=kLoop, calls=%fused_computation.10 | loop fusion | flops 786432 | bytes 1835008 | tf_op jit(solution)/shard_map/add | solution.py:400
  (100 shorter events, 28.8 us)
Async XLA Ops:
  5.1 26.4 %collective-permute-start = (f32[8,136,512]{2,1,0:T(8,128)}, f32[8,136,512]{2,1,0:T(8,128)S(1)}, u32[]{:S(2)}, u32[]{:S(2)}) collective-permute-start(f32[8,136,512]{2,1,0:T(8,128)} %teacher.3), channel_id=1, source_target_pairs={{0,1},{1,0},{2,3},{3,2},{4,5},{5,4},{6,7},{7,6},{8,9},{9,8},{10,11... | collective-permute-start | bytes 6684680 | tf_op jit(solution)/shard_map/ppermute | solution.py:29
  6.9 11.3 %collective-permute-start.5 = (bf16[2,128,256]{2,1,0:T(8,128)(2,1)}, bf16[2,128,256]{2,1,0:T(8,128)(2,1)S(1)}, u32[]{:S(2)}, u32[]{:S(2)}) collective-permute-start(bf16[2,128,256]{2,1,0:T(8,128)(2,1)} %get-tuple-element.16), channel_id=1, source_target_pairs={{0,8},{1,9},{2,10},{3,11},{4,12},{5,13},{6,14},{7,15},{8,16},{9,17... | collective-permute-start | bytes 393224 | tf_op jit(solution)/shard_map/ppermute | solution.py:29
  10.2 15.3 %collective-permute-start.6 = (bf16[2,128,256]{2,1,0:T(8,128)(2,1)}, bf16[2,128,256]{2,1,0:T(8,128)(2,1)S(1)}, u32[]{:S(2)}, u32[]{:S(2)}) collective-permute-start(bf16[2,128,256]{2,1,0:T(8,128)(2,1)} %get-tuple-element.17), channel_id=1, source_target_pairs={{0,16},{1,17},{2,18},{3,19},{4,20},{5,21},{6,22},{7,23},{8,24},{9,... | collective-permute-start | bytes 393224 | tf_op jit(solution)/shard_map/ppermute | solution.py:29
  15.6 13.1 %collective-permute-start.7 = (bf16[2,128,256]{2,1,0:T(8,128)(2,1)}, bf16[2,128,256]{2,1,0:T(8,128)(2,1)S(1)}, u32[]{:S(2)}, u32[]{:S(2)}) collective-permute-start(bf16[2,128,256]{2,1,0:T(8,128)(2,1)} %get-tuple-element.18), channel_id=1, source_target_pairs={{0,24},{1,25},{2,26},{3,27},{4,28},{5,29},{6,30},{7,31},{8,0},{9,1... | collective-permute-start | bytes 393224 | tf_op jit(solution)/shard_map/ppermute | solution.py:29
  18.3 13.3 %collective-permute-start.8 = (bf16[2,128,256]{2,1,0:T(8,128)(2,1)S(1)}, bf16[2,128,256]{2,1,0:T(8,128)(2,1)S(1)}, u32[]{:S(2)}, u32[]{:S(2)}) collective-permute-start(bf16[2,128,256]{2,1,0:T(8,128)(2,1)S(1)} %collective-permute-done.5.refs_4_), channel_id=1, source_target_pairs={{0,1},{1,0},{2,3},{3,2},{4,5},{5,4},{6,7},{7,6},{8,9},{9,8},{10,11... | collective-permute-start | bytes 393224 | tf_op jit(solution)/shard_map/ppermute | solution.py:29
  18.3 19.5 %collective-permute-start.11 = (bf16[256,512]{1,0:T(8,128)(2,1)}, bf16[256,512]{1,0:T(8,128)(2,1)}, u32[]{:S(2)}, u32[]{:S(2)}) collective-permute-start(bf16[256,512]{1,0:T(8,128)(2,1)} %refs_10_.1), channel_id=1, source_target_pairs={{0,32},{1,33},{2,34},{3,35},{4,36},{5,37},{6,38},{7,39},{8,40},{9,... | collective-permute-start | bytes 786440 | tf_op jit(solution)/shard_map/ppermute | solution.py:29
  25.5 14.0 %collective-permute-start.12 = (bf16[256,512]{1,0:T(8,128)(2,1)}, bf16[256,512]{1,0:T(8,128)(2,1)}, u32[]{:S(2)}, u32[]{:S(2)}) collective-permute-start(bf16[256,512]{1,0:T(8,128)(2,1)} %refs_10_.1), channel_id=1, source_target_pairs={{0,64},{1,65},{2,66},{3,67},{4,68},{5,69},{6,70},{7,71},{8,72},{9,... | collective-permute-start | bytes 786440 | tf_op jit(solution)/shard_map/ppermute | solution.py:29
  28.7 12.2 %collective-permute-start.13 = (bf16[256,512]{1,0:T(8,128)(2,1)}, bf16[256,512]{1,0:T(8,128)(2,1)}, u32[]{:S(2)}, u32[]{:S(2)}) collective-permute-start(bf16[256,512]{1,0:T(8,128)(2,1)} %refs_10_.1), channel_id=1, source_target_pairs={{0,96},{1,97},{2,98},{3,99},{4,100},{5,101},{6,102},{7,103},{8,104... | collective-permute-start | bytes 786440 | tf_op jit(solution)/shard_map/ppermute | solution.py:29
  31.6 3.6 %collective-permute-start.10 = (bf16[2,128,256]{2,1,0:T(8,128)(2,1)S(1)}, bf16[2,128,256]{2,1,0:T(8,128)(2,1)S(1)}, u32[]{:S(2)}, u32[]{:S(2)}) collective-permute-start(bf16[2,128,256]{2,1,0:T(8,128)(2,1)S(1)} %collective-permute-done.7.refs_6_), channel_id=1, source_target_pairs={{0,1},{1,0},{2,3},{3,2},{4,5},{5,4},{6,7},{7,6},{8,9},{9,8},{10,11... | collective-permute-start | bytes 393224 | tf_op jit(solution)/shard_map/ppermute | solution.py:29
  34.6 20.6 %collective-permute-start.3 = (f16[2,136,512]{2,1,0:T(8,128)(2,1)}, f16[2,136,512]{2,1,0:T(8,128)(2,1)S(1)}, u32[]{:S(2)}, u32[]{:S(2)}) collective-permute-start(f16[2,136,512]{2,1,0:T(8,128)(2,1)} %get-tuple-element.40), channel_id=1, source_target_pairs={{0,6},{1,7},{2,0},{3,1},{4,2},{5,3},{6,4},{7,5},{8,14},{9,15},{10,... | collective-permute-start | bytes 835592 | tf_op jit(solution)/shard_map/ppermute | solution.py:29
  35.2 23.8 %collective-permute-start.2 = (f16[2,136,512]{2,1,0:T(8,128)(2,1)S(1)}, f16[2,136,512]{2,1,0:T(8,128)(2,1)S(1)}, u32[]{:S(2)}, u32[]{:S(2)}) collective-permute-start(f16[2,136,512]{2,1,0:T(8,128)(2,1)S(1)} %get-tuple-element.41), channel_id=1, source_target_pairs={{0,4},{1,5},{2,6},{3,7},{4,0},{5,1},{6,2},{7,3},{8,12},{9,13},{10,... | collective-permute-start | bytes 835592 | tf_op jit(solution)/shard_map/ppermute | solution.py:29
  37.7 21.3 %collective-permute-start.1 = (f16[2,136,512]{2,1,0:T(8,128)(2,1)S(1)}, f16[2,136,512]{2,1,0:T(8,128)(2,1)}, u32[]{:S(2)}, u32[]{:S(2)}) collective-permute-start(f16[2,136,512]{2,1,0:T(8,128)(2,1)S(1)} %get-tuple-element.39), channel_id=1, source_target_pairs={{0,2},{1,3},{2,4},{3,5},{4,6},{5,7},{6,0},{7,1},{8,10},{9,11},{10,... | collective-permute-start | bytes 835592 | tf_op jit(solution)/shard_map/ppermute | solution.py:29
  47.1 13.5 %collective-permute-start.16 = (f16[128,512]{1,0:T(8,128)(2,1)S(1)}, f16[128,512]{1,0:T(8,128)(2,1)S(1)}, u32[]{:S(2)}, u32[]{:S(2)}) collective-permute-start(f16[128,512]{1,0:T(8,128)(2,1)S(1)} %get-tuple-element.46), channel_id=1, source_target_pairs={{0,8},{1,9},{2,10},{3,11},{4,12},{5,13},{6,14},{7,15},{8,16},{9,17... | collective-permute-start | bytes 393224 | tf_op jit(solution)/shard_map/ppermute | solution.py:29
  50.9 13.5 %collective-permute-start.15 = (f16[128,512]{1,0:T(8,128)(2,1)S(1)}, f16[128,512]{1,0:T(8,128)(2,1)S(1)}, u32[]{:S(2)}, u32[]{:S(2)}) collective-permute-start(f16[128,512]{1,0:T(8,128)(2,1)S(1)} %get-tuple-element.47), channel_id=1, source_target_pairs={{0,16},{1,17},{2,18},{3,19},{4,20},{5,21},{6,22},{7,23},{8,24},{9,... | collective-permute-start | bytes 393224 | tf_op jit(solution)/shard_map/ppermute | solution.py:29
  55.2 11.3 %collective-permute-start.14 = (f16[128,512]{1,0:T(8,128)(2,1)S(1)}, f16[128,512]{1,0:T(8,128)(2,1)S(1)}, u32[]{:S(2)}, u32[]{:S(2)}) collective-permute-start(f16[128,512]{1,0:T(8,128)(2,1)S(1)} %get-tuple-element.45), channel_id=1, source_target_pairs={{0,24},{1,25},{2,26},{3,27},{4,28},{5,29},{6,30},{7,31},{8,0},{9,1... | collective-permute-start | bytes 393224 | tf_op jit(solution)/shard_map/ppermute | solution.py:29
  60.4 7.4 %collective-permute-start.4 = (f16[136,512]{1,0:T(8,128)(2,1)S(1)}, f16[136,512]{1,0:T(8,128)(2,1)S(1)}, u32[]{:S(2)}, u32[]{:S(2)}) collective-permute-start(f16[136,512]{1,0:T(8,128)(2,1)S(1)} %fusion.16), channel_id=1, source_target_pairs={{0,128},{1,129},{2,130},{3,131},{4,132},{5,133},{6,134},{7,135},{8... | collective-permute-start | bytes 417800 | tf_op jit(solution)/shard_map/ppermute | solution.py:29
  68.4 3.1 %collective-permute-start.19 = (f32[5,128]{1,0:T(8,128)S(1)}, f32[5,128]{1,0:T(8,128)S(1)}, u32[]{:S(2)}, u32[]{:S(2)}) collective-permute-start(f32[5,128]{1,0:T(8,128)S(1)} %stack.38), channel_id=1, source_target_pairs={{0,3},{1,2},{2,1},{3,0},{4,7},{5,6},{6,5},{7,4},{8,11},{9,10},{10,... | collective-permute-start | bytes 7688 | tf_op jit(solution)/shard_map/ppermute | solution.py:29
  68.5 3.7 %collective-permute-start.18 = (f32[5,128]{1,0:T(8,128)S(1)}, f32[5,128]{1,0:T(8,128)S(1)}, u32[]{:S(2)}, u32[]{:S(2)}) collective-permute-start(f32[5,128]{1,0:T(8,128)S(1)} %stack.38), channel_id=1, source_target_pairs={{0,2},{1,3},{2,0},{3,1},{4,6},{5,7},{6,4},{7,5},{8,10},{9,11},{10,... | collective-permute-start | bytes 7688 | tf_op jit(solution)/shard_map/ppermute | solution.py:29
  72.5 9.3 %collective-permute-start.23 = (bf16[128,512]{1,0:T(8,128)(2,1)S(1)}, bf16[128,512]{1,0:T(8,128)(2,1)S(1)}, u32[]{:S(2)}, u32[]{:S(2)}) collective-permute-start(bf16[128,512]{1,0:T(8,128)(2,1)S(1)} %subtract_convert_fusion.refs_0_), channel_id=1, source_target_pairs={{0,8},{1,9},{2,10},{3,11},{4,12},{5,13},{6,14},{7,15},{8,16},{9,17... | collective-permute-start | bytes 393224 | tf_op jit(solution)/shard_map/ppermute | solution.py:29
  74.8 14.4 %collective-permute-start.24 = (bf16[128,512]{1,0:T(8,128)(2,1)S(1)}, bf16[128,512]{1,0:T(8,128)(2,1)S(1)}, u32[]{:S(2)}, u32[]{:S(2)}) collective-permute-start(bf16[128,512]{1,0:T(8,128)(2,1)S(1)} %subtract_convert_fusion.refs_0_), channel_id=1, source_target_pairs={{0,16},{1,17},{2,18},{3,19},{4,20},{5,21},{6,22},{7,23},{8,24},{9,... | collective-permute-start | bytes 393224 | tf_op jit(solution)/shard_map/ppermute | solution.py:29
  78.0 11.2 %collective-permute-start.25 = (bf16[128,512]{1,0:T(8,128)(2,1)S(1)}, bf16[128,512]{1,0:T(8,128)(2,1)S(1)}, u32[]{:S(2)}, u32[]{:S(2)}) collective-permute-start(bf16[128,512]{1,0:T(8,128)(2,1)S(1)} %subtract_convert_fusion.refs_0_), channel_id=1, source_target_pairs={{0,24},{1,25},{2,26},{3,27},{4,28},{5,29},{6,30},{7,31},{8,0},{9,1... | collective-permute-start | bytes 393224 | tf_op jit(solution)/shard_map/ppermute | solution.py:29
  98.9 16.2 %collective-permute-start.29 = (bf16[2,128,256]{2,1,0:T(8,128)(2,1)S(1)}, bf16[2,128,256]{2,1,0:T(8,128)(2,1)S(1)}, u32[]{:S(2)}, u32[]{:S(2)}) collective-permute-start(bf16[2,128,256]{2,1,0:T(8,128)(2,1)S(1)} %get-tuple-element.43), channel_id=1, source_target_pairs={{0,6},{1,7},{2,0},{3,1},{4,2},{5,3},{6,4},{7,5},{8,14},{9,15},{10,... | collective-permute-start | bytes 393224 | tf_op jit(solution)/shard_map/ppermute | solution.py:29
  100.4 14.7 %collective-permute-start.28 = (bf16[2,128,256]{2,1,0:T(8,128)(2,1)S(1)}, bf16[2,128,256]{2,1,0:T(8,128)(2,1)S(1)}, u32[]{:S(2)}, u32[]{:S(2)}) collective-permute-start(bf16[2,128,256]{2,1,0:T(8,128)(2,1)S(1)} %get-tuple-element.44), channel_id=1, source_target_pairs={{0,4},{1,5},{2,6},{3,7},{4,0},{5,1},{6,2},{7,3},{8,12},{9,13},{10,... | collective-permute-start | bytes 393224 | tf_op jit(solution)/shard_map/ppermute | solution.py:29
  102.5 12.6 %collective-permute-start.27 = (bf16[2,128,256]{2,1,0:T(8,128)(2,1)S(1)}, bf16[2,128,256]{2,1,0:T(8,128)(2,1)S(1)}, u32[]{:S(2)}, u32[]{:S(2)}) collective-permute-start(bf16[2,128,256]{2,1,0:T(8,128)(2,1)S(1)} %get-tuple-element.42), channel_id=1, source_target_pairs={{0,2},{1,3},{2,4},{3,5},{4,6},{5,7},{6,0},{7,1},{8,10},{9,11},{10,... | collective-permute-start | bytes 393224 | tf_op jit(solution)/shard_map/ppermute | solution.py:29
  104.0 6.1 %collective-permute-start.22 = (f32[1,128]{1,0:T(1,128)S(1)}, f32[1,128]{1,0:T(1,128)S(1)}, u32[]{:S(2)}, u32[]{:S(2)}) collective-permute-start(f32[1,128]{1,0:T(1,128)S(1)} %bitcast_multiply_fusion), channel_id=1, source_target_pairs={{0,132},{1,133},{2,134},{3,135},{4,128},{5,129},{6,130},{7,131},{8... | collective-permute-start | bytes 1544 | tf_op jit(solution)/shard_map/ppermute | solution.py:29
  104.1 7.3 %collective-permute-start.21 = (f32[1,128]{1,0:T(1,128)S(1)}, f32[1,128]{1,0:T(1,128)S(1)}, u32[]{:S(2)}, u32[]{:S(2)}) collective-permute-start(f32[1,128]{1,0:T(1,128)S(1)} %bitcast_multiply_fusion), channel_id=1, source_target_pairs={{0,128},{1,129},{2,130},{3,131},{4,132},{5,133},{6,134},{7,135},{8... | collective-permute-start | bytes 1544 | tf_op jit(solution)/shard_map/ppermute | solution.py:29
  110.0 5.1 %collective-permute-start.20 = (f32[1,128]{1,0:T(1,128)S(1)}, f32[1,128]{1,0:T(1,128)S(1)}, u32[]{:S(2)}, u32[]{:S(2)}) collective-permute-start(f32[1,128]{1,0:T(1,128)S(1)} %bitcast_multiply_fusion), channel_id=1, source_target_pairs={{0,4},{1,5},{2,6},{3,7},{4,0},{5,1},{6,2},{7,3},{8,12},{9,13},{10,... | collective-permute-start | bytes 1544 | tf_op jit(solution)/shard_map/ppermute | solution.py:29
  116.2 10.7 %collective-permute-start.30 = (f32[128,256]{1,0:T(8,128)S(1)}, f32[128,256]{1,0:T(8,128)S(1)}, u32[]{:S(2)}, u32[]{:S(2)}) collective-permute-start(f32[128,256]{1,0:T(8,128)S(1)} %slice_bitcast_fusion.1), channel_id=1, source_target_pairs={{0,128},{1,129},{2,130},{3,131},{4,132},{5,133},{6,134},{7,135},{8... | collective-permute-start | bytes 393224 | tf_op jit(solution)/shard_map/ppermute | solution.py:29
  120.8 11.6 %collective-permute-start.34 = (bf16[256,512]{1,0:T(8,128)(2,1)}, bf16[256,512]{1,0:T(8,128)(2,1)S(1)}, u32[]{:S(2)}, u32[]{:S(2)}) collective-permute-start(bf16[256,512]{1,0:T(8,128)(2,1)} %get-tuple-element.28), channel_id=1, source_target_pairs={{0,32},{1,33},{2,34},{3,35},{4,36},{5,37},{6,38},{7,39},{8,40},{9,... | collective-permute-start | bytes 786440 | tf_op jit(solution)/shard_map/ppermute | solution.py:29
  122.4 12.0 %collective-permute-start.33 = (bf16[256,512]{1,0:T(8,128)(2,1)}, bf16[256,512]{1,0:T(8,128)(2,1)S(1)}, u32[]{:S(2)}, u32[]{:S(2)}) collective-permute-start(bf16[256,512]{1,0:T(8,128)(2,1)} %get-tuple-element.27), channel_id=1, source_target_pairs={{0,64},{1,65},{2,66},{3,67},{4,68},{5,69},{6,70},{7,71},{8,72},{9,... | collective-permute-start | bytes 786440 | tf_op jit(solution)/shard_map/ppermute | solution.py:29
  125.4 9.1 %collective-permute-start.32 = (bf16[256,512]{1,0:T(8,128)(2,1)}, bf16[256,512]{1,0:T(8,128)(2,1)S(1)}, u32[]{:S(2)}, u32[]{:S(2)}) collective-permute-start(bf16[256,512]{1,0:T(8,128)(2,1)} %get-tuple-element.26), channel_id=1, source_target_pairs={{0,96},{1,97},{2,98},{3,99},{4,100},{5,101},{6,102},{7,103},{8,104... | collective-permute-start | bytes 786440 | tf_op jit(solution)/shard_map/ppermute | solution.py:29
  126.9 11.0 %collective-permute-start.31 = (bf16[128,256]{1,0:T(8,128)(2,1)S(1)}, bf16[128,256]{1,0:T(8,128)(2,1)S(1)}, u32[]{:S(2)}, u32[]{:S(2)}) collective-permute-start(bf16[128,256]{1,0:T(8,128)(2,1)S(1)} %fusion.18), channel_id=1, source_target_pairs={{0,0},{1,8},{2,16},{3,24},{4,4},{5,12},{6,20},{7,28},{8,1},{9,9},{... | collective-permute-start | bytes 196616 | tf_op jit(solution)/shard_map/ppermute | solution.py:29
  (15 other events, 104.6 us)

commit v7 on v5

--- a/solution.py
+++ b/solution.py
@@ -140,40 +140,22 @@
     )(index, hidden, gain, head, head, head, head)
 
 
-ANYWHERE = pl.BlockSpec(memory_space=pl.ANY)
-
-
-def loads(sources, targets, sems):
-    copies = [
-        pltpu.make_async_copy(source, target, sems.at[i]) for i, (source, target) in enumerate(zip(sources, targets))
-    ]
-    for copy in copies:
-        copy.start()
-    return copies
-
-
 def student_kernel(index_ref, *refs):
     own_refs, near_refs, far_refs, head_refs = refs[:4], refs[4:7], refs[7:10], refs[10:14]
-    first_ref, out_ref, hidden_ref, head_ref, sems = refs[14:]
+    first_ref, out_ref, hidden_ref, head_ref = refs[14:]
     core = index_ref[0] % 2
 
     def spot(k, side, p):
         return pl.ds(128 * k, 128), pl.ds(pl.multiple_of((2 * side + p) * 256, 256), 256)
 
-    copies = loads(
-        [*head_refs]
-        + [near_refs[k - 1].at[p] for k in (1, 2, 3) for p in range(2)]
-        + [far_refs[k - 1].at[p] for k in (1, 2, 3) for p in range(2)],
-        [head_ref.at[pl.ds(256 * j, 256)] for j in range(4)]
-        + [hidden_ref.at[spot(k, core, p)] for k in (1, 2, 3) for p in range(2)]
-        + [hidden_ref.at[spot(k, 1 - core, p)] for k in (1, 2, 3) for p in range(2)],
-        sems,
-    )
     for p in range(2):
         hidden_ref[spot(0, core, p)] = own_refs[p][...]
         hidden_ref[spot(0, 1 - core, p)] = own_refs[2 + p][...]
-    for copy in copies:
-        copy.wait()
+        for k in (1, 2, 3):
+            hidden_ref[spot(k, core, p)] = near_refs[k - 1][p]
+            hidden_ref[spot(k, 1 - core, p)] = far_refs[k - 1][p]
+    for j in range(4):
+        head_ref[256 * j : 256 * (j + 1)] = head_refs[j][...]
     scores = jnp.dot(hidden_ref[...], head_ref[...], preferred_element_type=jnp.float32)
     first_ref[...] = scores[:128]
     for k in (1, 2, 3):
@@ -190,9 +172,9 @@
             num_scalar_prefetch=1,
             grid=(1,),
             in_specs=[hidden_block(0, p) for p in range(4)]
-            + [ANYWHERE] * 10,
+            + [whole(2, 128, 256)] * 6
+            + [whole(256, 512)] * 4,
             out_specs=(whole(128, 512), whole(3, 128, 512), whole(512, 1024), whole(1024, 512)),
-            scratch_shapes=[pltpu.SemaphoreType.DMA((16,))],
         ),
         out_shape=(
             jax.ShapeDtypeStruct((128, 512), jnp.float32),
@@ -349,8 +331,9 @@
     own, other = hidden_grad_parts(index, grad_slots, head)
     other = to_core(other)
     head_grad, *parts = head_grad_parts(hidden, grad_slots)
-    for j in (1, 2, 3):
-        head_grad = head_grad + to_y(parts[j - 1], -j).astype(f32)
+    parts = [to_y(parts[j - 1], -j) for j in (1, 2, 3)]
+    for part in parts:
+        head_grad = head_grad + part.astype(f32)
     by_x = own[:2] + other[:2]
     for step in (1, 2, 3):
         part = own[2 * step : 2 * step + 2] + other[2 * step : 2 * step + 2]

time: 133 us -> 132 us (level)
  no operation moved by 1% of the time
where the time goes in v7:
time: 132 us; the launch traced here: 130 us
  starting transfers between devices  67.2 us (51%)
  waiting for transfers between devices  28.6 us (22%)
  Pallas kernels  20.8 us (16%)
  other arithmetic  11.5 us (9%)
    ppermute x35, starting transfers between devices, send(): return lax.ppermute(value, ALL, pairs)  67.2 us
    ppermute x35, waiting for transfers between devices, send(): return lax.ppermute(value, ALL, pairs)  28.6 us
    pallas_call x2, Pallas kernels, teacher_parts(): pl.pallas_call(teacher_kernel, grid_spec=pltpu.PrefetchScalarGridSpec(num...  8.82 us
    pallas_call x1, Pallas kernels, student_parts(): pl.pallas_call(student_kernel, grid_spec=pltpu.PrefetchScalarGridSpec(num...  3.68 us
    pallas_call x1, Pallas kernels, hidden_grad_parts(): pl.pallas_call(hidden_grad_kernel, in_specs=[pl.BlockSpec(memory_space=pl...  3.53 us
    pallas_call x1, Pallas kernels, head_grad_parts(): pl.pallas_call(head_grad_kernel, out_shape=(jax.ShapeDtypeStruct((256, 51...  2.94 us
  transfers between devices with their start and end apart: 35, of which 13 were waited for; matrix products, arithmetic and copies ran while one was open for 7% of the time, Pallas kernels for 10%

profile of v7, /device:TPU:2, one launch (start us, length us, event | category | flops | bytes accessed | tf_op | source)
XLA Modules:
  0.0 130.0 jit_solution(4440026228681713786)
XLA Ops:
  0.6 4.5 %teacher.3 = f32[8,136,512]{2,1,0:T(8,128)} custom-call(s32[1]{0:T(128)} %bitcast.index_ref, bf16[128,512]{1,0:T(8,128)(2,1)} %hidden_ref.3, bf16[512]{0:T(512)(128)(2,1)} %gain_ref.3, bf16[512,8192]{1,0:T(8,128)(2,1)} %refs_3_.5, bf16[512,8192]{1,0:T(8,128)(2,1)} %refs_3_.5, bf16[512,8192]{1,0:T(8,128)(2,1)} %refs_3_.5, bf16[512,8192]{1,0:T(8,128)(2,1)} %refs_3_.5), custom_call_target="tpu_custom_call" | custom-call | tf_op jit(solution)/shard_map/teacher/pallas_call | solution.py:125
  5.1 1.8 %pick.1 = (bf16[2,128,256]{2,1,0:T(8,128)(2,1)}, bf16[2,128,256]{2,1,0:T(8,128)(2,1)}, bf16[2,128,256]{2,1,0:T(8,128)(2,1)}) custom-call(s32[1]{0:T(128)} %bitcast.index_ref, bf16[128,4096]{1,0:T(8,128)(2,1)} %refs_3_.7, bf16[128,4096]{1,0:T(8,128)(2,1)} %refs_3_.7, bf16[128,4096]{1,0:T(8,128)(2,1)} %refs_3_.7, bf16[128,4096]{1,0:T(8,128)(2,1)} %refs_3_.7, ...), custom_call_target="tpu_custom_call" | custom-call | tf_op jit(solution)/shard_map/pick/pallas_call | solution.py:72
  6.9 3.3 %collective-permute-start.5 = (bf16[2,128,256]{2,1,0:T(8,128)(2,1)}, bf16[2,128,256]{2,1,0:T(8,128)(2,1)S(1)}, u32[]{:S(2)}, u32[]{:S(2)}) collective-permute-start(bf16[2,128,256]{2,1,0:T(8,128)(2,1)} %get-tuple-element.16), channel_id=1, source_target_pairs={{0,8},{1,9},{2,10},{3,11},{4,12},{5,13},{6,14},{7,15},{8,16},{9,17... | collective-permute-start | bytes 393224 | tf_op jit(solution)/shard_map/ppermute | solution.py:29
  10.2 5.4 %collective-permute-start.6 = (bf16[2,128,256]{2,1,0:T(8,128)(2,1)}, bf16[2,128,256]{2,1,0:T(8,128)(2,1)S(1)}, u32[]{:S(2)}, u32[]{:S(2)}) collective-permute-start(bf16[2,128,256]{2,1,0:T(8,128)(2,1)} %get-tuple-element.17), channel_id=1, source_target_pairs={{0,16},{1,17},{2,18},{3,19},{4,20},{5,21},{6,22},{7,23},{8,24},{9,... | collective-permute-start | bytes 393224 | tf_op jit(solution)/shard_map/ppermute | solution.py:29
  15.6 2.7 %collective-permute-start.7 = (bf16[2,128,256]{2,1,0:T(8,128)(2,1)}, bf16[2,128,256]{2,1,0:T(8,128)(2,1)S(1)}, u32[]{:S(2)}, u32[]{:S(2)}) collective-permute-start(bf16[2,128,256]{2,1,0:T(8,128)(2,1)} %get-tuple-element.18), channel_id=1, source_target_pairs={{0,24},{1,25},{2,26},{3,27},{4,28},{5,29},{6,30},{7,31},{8,0},{9,1... | collective-permute-start | bytes 393224 | tf_op jit(solution)/shard_map/ppermute | solution.py:29
  19.9 4.3 %teacher.2 = f32[8,136,512]{2,1,0:T(8,128)} custom-call(s32[1]{0:T(128)} %bitcast.index_ref, bf16[128,512]{1,0:T(8,128)(2,1)} %hidden_ref.3, bf16[512]{0:T(512)(128)(2,1)} %gain_ref.3, bf16[512,8192]{1,0:T(8,128)(2,1)} %refs_3_.5, bf16[512,8192]{1,0:T(8,128)(2,1)} %refs_3_.5, bf16[512,8192]{1,0:T(8,128)(2,1)} %refs_3_.5, bf16[512,8192]{1,0:T(8,128)(2,1)} %refs_3_.5), custom_call_target="tpu_custom_call" | custom-call | tf_op jit(solution)/shard_map/teacher/pallas_call | solution.py:125
  25.5 3.2 %collective-permute-start.12 = (bf16[256,512]{1,0:T(8,128)(2,1)}, bf16[256,512]{1,0:T(8,128)(2,1)}, u32[]{:S(2)}, u32[]{:S(2)}) collective-permute-start(bf16[256,512]{1,0:T(8,128)(2,1)} %refs_10_.1), channel_id=1, source_target_pairs={{0,64},{1,65},{2,66},{3,67},{4,68},{5,69},{6,70},{7,71},{8,72},{9,... | collective-permute-start | bytes 786440 | tf_op jit(solution)/shard_map/ppermute | solution.py:29
  28.7 2.8 %collective-permute-start.13 = (bf16[256,512]{1,0:T(8,128)(2,1)}, bf16[256,512]{1,0:T(8,128)(2,1)}, u32[]{:S(2)}, u32[]{:S(2)}) collective-permute-start(bf16[256,512]{1,0:T(8,128)(2,1)} %refs_10_.1), channel_id=1, source_target_pairs={{0,96},{1,97},{2,98},{3,99},{4,100},{5,101},{6,102},{7,103},{8,104... | collective-permute-start | bytes 786440 | tf_op jit(solution)/shard_map/ppermute | solution.py:29
  32.1 2.5 %fusion.2 = (f16[2,136,512]{2,1,0:T(8,128)(2,1)S(1)}, f16[2,136,512]{2,1,0:T(8,128)(2,1)}, f16[2,136,512]{2,1,0:T(8,128)(2,1)S(1)}) fusion(f32[8,136,512]{2,1,0:T(8,128)S(1)} %collective-permute-done, f32[8,136,512]{2,1,0:T(8,128)} %teacher.2), kind=kLoop, calls=%fused_computation.5 | loop fusion | flops 835584 | bytes 4177920 | tf_op jit(solution)/shard_map/convert_element_type | solution.py:267
  35.2 2.5 %collective-permute-start.2 = (f16[2,136,512]{2,1,0:T(8,128)(2,1)S(1)}, f16[2,136,512]{2,1,0:T(8,128)(2,1)S(1)}, u32[]{:S(2)}, u32[]{:S(2)}) collective-permute-start(f16[2,136,512]{2,1,0:T(8,128)(2,1)S(1)} %get-tuple-element.41), channel_id=1, source_target_pairs={{0,4},{1,5},{2,6},{3,7},{4,0},{5,1},{6,2},{7,3},{8,12},{9,13},{10,... | collective-permute-start | bytes 835592 | tf_op jit(solution)/shard_map/ppermute | solution.py:29
  37.7 1.8 %collective-permute-start.1 = (f16[2,136,512]{2,1,0:T(8,128)(2,1)S(1)}, f16[2,136,512]{2,1,0:T(8,128)(2,1)}, u32[]{:S(2)}, u32[]{:S(2)}) collective-permute-start(f16[2,136,512]{2,1,0:T(8,128)(2,1)S(1)} %get-tuple-element.39), channel_id=1, source_target_pairs={{0,2},{1,3},{2,4},{3,5},{4,6},{5,7},{6,0},{7,1},{8,10},{9,11},{10,... | collective-permute-start | bytes 835592 | tf_op jit(solution)/shard_map/ppermute | solution.py:29
  40.9 3.7 %student.1 = (f32[128,512]{1,0:T(8,128)}, f32[3,128,512]{2,1,0:T(8,128)}, bf16[512,1024]{1,0:T(8,128)(2,1)}, bf16[1024,512]{1,0:T(8,128)(2,1)}) custom-call(s32[1]{0:T(128)} %bitcast.index_ref, bf16[128,4096]{1,0:T(8,128)(2,1)} %refs_3_.7, bf16[128,4096]{1,0:T(8,128)(2,1)} %refs_3_.7, bf16[128,4096]{1,0:T(8,128)(2,1)} %refs_3_.7, bf16[128,4096]{1,0:T(8,128)(2,1)} %refs_3_.7, ...), custom_call_target="tpu_custom_call" | custom-call | tf_op jit(solution)/shard_map/student/pallas_call | solution.py:169
  45.9 3.8 %collective-permute-start.16 = (f16[128,512]{1,0:T(8,128)(2,1)S(1)}, f16[128,512]{1,0:T(8,128)(2,1)S(1)}, u32[]{:S(2)}, u32[]{:S(2)}) collective-permute-start(f16[128,512]{1,0:T(8,128)(2,1)S(1)} %get-tuple-element.46), channel_id=1, source_target_pairs={{0,8},{1,9},{2,10},{3,11},{4,12},{5,13},{6,14},{7,15},{8,16},{9,17... | collective-permute-start | bytes 393224 | tf_op jit(solution)/shard_map/ppermute | solution.py:29
  49.8 4.3 %collective-permute-start.15 = (f16[128,512]{1,0:T(8,128)(2,1)S(1)}, f16[128,512]{1,0:T(8,128)(2,1)S(1)}, u32[]{:S(2)}, u32[]{:S(2)}) collective-permute-start(f16[128,512]{1,0:T(8,128)(2,1)S(1)} %get-tuple-element.47), channel_id=1, source_target_pairs={{0,16},{1,17},{2,18},{3,19},{4,20},{5,21},{6,22},{7,23},{8,24},{9,... | collective-permute-start | bytes 393224 | tf_op jit(solution)/shard_map/ppermute | solution.py:29
  54.1 3.9 %collective-permute-start.14 = (f16[128,512]{1,0:T(8,128)(2,1)S(1)}, f16[128,512]{1,0:T(8,128)(2,1)S(1)}, u32[]{:S(2)}, u32[]{:S(2)}) collective-permute-start(f16[128,512]{1,0:T(8,128)(2,1)S(1)} %get-tuple-element.45), channel_id=1, source_target_pairs={{0,24},{1,25},{2,26},{3,27},{4,28},{5,29},{6,30},{7,31},{8,0},{9,1... | collective-permute-start | bytes 393224 | tf_op jit(solution)/shard_map/ppermute | solution.py:29
  59.4 3.8 %collective-permute-done.15 = f16[128,512]{1,0:T(8,128)(2,1)S(1)} collective-permute-done((f16[128,512]{1,0:T(8,128)(2,1)S(1)}, f16[128,512]{1,0:T(8,128)(2,1)S(1)}, u32[]{:S(2)}, u32[]{:S(2)}) %collective-permute-start.15) | collective-permute-done | bytes 131104 | tf_op jit(solution)/shard_map/ppermute | solution.py:29
  63.2 2.1 %collective-permute-done.14 = f16[128,512]{1,0:T(8,128)(2,1)S(1)} collective-permute-done((f16[128,512]{1,0:T(8,128)(2,1)S(1)}, f16[128,512]{1,0:T(8,128)(2,1)S(1)}, u32[]{:S(2)}, u32[]{:S(2)}) %collective-permute-start.14) | collective-permute-done | bytes 131104 | tf_op jit(solution)/shard_map/ppermute | solution.py:29
  71.4 2.3 %collective-permute-start.23 = (bf16[128,512]{1,0:T(8,128)(2,1)S(1)}, bf16[128,512]{1,0:T(8,128)(2,1)S(1)}, u32[]{:S(2)}, u32[]{:S(2)}) collective-permute-start(bf16[128,512]{1,0:T(8,128)(2,1)S(1)} %subtract_convert_fusion.refs_0_), channel_id=1, source_target_pairs={{0,8},{1,9},{2,10},{3,11},{4,12},{5,13},{6,14},{7,15},{8,16},{9,17... | collective-permute-start | bytes 393224 | tf_op jit(solution)/shard_map/ppermute | solution.py:29
  73.6 3.2 %collective-permute-start.24 = (bf16[128,512]{1,0:T(8,128)(2,1)S(1)}, bf16[128,512]{1,0:T(8,128)(2,1)S(1)}, u32[]{:S(2)}, u32[]{:S(2)}) collective-permute-start(bf16[128,512]{1,0:T(8,128)(2,1)S(1)} %subtract_convert_fusion.refs_0_), channel_id=1, source_target_pairs={{0,16},{1,17},{2,18},{3,19},{4,20},{5,21},{6,22},{7,23},{8,24},{9,... | collective-permute-start | bytes 393224 | tf_op jit(solution)/shard_map/ppermute | solution.py:29
  78.4 2.3 %collective-permute-done.23.refs_1_ = bf16[128,512]{1,0:T(8,128)(2,1)S(1)} collective-permute-done((bf16[128,512]{1,0:T(8,128)(2,1)S(1)}, bf16[128,512]{1,0:T(8,128)(2,1)S(1)}, u32[]{:S(2)}, u32[]{:S(2)}) %collective-permute-start.23) | collective-permute-done | bytes 131104 | tf_op jit(solution)/shard_map/ppermute | solution.py:29
  80.7 7.4 %collective-permute-done.24.refs_2_ = bf16[128,512]{1,0:T(8,128)(2,1)S(1)} collective-permute-done((bf16[128,512]{1,0:T(8,128)(2,1)S(1)}, bf16[128,512]{1,0:T(8,128)(2,1)S(1)}, u32[]{:S(2)}, u32[]{:S(2)}) %collective-permute-start.24) | collective-permute-done | bytes 131104 | tf_op jit(solution)/shard_map/ppermute | solution.py:29
  88.8 3.5 %hidden_grad.1 = (f32[8,128,256]{2,1,0:T(8,128)}, f32[8,128,256]{2,1,0:T(8,128)}) custom-call(s32[1]{0:T(128)} %bitcast.index_ref, bf16[128,512]{1,0:T(8,128)(2,1)} %copy-done, bf16[128,512]{1,0:T(8,128)(2,1)} %copy-done.1, bf16[128,512]{1,0:T(8,128)(2,1)} %copy-done.2, bf16[128,512]{1,0:T(8,128)(2,1)} %copy-done.3, bf16[1024,512]{1,0:T(8,128)(2,1)} %get-tuple-element.21.refs_4_), custom_call_target="tpu_custom_call" | custom-call | tf_op jit(solution)/shard_map/hidden_grad/pallas_call | solution.py:241
  92.5 3.8 %collective-permute-start.21 = (f32[1,128]{1,0:T(1,128)S(1)}, f32[1,128]{1,0:T(1,128)S(1)}, u32[]{:S(2)}, u32[]{:S(2)}) collective-permute-start(f32[1,128]{1,0:T(1,128)S(1)} %bitcast_multiply_fusion), channel_id=1, source_target_pairs={{0,128},{1,129},{2,130},{3,131},{4,132},{5,133},{6,134},{7,135},{8... | collective-permute-start | bytes 1544 | tf_op jit(solution)/shard_map/ppermute | solution.py:29
  98.5 3.0 %collective-permute-done.20 = f32[1,128]{1,0:T(1,128)S(1)} collective-permute-done((f32[1,128]{1,0:T(1,128)S(1)}, f32[1,128]{1,0:T(1,128)S(1)}, u32[]{:S(2)}, u32[]{:S(2)}) %collective-permute-start.20) | collective-permute-done | bytes 544 | tf_op jit(solution)/shard_map/ppermute | solution.py:29
  102.7 1.9 %collective-permute-start.29 = (bf16[2,128,256]{2,1,0:T(8,128)(2,1)S(1)}, bf16[2,128,256]{2,1,0:T(8,128)(2,1)S(1)}, u32[]{:S(2)}, u32[]{:S(2)}) collective-permute-start(bf16[2,128,256]{2,1,0:T(8,128)(2,1)S(1)} %get-tuple-element.43), channel_id=1, source_target_pairs={{0,6},{1,7},{2,0},{3,1},{4,2},{5,3},{6,4},{7,5},{8,14},{9,15},{10,... | collective-permute-start | bytes 393224 | tf_op jit(solution)/shard_map/ppermute | solution.py:29
  104.7 1.8 %collective-permute-start.27 = (bf16[2,128,256]{2,1,0:T(8,128)(2,1)S(1)}, bf16[2,128,256]{2,1,0:T(8,128)(2,1)S(1)}, u32[]{:S(2)}, u32[]{:S(2)}) collective-permute-start(bf16[2,128,256]{2,1,0:T(8,128)(2,1)S(1)} %get-tuple-element.42), channel_id=1, source_target_pairs={{0,2},{1,3},{2,4},{3,5},{4,6},{5,7},{6,0},{7,1},{8,10},{9,11},{10,... | collective-permute-start | bytes 393224 | tf_op jit(solution)/shard_map/ppermute | solution.py:29
  107.1 2.9 %head_grad.1 = (f32[256,512]{1,0:T(8,128)}, bf16[256,512]{1,0:T(8,128)(2,1)}, bf16[256,512]{1,0:T(8,128)(2,1)}, bf16[256,512]{1,0:T(8,128)(2,1)}) custom-call(bf16[512,1024]{1,0:T(8,128)(2,1)} %get-tuple-element.24.hidden_ref, bf16[128,512]{1,0:T(8,128)(2,1)} %copy-done, bf16[128,512]{1,0:T(8,128)(2,1)} %copy-done.1, bf16[128,512]{1,0:T(8,128)(2,1)} %copy-done.2, ...), custom_call_target="tpu_custom_call" | custom-call | tf_op jit(solution)/shard_map/head_grad/pallas_call | solution.py:207
  111.6 3.0 %collective-permute-start.33 = (bf16[256,512]{1,0:T(8,128)(2,1)}, bf16[256,512]{1,0:T(8,128)(2,1)S(1)}, u32[]{:S(2)}, u32[]{:S(2)}) collective-permute-start(bf16[256,512]{1,0:T(8,128)(2,1)} %get-tuple-element.27), channel_id=1, source_target_pairs={{0,64},{1,65},{2,66},{3,67},{4,68},{5,69},{6,70},{7,71},{8,72},{9,... | collective-permute-start | bytes 786440 | tf_op jit(solution)/shard_map/ppermute | solution.py:29
  116.5 1.9 %collective-permute-start.31 = (bf16[128,256]{1,0:T(8,128)(2,1)S(1)}, bf16[128,256]{1,0:T(8,128)(2,1)S(1)}, u32[]{:S(2)}, u32[]{:S(2)}) collective-permute-start(bf16[128,256]{1,0:T(8,128)(2,1)S(1)} %get-tuple-element.49), channel_id=1, source_target_pairs={{0,128},{1,136},{2,144},{3,152},{4,132},{5,140},{6,148},{7,156},{8... | collective-permute-start | bytes 196616 | tf_op jit(solution)/shard_map/ppermute | solution.py:29
  118.4 5.5 %collective-permute-start.30 = (bf16[128,256]{1,0:T(8,128)(2,1)S(1)}, bf16[128,256]{1,0:T(8,128)(2,1)S(1)}, u32[]{:S(2)}, u32[]{:S(2)}) collective-permute-start(bf16[128,256]{1,0:T(8,128)(2,1)S(1)} %get-tuple-element.48), channel_id=1, source_target_pairs={{0,0},{1,8},{2,16},{3,24},{4,4},{5,12},{6,20},{7,28},{8,1},{9,9},{... | collective-permute-start | bytes 196616 | tf_op jit(solution)/shard_map/ppermute | solution.py:29
  124.6 2.0 %convert_add_fusion = f32[256,512]{1,0:T(8,128)} fusion(bf16[256,512]{1,0:T(8,128)(2,1)S(1)} %collective-permute-done.34, bf16[256,512]{1,0:T(8,128)(2,1)S(1)} %collective-permute-done.33, f32[256,512]{1,0:T(8,128)} %get-tuple-element.25, bf16[256,512]{1,0:T(8,128)(2,1)S(1)} %collective-permute-done.32), kind=kLoop, calls=%fused_computation.10 | loop fusion | flops 786432 | bytes 1835008 | tf_op jit(solution)/shard_map/add | solution.py:336
  126.5 2.8 %collective-permute-done.30 = bf16[128,256]{1,0:T(8,128)(2,1)S(1)} collective-permute-done((bf16[128,256]{1,0:T(8,128)(2,1)S(1)}, bf16[128,256]{1,0:T(8,128)(2,1)S(1)}, u32[]{:S(2)}, u32[]{:S(2)}) %collective-permute-start.30) | collective-permute-done | bytes 65568 | tf_op jit(solution)/shard_map/ppermute | solution.py:29
  (99 shorter events, 25.5 us)
Async XLA Ops:
  5.1 26.4 %collective-permute-start = (f32[8,136,512]{2,1,0:T(8,128)}, f32[8,136,512]{2,1,0:T(8,128)S(1)}, u32[]{:S(2)}, u32[]{:S(2)}) collective-permute-start(f32[8,136,512]{2,1,0:T(8,128)} %teacher.3), channel_id=1, source_target_pairs={{0,1},{1,0},{2,3},{3,2},{4,5},{5,4},{6,7},{7,6},{8,9},{9,8},{10,11... | collective-permute-start | bytes 6684680 | tf_op jit(solution)/shard_map/ppermute | solution.py:29
  6.9 11.3 %collective-permute-start.5 = (bf16[2,128,256]{2,1,0:T(8,128)(2,1)}, bf16[2,128,256]{2,1,0:T(8,128)(2,1)S(1)}, u32[]{:S(2)}, u32[]{:S(2)}) collective-permute-start(bf16[2,128,256]{2,1,0:T(8,128)(2,1)} %get-tuple-element.16), channel_id=1, source_target_pairs={{0,8},{1,9},{2,10},{3,11},{4,12},{5,13},{6,14},{7,15},{8,16},{9,17... | collective-permute-start | bytes 393224 | tf_op jit(solution)/shard_map/ppermute | solution.py:29
  10.2 15.3 %collective-permute-start.6 = (bf16[2,128,256]{2,1,0:T(8,128)(2,1)}, bf16[2,128,256]{2,1,0:T(8,128)(2,1)S(1)}, u32[]{:S(2)}, u32[]{:S(2)}) collective-permute-start(bf16[2,128,256]{2,1,0:T(8,128)(2,1)} %get-tuple-element.17), channel_id=1, source_target_pairs={{0,16},{1,17},{2,18},{3,19},{4,20},{5,21},{6,22},{7,23},{8,24},{9,... | collective-permute-start | bytes 393224 | tf_op jit(solution)/shard_map/ppermute | solution.py:29
  15.6 13.1 %collective-permute-start.7 = (bf16[2,128,256]{2,1,0:T(8,128)(2,1)}, bf16[2,128,256]{2,1,0:T(8,128)(2,1)S(1)}, u32[]{:S(2)}, u32[]{:S(2)}) collective-permute-start(bf16[2,128,256]{2,1,0:T(8,128)(2,1)} %get-tuple-element.18), channel_id=1, source_target_pairs={{0,24},{1,25},{2,26},{3,27},{4,28},{5,29},{6,30},{7,31},{8,0},{9,1... | collective-permute-start | bytes 393224 | tf_op jit(solution)/shard_map/ppermute | solution.py:29
  18.3 13.3 %collective-permute-start.8 = (bf16[2,128,256]{2,1,0:T(8,128)(2,1)S(1)}, bf16[2,128,256]{2,1,0:T(8,128)(2,1)S(1)}, u32[]{:S(2)}, u32[]{:S(2)}) collective-permute-start(bf16[2,128,256]{2,1,0:T(8,128)(2,1)S(1)} %collective-permute-done.5.refs_4_), channel_id=1, source_target_pairs={{0,1},{1,0},{2,3},{3,2},{4,5},{5,4},{6,7},{7,6},{8,9},{9,8},{10,11... | collective-permute-start | bytes 393224 | tf_op jit(solution)/shard_map/ppermute | solution.py:29
  18.3 19.5 %collective-permute-start.11 = (bf16[256,512]{1,0:T(8,128)(2,1)}, bf16[256,512]{1,0:T(8,128)(2,1)}, u32[]{:S(2)}, u32[]{:S(2)}) collective-permute-start(bf16[256,512]{1,0:T(8,128)(2,1)} %refs_10_.1), channel_id=1, source_target_pairs={{0,32},{1,33},{2,34},{3,35},{4,36},{5,37},{6,38},{7,39},{8,40},{9,... | collective-permute-start | bytes 786440 | tf_op jit(solution)/shard_map/ppermute | solution.py:29
  25.5 14.0 %collective-permute-start.12 = (bf16[256,512]{1,0:T(8,128)(2,1)}, bf16[256,512]{1,0:T(8,128)(2,1)}, u32[]{:S(2)}, u32[]{:S(2)}) collective-permute-start(bf16[256,512]{1,0:T(8,128)(2,1)} %refs_10_.1), channel_id=1, source_target_pairs={{0,64},{1,65},{2,66},{3,67},{4,68},{5,69},{6,70},{7,71},{8,72},{9,... | collective-permute-start | bytes 786440 | tf_op jit(solution)/shard_map/ppermute | solution.py:29
  28.7 12.2 %collective-permute-start.13 = (bf16[256,512]{1,0:T(8,128)(2,1)}, bf16[256,512]{1,0:T(8,128)(2,1)}, u32[]{:S(2)}, u32[]{:S(2)}) collective-permute-start(bf16[256,512]{1,0:T(8,128)(2,1)} %refs_10_.1), channel_id=1, source_target_pairs={{0,96},{1,97},{2,98},{3,99},{4,100},{5,101},{6,102},{7,103},{8,104... | collective-permute-start | bytes 786440 | tf_op jit(solution)/shard_map/ppermute | solution.py:29
  31.6 3.6 %collective-permute-start.10 = (bf16[2,128,256]{2,1,0:T(8,128)(2,1)S(1)}, bf16[2,128,256]{2,1,0:T(8,128)(2,1)S(1)}, u32[]{:S(2)}, u32[]{:S(2)}) collective-permute-start(bf16[2,128,256]{2,1,0:T(8,128)(2,1)S(1)} %collective-permute-done.7.refs_6_), channel_id=1, source_target_pairs={{0,1},{1,0},{2,3},{3,2},{4,5},{5,4},{6,7},{7,6},{8,9},{9,8},{10,11... | collective-permute-start | bytes 393224 | tf_op jit(solution)/shard_map/ppermute | solution.py:29
  34.6 19.5 %collective-permute-start.3 = (f16[2,136,512]{2,1,0:T(8,128)(2,1)}, f16[2,136,512]{2,1,0:T(8,128)(2,1)S(1)}, u32[]{:S(2)}, u32[]{:S(2)}) collective-permute-start(f16[2,136,512]{2,1,0:T(8,128)(2,1)} %get-tuple-element.40), channel_id=1, source_target_pairs={{0,6},{1,7},{2,0},{3,1},{4,2},{5,3},{6,4},{7,5},{8,14},{9,15},{10,... | collective-permute-start | bytes 835592 | tf_op jit(solution)/shard_map/ppermute | solution.py:29
  35.2 22.7 %collective-permute-start.2 = (f16[2,136,512]{2,1,0:T(8,128)(2,1)S(1)}, f16[2,136,512]{2,1,0:T(8,128)(2,1)S(1)}, u32[]{:S(2)}, u32[]{:S(2)}) collective-permute-start(f16[2,136,512]{2,1,0:T(8,128)(2,1)S(1)} %get-tuple-element.41), channel_id=1, source_target_pairs={{0,4},{1,5},{2,6},{3,7},{4,0},{5,1},{6,2},{7,3},{8,12},{9,13},{10,... | collective-permute-start | bytes 835592 | tf_op jit(solution)/shard_map/ppermute | solution.py:29
  37.7 20.2 %collective-permute-start.1 = (f16[2,136,512]{2,1,0:T(8,128)(2,1)S(1)}, f16[2,136,512]{2,1,0:T(8,128)(2,1)}, u32[]{:S(2)}, u32[]{:S(2)}) collective-permute-start(f16[2,136,512]{2,1,0:T(8,128)(2,1)S(1)} %get-tuple-element.39), channel_id=1, source_target_pairs={{0,2},{1,3},{2,4},{3,5},{4,6},{5,7},{6,0},{7,1},{8,10},{9,11},{10,... | collective-permute-start | bytes 835592 | tf_op jit(solution)/shard_map/ppermute | solution.py:29
  45.9 13.5 %collective-permute-start.16 = (f16[128,512]{1,0:T(8,128)(2,1)S(1)}, f16[128,512]{1,0:T(8,128)(2,1)S(1)}, u32[]{:S(2)}, u32[]{:S(2)}) collective-permute-start(f16[128,512]{1,0:T(8,128)(2,1)S(1)} %get-tuple-element.46), channel_id=1, source_target_pairs={{0,8},{1,9},{2,10},{3,11},{4,12},{5,13},{6,14},{7,15},{8,16},{9,17... | collective-permute-start | bytes 393224 | tf_op jit(solution)/shard_map/ppermute | solution.py:29
  49.8 13.5 %collective-permute-start.15 = (f16[128,512]{1,0:T(8,128)(2,1)S(1)}, f16[128,512]{1,0:T(8,128)(2,1)S(1)}, u32[]{:S(2)}, u32[]{:S(2)}) collective-permute-start(f16[128,512]{1,0:T(8,128)(2,1)S(1)} %get-tuple-element.47), channel_id=1, source_target_pairs={{0,16},{1,17},{2,18},{3,19},{4,20},{5,21},{6,22},{7,23},{8,24},{9,... | collective-permute-start | bytes 393224 | tf_op jit(solution)/shard_map/ppermute | solution.py:29
  54.1 11.3 %collective-permute-start.14 = (f16[128,512]{1,0:T(8,128)(2,1)S(1)}, f16[128,512]{1,0:T(8,128)(2,1)S(1)}, u32[]{:S(2)}, u32[]{:S(2)}) collective-permute-start(f16[128,512]{1,0:T(8,128)(2,1)S(1)} %get-tuple-element.45), channel_id=1, source_target_pairs={{0,24},{1,25},{2,26},{3,27},{4,28},{5,29},{6,30},{7,31},{8,0},{9,1... | collective-permute-start | bytes 393224 | tf_op jit(solution)/shard_map/ppermute | solution.py:29
  59.3 7.4 %collective-permute-start.4 = (f16[136,512]{1,0:T(8,128)(2,1)S(1)}, f16[136,512]{1,0:T(8,128)(2,1)S(1)}, u32[]{:S(2)}, u32[]{:S(2)}) collective-permute-start(f16[136,512]{1,0:T(8,128)(2,1)S(1)} %fusion.17), channel_id=1, source_target_pairs={{0,128},{1,129},{2,130},{3,131},{4,132},{5,133},{6,134},{7,135},{8... | collective-permute-start | bytes 417800 | tf_op jit(solution)/shard_map/ppermute | solution.py:29
  67.4 3.7 %collective-permute-start.18 = (f32[5,128]{1,0:T(8,128)S(1)}, f32[5,128]{1,0:T(8,128)S(1)}, u32[]{:S(2)}, u32[]{:S(2)}) collective-permute-start(f32[5,128]{1,0:T(8,128)S(1)} %stack.38), channel_id=1, source_target_pairs={{0,2},{1,3},{2,0},{3,1},{4,6},{5,7},{6,4},{7,5},{8,10},{9,11},{10,... | collective-permute-start | bytes 7688 | tf_op jit(solution)/shard_map/ppermute | solution.py:29
  71.4 9.3 %collective-permute-start.23 = (bf16[128,512]{1,0:T(8,128)(2,1)S(1)}, bf16[128,512]{1,0:T(8,128)(2,1)S(1)}, u32[]{:S(2)}, u32[]{:S(2)}) collective-permute-start(bf16[128,512]{1,0:T(8,128)(2,1)S(1)} %subtract_convert_fusion.refs_0_), channel_id=1, source_target_pairs={{0,8},{1,9},{2,10},{3,11},{4,12},{5,13},{6,14},{7,15},{8,16},{9,17... | collective-permute-start | bytes 393224 | tf_op jit(solution)/shard_map/ppermute | solution.py:29
  73.6 14.4 %collective-permute-start.24 = (bf16[128,512]{1,0:T(8,128)(2,1)S(1)}, bf16[128,512]{1,0:T(8,128)(2,1)S(1)}, u32[]{:S(2)}, u32[]{:S(2)}) collective-permute-start(bf16[128,512]{1,0:T(8,128)(2,1)S(1)} %subtract_convert_fusion.refs_0_), channel_id=1, source_target_pairs={{0,16},{1,17},{2,18},{3,19},{4,20},{5,21},{6,22},{7,23},{8,24},{9,... | collective-permute-start | bytes 393224 | tf_op jit(solution)/shard_map/ppermute | solution.py:29
  76.8 11.2 %collective-permute-start.25 = (bf16[128,512]{1,0:T(8,128)(2,1)S(1)}, bf16[128,512]{1,0:T(8,128)(2,1)S(1)}, u32[]{:S(2)}, u32[]{:S(2)}) collective-permute-start(bf16[128,512]{1,0:T(8,128)(2,1)S(1)} %subtract_convert_fusion.refs_0_), channel_id=1, source_target_pairs={{0,24},{1,25},{2,26},{3,27},{4,28},{5,29},{6,30},{7,31},{8,0},{9,1... | collective-permute-start | bytes 393224 | tf_op jit(solution)/shard_map/ppermute | solution.py:29
  92.3 9.1 %collective-permute-start.26 = (f32[8,128,256]{2,1,0:T(8,128)}, f32[8,128,256]{2,1,0:T(8,128)S(1)}, u32[]{:S(2)}, u32[]{:S(2)}) collective-permute-start(f32[8,128,256]{2,1,0:T(8,128)} %get-tuple-element.23), channel_id=1, source_target_pairs={{0,1},{1,0},{2,3},{3,2},{4,5},{5,4},{6,7},{7,6},{8,9},{9,8},{10,11... | collective-permute-start | bytes 3145736 | tf_op jit(solution)/shard_map/ppermute | solution.py:29
  92.4 6.1 %collective-permute-start.22 = (f32[1,128]{1,0:T(1,128)S(1)}, f32[1,128]{1,0:T(1,128)S(1)}, u32[]{:S(2)}, u32[]{:S(2)}) collective-permute-start(f32[1,128]{1,0:T(1,128)S(1)} %bitcast_multiply_fusion), channel_id=1, source_target_pairs={{0,132},{1,133},{2,134},{3,135},{4,128},{5,129},{6,130},{7,131},{8... | collective-permute-start | bytes 1544 | tf_op jit(solution)/shard_map/ppermute | solution.py:29
  92.5 6.0 %collective-permute-start.21 = (f32[1,128]{1,0:T(1,128)S(1)}, f32[1,128]{1,0:T(1,128)S(1)}, u32[]{:S(2)}, u32[]{:S(2)}) collective-permute-start(f32[1,128]{1,0:T(1,128)S(1)} %bitcast_multiply_fusion), channel_id=1, source_target_pairs={{0,128},{1,129},{2,130},{3,131},{4,132},{5,133},{6,134},{7,135},{8... | collective-permute-start | bytes 1544 | tf_op jit(solution)/shard_map/ppermute | solution.py:29
  96.4 5.1 %collective-permute-start.20 = (f32[1,128]{1,0:T(1,128)S(1)}, f32[1,128]{1,0:T(1,128)S(1)}, u32[]{:S(2)}, u32[]{:S(2)}) collective-permute-start(f32[1,128]{1,0:T(1,128)S(1)} %bitcast_multiply_fusion), channel_id=1, source_target_pairs={{0,4},{1,5},{2,6},{3,7},{4,0},{5,1},{6,2},{7,3},{8,12},{9,13},{10,... | collective-permute-start | bytes 1544 | tf_op jit(solution)/shard_map/ppermute | solution.py:29
  102.7 11.9 %collective-permute-start.29 = (bf16[2,128,256]{2,1,0:T(8,128)(2,1)S(1)}, bf16[2,128,256]{2,1,0:T(8,128)(2,1)S(1)}, u32[]{:S(2)}, u32[]{:S(2)}) collective-permute-start(bf16[2,128,256]{2,1,0:T(8,128)(2,1)S(1)} %get-tuple-element.43), channel_id=1, source_target_pairs={{0,6},{1,7},{2,0},{3,1},{4,2},{5,3},{6,4},{7,5},{8,14},{9,15},{10,... | collective-permute-start | bytes 393224 | tf_op jit(solution)/shard_map/ppermute | solution.py:29
  104.5 11.0 %collective-permute-start.28 = (bf16[2,128,256]{2,1,0:T(8,128)(2,1)S(1)}, bf16[2,128,256]{2,1,0:T(8,128)(2,1)S(1)}, u32[]{:S(2)}, u32[]{:S(2)}) collective-permute-start(bf16[2,128,256]{2,1,0:T(8,128)(2,1)S(1)} %get-tuple-element.44), channel_id=1, source_target_pairs={{0,4},{1,5},{2,6},{3,7},{4,0},{5,1},{6,2},{7,3},{8,12},{9,13},{10,... | collective-permute-start | bytes 393224 | tf_op jit(solution)/shard_map/ppermute | solution.py:29
  104.7 10.8 %collective-permute-start.27 = (bf16[2,128,256]{2,1,0:T(8,128)(2,1)S(1)}, bf16[2,128,256]{2,1,0:T(8,128)(2,1)S(1)}, u32[]{:S(2)}, u32[]{:S(2)}) collective-permute-start(bf16[2,128,256]{2,1,0:T(8,128)(2,1)S(1)} %get-tuple-element.42), channel_id=1, source_target_pairs={{0,2},{1,3},{2,4},{3,5},{4,6},{5,7},{6,0},{7,1},{8,10},{9,11},{10,... | collective-permute-start | bytes 393224 | tf_op jit(solution)/shard_map/ppermute | solution.py:29
  110.1 13.9 %collective-permute-start.34 = (bf16[256,512]{1,0:T(8,128)(2,1)}, bf16[256,512]{1,0:T(8,128)(2,1)S(1)}, u32[]{:S(2)}, u32[]{:S(2)}) collective-permute-start(bf16[256,512]{1,0:T(8,128)(2,1)} %get-tuple-element.28), channel_id=1, source_target_pairs={{0,32},{1,33},{2,34},{3,35},{4,36},{5,37},{6,38},{7,39},{8,40},{9,... | collective-permute-start | bytes 786440 | tf_op jit(solution)/shard_map/ppermute | solution.py:29
  111.6 13.0 %collective-permute-start.33 = (bf16[256,512]{1,0:T(8,128)(2,1)}, bf16[256,512]{1,0:T(8,128)(2,1)S(1)}, u32[]{:S(2)}, u32[]{:S(2)}) collective-permute-start(bf16[256,512]{1,0:T(8,128)(2,1)} %get-tuple-element.27), channel_id=1, source_target_pairs={{0,64},{1,65},{2,66},{3,67},{4,68},{5,69},{6,70},{7,71},{8,72},{9,... | collective-permute-start | bytes 786440 | tf_op jit(solution)/shard_map/ppermute | solution.py:29
  114.6 10.0 %collective-permute-start.32 = (bf16[256,512]{1,0:T(8,128)(2,1)}, bf16[256,512]{1,0:T(8,128)(2,1)S(1)}, u32[]{:S(2)}, u32[]{:S(2)}) collective-permute-start(bf16[256,512]{1,0:T(8,128)(2,1)} %get-tuple-element.26), channel_id=1, source_target_pairs={{0,96},{1,97},{2,98},{3,99},{4,100},{5,101},{6,102},{7,103},{8,104... | collective-permute-start | bytes 786440 | tf_op jit(solution)/shard_map/ppermute | solution.py:29
  116.5 10.0 %collective-permute-start.31 = (bf16[128,256]{1,0:T(8,128)(2,1)S(1)}, bf16[128,256]{1,0:T(8,128)(2,1)S(1)}, u32[]{:S(2)}, u32[]{:S(2)}) collective-permute-start(bf16[128,256]{1,0:T(8,128)(2,1)S(1)} %get-tuple-element.49), channel_id=1, source_target_pairs={{0,128},{1,136},{2,144},{3,152},{4,132},{5,140},{6,148},{7,156},{8... | collective-permute-start | bytes 196616 | tf_op jit(solution)/shard_map/ppermute | solution.py:29
  118.4 11.0 %collective-permute-start.30 = (bf16[128,256]{1,0:T(8,128)(2,1)S(1)}, bf16[128,256]{1,0:T(8,128)(2,1)S(1)}, u32[]{:S(2)}, u32[]{:S(2)}) collective-permute-start(bf16[128,256]{1,0:T(8,128)(2,1)S(1)} %get-tuple-element.48), channel_id=1, source_target_pairs={{0,0},{1,8},{2,16},{3,24},{4,4},{5,12},{6,20},{7,28},{8,1},{9,9},{... | collective-permute-start | bytes 196616 | tf_op jit(solution)/shard_map/ppermute | solution.py:29
  (15 other events, 104.7 us)

commit v8 on v7

--- a/solution.py
+++ b/solution.py
@@ -43,6 +43,13 @@
 
 def to_zl(value):
     return send(value, lambda zl, y, zh, x, core: (1 - zl, y, zh, x, core))
+
+
+def round_ring(to, values, sign=1):
+    received = []
+    for step, value in zip((1, 2, 3), values):
+        received.append(to(value, sign * step))
+    return received
 
 
 def to_core(value):
@@ -254,23 +261,24 @@
     index = lax.axis_index(ALL).reshape(1)
 
     halves = picked_blocks(index, student_hidden)
-    near = [to_zh(halves[k - 1], k) for k in (1, 2, 3)]
-    head_slots = [student_head] + [to_y(student_head, j) for j in (1, 2, 3)]
+    near = round_ring(to_zh, halves)
+    head_slots = [student_head, *round_ring(to_y, [student_head] * 3)]
     far = [to_core(half) for half in near]
 
     other = teacher_parts(index, teacher_hidden, teacher_gain, teacher_head, 1)
     other = to_core(other)
     parts = teacher_parts(index, teacher_hidden, teacher_gain, teacher_head, 0)
     by_x = parts[:2] + other[:2]
-    for step in (1, 2, 3):
-        part = parts[2 * step : 2 * step + 2] + other[2 * step : 2 * step + 2]
-        by_x = by_x + to_x(part.astype(f16), step).astype(f32)
+    pieces = [
+        (parts[2 * step : 2 * step + 2] + other[2 * step : 2 * step + 2]).astype(f16) for step in (1, 2, 3)
+    ]
+    for piece in round_ring(to_x, pieces):
+        by_x = by_x + piece.astype(f32)
     teacher = by_x[0] + to_zl(by_x[1].astype(f16)).astype(f32)
 
     student, parts, hidden, head = student_parts(index, student_hidden, near, far, head_slots)
-    parts = parts.astype(f16)
-    for k in (1, 2, 3):
-        student = student + to_zh(parts[k - 1], -k).astype(f32)
+    for part in round_ring(to_zh, parts.astype(f16), -1):
+        student = student + part.astype(f32)
 
     row_scale = lax.rsqrt(teacher[128, :128] * (8 / DT) + epsilon)
     teacher = teacher[:128] * row_scale[:, None]
@@ -327,17 +335,19 @@
         [lax.dynamic_slice_in_dim(kl, book ^ i, 1, 0) for i in range(C)]
     )
 
-    grad_slots = [score_grad] + [to_zh(score_grad, k) for k in (1, 2, 3)]
+    grad_slots = [score_grad, *round_ring(to_zh, [score_grad] * 3)]
     own, other = hidden_grad_parts(index, grad_slots, head)
     other = to_core(other)
     head_grad, *parts = head_grad_parts(hidden, grad_slots)
-    parts = [to_y(parts[j - 1], -j) for j in (1, 2, 3)]
+    parts = round_ring(to_y, parts, -1)
     for part in parts:
         head_grad = head_grad + part.astype(f32)
     by_x = own[:2] + other[:2]
-    for step in (1, 2, 3):
-        part = own[2 * step : 2 * step + 2] + other[2 * step : 2 * step + 2]
-        by_x = by_x + to_x(part.astype(bf16), step).astype(f32)
+    pieces = [
+        (own[2 * step : 2 * step + 2] + other[2 * step : 2 * step + 2]).astype(bf16) for step in (1, 2, 3)
+    ]
+    for piece in round_ring(to_x, pieces):
+        by_x = by_x + piece.astype(f32)
 
     def home(zl, y, zh, x, core):
         return zl, y, x % 2 * 2 + core, x // 2 * 2 + zh // 2, zh % 2

time: 132 us -> 132 us (level)
  no operation moved by 1% of the time
where the time goes in v8:
time: 132 us; the launch traced here: 130 us
  starting transfers between devices  67.2 us (51%)
  waiting for transfers between devices  28.6 us (22%)
  Pallas kernels  20.8 us (16%)
  other arithmetic  11.5 us (9%)
    ppermute x35, starting transfers between devices, send(): return lax.ppermute(value, ALL, pairs)  67.2 us
    ppermute x35, waiting for transfers between devices, send(): return lax.ppermute(value, ALL, pairs)  28.6 us
    pallas_call x2, Pallas kernels, teacher_parts(): pl.pallas_call(teacher_kernel, grid_spec=pltpu.PrefetchScalarGridSpec(num...  8.82 us
    pallas_call x1, Pallas kernels, student_parts(): pl.pallas_call(student_kernel, grid_spec=pltpu.PrefetchScalarGridSpec(num...  3.68 us
    pallas_call x1, Pallas kernels, hidden_grad_parts(): pl.pallas_call(hidden_grad_kernel, in_specs=[pl.BlockSpec(memory_space=pl...  3.53 us
    pallas_call x1, Pallas kernels, head_grad_parts(): pl.pallas_call(head_grad_kernel, out_shape=(jax.ShapeDtypeStruct((256, 51...  2.94 us
  transfers between devices with their start and end apart: 35, of which 13 were waited for; matrix products, arithmetic and copies ran while one was open for 7% of the time, Pallas kernels for 10%

profile of v8, /device:TPU:2, one launch (start us, length us, event | category | flops | bytes accessed | tf_op | source)
XLA Modules:
  0.0 130.0 jit_solution(4440026228681713786)
XLA Ops:
  0.6 4.5 %teacher.3 = f32[8,136,512]{2,1,0:T(8,128)} custom-call(s32[1]{0:T(128)} %bitcast.index_ref, bf16[128,512]{1,0:T(8,128)(2,1)} %hidden_ref.3, bf16[512]{0:T(512)(128)(2,1)} %gain_ref.3, bf16[512,8192]{1,0:T(8,128)(2,1)} %refs_3_.5, bf16[512,8192]{1,0:T(8,128)(2,1)} %refs_3_.5, bf16[512,8192]{1,0:T(8,128)(2,1)} %refs_3_.5, bf16[512,8192]{1,0:T(8,128)(2,1)} %refs_3_.5), custom_call_target="tpu_custom_call" | custom-call | tf_op jit(solution)/shard_map/teacher/pallas_call | solution.py:132
  5.1 1.8 %pick.1 = (bf16[2,128,256]{2,1,0:T(8,128)(2,1)}, bf16[2,128,256]{2,1,0:T(8,128)(2,1)}, bf16[2,128,256]{2,1,0:T(8,128)(2,1)}) custom-call(s32[1]{0:T(128)} %bitcast.index_ref, bf16[128,4096]{1,0:T(8,128)(2,1)} %refs_3_.7, bf16[128,4096]{1,0:T(8,128)(2,1)} %refs_3_.7, bf16[128,4096]{1,0:T(8,128)(2,1)} %refs_3_.7, bf16[128,4096]{1,0:T(8,128)(2,1)} %refs_3_.7, ...), custom_call_target="tpu_custom_call" | custom-call | tf_op jit(solution)/shard_map/pick/pallas_call | solution.py:79
  6.9 3.3 %collective-permute-start.5 = (bf16[2,128,256]{2,1,0:T(8,128)(2,1)}, bf16[2,128,256]{2,1,0:T(8,128)(2,1)S(1)}, u32[]{:S(2)}, u32[]{:S(2)}) collective-permute-start(bf16[2,128,256]{2,1,0:T(8,128)(2,1)} %get-tuple-element.16), channel_id=1, source_target_pairs={{0,8},{1,9},{2,10},{3,11},{4,12},{5,13},{6,14},{7,15},{8,16},{9,17... | collective-permute-start | bytes 393224 | tf_op jit(solution)/shard_map/ppermute | solution.py:29
  10.2 5.4 %collective-permute-start.6 = (bf16[2,128,256]{2,1,0:T(8,128)(2,1)}, bf16[2,128,256]{2,1,0:T(8,128)(2,1)S(1)}, u32[]{:S(2)}, u32[]{:S(2)}) collective-permute-start(bf16[2,128,256]{2,1,0:T(8,128)(2,1)} %get-tuple-element.17), channel_id=1, source_target_pairs={{0,16},{1,17},{2,18},{3,19},{4,20},{5,21},{6,22},{7,23},{8,24},{9,... | collective-permute-start | bytes 393224 | tf_op jit(solution)/shard_map/ppermute | solution.py:29
  15.6 2.7 %collective-permute-start.7 = (bf16[2,128,256]{2,1,0:T(8,128)(2,1)}, bf16[2,128,256]{2,1,0:T(8,128)(2,1)S(1)}, u32[]{:S(2)}, u32[]{:S(2)}) collective-permute-start(bf16[2,128,256]{2,1,0:T(8,128)(2,1)} %get-tuple-element.18), channel_id=1, source_target_pairs={{0,24},{1,25},{2,26},{3,27},{4,28},{5,29},{6,30},{7,31},{8,0},{9,1... | collective-permute-start | bytes 393224 | tf_op jit(solution)/shard_map/ppermute | solution.py:29
  19.9 4.3 %teacher.2 = f32[8,136,512]{2,1,0:T(8,128)} custom-call(s32[1]{0:T(128)} %bitcast.index_ref, bf16[128,512]{1,0:T(8,128)(2,1)} %hidden_ref.3, bf16[512]{0:T(512)(128)(2,1)} %gain_ref.3, bf16[512,8192]{1,0:T(8,128)(2,1)} %refs_3_.5, bf16[512,8192]{1,0:T(8,128)(2,1)} %refs_3_.5, bf16[512,8192]{1,0:T(8,128)(2,1)} %refs_3_.5, bf16[512,8192]{1,0:T(8,128)(2,1)} %refs_3_.5), custom_call_target="tpu_custom_call" | custom-call | tf_op jit(solution)/shard_map/teacher/pallas_call | solution.py:132
  25.5 3.2 %collective-permute-start.12 = (bf16[256,512]{1,0:T(8,128)(2,1)}, bf16[256,512]{1,0:T(8,128)(2,1)}, u32[]{:S(2)}, u32[]{:S(2)}) collective-permute-start(bf16[256,512]{1,0:T(8,128)(2,1)} %refs_10_.1), channel_id=1, source_target_pairs={{0,64},{1,65},{2,66},{3,67},{4,68},{5,69},{6,70},{7,71},{8,72},{9,... | collective-permute-start | bytes 786440 | tf_op jit(solution)/shard_map/ppermute | solution.py:29
  28.7 2.8 %collective-permute-start.13 = (bf16[256,512]{1,0:T(8,128)(2,1)}, bf16[256,512]{1,0:T(8,128)(2,1)}, u32[]{:S(2)}, u32[]{:S(2)}) collective-permute-start(bf16[256,512]{1,0:T(8,128)(2,1)} %refs_10_.1), channel_id=1, source_target_pairs={{0,96},{1,97},{2,98},{3,99},{4,100},{5,101},{6,102},{7,103},{8,104... | collective-permute-start | bytes 786440 | tf_op jit(solution)/shard_map/ppermute | solution.py:29
  32.1 2.5 %fusion.2 = (f16[2,136,512]{2,1,0:T(8,128)(2,1)S(1)}, f16[2,136,512]{2,1,0:T(8,128)(2,1)}, f16[2,136,512]{2,1,0:T(8,128)(2,1)S(1)}) fusion(f32[8,136,512]{2,1,0:T(8,128)S(1)} %collective-permute-done, f32[8,136,512]{2,1,0:T(8,128)} %teacher.2), kind=kLoop, calls=%fused_computation.5 | loop fusion | flops 835584 | bytes 4177920 | tf_op jit(solution)/shard_map/convert_element_type | solution.py:273
  35.2 2.5 %collective-permute-start.2 = (f16[2,136,512]{2,1,0:T(8,128)(2,1)S(1)}, f16[2,136,512]{2,1,0:T(8,128)(2,1)S(1)}, u32[]{:S(2)}, u32[]{:S(2)}) collective-permute-start(f16[2,136,512]{2,1,0:T(8,128)(2,1)S(1)} %get-tuple-element.41), channel_id=1, source_target_pairs={{0,4},{1,5},{2,6},{3,7},{4,0},{5,1},{6,2},{7,3},{8,12},{9,13},{10,... | collective-permute-start | bytes 835592 | tf_op jit(solution)/shard_map/ppermute | solution.py:29
  37.7 1.8 %collective-permute-start.1 = (f16[2,136,512]{2,1,0:T(8,128)(2,1)S(1)}, f16[2,136,512]{2,1,0:T(8,128)(2,1)}, u32[]{:S(2)}, u32[]{:S(2)}) collective-permute-start(f16[2,136,512]{2,1,0:T(8,128)(2,1)S(1)} %get-tuple-element.39), channel_id=1, source_target_pairs={{0,2},{1,3},{2,4},{3,5},{4,6},{5,7},{6,0},{7,1},{8,10},{9,11},{10,... | collective-permute-start | bytes 835592 | tf_op jit(solution)/shard_map/ppermute | solution.py:29
  40.9 3.7 %student.1 = (f32[128,512]{1,0:T(8,128)}, f32[3,128,512]{2,1,0:T(8,128)}, bf16[512,1024]{1,0:T(8,128)(2,1)}, bf16[1024,512]{1,0:T(8,128)(2,1)}) custom-call(s32[1]{0:T(128)} %bitcast.index_ref, bf16[128,4096]{1,0:T(8,128)(2,1)} %refs_3_.7, bf16[128,4096]{1,0:T(8,128)(2,1)} %refs_3_.7, bf16[128,4096]{1,0:T(8,128)(2,1)} %refs_3_.7, bf16[128,4096]{1,0:T(8,128)(2,1)} %refs_3_.7, ...), custom_call_target="tpu_custom_call" | custom-call | tf_op jit(solution)/shard_map/student/pallas_call | solution.py:176
  45.9 3.8 %collective-permute-start.16 = (f16[128,512]{1,0:T(8,128)(2,1)S(1)}, f16[128,512]{1,0:T(8,128)(2,1)S(1)}, u32[]{:S(2)}, u32[]{:S(2)}) collective-permute-start(f16[128,512]{1,0:T(8,128)(2,1)S(1)} %get-tuple-element.46), channel_id=1, source_target_pairs={{0,8},{1,9},{2,10},{3,11},{4,12},{5,13},{6,14},{7,15},{8,16},{9,17... | collective-permute-start | bytes 393224 | tf_op jit(solution)/shard_map/ppermute | solution.py:29
  49.8 4.3 %collective-permute-start.15 = (f16[128,512]{1,0:T(8,128)(2,1)S(1)}, f16[128,512]{1,0:T(8,128)(2,1)S(1)}, u32[]{:S(2)}, u32[]{:S(2)}) collective-permute-start(f16[128,512]{1,0:T(8,128)(2,1)S(1)} %get-tuple-element.47), channel_id=1, source_target_pairs={{0,16},{1,17},{2,18},{3,19},{4,20},{5,21},{6,22},{7,23},{8,24},{9,... | collective-permute-start | bytes 393224 | tf_op jit(solution)/shard_map/ppermute | solution.py:29
  54.1 3.9 %collective-permute-start.14 = (f16[128,512]{1,0:T(8,128)(2,1)S(1)}, f16[128,512]{1,0:T(8,128)(2,1)S(1)}, u32[]{:S(2)}, u32[]{:S(2)}) collective-permute-start(f16[128,512]{1,0:T(8,128)(2,1)S(1)} %get-tuple-element.45), channel_id=1, source_target_pairs={{0,24},{1,25},{2,26},{3,27},{4,28},{5,29},{6,30},{7,31},{8,0},{9,1... | collective-permute-start | bytes 393224 | tf_op jit(solution)/shard_map/ppermute | solution.py:29
  59.4 3.8 %collective-permute-done.15 = f16[128,512]{1,0:T(8,128)(2,1)S(1)} collective-permute-done((f16[128,512]{1,0:T(8,128)(2,1)S(1)}, f16[128,512]{1,0:T(8,128)(2,1)S(1)}, u32[]{:S(2)}, u32[]{:S(2)}) %collective-permute-start.15) | collective-permute-done | bytes 131104 | tf_op jit(solution)/shard_map/ppermute | solution.py:29
  63.2 2.1 %collective-permute-done.14 = f16[128,512]{1,0:T(8,128)(2,1)S(1)} collective-permute-done((f16[128,512]{1,0:T(8,128)(2,1)S(1)}, f16[128,512]{1,0:T(8,128)(2,1)S(1)}, u32[]{:S(2)}, u32[]{:S(2)}) %collective-permute-start.14) | collective-permute-done | bytes 131104 | tf_op jit(solution)/shard_map/ppermute | solution.py:29
  71.4 2.3 %collective-permute-start.23 = (bf16[128,512]{1,0:T(8,128)(2,1)S(1)}, bf16[128,512]{1,0:T(8,128)(2,1)S(1)}, u32[]{:S(2)}, u32[]{:S(2)}) collective-permute-start(bf16[128,512]{1,0:T(8,128)(2,1)S(1)} %subtract_convert_fusion.refs_0_), channel_id=1, source_target_pairs={{0,8},{1,9},{2,10},{3,11},{4,12},{5,13},{6,14},{7,15},{8,16},{9,17... | collective-permute-start | bytes 393224 | tf_op jit(solution)/shard_map/ppermute | solution.py:29
  73.6 3.2 %collective-permute-start.24 = (bf16[128,512]{1,0:T(8,128)(2,1)S(1)}, bf16[128,512]{1,0:T(8,128)(2,1)S(1)}, u32[]{:S(2)}, u32[]{:S(2)}) collective-permute-start(bf16[128,512]{1,0:T(8,128)(2,1)S(1)} %subtract_convert_fusion.refs_0_), channel_id=1, source_target_pairs={{0,16},{1,17},{2,18},{3,19},{4,20},{5,21},{6,22},{7,23},{8,24},{9,... | collective-permute-start | bytes 393224 | tf_op jit(solution)/shard_map/ppermute | solution.py:29
  78.4 2.3 %collective-permute-done.23.refs_1_ = bf16[128,512]{1,0:T(8,128)(2,1)S(1)} collective-permute-done((bf16[128,512]{1,0:T(8,128)(2,1)S(1)}, bf16[128,512]{1,0:T(8,128)(2,1)S(1)}, u32[]{:S(2)}, u32[]{:S(2)}) %collective-permute-start.23) | collective-permute-done | bytes 131104 | tf_op jit(solution)/shard_map/ppermute | solution.py:29
  80.7 7.4 %collective-permute-done.24.refs_2_ = bf16[128,512]{1,0:T(8,128)(2,1)S(1)} collective-permute-done((bf16[128,512]{1,0:T(8,128)(2,1)S(1)}, bf16[128,512]{1,0:T(8,128)(2,1)S(1)}, u32[]{:S(2)}, u32[]{:S(2)}) %collective-permute-start.24) | collective-permute-done | bytes 131104 | tf_op jit(solution)/shard_map/ppermute | solution.py:29
  88.8 3.5 %hidden_grad.1 = (f32[8,128,256]{2,1,0:T(8,128)}, f32[8,128,256]{2,1,0:T(8,128)}) custom-call(s32[1]{0:T(128)} %bitcast.index_ref, bf16[128,512]{1,0:T(8,128)(2,1)} %copy-done, bf16[128,512]{1,0:T(8,128)(2,1)} %copy-done.1, bf16[128,512]{1,0:T(8,128)(2,1)} %copy-done.2, bf16[128,512]{1,0:T(8,128)(2,1)} %copy-done.3, bf16[1024,512]{1,0:T(8,128)(2,1)} %get-tuple-element.21.refs_4_), custom_call_target="tpu_custom_call" | custom-call | tf_op jit(solution)/shard_map/hidden_grad/pallas_call | solution.py:248
  92.5 3.8 %collective-permute-start.21 = (f32[1,128]{1,0:T(1,128)S(1)}, f32[1,128]{1,0:T(1,128)S(1)}, u32[]{:S(2)}, u32[]{:S(2)}) collective-permute-start(f32[1,128]{1,0:T(1,128)S(1)} %bitcast_multiply_fusion), channel_id=1, source_target_pairs={{0,128},{1,129},{2,130},{3,131},{4,132},{5,133},{6,134},{7,135},{8... | collective-permute-start | bytes 1544 | tf_op jit(solution)/shard_map/ppermute | solution.py:29
  98.5 3.0 %collective-permute-done.20 = f32[1,128]{1,0:T(1,128)S(1)} collective-permute-done((f32[1,128]{1,0:T(1,128)S(1)}, f32[1,128]{1,0:T(1,128)S(1)}, u32[]{:S(2)}, u32[]{:S(2)}) %collective-permute-start.20) | collective-permute-done | bytes 544 | tf_op jit(solution)/shard_map/ppermute | solution.py:29
  102.7 1.9 %collective-permute-start.29 = (bf16[2,128,256]{2,1,0:T(8,128)(2,1)S(1)}, bf16[2,128,256]{2,1,0:T(8,128)(2,1)S(1)}, u32[]{:S(2)}, u32[]{:S(2)}) collective-permute-start(bf16[2,128,256]{2,1,0:T(8,128)(2,1)S(1)} %get-tuple-element.43), channel_id=1, source_target_pairs={{0,6},{1,7},{2,0},{3,1},{4,2},{5,3},{6,4},{7,5},{8,14},{9,15},{10,... | collective-permute-start | bytes 393224 | tf_op jit(solution)/shard_map/ppermute | solution.py:29
  104.7 1.8 %collective-permute-start.27 = (bf16[2,128,256]{2,1,0:T(8,128)(2,1)S(1)}, bf16[2,128,256]{2,1,0:T(8,128)(2,1)S(1)}, u32[]{:S(2)}, u32[]{:S(2)}) collective-permute-start(bf16[2,128,256]{2,1,0:T(8,128)(2,1)S(1)} %get-tuple-element.42), channel_id=1, source_target_pairs={{0,2},{1,3},{2,4},{3,5},{4,6},{5,7},{6,0},{7,1},{8,10},{9,11},{10,... | collective-permute-start | bytes 393224 | tf_op jit(solution)/shard_map/ppermute | solution.py:29
  107.1 2.9 %head_grad.1 = (f32[256,512]{1,0:T(8,128)}, bf16[256,512]{1,0:T(8,128)(2,1)}, bf16[256,512]{1,0:T(8,128)(2,1)}, bf16[256,512]{1,0:T(8,128)(2,1)}) custom-call(bf16[512,1024]{1,0:T(8,128)(2,1)} %get-tuple-element.24.hidden_ref, bf16[128,512]{1,0:T(8,128)(2,1)} %copy-done, bf16[128,512]{1,0:T(8,128)(2,1)} %copy-done.1, bf16[128,512]{1,0:T(8,128)(2,1)} %copy-done.2, ...), custom_call_target="tpu_custom_call" | custom-call | tf_op jit(solution)/shard_map/head_grad/pallas_call | solution.py:214
  111.6 3.0 %collective-permute-start.33 = (bf16[256,512]{1,0:T(8,128)(2,1)}, bf16[256,512]{1,0:T(8,128)(2,1)S(1)}, u32[]{:S(2)}, u32[]{:S(2)}) collective-permute-start(bf16[256,512]{1,0:T(8,128)(2,1)} %get-tuple-element.27), channel_id=1, source_target_pairs={{0,64},{1,65},{2,66},{3,67},{4,68},{5,69},{6,70},{7,71},{8,72},{9,... | collective-permute-start | bytes 786440 | tf_op jit(solution)/shard_map/ppermute | solution.py:29
  116.5 1.9 %collective-permute-start.31 = (bf16[128,256]{1,0:T(8,128)(2,1)S(1)}, bf16[128,256]{1,0:T(8,128)(2,1)S(1)}, u32[]{:S(2)}, u32[]{:S(2)}) collective-permute-start(bf16[128,256]{1,0:T(8,128)(2,1)S(1)} %get-tuple-element.49), channel_id=1, source_target_pairs={{0,128},{1,136},{2,144},{3,152},{4,132},{5,140},{6,148},{7,156},{8... | collective-permute-start | bytes 196616 | tf_op jit(solution)/shard_map/ppermute | solution.py:29
  118.4 5.5 %collective-permute-start.30 = (bf16[128,256]{1,0:T(8,128)(2,1)S(1)}, bf16[128,256]{1,0:T(8,128)(2,1)S(1)}, u32[]{:S(2)}, u32[]{:S(2)}) collective-permute-start(bf16[128,256]{1,0:T(8,128)(2,1)S(1)} %get-tuple-element.48), channel_id=1, source_target_pairs={{0,0},{1,8},{2,16},{3,24},{4,4},{5,12},{6,20},{7,28},{8,1},{9,9},{... | collective-permute-start | bytes 196616 | tf_op jit(solution)/shard_map/ppermute | solution.py:29
  124.6 2.0 %convert_add_fusion = f32[256,512]{1,0:T(8,128)} fusion(bf16[256,512]{1,0:T(8,128)(2,1)S(1)} %collective-permute-done.34, bf16[256,512]{1,0:T(8,128)(2,1)S(1)} %collective-permute-done.33, f32[256,512]{1,0:T(8,128)} %get-tuple-element.25, bf16[256,512]{1,0:T(8,128)(2,1)S(1)} %collective-permute-done.32), kind=kLoop, calls=%fused_computation.10 | loop fusion | flops 786432 | bytes 1835008 | tf_op jit(solution)/shard_map/add | solution.py:344
  126.5 2.8 %collective-permute-done.30 = bf16[128,256]{1,0:T(8,128)(2,1)S(1)} collective-permute-done((bf16[128,256]{1,0:T(8,128)(2,1)S(1)}, bf16[128,256]{1,0:T(8,128)(2,1)S(1)}, u32[]{:S(2)}, u32[]{:S(2)}) %collective-permute-start.30) | collective-permute-done | bytes 65568 | tf_op jit(solution)/shard_map/ppermute | solution.py:29
  (99 shorter events, 25.5 us)
Async XLA Ops:
  5.1 26.4 %collective-permute-start = (f32[8,136,512]{2,1,0:T(8,128)}, f32[8,136,512]{2,1,0:T(8,128)S(1)}, u32[]{:S(2)}, u32[]{:S(2)}) collective-permute-start(f32[8,136,512]{2,1,0:T(8,128)} %teacher.3), channel_id=1, source_target_pairs={{0,1},{1,0},{2,3},{3,2},{4,5},{5,4},{6,7},{7,6},{8,9},{9,8},{10,11... | collective-permute-start | bytes 6684680 | tf_op jit(solution)/shard_map/ppermute | solution.py:29
  6.9 11.3 %collective-permute-start.5 = (bf16[2,128,256]{2,1,0:T(8,128)(2,1)}, bf16[2,128,256]{2,1,0:T(8,128)(2,1)S(1)}, u32[]{:S(2)}, u32[]{:S(2)}) collective-permute-start(bf16[2,128,256]{2,1,0:T(8,128)(2,1)} %get-tuple-element.16), channel_id=1, source_target_pairs={{0,8},{1,9},{2,10},{3,11},{4,12},{5,13},{6,14},{7,15},{8,16},{9,17... | collective-permute-start | bytes 393224 | tf_op jit(solution)/shard_map/ppermute | solution.py:29
  10.2 15.3 %collective-permute-start.6 = (bf16[2,128,256]{2,1,0:T(8,128)(2,1)}, bf16[2,128,256]{2,1,0:T(8,128)(2,1)S(1)}, u32[]{:S(2)}, u32[]{:S(2)}) collective-permute-start(bf16[2,128,256]{2,1,0:T(8,128)(2,1)} %get-tuple-element.17), channel_id=1, source_target_pairs={{0,16},{1,17},{2,18},{3,19},{4,20},{5,21},{6,22},{7,23},{8,24},{9,... | collective-permute-start | bytes 393224 | tf_op jit(solution)/shard_map/ppermute | solution.py:29
  15.6 13.1 %collective-permute-start.7 = (bf16[2,128,256]{2,1,0:T(8,128)(2,1)}, bf16[2,128,256]{2,1,0:T(8,128)(2,1)S(1)}, u32[]{:S(2)}, u32[]{:S(2)}) collective-permute-start(bf16[2,128,256]{2,1,0:T(8,128)(2,1)} %get-tuple-element.18), channel_id=1, source_target_pairs={{0,24},{1,25},{2,26},{3,27},{4,28},{5,29},{6,30},{7,31},{8,0},{9,1... | collective-permute-start | bytes 393224 | tf_op jit(solution)/shard_map/ppermute | solution.py:29
  18.3 13.3 %collective-permute-start.8 = (bf16[2,128,256]{2,1,0:T(8,128)(2,1)S(1)}, bf16[2,128,256]{2,1,0:T(8,128)(2,1)S(1)}, u32[]{:S(2)}, u32[]{:S(2)}) collective-permute-start(bf16[2,128,256]{2,1,0:T(8,128)(2,1)S(1)} %collective-permute-done.5.refs_4_), channel_id=1, source_target_pairs={{0,1},{1,0},{2,3},{3,2},{4,5},{5,4},{6,7},{7,6},{8,9},{9,8},{10,11... | collective-permute-start | bytes 393224 | tf_op jit(solution)/shard_map/ppermute | solution.py:29
  18.3 19.5 %collective-permute-start.11 = (bf16[256,512]{1,0:T(8,128)(2,1)}, bf16[256,512]{1,0:T(8,128)(2,1)}, u32[]{:S(2)}, u32[]{:S(2)}) collective-permute-start(bf16[256,512]{1,0:T(8,128)(2,1)} %refs_10_.1), channel_id=1, source_target_pairs={{0,32},{1,33},{2,34},{3,35},{4,36},{5,37},{6,38},{7,39},{8,40},{9,... | collective-permute-start | bytes 786440 | tf_op jit(solution)/shard_map/ppermute | solution.py:29
  25.5 14.0 %collective-permute-start.12 = (bf16[256,512]{1,0:T(8,128)(2,1)}, bf16[256,512]{1,0:T(8,128)(2,1)}, u32[]{:S(2)}, u32[]{:S(2)}) collective-permute-start(bf16[256,512]{1,0:T(8,128)(2,1)} %refs_10_.1), channel_id=1, source_target_pairs={{0,64},{1,65},{2,66},{3,67},{4,68},{5,69},{6,70},{7,71},{8,72},{9,... | collective-permute-start | bytes 786440 | tf_op jit(solution)/shard_map/ppermute | solution.py:29
  28.7 12.2 %collective-permute-start.13 = (bf16[256,512]{1,0:T(8,128)(2,1)}, bf16[256,512]{1,0:T(8,128)(2,1)}, u32[]{:S(2)}, u32[]{:S(2)}) collective-permute-start(bf16[256,512]{1,0:T(8,128)(2,1)} %refs_10_.1), channel_id=1, source_target_pairs={{0,96},{1,97},{2,98},{3,99},{4,100},{5,101},{6,102},{7,103},{8,104... | collective-permute-start | bytes 786440 | tf_op jit(solution)/shard_map/ppermute | solution.py:29
  31.6 3.6 %collective-permute-start.10 = (bf16[2,128,256]{2,1,0:T(8,128)(2,1)S(1)}, bf16[2,128,256]{2,1,0:T(8,128)(2,1)S(1)}, u32[]{:S(2)}, u32[]{:S(2)}) collective-permute-start(bf16[2,128,256]{2,1,0:T(8,128)(2,1)S(1)} %collective-permute-done.7.refs_6_), channel_id=1, source_target_pairs={{0,1},{1,0},{2,3},{3,2},{4,5},{5,4},{6,7},{7,6},{8,9},{9,8},{10,11... | collective-permute-start | bytes 393224 | tf_op jit(solution)/shard_map/ppermute | solution.py:29
  34.6 19.5 %collective-permute-start.3 = (f16[2,136,512]{2,1,0:T(8,128)(2,1)}, f16[2,136,512]{2,1,0:T(8,128)(2,1)S(1)}, u32[]{:S(2)}, u32[]{:S(2)}) collective-permute-start(f16[2,136,512]{2,1,0:T(8,128)(2,1)} %get-tuple-element.40), channel_id=1, source_target_pairs={{0,6},{1,7},{2,0},{3,1},{4,2},{5,3},{6,4},{7,5},{8,14},{9,15},{10,... | collective-permute-start | bytes 835592 | tf_op jit(solution)/shard_map/ppermute | solution.py:29
  35.2 22.7 %collective-permute-start.2 = (f16[2,136,512]{2,1,0:T(8,128)(2,1)S(1)}, f16[2,136,512]{2,1,0:T(8,128)(2,1)S(1)}, u32[]{:S(2)}, u32[]{:S(2)}) collective-permute-start(f16[2,136,512]{2,1,0:T(8,128)(2,1)S(1)} %get-tuple-element.41), channel_id=1, source_target_pairs={{0,4},{1,5},{2,6},{3,7},{4,0},{5,1},{6,2},{7,3},{8,12},{9,13},{10,... | collective-permute-start | bytes 835592 | tf_op jit(solution)/shard_map/ppermute | solution.py:29
  37.7 20.2 %collective-permute-start.1 = (f16[2,136,512]{2,1,0:T(8,128)(2,1)S(1)}, f16[2,136,512]{2,1,0:T(8,128)(2,1)}, u32[]{:S(2)}, u32[]{:S(2)}) collective-permute-start(f16[2,136,512]{2,1,0:T(8,128)(2,1)S(1)} %get-tuple-element.39), channel_id=1, source_target_pairs={{0,2},{1,3},{2,4},{3,5},{4,6},{5,7},{6,0},{7,1},{8,10},{9,11},{10,... | collective-permute-start | bytes 835592 | tf_op jit(solution)/shard_map/ppermute | solution.py:29
  45.9 13.5 %collective-permute-start.16 = (f16[128,512]{1,0:T(8,128)(2,1)S(1)}, f16[128,512]{1,0:T(8,128)(2,1)S(1)}, u32[]{:S(2)}, u32[]{:S(2)}) collective-permute-start(f16[128,512]{1,0:T(8,128)(2,1)S(1)} %get-tuple-element.46), channel_id=1, source_target_pairs={{0,8},{1,9},{2,10},{3,11},{4,12},{5,13},{6,14},{7,15},{8,16},{9,17... | collective-permute-start | bytes 393224 | tf_op jit(solution)/shard_map/ppermute | solution.py:29
  49.8 13.5 %collective-permute-start.15 = (f16[128,512]{1,0:T(8,128)(2,1)S(1)}, f16[128,512]{1,0:T(8,128)(2,1)S(1)}, u32[]{:S(2)}, u32[]{:S(2)}) collective-permute-start(f16[128,512]{1,0:T(8,128)(2,1)S(1)} %get-tuple-element.47), channel_id=1, source_target_pairs={{0,16},{1,17},{2,18},{3,19},{4,20},{5,21},{6,22},{7,23},{8,24},{9,... | collective-permute-start | bytes 393224 | tf_op jit(solution)/shard_map/ppermute | solution.py:29
  54.1 11.3 %collective-permute-start.14 = (f16[128,512]{1,0:T(8,128)(2,1)S(1)}, f16[128,512]{1,0:T(8,128)(2,1)S(1)}, u32[]{:S(2)}, u32[]{:S(2)}) collective-permute-start(f16[128,512]{1,0:T(8,128)(2,1)S(1)} %get-tuple-element.45), channel_id=1, source_target_pairs={{0,24},{1,25},{2,26},{3,27},{4,28},{5,29},{6,30},{7,31},{8,0},{9,1... | collective-permute-start | bytes 393224 | tf_op jit(solution)/shard_map/ppermute | solution.py:29
  59.3 7.4 %collective-permute-start.4 = (f16[136,512]{1,0:T(8,128)(2,1)S(1)}, f16[136,512]{1,0:T(8,128)(2,1)S(1)}, u32[]{:S(2)}, u32[]{:S(2)}) collective-permute-start(f16[136,512]{1,0:T(8,128)(2,1)S(1)} %fusion.17), channel_id=1, source_target_pairs={{0,128},{1,129},{2,130},{3,131},{4,132},{5,133},{6,134},{7,135},{8... | collective-permute-start | bytes 417800 | tf_op jit(solution)/shard_map/ppermute | solution.py:29
  67.4 3.7 %collective-permute-start.18 = (f32[5,128]{1,0:T(8,128)S(1)}, f32[5,128]{1,0:T(8,128)S(1)}, u32[]{:S(2)}, u32[]{:S(2)}) collective-permute-start(f32[5,128]{1,0:T(8,128)S(1)} %stack.38), channel_id=1, source_target_pairs={{0,2},{1,3},{2,0},{3,1},{4,6},{5,7},{6,4},{7,5},{8,10},{9,11},{10,... | collective-permute-start | bytes 7688 | tf_op jit(solution)/shard_map/ppermute | solution.py:29
  71.4 9.3 %collective-permute-start.23 = (bf16[128,512]{1,0:T(8,128)(2,1)S(1)}, bf16[128,512]{1,0:T(8,128)(2,1)S(1)}, u32[]{:S(2)}, u32[]{:S(2)}) collective-permute-start(bf16[128,512]{1,0:T(8,128)(2,1)S(1)} %subtract_convert_fusion.refs_0_), channel_id=1, source_target_pairs={{0,8},{1,9},{2,10},{3,11},{4,12},{5,13},{6,14},{7,15},{8,16},{9,17... | collective-permute-start | bytes 393224 | tf_op jit(solution)/shard_map/ppermute | solution.py:29
  73.6 14.4 %collective-permute-start.24 = (bf16[128,512]{1,0:T(8,128)(2,1)S(1)}, bf16[128,512]{1,0:T(8,128)(2,1)S(1)}, u32[]{:S(2)}, u32[]{:S(2)}) collective-permute-start(bf16[128,512]{1,0:T(8,128)(2,1)S(1)} %subtract_convert_fusion.refs_0_), channel_id=1, source_target_pairs={{0,16},{1,17},{2,18},{3,19},{4,20},{5,21},{6,22},{7,23},{8,24},{9,... | collective-permute-start | bytes 393224 | tf_op jit(solution)/shard_map/ppermute | solution.py:29
  76.8 11.2 %collective-permute-start.25 = (bf16[128,512]{1,0:T(8,128)(2,1)S(1)}, bf16[128,512]{1,0:T(8,128)(2,1)S(1)}, u32[]{:S(2)}, u32[]{:S(2)}) collective-permute-start(bf16[128,512]{1,0:T(8,128)(2,1)S(1)} %subtract_convert_fusion.refs_0_), channel_id=1, source_target_pairs={{0,24},{1,25},{2,26},{3,27},{4,28},{5,29},{6,30},{7,31},{8,0},{9,1... | collective-permute-start | bytes 393224 | tf_op jit(solution)/shard_map/ppermute | solution.py:29
  92.3 9.1 %collective-permute-start.26 = (f32[8,128,256]{2,1,0:T(8,128)}, f32[8,128,256]{2,1,0:T(8,128)S(1)}, u32[]{:S(2)}, u32[]{:S(2)}) collective-permute-start(f32[8,128,256]{2,1,0:T(8,128)} %get-tuple-element.23), channel_id=1, source_target_pairs={{0,1},{1,0},{2,3},{3,2},{4,5},{5,4},{6,7},{7,6},{8,9},{9,8},{10,11... | collective-permute-start | bytes 3145736 | tf_op jit(solution)/shard_map/ppermute | solution.py:29
  92.4 6.1 %collective-permute-start.22 = (f32[1,128]{1,0:T(1,128)S(1)}, f32[1,128]{1,0:T(1,128)S(1)}, u32[]{:S(2)}, u32[]{:S(2)}) collective-permute-start(f32[1,128]{1,0:T(1,128)S(1)} %bitcast_multiply_fusion), channel_id=1, source_target_pairs={{0,132},{1,133},{2,134},{3,135},{4,128},{5,129},{6,130},{7,131},{8... | collective-permute-start | bytes 1544 | tf_op jit(solution)/shard_map/ppermute | solution.py:29
  92.5 6.0 %collective-permute-start.21 = (f32[1,128]{1,0:T(1,128)S(1)}, f32[1,128]{1,0:T(1,128)S(1)}, u32[]{:S(2)}, u32[]{:S(2)}) collective-permute-start(f32[1,128]{1,0:T(1,128)S(1)} %bitcast_multiply_fusion), channel_id=1, source_target_pairs={{0,128},{1,129},{2,130},{3,131},{4,132},{5,133},{6,134},{7,135},{8... | collective-permute-start | bytes 1544 | tf_op jit(solution)/shard_map/ppermute | solution.py:29
  96.4 5.1 %collective-permute-start.20 = (f32[1,128]{1,0:T(1,128)S(1)}, f32[1,128]{1,0:T(1,128)S(1)}, u32[]{:S(2)}, u32[]{:S(2)}) collective-permute-start(f32[1,128]{1,0:T(1,128)S(1)} %bitcast_multiply_fusion), channel_id=1, source_target_pairs={{0,4},{1,5},{2,6},{3,7},{4,0},{5,1},{6,2},{7,3},{8,12},{9,13},{10,... | collective-permute-start | bytes 1544 | tf_op jit(solution)/shard_map/ppermute | solution.py:29
  102.7 11.9 %collective-permute-start.29 = (bf16[2,128,256]{2,1,0:T(8,128)(2,1)S(1)}, bf16[2,128,256]{2,1,0:T(8,128)(2,1)S(1)}, u32[]{:S(2)}, u32[]{:S(2)}) collective-permute-start(bf16[2,128,256]{2,1,0:T(8,128)(2,1)S(1)} %get-tuple-element.43), channel_id=1, source_target_pairs={{0,6},{1,7},{2,0},{3,1},{4,2},{5,3},{6,4},{7,5},{8,14},{9,15},{10,... | collective-permute-start | bytes 393224 | tf_op jit(solution)/shard_map/ppermute | solution.py:29
  104.5 11.0 %collective-permute-start.28 = (bf16[2,128,256]{2,1,0:T(8,128)(2,1)S(1)}, bf16[2,128,256]{2,1,0:T(8,128)(2,1)S(1)}, u32[]{:S(2)}, u32[]{:S(2)}) collective-permute-start(bf16[2,128,256]{2,1,0:T(8,128)(2,1)S(1)} %get-tuple-element.44), channel_id=1, source_target_pairs={{0,4},{1,5},{2,6},{3,7},{4,0},{5,1},{6,2},{7,3},{8,12},{9,13},{10,... | collective-permute-start | bytes 393224 | tf_op jit(solution)/shard_map/ppermute | solution.py:29
  104.7 10.8 %collective-permute-start.27 = (bf16[2,128,256]{2,1,0:T(8,128)(2,1)S(1)}, bf16[2,128,256]{2,1,0:T(8,128)(2,1)S(1)}, u32[]{:S(2)}, u32[]{:S(2)}) collective-permute-start(bf16[2,128,256]{2,1,0:T(8,128)(2,1)S(1)} %get-tuple-element.42), channel_id=1, source_target_pairs={{0,2},{1,3},{2,4},{3,5},{4,6},{5,7},{6,0},{7,1},{8,10},{9,11},{10,... | collective-permute-start | bytes 393224 | tf_op jit(solution)/shard_map/ppermute | solution.py:29
  110.1 13.9 %collective-permute-start.34 = (bf16[256,512]{1,0:T(8,128)(2,1)}, bf16[256,512]{1,0:T(8,128)(2,1)S(1)}, u32[]{:S(2)}, u32[]{:S(2)}) collective-permute-start(bf16[256,512]{1,0:T(8,128)(2,1)} %get-tuple-element.28), channel_id=1, source_target_pairs={{0,32},{1,33},{2,34},{3,35},{4,36},{5,37},{6,38},{7,39},{8,40},{9,... | collective-permute-start | bytes 786440 | tf_op jit(solution)/shard_map/ppermute | solution.py:29
  111.6 13.0 %collective-permute-start.33 = (bf16[256,512]{1,0:T(8,128)(2,1)}, bf16[256,512]{1,0:T(8,128)(2,1)S(1)}, u32[]{:S(2)}, u32[]{:S(2)}) collective-permute-start(bf16[256,512]{1,0:T(8,128)(2,1)} %get-tuple-element.27), channel_id=1, source_target_pairs={{0,64},{1,65},{2,66},{3,67},{4,68},{5,69},{6,70},{7,71},{8,72},{9,... | collective-permute-start | bytes 786440 | tf_op jit(solution)/shard_map/ppermute | solution.py:29
  114.6 10.0 %collective-permute-start.32 = (bf16[256,512]{1,0:T(8,128)(2,1)}, bf16[256,512]{1,0:T(8,128)(2,1)S(1)}, u32[]{:S(2)}, u32[]{:S(2)}) collective-permute-start(bf16[256,512]{1,0:T(8,128)(2,1)} %get-tuple-element.26), channel_id=1, source_target_pairs={{0,96},{1,97},{2,98},{3,99},{4,100},{5,101},{6,102},{7,103},{8,104... | collective-permute-start | bytes 786440 | tf_op jit(solution)/shard_map/ppermute | solution.py:29
  116.5 10.0 %collective-permute-start.31 = (bf16[128,256]{1,0:T(8,128)(2,1)S(1)}, bf16[128,256]{1,0:T(8,128)(2,1)S(1)}, u32[]{:S(2)}, u32[]{:S(2)}) collective-permute-start(bf16[128,256]{1,0:T(8,128)(2,1)S(1)} %get-tuple-element.49), channel_id=1, source_target_pairs={{0,128},{1,136},{2,144},{3,152},{4,132},{5,140},{6,148},{7,156},{8... | collective-permute-start | bytes 196616 | tf_op jit(solution)/shard_map/ppermute | solution.py:29
  118.4 11.0 %collective-permute-start.30 = (bf16[128,256]{1,0:T(8,128)(2,1)S(1)}, bf16[128,256]{1,0:T(8,128)(2,1)S(1)}, u32[]{:S(2)}, u32[]{:S(2)}) collective-permute-start(bf16[128,256]{1,0:T(8,128)(2,1)S(1)} %get-tuple-element.48), channel_id=1, source_target_pairs={{0,0},{1,8},{2,16},{3,24},{4,4},{5,12},{6,20},{7,28},{8,1},{9,9},{... | collective-permute-start | bytes 196616 | tf_op jit(solution)/shard_map/ppermute | solution.py:29
  (15 other events, 104.7 us)

commit v9 on v8

--- a/solution.py
+++ b/solution.py
@@ -342,20 +342,21 @@
     parts = round_ring(to_y, parts, -1)
     for part in parts:
         head_grad = head_grad + part.astype(f32)
-    by_x = own[:2] + other[:2]
-    pieces = [
-        (own[2 * step : 2 * step + 2] + other[2 * step : 2 * step + 2]).astype(bf16) for step in (1, 2, 3)
-    ]
-    for piece in round_ring(to_x, pieces):
-        by_x = by_x + piece.astype(f32)
+    pieces = [own[i] + other[i] for i in range(8)]
+    hidden_grad = pieces[0]
+    for piece in round_ring(to_x, [pieces[i].astype(bf16) for i in (2, 4, 6)]):
+        hidden_grad = hidden_grad + piece.astype(f32)
+    for step in (2, 1, 3, 0):
+        piece = send(
+            pieces[2 * step + 1].astype(bf16),
+            lambda zl, y, zh, x, core: (1 - zl, y, zh, x + step, core),
+        )
+        hidden_grad = hidden_grad + piece.astype(f32)
 
     def home(zl, y, zh, x, core):
         return zl, y, x % 2 * 2 + core, x // 2 * 2 + zh // 2, zh % 2
 
-    by_x = by_x.astype(bf16)
-    hidden_grad = send(by_x[0], home).astype(f32) + send(
-        by_x[1], lambda zl, y, zh, x, core: home(1 - zl, y, zh, x, core)
-    ).astype(f32)
+    hidden_grad = send(hidden_grad.astype(bf16), home).astype(f32)
     return (kl_terms, hidden_grad, head_grad)
 
 

time: 132 us -> 138 us (1.045); the launches traced: 130 us -> 138 us
  starting transfers between devices: 67.2 us -> 74.1 us
    ppermute x35 -> x38, starting transfers between devices: 67.2 us -> 74.1 us  [send(): return lax.ppermute(value, ALL, pairs)]
    convert_element_type x2 -> x3, other arithmetic: 2.21 us -> 2.99 us  [the longest x2 1.65 us: step(): hidden_grad = send(hidden_grad.astype(bf16), home).astype(f32)]
    ppermute x35 -> x38, waiting for transfers between devices: 28.6 us -> 29.4 us  [send(): return lax.ppermute(value, ALL, pairs)]
  transfers between devices with their start and end apart: 35 -> 38, of which waited for: 13 -> 14; matrix products, arithmetic and copies ran while one was open for 7% -> 7% of each run, Pallas kernels for 10% -> 9%
where the time goes in v9:
time: 138 us
  starting transfers between devices  74.1 us (54%)
  waiting for transfers between devices  29.4 us (21%)
  Pallas kernels  20.8 us (15%)
  other arithmetic  11.6 us (8%)
    ppermute x38, starting transfers between devices, send(): return lax.ppermute(value, ALL, pairs)  74.1 us
    ppermute x38, waiting for transfers between devices, send(): return lax.ppermute(value, ALL, pairs)  29.4 us
    pallas_call x2, Pallas kernels, teacher_parts(): pl.pallas_call(teacher_kernel, grid_spec=pltpu.PrefetchScalarGridSpec(num...  8.79 us
    pallas_call x1, Pallas kernels, student_parts(): pl.pallas_call(student_kernel, grid_spec=pltpu.PrefetchScalarGridSpec(num...  3.74 us
    pallas_call x1, Pallas kernels, hidden_grad_parts(): pl.pallas_call(hidden_grad_kernel, in_specs=[pl.BlockSpec(memory_space=pl...  3.54 us
    pallas_call x1, Pallas kernels, head_grad_parts(): pl.pallas_call(head_grad_kernel, out_shape=(jax.ShapeDtypeStruct((256, 51...  2.94 us
  transfers between devices with their start and end apart: 38, of which 14 were waited for; matrix products, arithmetic and copies ran while one was open for 7% of the time, Pallas kernels for 9%

profile of v9, /device:TPU:2, one launch (start us, length us, event | category | flops | bytes accessed | tf_op | source)
XLA Modules:
  0.0 137.8 jit_solution(162813030950290287)
XLA Ops:
  0.6 4.5 %teacher.3 = f32[8,136,512]{2,1,0:T(8,128)} custom-call(s32[1]{0:T(128)} %bitcast.index_ref, bf16[128,512]{1,0:T(8,128)(2,1)} %hidden_ref.3, bf16[512]{0:T(512)(128)(2,1)} %gain_ref.3, bf16[512,8192]{1,0:T(8,128)(2,1)} %refs_3_.5, bf16[512,8192]{1,0:T(8,128)(2,1)} %refs_3_.5, bf16[512,8192]{1,0:T(8,128)(2,1)} %refs_3_.5, bf16[512,8192]{1,0:T(8,128)(2,1)} %refs_3_.5), custom_call_target="tpu_custom_call" | custom-call | tf_op jit(solution)/shard_map/teacher/pallas_call | solution.py:132
  5.1 1.8 %pick.1 = (bf16[2,128,256]{2,1,0:T(8,128)(2,1)}, bf16[2,128,256]{2,1,0:T(8,128)(2,1)}, bf16[2,128,256]{2,1,0:T(8,128)(2,1)}) custom-call(s32[1]{0:T(128)} %bitcast.index_ref, bf16[128,4096]{1,0:T(8,128)(2,1)} %refs_3_.7, bf16[128,4096]{1,0:T(8,128)(2,1)} %refs_3_.7, bf16[128,4096]{1,0:T(8,128)(2,1)} %refs_3_.7, bf16[128,4096]{1,0:T(8,128)(2,1)} %refs_3_.7, ...), custom_call_target="tpu_custom_call" | custom-call | tf_op jit(solution)/shard_map/pick/pallas_call | solution.py:79
  6.9 3.3 %collective-permute-start.5 = (bf16[2,128,256]{2,1,0:T(8,128)(2,1)}, bf16[2,128,256]{2,1,0:T(8,128)(2,1)S(1)}, u32[]{:S(2)}, u32[]{:S(2)}) collective-permute-start(bf16[2,128,256]{2,1,0:T(8,128)(2,1)} %get-tuple-element.16), channel_id=1, source_target_pairs={{0,8},{1,9},{2,10},{3,11},{4,12},{5,13},{6,14},{7,15},{8,16},{9,17... | collective-permute-start | bytes 393224 | tf_op jit(solution)/shard_map/ppermute | solution.py:29
  10.2 5.4 %collective-permute-start.6 = (bf16[2,128,256]{2,1,0:T(8,128)(2,1)}, bf16[2,128,256]{2,1,0:T(8,128)(2,1)S(1)}, u32[]{:S(2)}, u32[]{:S(2)}) collective-permute-start(bf16[2,128,256]{2,1,0:T(8,128)(2,1)} %get-tuple-element.17), channel_id=1, source_target_pairs={{0,16},{1,17},{2,18},{3,19},{4,20},{5,21},{6,22},{7,23},{8,24},{9,... | collective-permute-start | bytes 393224 | tf_op jit(solution)/shard_map/ppermute | solution.py:29
  15.6 2.7 %collective-permute-start.7 = (bf16[2,128,256]{2,1,0:T(8,128)(2,1)}, bf16[2,128,256]{2,1,0:T(8,128)(2,1)S(1)}, u32[]{:S(2)}, u32[]{:S(2)}) collective-permute-start(bf16[2,128,256]{2,1,0:T(8,128)(2,1)} %get-tuple-element.18), channel_id=1, source_target_pairs={{0,24},{1,25},{2,26},{3,27},{4,28},{5,29},{6,30},{7,31},{8,0},{9,1... | collective-permute-start | bytes 393224 | tf_op jit(solution)/shard_map/ppermute | solution.py:29
  19.9 4.3 %teacher.2 = f32[8,136,512]{2,1,0:T(8,128)} custom-call(s32[1]{0:T(128)} %bitcast.index_ref, bf16[128,512]{1,0:T(8,128)(2,1)} %hidden_ref.3, bf16[512]{0:T(512)(128)(2,1)} %gain_ref.3, bf16[512,8192]{1,0:T(8,128)(2,1)} %refs_3_.5, bf16[512,8192]{1,0:T(8,128)(2,1)} %refs_3_.5, bf16[512,8192]{1,0:T(8,128)(2,1)} %refs_3_.5, bf16[512,8192]{1,0:T(8,128)(2,1)} %refs_3_.5), custom_call_target="tpu_custom_call" | custom-call | tf_op jit(solution)/shard_map/teacher/pallas_call | solution.py:132
  25.5 3.2 %collective-permute-start.12 = (bf16[256,512]{1,0:T(8,128)(2,1)}, bf16[256,512]{1,0:T(8,128)(2,1)}, u32[]{:S(2)}, u32[]{:S(2)}) collective-permute-start(bf16[256,512]{1,0:T(8,128)(2,1)} %refs_10_.1), channel_id=1, source_target_pairs={{0,64},{1,65},{2,66},{3,67},{4,68},{5,69},{6,70},{7,71},{8,72},{9,... | collective-permute-start | bytes 786440 | tf_op jit(solution)/shard_map/ppermute | solution.py:29
  28.7 2.8 %collective-permute-start.13 = (bf16[256,512]{1,0:T(8,128)(2,1)}, bf16[256,512]{1,0:T(8,128)(2,1)}, u32[]{:S(2)}, u32[]{:S(2)}) collective-permute-start(bf16[256,512]{1,0:T(8,128)(2,1)} %refs_10_.1), channel_id=1, source_target_pairs={{0,96},{1,97},{2,98},{3,99},{4,100},{5,101},{6,102},{7,103},{8,104... | collective-permute-start | bytes 786440 | tf_op jit(solution)/shard_map/ppermute | solution.py:29
  32.1 2.5 %fusion.2 = (f16[2,136,512]{2,1,0:T(8,128)(2,1)S(1)}, f16[2,136,512]{2,1,0:T(8,128)(2,1)}, f16[2,136,512]{2,1,0:T(8,128)(2,1)S(1)}) fusion(f32[8,136,512]{2,1,0:T(8,128)S(1)} %collective-permute-done, f32[8,136,512]{2,1,0:T(8,128)} %teacher.2), kind=kLoop, calls=%fused_computation.5 | loop fusion | flops 835584 | bytes 4177920 | tf_op jit(solution)/shard_map/convert_element_type | solution.py:273
  35.2 2.5 %collective-permute-start.2 = (f16[2,136,512]{2,1,0:T(8,128)(2,1)S(1)}, f16[2,136,512]{2,1,0:T(8,128)(2,1)S(1)}, u32[]{:S(2)}, u32[]{:S(2)}) collective-permute-start(f16[2,136,512]{2,1,0:T(8,128)(2,1)S(1)} %get-tuple-element.41), channel_id=1, source_target_pairs={{0,4},{1,5},{2,6},{3,7},{4,0},{5,1},{6,2},{7,3},{8,12},{9,13},{10,... | collective-permute-start | bytes 835592 | tf_op jit(solution)/shard_map/ppermute | solution.py:29
  37.7 1.8 %collective-permute-start.1 = (f16[2,136,512]{2,1,0:T(8,128)(2,1)S(1)}, f16[2,136,512]{2,1,0:T(8,128)(2,1)}, u32[]{:S(2)}, u32[]{:S(2)}) collective-permute-start(f16[2,136,512]{2,1,0:T(8,128)(2,1)S(1)} %get-tuple-element.39), channel_id=1, source_target_pairs={{0,2},{1,3},{2,4},{3,5},{4,6},{5,7},{6,0},{7,1},{8,10},{9,11},{10,... | collective-permute-start | bytes 835592 | tf_op jit(solution)/shard_map/ppermute | solution.py:29
  40.9 3.7 %student.1 = (f32[128,512]{1,0:T(8,128)}, f32[3,128,512]{2,1,0:T(8,128)}, bf16[512,1024]{1,0:T(8,128)(2,1)}, bf16[1024,512]{1,0:T(8,128)(2,1)}) custom-call(s32[1]{0:T(128)} %bitcast.index_ref, bf16[128,4096]{1,0:T(8,128)(2,1)} %refs_3_.7, bf16[128,4096]{1,0:T(8,128)(2,1)} %refs_3_.7, bf16[128,4096]{1,0:T(8,128)(2,1)} %refs_3_.7, bf16[128,4096]{1,0:T(8,128)(2,1)} %refs_3_.7, ...), custom_call_target="tpu_custom_call" | custom-call | tf_op jit(solution)/shard_map/student/pallas_call | solution.py:176
  46.0 3.8 %collective-permute-start.16 = (f16[128,512]{1,0:T(8,128)(2,1)S(1)}, f16[128,512]{1,0:T(8,128)(2,1)S(1)}, u32[]{:S(2)}, u32[]{:S(2)}) collective-permute-start(f16[128,512]{1,0:T(8,128)(2,1)S(1)} %get-tuple-element.50), channel_id=1, source_target_pairs={{0,8},{1,9},{2,10},{3,11},{4,12},{5,13},{6,14},{7,15},{8,16},{9,17... | collective-permute-start | bytes 393224 | tf_op jit(solution)/shard_map/ppermute | solution.py:29
  49.8 4.3 %collective-permute-start.15 = (f16[128,512]{1,0:T(8,128)(2,1)S(1)}, f16[128,512]{1,0:T(8,128)(2,1)S(1)}, u32[]{:S(2)}, u32[]{:S(2)}) collective-permute-start(f16[128,512]{1,0:T(8,128)(2,1)S(1)} %get-tuple-element.51), channel_id=1, source_target_pairs={{0,16},{1,17},{2,18},{3,19},{4,20},{5,21},{6,22},{7,23},{8,24},{9,... | collective-permute-start | bytes 393224 | tf_op jit(solution)/shard_map/ppermute | solution.py:29
  54.1 3.9 %collective-permute-start.14 = (f16[128,512]{1,0:T(8,128)(2,1)S(1)}, f16[128,512]{1,0:T(8,128)(2,1)S(1)}, u32[]{:S(2)}, u32[]{:S(2)}) collective-permute-start(f16[128,512]{1,0:T(8,128)(2,1)S(1)} %get-tuple-element.49), channel_id=1, source_target_pairs={{0,24},{1,25},{2,26},{3,27},{4,28},{5,29},{6,30},{7,31},{8,0},{9,1... | collective-permute-start | bytes 393224 | tf_op jit(solution)/shard_map/ppermute | solution.py:29
  59.4 3.8 %collective-permute-done.15 = f16[128,512]{1,0:T(8,128)(2,1)S(1)} collective-permute-done((f16[128,512]{1,0:T(8,128)(2,1)S(1)}, f16[128,512]{1,0:T(8,128)(2,1)S(1)}, u32[]{:S(2)}, u32[]{:S(2)}) %collective-permute-start.15) | collective-permute-done | bytes 131104 | tf_op jit(solution)/shard_map/ppermute | solution.py:29
  63.3 2.1 %collective-permute-done.14 = f16[128,512]{1,0:T(8,128)(2,1)S(1)} collective-permute-done((f16[128,512]{1,0:T(8,128)(2,1)S(1)}, f16[128,512]{1,0:T(8,128)(2,1)S(1)}, u32[]{:S(2)}, u32[]{:S(2)}) %collective-permute-start.14) | collective-permute-done | bytes 131104 | tf_op jit(solution)/shard_map/ppermute | solution.py:29
  71.4 2.3 %collective-permute-start.23 = (bf16[128,512]{1,0:T(8,128)(2,1)S(1)}, bf16[128,512]{1,0:T(8,128)(2,1)S(1)}, u32[]{:S(2)}, u32[]{:S(2)}) collective-permute-start(bf16[128,512]{1,0:T(8,128)(2,1)S(1)} %subtract_convert_fusion.refs_0_), channel_id=1, source_target_pairs={{0,8},{1,9},{2,10},{3,11},{4,12},{5,13},{6,14},{7,15},{8,16},{9,17... | collective-permute-start | bytes 393224 | tf_op jit(solution)/shard_map/ppermute | solution.py:29
  73.6 3.2 %collective-permute-start.24 = (bf16[128,512]{1,0:T(8,128)(2,1)S(1)}, bf16[128,512]{1,0:T(8,128)(2,1)S(1)}, u32[]{:S(2)}, u32[]{:S(2)}) collective-permute-start(bf16[128,512]{1,0:T(8,128)(2,1)S(1)} %subtract_convert_fusion.refs_0_), channel_id=1, source_target_pairs={{0,16},{1,17},{2,18},{3,19},{4,20},{5,21},{6,22},{7,23},{8,24},{9,... | collective-permute-start | bytes 393224 | tf_op jit(solution)/shard_map/ppermute | solution.py:29
  78.4 2.3 %collective-permute-done.23.refs_1_ = bf16[128,512]{1,0:T(8,128)(2,1)S(1)} collective-permute-done((bf16[128,512]{1,0:T(8,128)(2,1)S(1)}, bf16[128,512]{1,0:T(8,128)(2,1)S(1)}, u32[]{:S(2)}, u32[]{:S(2)}) %collective-permute-start.23) | collective-permute-done | bytes 131104 | tf_op jit(solution)/shard_map/ppermute | solution.py:29
  80.7 7.4 %collective-permute-done.24.refs_2_ = bf16[128,512]{1,0:T(8,128)(2,1)S(1)} collective-permute-done((bf16[128,512]{1,0:T(8,128)(2,1)S(1)}, bf16[128,512]{1,0:T(8,128)(2,1)S(1)}, u32[]{:S(2)}, u32[]{:S(2)}) %collective-permute-start.24) | collective-permute-done | bytes 131104 | tf_op jit(solution)/shard_map/ppermute | solution.py:29
  88.8 3.5 %hidden_grad.1 = (f32[8,128,256]{2,1,0:T(8,128)}, f32[8,128,256]{2,1,0:T(8,128)}) custom-call(s32[1]{0:T(128)} %bitcast.index_ref, bf16[128,512]{1,0:T(8,128)(2,1)} %copy-done, bf16[128,512]{1,0:T(8,128)(2,1)} %copy-done.1, bf16[128,512]{1,0:T(8,128)(2,1)} %copy-done.2, bf16[128,512]{1,0:T(8,128)(2,1)} %copy-done.3, bf16[1024,512]{1,0:T(8,128)(2,1)} %get-tuple-element.21.refs_4_), custom_call_target="tpu_custom_call" | custom-call | tf_op jit(solution)/shard_map/hidden_grad/pallas_call | solution.py:248
  92.5 3.8 %collective-permute-start.21 = (f32[1,128]{1,0:T(1,128)S(1)}, f32[1,128]{1,0:T(1,128)S(1)}, u32[]{:S(2)}, u32[]{:S(2)}) collective-permute-start(f32[1,128]{1,0:T(1,128)S(1)} %bitcast_multiply_fusion), channel_id=1, source_target_pairs={{0,128},{1,129},{2,130},{3,131},{4,132},{5,133},{6,134},{7,135},{8... | collective-permute-start | bytes 1544 | tf_op jit(solution)/shard_map/ppermute | solution.py:29
  98.5 3.0 %collective-permute-done.20 = f32[1,128]{1,0:T(1,128)S(1)} collective-permute-done((f32[1,128]{1,0:T(1,128)S(1)}, f32[1,128]{1,0:T(1,128)S(1)}, u32[]{:S(2)}, u32[]{:S(2)}) %collective-permute-start.20) | collective-permute-done | bytes 544 | tf_op jit(solution)/shard_map/ppermute | solution.py:29
  102.9 3.2 %collective-permute-start.32 = (bf16[128,256]{1,0:T(8,128)(2,1)S(1)}, bf16[128,256]{1,0:T(8,128)(2,1)S(1)}, u32[]{:S(2)}, u32[]{:S(2)}) collective-permute-start(bf16[128,256]{1,0:T(8,128)(2,1)S(1)} %get-tuple-element.44), channel_id=1, source_target_pairs={{0,134},{1,135},{2,128},{3,129},{4,130},{5,131},{6,132},{7,133},{8... | collective-permute-start | bytes 196616 | tf_op jit(solution)/shard_map/ppermute | solution.py:29
  106.2 3.5 %collective-permute-start.30 = (bf16[128,256]{1,0:T(8,128)(2,1)S(1)}, bf16[128,256]{1,0:T(8,128)(2,1)S(1)}, u32[]{:S(2)}, u32[]{:S(2)}) collective-permute-start(bf16[128,256]{1,0:T(8,128)(2,1)S(1)} %get-tuple-element.46), channel_id=1, source_target_pairs={{0,132},{1,133},{2,134},{3,135},{4,128},{5,129},{6,130},{7,131},{8... | collective-permute-start | bytes 196616 | tf_op jit(solution)/shard_map/ppermute | solution.py:29
  109.9 2.9 %head_grad.1 = (f32[256,512]{1,0:T(8,128)}, bf16[256,512]{1,0:T(8,128)(2,1)}, bf16[256,512]{1,0:T(8,128)(2,1)}, bf16[256,512]{1,0:T(8,128)(2,1)}) custom-call(bf16[512,1024]{1,0:T(8,128)(2,1)} %get-tuple-element.24.hidden_ref, bf16[128,512]{1,0:T(8,128)(2,1)} %copy-done, bf16[128,512]{1,0:T(8,128)(2,1)} %copy-done.1, bf16[128,512]{1,0:T(8,128)(2,1)} %copy-done.2, ...), custom_call_target="tpu_custom_call" | custom-call | tf_op jit(solution)/shard_map/head_grad/pallas_call | solution.py:214
  112.8 1.7 %collective-permute-start.37 = (bf16[256,512]{1,0:T(8,128)(2,1)}, bf16[256,512]{1,0:T(8,128)(2,1)S(1)}, u32[]{:S(2)}, u32[]{:S(2)}) collective-permute-start(bf16[256,512]{1,0:T(8,128)(2,1)} %get-tuple-element.28), channel_id=1, source_target_pairs={{0,32},{1,33},{2,34},{3,35},{4,36},{5,37},{6,38},{7,39},{8,40},{9,... | collective-permute-start | bytes 786440 | tf_op jit(solution)/shard_map/ppermute | solution.py:29
  114.5 3.0 %collective-permute-start.36 = (bf16[256,512]{1,0:T(8,128)(2,1)}, bf16[256,512]{1,0:T(8,128)(2,1)S(1)}, u32[]{:S(2)}, u32[]{:S(2)}) collective-permute-start(bf16[256,512]{1,0:T(8,128)(2,1)} %get-tuple-element.27), channel_id=1, source_target_pairs={{0,64},{1,65},{2,66},{3,67},{4,68},{5,69},{6,70},{7,71},{8,72},{9,... | collective-permute-start | bytes 786440 | tf_op jit(solution)/shard_map/ppermute | solution.py:29
  118.4 2.1 %collective-permute-start.28 = (bf16[128,256]{1,0:T(8,128)(2,1)S(1)}, bf16[128,256]{1,0:T(8,128)(2,1)S(1)}, u32[]{:S(2)}, u32[]{:S(2)}) collective-permute-start(bf16[128,256]{1,0:T(8,128)(2,1)S(1)} %get-tuple-element.48), channel_id=1, source_target_pairs={{0,4},{1,5},{2,6},{3,7},{4,0},{5,1},{6,2},{7,3},{8,12},{9,13},{10,... | collective-permute-start | bytes 196616 | tf_op jit(solution)/shard_map/ppermute | solution.py:29
  126.1 7.4 %collective-permute-start.34 = (bf16[128,256]{1,0:T(8,128)(2,1)S(1)}, bf16[128,256]{1,0:T(8,128)(2,1)S(1)}, u32[]{:S(2)}, u32[]{:S(2)}) collective-permute-start(bf16[128,256]{1,0:T(8,128)(2,1)S(1)} %fusion.26), channel_id=1, source_target_pairs={{0,0},{1,8},{2,16},{3,24},{4,4},{5,12},{6,20},{7,28},{8,1},{9,9},{... | collective-permute-start | bytes 196616 | tf_op jit(solution)/shard_map/ppermute | solution.py:29
  133.6 2.0 %convert_add_fusion = f32[256,512]{1,0:T(8,128)} fusion(bf16[256,512]{1,0:T(8,128)(2,1)S(1)} %collective-permute-done.37, bf16[256,512]{1,0:T(8,128)(2,1)S(1)} %collective-permute-done.36, f32[256,512]{1,0:T(8,128)} %get-tuple-element.25, bf16[256,512]{1,0:T(8,128)(2,1)S(1)} %collective-permute-done.35), kind=kLoop, calls=%fused_computation.10 | loop fusion | flops 786432 | bytes 1835008 | tf_op jit(solution)/shard_map/add | solution.py:344
  (104 shorter events, 29.1 us)
Async XLA Ops:
  5.1 26.4 %collective-permute-start = (f32[8,136,512]{2,1,0:T(8,128)}, f32[8,136,512]{2,1,0:T(8,128)S(1)}, u32[]{:S(2)}, u32[]{:S(2)}) collective-permute-start(f32[8,136,512]{2,1,0:T(8,128)} %teacher.3), channel_id=1, source_target_pairs={{0,1},{1,0},{2,3},{3,2},{4,5},{5,4},{6,7},{7,6},{8,9},{9,8},{10,11... | collective-permute-start | bytes 6684680 | tf_op jit(solution)/shard_map/ppermute | solution.py:29
  6.9 11.3 %collective-permute-start.5 = (bf16[2,128,256]{2,1,0:T(8,128)(2,1)}, bf16[2,128,256]{2,1,0:T(8,128)(2,1)S(1)}, u32[]{:S(2)}, u32[]{:S(2)}) collective-permute-start(bf16[2,128,256]{2,1,0:T(8,128)(2,1)} %get-tuple-element.16), channel_id=1, source_target_pairs={{0,8},{1,9},{2,10},{3,11},{4,12},{5,13},{6,14},{7,15},{8,16},{9,17... | collective-permute-start | bytes 393224 | tf_op jit(solution)/shard_map/ppermute | solution.py:29
  10.2 15.3 %collective-permute-start.6 = (bf16[2,128,256]{2,1,0:T(8,128)(2,1)}, bf16[2,128,256]{2,1,0:T(8,128)(2,1)S(1)}, u32[]{:S(2)}, u32[]{:S(2)}) collective-permute-start(bf16[2,128,256]{2,1,0:T(8,128)(2,1)} %get-tuple-element.17), channel_id=1, source_target_pairs={{0,16},{1,17},{2,18},{3,19},{4,20},{5,21},{6,22},{7,23},{8,24},{9,... | collective-permute-start | bytes 393224 | tf_op jit(solution)/shard_map/ppermute | solution.py:29
  15.6 13.1 %collective-permute-start.7 = (bf16[2,128,256]{2,1,0:T(8,128)(2,1)}, bf16[2,128,256]{2,1,0:T(8,128)(2,1)S(1)}, u32[]{:S(2)}, u32[]{:S(2)}) collective-permute-start(bf16[2,128,256]{2,1,0:T(8,128)(2,1)} %get-tuple-element.18), channel_id=1, source_target_pairs={{0,24},{1,25},{2,26},{3,27},{4,28},{5,29},{6,30},{7,31},{8,0},{9,1... | collective-permute-start | bytes 393224 | tf_op jit(solution)/shard_map/ppermute | solution.py:29
  18.2 13.3 %collective-permute-start.8 = (bf16[2,128,256]{2,1,0:T(8,128)(2,1)S(1)}, bf16[2,128,256]{2,1,0:T(8,128)(2,1)S(1)}, u32[]{:S(2)}, u32[]{:S(2)}) collective-permute-start(bf16[2,128,256]{2,1,0:T(8,128)(2,1)S(1)} %collective-permute-done.5.refs_4_), channel_id=1, source_target_pairs={{0,1},{1,0},{2,3},{3,2},{4,5},{5,4},{6,7},{7,6},{8,9},{9,8},{10,11... | collective-permute-start | bytes 393224 | tf_op jit(solution)/shard_map/ppermute | solution.py:29
  18.2 19.5 %collective-permute-start.11 = (bf16[256,512]{1,0:T(8,128)(2,1)}, bf16[256,512]{1,0:T(8,128)(2,1)}, u32[]{:S(2)}, u32[]{:S(2)}) collective-permute-start(bf16[256,512]{1,0:T(8,128)(2,1)} %refs_10_.1), channel_id=1, source_target_pairs={{0,32},{1,33},{2,34},{3,35},{4,36},{5,37},{6,38},{7,39},{8,40},{9,... | collective-permute-start | bytes 786440 | tf_op jit(solution)/shard_map/ppermute | solution.py:29
  25.5 14.0 %collective-permute-start.12 = (bf16[256,512]{1,0:T(8,128)(2,1)}, bf16[256,512]{1,0:T(8,128)(2,1)}, u32[]{:S(2)}, u32[]{:S(2)}) collective-permute-start(bf16[256,512]{1,0:T(8,128)(2,1)} %refs_10_.1), channel_id=1, source_target_pairs={{0,64},{1,65},{2,66},{3,67},{4,68},{5,69},{6,70},{7,71},{8,72},{9,... | collective-permute-start | bytes 786440 | tf_op jit(solution)/shard_map/ppermute | solution.py:29
  28.7 12.2 %collective-permute-start.13 = (bf16[256,512]{1,0:T(8,128)(2,1)}, bf16[256,512]{1,0:T(8,128)(2,1)}, u32[]{:S(2)}, u32[]{:S(2)}) collective-permute-start(bf16[256,512]{1,0:T(8,128)(2,1)} %refs_10_.1), channel_id=1, source_target_pairs={{0,96},{1,97},{2,98},{3,99},{4,100},{5,101},{6,102},{7,103},{8,104... | collective-permute-start | bytes 786440 | tf_op jit(solution)/shard_map/ppermute | solution.py:29
  34.6 19.5 %collective-permute-start.3 = (f16[2,136,512]{2,1,0:T(8,128)(2,1)}, f16[2,136,512]{2,1,0:T(8,128)(2,1)S(1)}, u32[]{:S(2)}, u32[]{:S(2)}) collective-permute-start(f16[2,136,512]{2,1,0:T(8,128)(2,1)} %get-tuple-element.40), channel_id=1, source_target_pairs={{0,6},{1,7},{2,0},{3,1},{4,2},{5,3},{6,4},{7,5},{8,14},{9,15},{10,... | collective-permute-start | bytes 835592 | tf_op jit(solution)/shard_map/ppermute | solution.py:29
  35.2 22.8 %collective-permute-start.2 = (f16[2,136,512]{2,1,0:T(8,128)(2,1)S(1)}, f16[2,136,512]{2,1,0:T(8,128)(2,1)S(1)}, u32[]{:S(2)}, u32[]{:S(2)}) collective-permute-start(f16[2,136,512]{2,1,0:T(8,128)(2,1)S(1)} %get-tuple-element.41), channel_id=1, source_target_pairs={{0,4},{1,5},{2,6},{3,7},{4,0},{5,1},{6,2},{7,3},{8,12},{9,13},{10,... | collective-permute-start | bytes 835592 | tf_op jit(solution)/shard_map/ppermute | solution.py:29
  37.7 20.2 %collective-permute-start.1 = (f16[2,136,512]{2,1,0:T(8,128)(2,1)S(1)}, f16[2,136,512]{2,1,0:T(8,128)(2,1)}, u32[]{:S(2)}, u32[]{:S(2)}) collective-permute-start(f16[2,136,512]{2,1,0:T(8,128)(2,1)S(1)} %get-tuple-element.39), channel_id=1, source_target_pairs={{0,2},{1,3},{2,4},{3,5},{4,6},{5,7},{6,0},{7,1},{8,10},{9,11},{10,... | collective-permute-start | bytes 835592 | tf_op jit(solution)/shard_map/ppermute | solution.py:29
  46.0 13.5 %collective-permute-start.16 = (f16[128,512]{1,0:T(8,128)(2,1)S(1)}, f16[128,512]{1,0:T(8,128)(2,1)S(1)}, u32[]{:S(2)}, u32[]{:S(2)}) collective-permute-start(f16[128,512]{1,0:T(8,128)(2,1)S(1)} %get-tuple-element.50), channel_id=1, source_target_pairs={{0,8},{1,9},{2,10},{3,11},{4,12},{5,13},{6,14},{7,15},{8,16},{9,17... | collective-permute-start | bytes 393224 | tf_op jit(solution)/shard_map/ppermute | solution.py:29
  49.8 13.5 %collective-permute-start.15 = (f16[128,512]{1,0:T(8,128)(2,1)S(1)}, f16[128,512]{1,0:T(8,128)(2,1)S(1)}, u32[]{:S(2)}, u32[]{:S(2)}) collective-permute-start(f16[128,512]{1,0:T(8,128)(2,1)S(1)} %get-tuple-element.51), channel_id=1, source_target_pairs={{0,16},{1,17},{2,18},{3,19},{4,20},{5,21},{6,22},{7,23},{8,24},{9,... | collective-permute-start | bytes 393224 | tf_op jit(solution)/shard_map/ppermute | solution.py:29
  54.1 11.3 %collective-permute-start.14 = (f16[128,512]{1,0:T(8,128)(2,1)S(1)}, f16[128,512]{1,0:T(8,128)(2,1)S(1)}, u32[]{:S(2)}, u32[]{:S(2)}) collective-permute-start(f16[128,512]{1,0:T(8,128)(2,1)S(1)} %get-tuple-element.49), channel_id=1, source_target_pairs={{0,24},{1,25},{2,26},{3,27},{4,28},{5,29},{6,30},{7,31},{8,0},{9,1... | collective-permute-start | bytes 393224 | tf_op jit(solution)/shard_map/ppermute | solution.py:29
  59.3 7.4 %collective-permute-start.4 = (f16[136,512]{1,0:T(8,128)(2,1)S(1)}, f16[136,512]{1,0:T(8,128)(2,1)S(1)}, u32[]{:S(2)}, u32[]{:S(2)}) collective-permute-start(f16[136,512]{1,0:T(8,128)(2,1)S(1)} %fusion.10), channel_id=1, source_target_pairs={{0,128},{1,129},{2,130},{3,131},{4,132},{5,133},{6,134},{7,135},{8... | collective-permute-start | bytes 417800 | tf_op jit(solution)/shard_map/ppermute | solution.py:29
  71.4 9.3 %collective-permute-start.23 = (bf16[128,512]{1,0:T(8,128)(2,1)S(1)}, bf16[128,512]{1,0:T(8,128)(2,1)S(1)}, u32[]{:S(2)}, u32[]{:S(2)}) collective-permute-start(bf16[128,512]{1,0:T(8,128)(2,1)S(1)} %subtract_convert_fusion.refs_0_), channel_id=1, source_target_pairs={{0,8},{1,9},{2,10},{3,11},{4,12},{5,13},{6,14},{7,15},{8,16},{9,17... | collective-permute-start | bytes 393224 | tf_op jit(solution)/shard_map/ppermute | solution.py:29
  73.6 14.4 %collective-permute-start.24 = (bf16[128,512]{1,0:T(8,128)(2,1)S(1)}, bf16[128,512]{1,0:T(8,128)(2,1)S(1)}, u32[]{:S(2)}, u32[]{:S(2)}) collective-permute-start(bf16[128,512]{1,0:T(8,128)(2,1)S(1)} %subtract_convert_fusion.refs_0_), channel_id=1, source_target_pairs={{0,16},{1,17},{2,18},{3,19},{4,20},{5,21},{6,22},{7,23},{8,24},{9,... | collective-permute-start | bytes 393224 | tf_op jit(solution)/shard_map/ppermute | solution.py:29
  76.9 11.2 %collective-permute-start.25 = (bf16[128,512]{1,0:T(8,128)(2,1)S(1)}, bf16[128,512]{1,0:T(8,128)(2,1)S(1)}, u32[]{:S(2)}, u32[]{:S(2)}) collective-permute-start(bf16[128,512]{1,0:T(8,128)(2,1)S(1)} %subtract_convert_fusion.refs_0_), channel_id=1, source_target_pairs={{0,24},{1,25},{2,26},{3,27},{4,28},{5,29},{6,30},{7,31},{8,0},{9,1... | collective-permute-start | bytes 393224 | tf_op jit(solution)/shard_map/ppermute | solution.py:29
  92.3 9.1 %collective-permute-start.26 = (f32[8,128,256]{2,1,0:T(8,128)}, f32[8,128,256]{2,1,0:T(8,128)S(1)}, u32[]{:S(2)}, u32[]{:S(2)}) collective-permute-start(f32[8,128,256]{2,1,0:T(8,128)} %get-tuple-element.23), channel_id=1, source_target_pairs={{0,1},{1,0},{2,3},{3,2},{4,5},{5,4},{6,7},{7,6},{8,9},{9,8},{10,11... | collective-permute-start | bytes 3145736 | tf_op jit(solution)/shard_map/ppermute | solution.py:29
  92.4 6.1 %collective-permute-start.22 = (f32[1,128]{1,0:T(1,128)S(1)}, f32[1,128]{1,0:T(1,128)S(1)}, u32[]{:S(2)}, u32[]{:S(2)}) collective-permute-start(f32[1,128]{1,0:T(1,128)S(1)} %bitcast_multiply_fusion), channel_id=1, source_target_pairs={{0,132},{1,133},{2,134},{3,135},{4,128},{5,129},{6,130},{7,131},{8... | collective-permute-start | bytes 1544 | tf_op jit(solution)/shard_map/ppermute | solution.py:29
  92.5 6.0 %collective-permute-start.21 = (f32[1,128]{1,0:T(1,128)S(1)}, f32[1,128]{1,0:T(1,128)S(1)}, u32[]{:S(2)}, u32[]{:S(2)}) collective-permute-start(f32[1,128]{1,0:T(1,128)S(1)} %bitcast_multiply_fusion), channel_id=1, source_target_pairs={{0,128},{1,129},{2,130},{3,131},{4,132},{5,133},{6,134},{7,135},{8... | collective-permute-start | bytes 1544 | tf_op jit(solution)/shard_map/ppermute | solution.py:29
  96.4 5.1 %collective-permute-start.20 = (f32[1,128]{1,0:T(1,128)S(1)}, f32[1,128]{1,0:T(1,128)S(1)}, u32[]{:S(2)}, u32[]{:S(2)}) collective-permute-start(f32[1,128]{1,0:T(1,128)S(1)} %bitcast_multiply_fusion), channel_id=1, source_target_pairs={{0,4},{1,5},{2,6},{3,7},{4,0},{5,1},{6,2},{7,3},{8,12},{9,13},{10,... | collective-permute-start | bytes 1544 | tf_op jit(solution)/shard_map/ppermute | solution.py:29
  102.8 10.0 %collective-permute-start.33 = (bf16[128,256]{1,0:T(8,128)(2,1)S(1)}, bf16[128,256]{1,0:T(8,128)(2,1)S(1)}, u32[]{:S(2)}, u32[]{:S(2)}) collective-permute-start(bf16[128,256]{1,0:T(8,128)(2,1)S(1)} %get-tuple-element.43), channel_id=1, source_target_pairs={{0,128},{1,129},{2,130},{3,131},{4,132},{5,133},{6,134},{7,135},{8... | collective-permute-start | bytes 196616 | tf_op jit(solution)/shard_map/ppermute | solution.py:29
  102.9 11.6 %collective-permute-start.32 = (bf16[128,256]{1,0:T(8,128)(2,1)S(1)}, bf16[128,256]{1,0:T(8,128)(2,1)S(1)}, u32[]{:S(2)}, u32[]{:S(2)}) collective-permute-start(bf16[128,256]{1,0:T(8,128)(2,1)S(1)} %get-tuple-element.44), channel_id=1, source_target_pairs={{0,134},{1,135},{2,128},{3,129},{4,130},{5,131},{6,132},{7,133},{8... | collective-permute-start | bytes 196616 | tf_op jit(solution)/shard_map/ppermute | solution.py:29
  106.2 11.3 %collective-permute-start.31 = (bf16[128,256]{1,0:T(8,128)(2,1)S(1)}, bf16[128,256]{1,0:T(8,128)(2,1)S(1)}, u32[]{:S(2)}, u32[]{:S(2)}) collective-permute-start(bf16[128,256]{1,0:T(8,128)(2,1)S(1)} %get-tuple-element.45), channel_id=1, source_target_pairs={{0,130},{1,131},{2,132},{3,133},{4,134},{5,135},{6,128},{7,129},{8... | collective-permute-start | bytes 196616 | tf_op jit(solution)/shard_map/ppermute | solution.py:29
  106.2 12.2 %collective-permute-start.30 = (bf16[128,256]{1,0:T(8,128)(2,1)S(1)}, bf16[128,256]{1,0:T(8,128)(2,1)S(1)}, u32[]{:S(2)}, u32[]{:S(2)}) collective-permute-start(bf16[128,256]{1,0:T(8,128)(2,1)S(1)} %get-tuple-element.46), channel_id=1, source_target_pairs={{0,132},{1,133},{2,134},{3,135},{4,128},{5,129},{6,130},{7,131},{8... | collective-permute-start | bytes 196616 | tf_op jit(solution)/shard_map/ppermute | solution.py:29
  109.6 10.9 %collective-permute-start.29 = (bf16[128,256]{1,0:T(8,128)(2,1)S(1)}, bf16[128,256]{1,0:T(8,128)(2,1)S(1)}, u32[]{:S(2)}, u32[]{:S(2)}) collective-permute-start(bf16[128,256]{1,0:T(8,128)(2,1)S(1)} %get-tuple-element.47), channel_id=1, source_target_pairs={{0,6},{1,7},{2,0},{3,1},{4,2},{5,3},{6,4},{7,5},{8,14},{9,15},{10,... | collective-permute-start | bytes 196616 | tf_op jit(solution)/shard_map/ppermute | solution.py:29
  112.8 20.7 %collective-permute-start.37 = (bf16[256,512]{1,0:T(8,128)(2,1)}, bf16[256,512]{1,0:T(8,128)(2,1)S(1)}, u32[]{:S(2)}, u32[]{:S(2)}) collective-permute-start(bf16[256,512]{1,0:T(8,128)(2,1)} %get-tuple-element.28), channel_id=1, source_target_pairs={{0,32},{1,33},{2,34},{3,35},{4,36},{5,37},{6,38},{7,39},{8,40},{9,... | collective-permute-start | bytes 786440 | tf_op jit(solution)/shard_map/ppermute | solution.py:29
  114.5 19.0 %collective-permute-start.36 = (bf16[256,512]{1,0:T(8,128)(2,1)}, bf16[256,512]{1,0:T(8,128)(2,1)S(1)}, u32[]{:S(2)}, u32[]{:S(2)}) collective-permute-start(bf16[256,512]{1,0:T(8,128)(2,1)} %get-tuple-element.27), channel_id=1, source_target_pairs={{0,64},{1,65},{2,66},{3,67},{4,68},{5,69},{6,70},{7,71},{8,72},{9,... | collective-permute-start | bytes 786440 | tf_op jit(solution)/shard_map/ppermute | solution.py:29
  117.5 16.1 %collective-permute-start.35 = (bf16[256,512]{1,0:T(8,128)(2,1)}, bf16[256,512]{1,0:T(8,128)(2,1)S(1)}, u32[]{:S(2)}, u32[]{:S(2)}) collective-permute-start(bf16[256,512]{1,0:T(8,128)(2,1)} %get-tuple-element.26), channel_id=1, source_target_pairs={{0,96},{1,97},{2,98},{3,99},{4,100},{5,101},{6,102},{7,103},{8,104... | collective-permute-start | bytes 786440 | tf_op jit(solution)/shard_map/ppermute | solution.py:29
  118.4 5.8 %collective-permute-start.28 = (bf16[128,256]{1,0:T(8,128)(2,1)S(1)}, bf16[128,256]{1,0:T(8,128)(2,1)S(1)}, u32[]{:S(2)}, u32[]{:S(2)}) collective-permute-start(bf16[128,256]{1,0:T(8,128)(2,1)S(1)} %get-tuple-element.48), channel_id=1, source_target_pairs={{0,4},{1,5},{2,6},{3,7},{4,0},{5,1},{6,2},{7,3},{8,12},{9,13},{10,... | collective-permute-start | bytes 196616 | tf_op jit(solution)/shard_map/ppermute | solution.py:29
  126.1 11.0 %collective-permute-start.34 = (bf16[128,256]{1,0:T(8,128)(2,1)S(1)}, bf16[128,256]{1,0:T(8,128)(2,1)S(1)}, u32[]{:S(2)}, u32[]{:S(2)}) collective-permute-start(bf16[128,256]{1,0:T(8,128)(2,1)S(1)} %fusion.26), channel_id=1, source_target_pairs={{0,0},{1,8},{2,16},{3,24},{4,4},{5,12},{6,20},{7,28},{8,1},{9,9},{... | collective-permute-start | bytes 196616 | tf_op jit(solution)/shard_map/ppermute | solution.py:29
  (18 other events, 116.7 us)

commit v10 on v8

--- a/solution.py
+++ b/solution.py
@@ -353,9 +353,9 @@
         return zl, y, x % 2 * 2 + core, x // 2 * 2 + zh // 2, zh % 2
 
     by_x = by_x.astype(bf16)
-    hidden_grad = send(by_x[0], home).astype(f32) + send(
-        by_x[1], lambda zl, y, zh, x, core: home(1 - zl, y, zh, x, core)
-    ).astype(f32)
+    same = send(by_x[0], home)
+    other = send(by_x[1], lambda zl, y, zh, x, core: home(1 - zl, y, zh, x, core))
+    hidden_grad = same.astype(f32) + other.astype(f32)
     return (kl_terms, hidden_grad, head_grad)
 
 

time: 132 us -> 132 us (level)
  no operation moved by 1% of the time
where the time goes in v10:
time: 132 us; the launch traced here: 130 us
  starting transfers between devices  67.2 us (51%)
  waiting for transfers between devices  28.6 us (22%)
  Pallas kernels  20.8 us (16%)
  other arithmetic  11.5 us (9%)
    ppermute x35, starting transfers between devices, send(): return lax.ppermute(value, ALL, pairs)  67.2 us
    ppermute x35, waiting for transfers between devices, send(): return lax.ppermute(value, ALL, pairs)  28.6 us
    pallas_call x2, Pallas kernels, teacher_parts(): pl.pallas_call(teacher_kernel, grid_spec=pltpu.PrefetchScalarGridSpec(num...  8.82 us
    pallas_call x1, Pallas kernels, student_parts(): pl.pallas_call(student_kernel, grid_spec=pltpu.PrefetchScalarGridSpec(num...  3.68 us
    pallas_call x1, Pallas kernels, hidden_grad_parts(): pl.pallas_call(hidden_grad_kernel, in_specs=[pl.BlockSpec(memory_space=pl...  3.53 us
    pallas_call x1, Pallas kernels, head_grad_parts(): pl.pallas_call(head_grad_kernel, out_shape=(jax.ShapeDtypeStruct((256, 51...  2.94 us
  transfers between devices with their start and end apart: 35, of which 13 were waited for; matrix products, arithmetic and copies ran while one was open for 7% of the time, Pallas kernels for 10%

profile of v10, /device:TPU:2, one launch (start us, length us, event | category | flops | bytes accessed | tf_op | source)
XLA Modules:
  0.0 130.0 jit_solution(4440026228681713786)
XLA Ops:
  0.6 4.5 %teacher.3 = f32[8,136,512]{2,1,0:T(8,128)} custom-call(s32[1]{0:T(128)} %bitcast.index_ref, bf16[128,512]{1,0:T(8,128)(2,1)} %hidden_ref.3, bf16[512]{0:T(512)(128)(2,1)} %gain_ref.3, bf16[512,8192]{1,0:T(8,128)(2,1)} %refs_3_.5, bf16[512,8192]{1,0:T(8,128)(2,1)} %refs_3_.5, bf16[512,8192]{1,0:T(8,128)(2,1)} %refs_3_.5, bf16[512,8192]{1,0:T(8,128)(2,1)} %refs_3_.5), custom_call_target="tpu_custom_call" | custom-call | tf_op jit(solution)/shard_map/teacher/pallas_call | solution.py:132
  5.1 1.8 %pick.1 = (bf16[2,128,256]{2,1,0:T(8,128)(2,1)}, bf16[2,128,256]{2,1,0:T(8,128)(2,1)}, bf16[2,128,256]{2,1,0:T(8,128)(2,1)}) custom-call(s32[1]{0:T(128)} %bitcast.index_ref, bf16[128,4096]{1,0:T(8,128)(2,1)} %refs_3_.7, bf16[128,4096]{1,0:T(8,128)(2,1)} %refs_3_.7, bf16[128,4096]{1,0:T(8,128)(2,1)} %refs_3_.7, bf16[128,4096]{1,0:T(8,128)(2,1)} %refs_3_.7, ...), custom_call_target="tpu_custom_call" | custom-call | tf_op jit(solution)/shard_map/pick/pallas_call | solution.py:79
  6.9 3.3 %collective-permute-start.5 = (bf16[2,128,256]{2,1,0:T(8,128)(2,1)}, bf16[2,128,256]{2,1,0:T(8,128)(2,1)S(1)}, u32[]{:S(2)}, u32[]{:S(2)}) collective-permute-start(bf16[2,128,256]{2,1,0:T(8,128)(2,1)} %get-tuple-element.16), channel_id=1, source_target_pairs={{0,8},{1,9},{2,10},{3,11},{4,12},{5,13},{6,14},{7,15},{8,16},{9,17... | collective-permute-start | bytes 393224 | tf_op jit(solution)/shard_map/ppermute | solution.py:29
  10.2 5.4 %collective-permute-start.6 = (bf16[2,128,256]{2,1,0:T(8,128)(2,1)}, bf16[2,128,256]{2,1,0:T(8,128)(2,1)S(1)}, u32[]{:S(2)}, u32[]{:S(2)}) collective-permute-start(bf16[2,128,256]{2,1,0:T(8,128)(2,1)} %get-tuple-element.17), channel_id=1, source_target_pairs={{0,16},{1,17},{2,18},{3,19},{4,20},{5,21},{6,22},{7,23},{8,24},{9,... | collective-permute-start | bytes 393224 | tf_op jit(solution)/shard_map/ppermute | solution.py:29
  15.6 2.7 %collective-permute-start.7 = (bf16[2,128,256]{2,1,0:T(8,128)(2,1)}, bf16[2,128,256]{2,1,0:T(8,128)(2,1)S(1)}, u32[]{:S(2)}, u32[]{:S(2)}) collective-permute-start(bf16[2,128,256]{2,1,0:T(8,128)(2,1)} %get-tuple-element.18), channel_id=1, source_target_pairs={{0,24},{1,25},{2,26},{3,27},{4,28},{5,29},{6,30},{7,31},{8,0},{9,1... | collective-permute-start | bytes 393224 | tf_op jit(solution)/shard_map/ppermute | solution.py:29
  19.9 4.3 %teacher.2 = f32[8,136,512]{2,1,0:T(8,128)} custom-call(s32[1]{0:T(128)} %bitcast.index_ref, bf16[128,512]{1,0:T(8,128)(2,1)} %hidden_ref.3, bf16[512]{0:T(512)(128)(2,1)} %gain_ref.3, bf16[512,8192]{1,0:T(8,128)(2,1)} %refs_3_.5, bf16[512,8192]{1,0:T(8,128)(2,1)} %refs_3_.5, bf16[512,8192]{1,0:T(8,128)(2,1)} %refs_3_.5, bf16[512,8192]{1,0:T(8,128)(2,1)} %refs_3_.5), custom_call_target="tpu_custom_call" | custom-call | tf_op jit(solution)/shard_map/teacher/pallas_call | solution.py:132
  25.5 3.2 %collective-permute-start.12 = (bf16[256,512]{1,0:T(8,128)(2,1)}, bf16[256,512]{1,0:T(8,128)(2,1)}, u32[]{:S(2)}, u32[]{:S(2)}) collective-permute-start(bf16[256,512]{1,0:T(8,128)(2,1)} %refs_10_.1), channel_id=1, source_target_pairs={{0,64},{1,65},{2,66},{3,67},{4,68},{5,69},{6,70},{7,71},{8,72},{9,... | collective-permute-start | bytes 786440 | tf_op jit(solution)/shard_map/ppermute | solution.py:29
  28.7 2.8 %collective-permute-start.13 = (bf16[256,512]{1,0:T(8,128)(2,1)}, bf16[256,512]{1,0:T(8,128)(2,1)}, u32[]{:S(2)}, u32[]{:S(2)}) collective-permute-start(bf16[256,512]{1,0:T(8,128)(2,1)} %refs_10_.1), channel_id=1, source_target_pairs={{0,96},{1,97},{2,98},{3,99},{4,100},{5,101},{6,102},{7,103},{8,104... | collective-permute-start | bytes 786440 | tf_op jit(solution)/shard_map/ppermute | solution.py:29
  32.1 2.5 %fusion.2 = (f16[2,136,512]{2,1,0:T(8,128)(2,1)S(1)}, f16[2,136,512]{2,1,0:T(8,128)(2,1)}, f16[2,136,512]{2,1,0:T(8,128)(2,1)S(1)}) fusion(f32[8,136,512]{2,1,0:T(8,128)S(1)} %collective-permute-done, f32[8,136,512]{2,1,0:T(8,128)} %teacher.2), kind=kLoop, calls=%fused_computation.5 | loop fusion | flops 835584 | bytes 4177920 | tf_op jit(solution)/shard_map/convert_element_type | solution.py:273
  35.2 2.5 %collective-permute-start.2 = (f16[2,136,512]{2,1,0:T(8,128)(2,1)S(1)}, f16[2,136,512]{2,1,0:T(8,128)(2,1)S(1)}, u32[]{:S(2)}, u32[]{:S(2)}) collective-permute-start(f16[2,136,512]{2,1,0:T(8,128)(2,1)S(1)} %get-tuple-element.41), channel_id=1, source_target_pairs={{0,4},{1,5},{2,6},{3,7},{4,0},{5,1},{6,2},{7,3},{8,12},{9,13},{10,... | collective-permute-start | bytes 835592 | tf_op jit(solution)/shard_map/ppermute | solution.py:29
  37.7 1.8 %collective-permute-start.1 = (f16[2,136,512]{2,1,0:T(8,128)(2,1)S(1)}, f16[2,136,512]{2,1,0:T(8,128)(2,1)}, u32[]{:S(2)}, u32[]{:S(2)}) collective-permute-start(f16[2,136,512]{2,1,0:T(8,128)(2,1)S(1)} %get-tuple-element.39), channel_id=1, source_target_pairs={{0,2},{1,3},{2,4},{3,5},{4,6},{5,7},{6,0},{7,1},{8,10},{9,11},{10,... | collective-permute-start | bytes 835592 | tf_op jit(solution)/shard_map/ppermute | solution.py:29
  40.9 3.7 %student.1 = (f32[128,512]{1,0:T(8,128)}, f32[3,128,512]{2,1,0:T(8,128)}, bf16[512,1024]{1,0:T(8,128)(2,1)}, bf16[1024,512]{1,0:T(8,128)(2,1)}) custom-call(s32[1]{0:T(128)} %bitcast.index_ref, bf16[128,4096]{1,0:T(8,128)(2,1)} %refs_3_.7, bf16[128,4096]{1,0:T(8,128)(2,1)} %refs_3_.7, bf16[128,4096]{1,0:T(8,128)(2,1)} %refs_3_.7, bf16[128,4096]{1,0:T(8,128)(2,1)} %refs_3_.7, ...), custom_call_target="tpu_custom_call" | custom-call | tf_op jit(solution)/shard_map/student/pallas_call | solution.py:176
  45.9 3.8 %collective-permute-start.16 = (f16[128,512]{1,0:T(8,128)(2,1)S(1)}, f16[128,512]{1,0:T(8,128)(2,1)S(1)}, u32[]{:S(2)}, u32[]{:S(2)}) collective-permute-start(f16[128,512]{1,0:T(8,128)(2,1)S(1)} %get-tuple-element.46), channel_id=1, source_target_pairs={{0,8},{1,9},{2,10},{3,11},{4,12},{5,13},{6,14},{7,15},{8,16},{9,17... | collective-permute-start | bytes 393224 | tf_op jit(solution)/shard_map/ppermute | solution.py:29
  49.8 4.3 %collective-permute-start.15 = (f16[128,512]{1,0:T(8,128)(2,1)S(1)}, f16[128,512]{1,0:T(8,128)(2,1)S(1)}, u32[]{:S(2)}, u32[]{:S(2)}) collective-permute-start(f16[128,512]{1,0:T(8,128)(2,1)S(1)} %get-tuple-element.47), channel_id=1, source_target_pairs={{0,16},{1,17},{2,18},{3,19},{4,20},{5,21},{6,22},{7,23},{8,24},{9,... | collective-permute-start | bytes 393224 | tf_op jit(solution)/shard_map/ppermute | solution.py:29
  54.1 3.9 %collective-permute-start.14 = (f16[128,512]{1,0:T(8,128)(2,1)S(1)}, f16[128,512]{1,0:T(8,128)(2,1)S(1)}, u32[]{:S(2)}, u32[]{:S(2)}) collective-permute-start(f16[128,512]{1,0:T(8,128)(2,1)S(1)} %get-tuple-element.45), channel_id=1, source_target_pairs={{0,24},{1,25},{2,26},{3,27},{4,28},{5,29},{6,30},{7,31},{8,0},{9,1... | collective-permute-start | bytes 393224 | tf_op jit(solution)/shard_map/ppermute | solution.py:29
  59.4 3.8 %collective-permute-done.15 = f16[128,512]{1,0:T(8,128)(2,1)S(1)} collective-permute-done((f16[128,512]{1,0:T(8,128)(2,1)S(1)}, f16[128,512]{1,0:T(8,128)(2,1)S(1)}, u32[]{:S(2)}, u32[]{:S(2)}) %collective-permute-start.15) | collective-permute-done | bytes 131104 | tf_op jit(solution)/shard_map/ppermute | solution.py:29
  63.2 2.1 %collective-permute-done.14 = f16[128,512]{1,0:T(8,128)(2,1)S(1)} collective-permute-done((f16[128,512]{1,0:T(8,128)(2,1)S(1)}, f16[128,512]{1,0:T(8,128)(2,1)S(1)}, u32[]{:S(2)}, u32[]{:S(2)}) %collective-permute-start.14) | collective-permute-done | bytes 131104 | tf_op jit(solution)/shard_map/ppermute | solution.py:29
  71.4 2.3 %collective-permute-start.23 = (bf16[128,512]{1,0:T(8,128)(2,1)S(1)}, bf16[128,512]{1,0:T(8,128)(2,1)S(1)}, u32[]{:S(2)}, u32[]{:S(2)}) collective-permute-start(bf16[128,512]{1,0:T(8,128)(2,1)S(1)} %subtract_convert_fusion.refs_0_), channel_id=1, source_target_pairs={{0,8},{1,9},{2,10},{3,11},{4,12},{5,13},{6,14},{7,15},{8,16},{9,17... | collective-permute-start | bytes 393224 | tf_op jit(solution)/shard_map/ppermute | solution.py:29
  73.6 3.2 %collective-permute-start.24 = (bf16[128,512]{1,0:T(8,128)(2,1)S(1)}, bf16[128,512]{1,0:T(8,128)(2,1)S(1)}, u32[]{:S(2)}, u32[]{:S(2)}) collective-permute-start(bf16[128,512]{1,0:T(8,128)(2,1)S(1)} %subtract_convert_fusion.refs_0_), channel_id=1, source_target_pairs={{0,16},{1,17},{2,18},{3,19},{4,20},{5,21},{6,22},{7,23},{8,24},{9,... | collective-permute-start | bytes 393224 | tf_op jit(solution)/shard_map/ppermute | solution.py:29
  78.4 2.3 %collective-permute-done.23.refs_1_ = bf16[128,512]{1,0:T(8,128)(2,1)S(1)} collective-permute-done((bf16[128,512]{1,0:T(8,128)(2,1)S(1)}, bf16[128,512]{1,0:T(8,128)(2,1)S(1)}, u32[]{:S(2)}, u32[]{:S(2)}) %collective-permute-start.23) | collective-permute-done | bytes 131104 | tf_op jit(solution)/shard_map/ppermute | solution.py:29
  80.7 7.4 %collective-permute-done.24.refs_2_ = bf16[128,512]{1,0:T(8,128)(2,1)S(1)} collective-permute-done((bf16[128,512]{1,0:T(8,128)(2,1)S(1)}, bf16[128,512]{1,0:T(8,128)(2,1)S(1)}, u32[]{:S(2)}, u32[]{:S(2)}) %collective-permute-start.24) | collective-permute-done | bytes 131104 | tf_op jit(solution)/shard_map/ppermute | solution.py:29
  88.8 3.5 %hidden_grad.1 = (f32[8,128,256]{2,1,0:T(8,128)}, f32[8,128,256]{2,1,0:T(8,128)}) custom-call(s32[1]{0:T(128)} %bitcast.index_ref, bf16[128,512]{1,0:T(8,128)(2,1)} %copy-done, bf16[128,512]{1,0:T(8,128)(2,1)} %copy-done.1, bf16[128,512]{1,0:T(8,128)(2,1)} %copy-done.2, bf16[128,512]{1,0:T(8,128)(2,1)} %copy-done.3, bf16[1024,512]{1,0:T(8,128)(2,1)} %get-tuple-element.21.refs_4_), custom_call_target="tpu_custom_call" | custom-call | tf_op jit(solution)/shard_map/hidden_grad/pallas_call | solution.py:248
  92.5 3.8 %collective-permute-start.21 = (f32[1,128]{1,0:T(1,128)S(1)}, f32[1,128]{1,0:T(1,128)S(1)}, u32[]{:S(2)}, u32[]{:S(2)}) collective-permute-start(f32[1,128]{1,0:T(1,128)S(1)} %bitcast_multiply_fusion), channel_id=1, source_target_pairs={{0,128},{1,129},{2,130},{3,131},{4,132},{5,133},{6,134},{7,135},{8... | collective-permute-start | bytes 1544 | tf_op jit(solution)/shard_map/ppermute | solution.py:29
  98.5 3.0 %collective-permute-done.20 = f32[1,128]{1,0:T(1,128)S(1)} collective-permute-done((f32[1,128]{1,0:T(1,128)S(1)}, f32[1,128]{1,0:T(1,128)S(1)}, u32[]{:S(2)}, u32[]{:S(2)}) %collective-permute-start.20) | collective-permute-done | bytes 544 | tf_op jit(solution)/shard_map/ppermute | solution.py:29
  102.7 1.9 %collective-permute-start.29 = (bf16[2,128,256]{2,1,0:T(8,128)(2,1)S(1)}, bf16[2,128,256]{2,1,0:T(8,128)(2,1)S(1)}, u32[]{:S(2)}, u32[]{:S(2)}) collective-permute-start(bf16[2,128,256]{2,1,0:T(8,128)(2,1)S(1)} %get-tuple-element.43), channel_id=1, source_target_pairs={{0,6},{1,7},{2,0},{3,1},{4,2},{5,3},{6,4},{7,5},{8,14},{9,15},{10,... | collective-permute-start | bytes 393224 | tf_op jit(solution)/shard_map/ppermute | solution.py:29
  104.7 1.8 %collective-permute-start.27 = (bf16[2,128,256]{2,1,0:T(8,128)(2,1)S(1)}, bf16[2,128,256]{2,1,0:T(8,128)(2,1)S(1)}, u32[]{:S(2)}, u32[]{:S(2)}) collective-permute-start(bf16[2,128,256]{2,1,0:T(8,128)(2,1)S(1)} %get-tuple-element.42), channel_id=1, source_target_pairs={{0,2},{1,3},{2,4},{3,5},{4,6},{5,7},{6,0},{7,1},{8,10},{9,11},{10,... | collective-permute-start | bytes 393224 | tf_op jit(solution)/shard_map/ppermute | solution.py:29
  107.1 2.9 %head_grad.1 = (f32[256,512]{1,0:T(8,128)}, bf16[256,512]{1,0:T(8,128)(2,1)}, bf16[256,512]{1,0:T(8,128)(2,1)}, bf16[256,512]{1,0:T(8,128)(2,1)}) custom-call(bf16[512,1024]{1,0:T(8,128)(2,1)} %get-tuple-element.24.hidden_ref, bf16[128,512]{1,0:T(8,128)(2,1)} %copy-done, bf16[128,512]{1,0:T(8,128)(2,1)} %copy-done.1, bf16[128,512]{1,0:T(8,128)(2,1)} %copy-done.2, ...), custom_call_target="tpu_custom_call" | custom-call | tf_op jit(solution)/shard_map/head_grad/pallas_call | solution.py:214
  111.6 3.0 %collective-permute-start.33 = (bf16[256,512]{1,0:T(8,128)(2,1)}, bf16[256,512]{1,0:T(8,128)(2,1)S(1)}, u32[]{:S(2)}, u32[]{:S(2)}) collective-permute-start(bf16[256,512]{1,0:T(8,128)(2,1)} %get-tuple-element.27), channel_id=1, source_target_pairs={{0,64},{1,65},{2,66},{3,67},{4,68},{5,69},{6,70},{7,71},{8,72},{9,... | collective-permute-start | bytes 786440 | tf_op jit(solution)/shard_map/ppermute | solution.py:29
  116.5 1.9 %collective-permute-start.31 = (bf16[128,256]{1,0:T(8,128)(2,1)S(1)}, bf16[128,256]{1,0:T(8,128)(2,1)S(1)}, u32[]{:S(2)}, u32[]{:S(2)}) collective-permute-start(bf16[128,256]{1,0:T(8,128)(2,1)S(1)} %get-tuple-element.49), channel_id=1, source_target_pairs={{0,128},{1,136},{2,144},{3,152},{4,132},{5,140},{6,148},{7,156},{8... | collective-permute-start | bytes 196616 | tf_op jit(solution)/shard_map/ppermute | solution.py:29
  118.4 5.5 %collective-permute-start.30 = (bf16[128,256]{1,0:T(8,128)(2,1)S(1)}, bf16[128,256]{1,0:T(8,128)(2,1)S(1)}, u32[]{:S(2)}, u32[]{:S(2)}) collective-permute-start(bf16[128,256]{1,0:T(8,128)(2,1)S(1)} %get-tuple-element.48), channel_id=1, source_target_pairs={{0,0},{1,8},{2,16},{3,24},{4,4},{5,12},{6,20},{7,28},{8,1},{9,9},{... | collective-permute-start | bytes 196616 | tf_op jit(solution)/shard_map/ppermute | solution.py:29
  124.6 2.0 %convert_add_fusion = f32[256,512]{1,0:T(8,128)} fusion(bf16[256,512]{1,0:T(8,128)(2,1)S(1)} %collective-permute-done.34, bf16[256,512]{1,0:T(8,128)(2,1)S(1)} %collective-permute-done.33, f32[256,512]{1,0:T(8,128)} %get-tuple-element.25, bf16[256,512]{1,0:T(8,128)(2,1)S(1)} %collective-permute-done.32), kind=kLoop, calls=%fused_computation.10 | loop fusion | flops 786432 | bytes 1835008 | tf_op jit(solution)/shard_map/add | solution.py:344
  126.5 2.8 %collective-permute-done.30 = bf16[128,256]{1,0:T(8,128)(2,1)S(1)} collective-permute-done((bf16[128,256]{1,0:T(8,128)(2,1)S(1)}, bf16[128,256]{1,0:T(8,128)(2,1)S(1)}, u32[]{:S(2)}, u32[]{:S(2)}) %collective-permute-start.30) | collective-permute-done | bytes 65568 | tf_op jit(solution)/shard_map/ppermute | solution.py:29
  (99 shorter events, 25.5 us)
Async XLA Ops:
  5.1 26.4 %collective-permute-start = (f32[8,136,512]{2,1,0:T(8,128)}, f32[8,136,512]{2,1,0:T(8,128)S(1)}, u32[]{:S(2)}, u32[]{:S(2)}) collective-permute-start(f32[8,136,512]{2,1,0:T(8,128)} %teacher.3), channel_id=1, source_target_pairs={{0,1},{1,0},{2,3},{3,2},{4,5},{5,4},{6,7},{7,6},{8,9},{9,8},{10,11... | collective-permute-start | bytes 6684680 | tf_op jit(solution)/shard_map/ppermute | solution.py:29
  6.9 11.3 %collective-permute-start.5 = (bf16[2,128,256]{2,1,0:T(8,128)(2,1)}, bf16[2,128,256]{2,1,0:T(8,128)(2,1)S(1)}, u32[]{:S(2)}, u32[]{:S(2)}) collective-permute-start(bf16[2,128,256]{2,1,0:T(8,128)(2,1)} %get-tuple-element.16), channel_id=1, source_target_pairs={{0,8},{1,9},{2,10},{3,11},{4,12},{5,13},{6,14},{7,15},{8,16},{9,17... | collective-permute-start | bytes 393224 | tf_op jit(solution)/shard_map/ppermute | solution.py:29
  10.2 15.3 %collective-permute-start.6 = (bf16[2,128,256]{2,1,0:T(8,128)(2,1)}, bf16[2,128,256]{2,1,0:T(8,128)(2,1)S(1)}, u32[]{:S(2)}, u32[]{:S(2)}) collective-permute-start(bf16[2,128,256]{2,1,0:T(8,128)(2,1)} %get-tuple-element.17), channel_id=1, source_target_pairs={{0,16},{1,17},{2,18},{3,19},{4,20},{5,21},{6,22},{7,23},{8,24},{9,... | collective-permute-start | bytes 393224 | tf_op jit(solution)/shard_map/ppermute | solution.py:29
  15.6 13.1 %collective-permute-start.7 = (bf16[2,128,256]{2,1,0:T(8,128)(2,1)}, bf16[2,128,256]{2,1,0:T(8,128)(2,1)S(1)}, u32[]{:S(2)}, u32[]{:S(2)}) collective-permute-start(bf16[2,128,256]{2,1,0:T(8,128)(2,1)} %get-tuple-element.18), channel_id=1, source_target_pairs={{0,24},{1,25},{2,26},{3,27},{4,28},{5,29},{6,30},{7,31},{8,0},{9,1... | collective-permute-start | bytes 393224 | tf_op jit(solution)/shard_map/ppermute | solution.py:29
  18.3 13.3 %collective-permute-start.8 = (bf16[2,128,256]{2,1,0:T(8,128)(2,1)S(1)}, bf16[2,128,256]{2,1,0:T(8,128)(2,1)S(1)}, u32[]{:S(2)}, u32[]{:S(2)}) collective-permute-start(bf16[2,128,256]{2,1,0:T(8,128)(2,1)S(1)} %collective-permute-done.5.refs_4_), channel_id=1, source_target_pairs={{0,1},{1,0},{2,3},{3,2},{4,5},{5,4},{6,7},{7,6},{8,9},{9,8},{10,11... | collective-permute-start | bytes 393224 | tf_op jit(solution)/shard_map/ppermute | solution.py:29
  18.3 19.5 %collective-permute-start.11 = (bf16[256,512]{1,0:T(8,128)(2,1)}, bf16[256,512]{1,0:T(8,128)(2,1)}, u32[]{:S(2)}, u32[]{:S(2)}) collective-permute-start(bf16[256,512]{1,0:T(8,128)(2,1)} %refs_10_.1), channel_id=1, source_target_pairs={{0,32},{1,33},{2,34},{3,35},{4,36},{5,37},{6,38},{7,39},{8,40},{9,... | collective-permute-start | bytes 786440 | tf_op jit(solution)/shard_map/ppermute | solution.py:29
  25.5 14.0 %collective-permute-start.12 = (bf16[256,512]{1,0:T(8,128)(2,1)}, bf16[256,512]{1,0:T(8,128)(2,1)}, u32[]{:S(2)}, u32[]{:S(2)}) collective-permute-start(bf16[256,512]{1,0:T(8,128)(2,1)} %refs_10_.1), channel_id=1, source_target_pairs={{0,64},{1,65},{2,66},{3,67},{4,68},{5,69},{6,70},{7,71},{8,72},{9,... | collective-permute-start | bytes 786440 | tf_op jit(solution)/shard_map/ppermute | solution.py:29
  28.7 12.2 %collective-permute-start.13 = (bf16[256,512]{1,0:T(8,128)(2,1)}, bf16[256,512]{1,0:T(8,128)(2,1)}, u32[]{:S(2)}, u32[]{:S(2)}) collective-permute-start(bf16[256,512]{1,0:T(8,128)(2,1)} %refs_10_.1), channel_id=1, source_target_pairs={{0,96},{1,97},{2,98},{3,99},{4,100},{5,101},{6,102},{7,103},{8,104... | collective-permute-start | bytes 786440 | tf_op jit(solution)/shard_map/ppermute | solution.py:29
  31.6 3.6 %collective-permute-start.10 = (bf16[2,128,256]{2,1,0:T(8,128)(2,1)S(1)}, bf16[2,128,256]{2,1,0:T(8,128)(2,1)S(1)}, u32[]{:S(2)}, u32[]{:S(2)}) collective-permute-start(bf16[2,128,256]{2,1,0:T(8,128)(2,1)S(1)} %collective-permute-done.7.refs_6_), channel_id=1, source_target_pairs={{0,1},{1,0},{2,3},{3,2},{4,5},{5,4},{6,7},{7,6},{8,9},{9,8},{10,11... | collective-permute-start | bytes 393224 | tf_op jit(solution)/shard_map/ppermute | solution.py:29
  34.6 19.5 %collective-permute-start.3 = (f16[2,136,512]{2,1,0:T(8,128)(2,1)}, f16[2,136,512]{2,1,0:T(8,128)(2,1)S(1)}, u32[]{:S(2)}, u32[]{:S(2)}) collective-permute-start(f16[2,136,512]{2,1,0:T(8,128)(2,1)} %get-tuple-element.40), channel_id=1, source_target_pairs={{0,6},{1,7},{2,0},{3,1},{4,2},{5,3},{6,4},{7,5},{8,14},{9,15},{10,... | collective-permute-start | bytes 835592 | tf_op jit(solution)/shard_map/ppermute | solution.py:29
  35.2 22.7 %collective-permute-start.2 = (f16[2,136,512]{2,1,0:T(8,128)(2,1)S(1)}, f16[2,136,512]{2,1,0:T(8,128)(2,1)S(1)}, u32[]{:S(2)}, u32[]{:S(2)}) collective-permute-start(f16[2,136,512]{2,1,0:T(8,128)(2,1)S(1)} %get-tuple-element.41), channel_id=1, source_target_pairs={{0,4},{1,5},{2,6},{3,7},{4,0},{5,1},{6,2},{7,3},{8,12},{9,13},{10,... | collective-permute-start | bytes 835592 | tf_op jit(solution)/shard_map/ppermute | solution.py:29
  37.7 20.2 %collective-permute-start.1 = (f16[2,136,512]{2,1,0:T(8,128)(2,1)S(1)}, f16[2,136,512]{2,1,0:T(8,128)(2,1)}, u32[]{:S(2)}, u32[]{:S(2)}) collective-permute-start(f16[2,136,512]{2,1,0:T(8,128)(2,1)S(1)} %get-tuple-element.39), channel_id=1, source_target_pairs={{0,2},{1,3},{2,4},{3,5},{4,6},{5,7},{6,0},{7,1},{8,10},{9,11},{10,... | collective-permute-start | bytes 835592 | tf_op jit(solution)/shard_map/ppermute | solution.py:29
  45.9 13.5 %collective-permute-start.16 = (f16[128,512]{1,0:T(8,128)(2,1)S(1)}, f16[128,512]{1,0:T(8,128)(2,1)S(1)}, u32[]{:S(2)}, u32[]{:S(2)}) collective-permute-start(f16[128,512]{1,0:T(8,128)(2,1)S(1)} %get-tuple-element.46), channel_id=1, source_target_pairs={{0,8},{1,9},{2,10},{3,11},{4,12},{5,13},{6,14},{7,15},{8,16},{9,17... | collective-permute-start | bytes 393224 | tf_op jit(solution)/shard_map/ppermute | solution.py:29
  49.8 13.5 %collective-permute-start.15 = (f16[128,512]{1,0:T(8,128)(2,1)S(1)}, f16[128,512]{1,0:T(8,128)(2,1)S(1)}, u32[]{:S(2)}, u32[]{:S(2)}) collective-permute-start(f16[128,512]{1,0:T(8,128)(2,1)S(1)} %get-tuple-element.47), channel_id=1, source_target_pairs={{0,16},{1,17},{2,18},{3,19},{4,20},{5,21},{6,22},{7,23},{8,24},{9,... | collective-permute-start | bytes 393224 | tf_op jit(solution)/shard_map/ppermute | solution.py:29
  54.1 11.3 %collective-permute-start.14 = (f16[128,512]{1,0:T(8,128)(2,1)S(1)}, f16[128,512]{1,0:T(8,128)(2,1)S(1)}, u32[]{:S(2)}, u32[]{:S(2)}) collective-permute-start(f16[128,512]{1,0:T(8,128)(2,1)S(1)} %get-tuple-element.45), channel_id=1, source_target_pairs={{0,24},{1,25},{2,26},{3,27},{4,28},{5,29},{6,30},{7,31},{8,0},{9,1... | collective-permute-start | bytes 393224 | tf_op jit(solution)/shard_map/ppermute | solution.py:29
  59.3 7.4 %collective-permute-start.4 = (f16[136,512]{1,0:T(8,128)(2,1)S(1)}, f16[136,512]{1,0:T(8,128)(2,1)S(1)}, u32[]{:S(2)}, u32[]{:S(2)}) collective-permute-start(f16[136,512]{1,0:T(8,128)(2,1)S(1)} %fusion.17), channel_id=1, source_target_pairs={{0,128},{1,129},{2,130},{3,131},{4,132},{5,133},{6,134},{7,135},{8... | collective-permute-start | bytes 417800 | tf_op jit(solution)/shard_map/ppermute | solution.py:29
  67.4 3.7 %collective-permute-start.18 = (f32[5,128]{1,0:T(8,128)S(1)}, f32[5,128]{1,0:T(8,128)S(1)}, u32[]{:S(2)}, u32[]{:S(2)}) collective-permute-start(f32[5,128]{1,0:T(8,128)S(1)} %stack.38), channel_id=1, source_target_pairs={{0,2},{1,3},{2,0},{3,1},{4,6},{5,7},{6,4},{7,5},{8,10},{9,11},{10,... | collective-permute-start | bytes 7688 | tf_op jit(solution)/shard_map/ppermute | solution.py:29
  71.4 9.3 %collective-permute-start.23 = (bf16[128,512]{1,0:T(8,128)(2,1)S(1)}, bf16[128,512]{1,0:T(8,128)(2,1)S(1)}, u32[]{:S(2)}, u32[]{:S(2)}) collective-permute-start(bf16[128,512]{1,0:T(8,128)(2,1)S(1)} %subtract_convert_fusion.refs_0_), channel_id=1, source_target_pairs={{0,8},{1,9},{2,10},{3,11},{4,12},{5,13},{6,14},{7,15},{8,16},{9,17... | collective-permute-start | bytes 393224 | tf_op jit(solution)/shard_map/ppermute | solution.py:29
  73.6 14.4 %collective-permute-start.24 = (bf16[128,512]{1,0:T(8,128)(2,1)S(1)}, bf16[128,512]{1,0:T(8,128)(2,1)S(1)}, u32[]{:S(2)}, u32[]{:S(2)}) collective-permute-start(bf16[128,512]{1,0:T(8,128)(2,1)S(1)} %subtract_convert_fusion.refs_0_), channel_id=1, source_target_pairs={{0,16},{1,17},{2,18},{3,19},{4,20},{5,21},{6,22},{7,23},{8,24},{9,... | collective-permute-start | bytes 393224 | tf_op jit(solution)/shard_map/ppermute | solution.py:29
  76.8 11.2 %collective-permute-start.25 = (bf16[128,512]{1,0:T(8,128)(2,1)S(1)}, bf16[128,512]{1,0:T(8,128)(2,1)S(1)}, u32[]{:S(2)}, u32[]{:S(2)}) collective-permute-start(bf16[128,512]{1,0:T(8,128)(2,1)S(1)} %subtract_convert_fusion.refs_0_), channel_id=1, source_target_pairs={{0,24},{1,25},{2,26},{3,27},{4,28},{5,29},{6,30},{7,31},{8,0},{9,1... | collective-permute-start | bytes 393224 | tf_op jit(solution)/shard_map/ppermute | solution.py:29
  92.3 9.1 %collective-permute-start.26 = (f32[8,128,256]{2,1,0:T(8,128)}, f32[8,128,256]{2,1,0:T(8,128)S(1)}, u32[]{:S(2)}, u32[]{:S(2)}) collective-permute-start(f32[8,128,256]{2,1,0:T(8,128)} %get-tuple-element.23), channel_id=1, source_target_pairs={{0,1},{1,0},{2,3},{3,2},{4,5},{5,4},{6,7},{7,6},{8,9},{9,8},{10,11... | collective-permute-start | bytes 3145736 | tf_op jit(solution)/shard_map/ppermute | solution.py:29
  92.4 6.1 %collective-permute-start.22 = (f32[1,128]{1,0:T(1,128)S(1)}, f32[1,128]{1,0:T(1,128)S(1)}, u32[]{:S(2)}, u32[]{:S(2)}) collective-permute-start(f32[1,128]{1,0:T(1,128)S(1)} %bitcast_multiply_fusion), channel_id=1, source_target_pairs={{0,132},{1,133},{2,134},{3,135},{4,128},{5,129},{6,130},{7,131},{8... | collective-permute-start | bytes 1544 | tf_op jit(solution)/shard_map/ppermute | solution.py:29
  92.5 6.0 %collective-permute-start.21 = (f32[1,128]{1,0:T(1,128)S(1)}, f32[1,128]{1,0:T(1,128)S(1)}, u32[]{:S(2)}, u32[]{:S(2)}) collective-permute-start(f32[1,128]{1,0:T(1,128)S(1)} %bitcast_multiply_fusion), channel_id=1, source_target_pairs={{0,128},{1,129},{2,130},{3,131},{4,132},{5,133},{6,134},{7,135},{8... | collective-permute-start | bytes 1544 | tf_op jit(solution)/shard_map/ppermute | solution.py:29
  96.4 5.1 %collective-permute-start.20 = (f32[1,128]{1,0:T(1,128)S(1)}, f32[1,128]{1,0:T(1,128)S(1)}, u32[]{:S(2)}, u32[]{:S(2)}) collective-permute-start(f32[1,128]{1,0:T(1,128)S(1)} %bitcast_multiply_fusion), channel_id=1, source_target_pairs={{0,4},{1,5},{2,6},{3,7},{4,0},{5,1},{6,2},{7,3},{8,12},{9,13},{10,... | collective-permute-start | bytes 1544 | tf_op jit(solution)/shard_map/ppermute | solution.py:29
  102.7 11.9 %collective-permute-start.29 = (bf16[2,128,256]{2,1,0:T(8,128)(2,1)S(1)}, bf16[2,128,256]{2,1,0:T(8,128)(2,1)S(1)}, u32[]{:S(2)}, u32[]{:S(2)}) collective-permute-start(bf16[2,128,256]{2,1,0:T(8,128)(2,1)S(1)} %get-tuple-element.43), channel_id=1, source_target_pairs={{0,6},{1,7},{2,0},{3,1},{4,2},{5,3},{6,4},{7,5},{8,14},{9,15},{10,... | collective-permute-start | bytes 393224 | tf_op jit(solution)/shard_map/ppermute | solution.py:29
  104.5 11.0 %collective-permute-start.28 = (bf16[2,128,256]{2,1,0:T(8,128)(2,1)S(1)}, bf16[2,128,256]{2,1,0:T(8,128)(2,1)S(1)}, u32[]{:S(2)}, u32[]{:S(2)}) collective-permute-start(bf16[2,128,256]{2,1,0:T(8,128)(2,1)S(1)} %get-tuple-element.44), channel_id=1, source_target_pairs={{0,4},{1,5},{2,6},{3,7},{4,0},{5,1},{6,2},{7,3},{8,12},{9,13},{10,... | collective-permute-start | bytes 393224 | tf_op jit(solution)/shard_map/ppermute | solution.py:29
  104.7 10.8 %collective-permute-start.27 = (bf16[2,128,256]{2,1,0:T(8,128)(2,1)S(1)}, bf16[2,128,256]{2,1,0:T(8,128)(2,1)S(1)}, u32[]{:S(2)}, u32[]{:S(2)}) collective-permute-start(bf16[2,128,256]{2,1,0:T(8,128)(2,1)S(1)} %get-tuple-element.42), channel_id=1, source_target_pairs={{0,2},{1,3},{2,4},{3,5},{4,6},{5,7},{6,0},{7,1},{8,10},{9,11},{10,... | collective-permute-start | bytes 393224 | tf_op jit(solution)/shard_map/ppermute | solution.py:29
  110.1 13.9 %collective-permute-start.34 = (bf16[256,512]{1,0:T(8,128)(2,1)}, bf16[256,512]{1,0:T(8,128)(2,1)S(1)}, u32[]{:S(2)}, u32[]{:S(2)}) collective-permute-start(bf16[256,512]{1,0:T(8,128)(2,1)} %get-tuple-element.28), channel_id=1, source_target_pairs={{0,32},{1,33},{2,34},{3,35},{4,36},{5,37},{6,38},{7,39},{8,40},{9,... | collective-permute-start | bytes 786440 | tf_op jit(solution)/shard_map/ppermute | solution.py:29
  111.6 13.0 %collective-permute-start.33 = (bf16[256,512]{1,0:T(8,128)(2,1)}, bf16[256,512]{1,0:T(8,128)(2,1)S(1)}, u32[]{:S(2)}, u32[]{:S(2)}) collective-permute-start(bf16[256,512]{1,0:T(8,128)(2,1)} %get-tuple-element.27), channel_id=1, source_target_pairs={{0,64},{1,65},{2,66},{3,67},{4,68},{5,69},{6,70},{7,71},{8,72},{9,... | collective-permute-start | bytes 786440 | tf_op jit(solution)/shard_map/ppermute | solution.py:29
  114.6 10.0 %collective-permute-start.32 = (bf16[256,512]{1,0:T(8,128)(2,1)}, bf16[256,512]{1,0:T(8,128)(2,1)S(1)}, u32[]{:S(2)}, u32[]{:S(2)}) collective-permute-start(bf16[256,512]{1,0:T(8,128)(2,1)} %get-tuple-element.26), channel_id=1, source_target_pairs={{0,96},{1,97},{2,98},{3,99},{4,100},{5,101},{6,102},{7,103},{8,104... | collective-permute-start | bytes 786440 | tf_op jit(solution)/shard_map/ppermute | solution.py:29
  116.5 10.0 %collective-permute-start.31 = (bf16[128,256]{1,0:T(8,128)(2,1)S(1)}, bf16[128,256]{1,0:T(8,128)(2,1)S(1)}, u32[]{:S(2)}, u32[]{:S(2)}) collective-permute-start(bf16[128,256]{1,0:T(8,128)(2,1)S(1)} %get-tuple-element.49), channel_id=1, source_target_pairs={{0,128},{1,136},{2,144},{3,152},{4,132},{5,140},{6,148},{7,156},{8... | collective-permute-start | bytes 196616 | tf_op jit(solution)/shard_map/ppermute | solution.py:29
  118.4 11.0 %collective-permute-start.30 = (bf16[128,256]{1,0:T(8,128)(2,1)S(1)}, bf16[128,256]{1,0:T(8,128)(2,1)S(1)}, u32[]{:S(2)}, u32[]{:S(2)}) collective-permute-start(bf16[128,256]{1,0:T(8,128)(2,1)S(1)} %get-tuple-element.48), channel_id=1, source_target_pairs={{0,0},{1,8},{2,16},{3,24},{4,4},{5,12},{6,20},{7,28},{8,1},{9,9},{... | collective-permute-start | bytes 196616 | tf_op jit(solution)/shard_map/ppermute | solution.py:29
  (15 other events, 104.7 us)
